TPU v7x, 32 devices: a whole 2x2x4 slice. The times are simulated.
32 devices in a mesh: dp: 4 (over z), ctx: 4 (over y, core), tp: 2 (over x).
Axes of the slice: x: 2, y: 2, z: 4, core: 2. Of those that a mesh axis runs over, the one named last changes fastest.
Arguments:
- tokens_in: bfloat16 [12, 1024, 768], P('dp', 'ctx'), may hold values from -6 to 6
- block_ids: int32 [12, 1024], P('dp'), may hold values from 0 to 7, never falling along the last dimension, each value on 1 to 256 neighbouring positions
- rel_buckets: int32 [2047], replicated, may hold values from 0 to 31
- routes: int32 [12, 1024, 2], P('dp', 'ctx'), may hold values from 0 to 7, all different within a row; in each aligned block of 256 rows (0 to 255, 256 to 511, ..., all dimensions but the last counted through in order) at most 128 rows name the same one
- attn_gain: bfloat16 [1, 768], P(None, 'dp'), may hold values from 0.25 to 1.75
- w_qkv: bfloat16 [1, 3, 768, 768], P(None, None, 'dp', 'tp'), may hold values from -0.21875 to 0.21875
- w_attn_out: bfloat16 [1, 768, 768], P(None, 'tp', 'dp'), may hold values from -0.4375 to 0.4375
- bias_table: bfloat16 [1, 32, 12], P(None, 'dp', 'tp'), may hold values from -4 to 4
- moe_gain: bfloat16 [1, 768], P(None, 'dp'), may hold values from 0.25 to 1.75
- w_router: bfloat16 [1, 768, 8], P(None, 'dp'), may hold values from -0.15625 to 0.15625
- w_expert_in: bfloat16 [1, 8, 768, 3072], P(None, 'dp', 'ctx', 'tp'), may hold values from -0.21875 to 0.21875
- w_expert_out: bfloat16 [1, 8, 3072, 768], P(None, 'dp', 'tp', 'ctx'), may hold values from -0.21875 to 0.21875
- cotangent: bfloat16 [12, 1024, 768], P('dp', 'ctx'), may hold values from -6 to 6
Outputs:
- tokens_out: bfloat16 [12, 1024, 768], P('dp', 'ctx')
- grad_tokens: float32 [12, 1024, 768], P('dp', 'ctx')
- grad_attn_gain: float32 [1, 768], P(None, 'dp')
- grad_qkv: float32 [1, 3, 768, 768], P(None, None, 'dp', 'tp')
- grad_attn_out: float32 [1, 768, 768], P(None, 'tp', 'dp')
- grad_bias_table: float32 [1, 32, 12], P(None, 'dp', 'tp')
- grad_moe_gain: float32 [1, 768], P(None, 'dp')
- grad_router: float32 [1, 768, 8], P(None, 'dp')
- grad_expert_in: float32 [1, 8, 768, 3072], P(None, 'dp', 'ctx', 'tp')
- grad_expert_out: float32 [1, 8, 3072, 768], P(None, 'dp', 'tp', 'ctx')
Inputs may be any that keep to these rules, and one draw needn't show every extreme that they name: `routes`: in each aligned block of 256 rows (one piece of one sequence), every row names 2 different experts, no expert is named by more than 128 rows, and in some or all blocks one expert is named by exactly 128 rows; every expert is named somewhere. `block_ids`: along each sequence the block numbers start at 0, never fall and rise by at most one; every block holds 1 to 256 tokens and one holds exactly 256.
All inputs are finite; a program needn't handle non-finite values.
Results may differ from a plain program's by a relative error of at most 0.015.
Values may be sent and summed in bfloat16 or wider, within the bound.
A program may use at most 256 MiB of HBM per device.

v0:
```python
import jax
import jax.numpy as jnp
from jax import lax
from jax.sharding import PartitionSpec as P

HD = 64
NB = 32


EPSILON = 1e-06
FULL_PRECISION = lax.Precision.HIGHEST
MASKED_SCORE = -1e30


def norm_rows(value_matrix, gain):
    factor = lax.rsqrt(jnp.mean(value_matrix * value_matrix, axis=-1, keepdims=True) + EPSILON)
    return value_matrix * factor * gain


def expand_bias(rel_bias, offset, row_count, col_count):
    head_count, span_len = rel_bias.shape
    seq_len = (span_len + 1) // 2
    band_len = row_count + col_count - 1
    window = lax.dynamic_slice_in_dim(rel_bias, offset - col_count + seq_len, band_len, 1)
    tiled = jnp.broadcast_to(window[:, None, :], (head_count, row_count, band_len)).reshape(
        head_count, row_count * band_len
    )
    padded = jnp.pad(tiled, ((0, 0), (0, row_count)))
    skewed = padded.reshape(head_count, row_count, band_len + 1)[:, :, :col_count]
    return skewed[:, :, ::-1]


def diagonal_sums(dscores, offset, rel_grad):
    head_count, row_count, col_count = dscores.shape
    seq_len = (rel_grad.shape[1] + 1) // 2
    band_len = row_count + col_count - 1
    padded = jnp.pad(dscores[:, :, ::-1], ((0, 0), (0, 0), (0, row_count)))
    skewed = padded.reshape(head_count, row_count * (col_count + row_count))[
        :, : row_count * band_len
    ].reshape(head_count, row_count, band_len)
    anchor = offset - col_count + seq_len
    current = lax.dynamic_slice_in_dim(rel_grad, anchor, band_len, 1)
    return lax.dynamic_update_slice_in_dim(rel_grad, current + jnp.sum(skewed, axis=1), anchor, 1)


def score_block(queries, key_rows, rel_bias, offset, ids_query, ids_key, score_scale):
    raw_scores = (
        jnp.einsum("qhd,khd->hqk", queries, key_rows, preferred_element_type=jnp.float32)
        * score_scale
    )
    scores = raw_scores + expand_bias(rel_bias, offset, queries.shape[0], key_rows.shape[0])
    visible = ids_key[None, :] <= ids_query[:, None]
    return (scores, visible)


def block_width(stretch_len, seq_len):
    return min(seq_len, max(stretch_len, 512))


def attend(queries, key_rows, value_rows, rel_bias, ids_all, q_start, score_scale):
    stretch_len, head_count, head_dim = queries.shape
    seq_len = key_rows.shape[0]
    key_block = block_width(stretch_len, seq_len)
    ids_query = lax.dynamic_slice_in_dim(ids_all, q_start, stretch_len)
    pieces = seq_len // key_block
    running_max = jnp.full((head_count, stretch_len), MASKED_SCORE, jnp.float32)
    running_sum = jnp.zeros((head_count, stretch_len), jnp.float32)
    for piece_index in range(pieces):
        key_start = piece_index * key_block
        scores, visible = score_block(
            queries,
            key_rows[key_start : key_start + key_block],
            rel_bias,
            q_start - key_start,
            ids_query,
            ids_all[key_start : key_start + key_block],
            score_scale,
        )
        masked = jnp.where(visible[None], scores, MASKED_SCORE)
        new_max = jnp.maximum(running_max, jnp.max(masked, axis=-1))
        weights = jnp.where(visible[None], jnp.exp(masked - new_max[:, :, None]), 0.0)
        running_sum = running_sum * jnp.exp(running_max - new_max) + jnp.sum(weights, axis=-1)
        running_max = new_max
    log_total = running_max + jnp.log(running_sum)
    output = jnp.zeros((stretch_len, head_count, head_dim), jnp.float32)
    for piece_index in range(pieces):
        key_start = piece_index * key_block
        scores, visible = score_block(
            queries,
            key_rows[key_start : key_start + key_block],
            rel_bias,
            q_start - key_start,
            ids_query,
            ids_all[key_start : key_start + key_block],
            score_scale,
        )
        prob_low = jnp.where(visible[None], jnp.exp(scores - log_total[:, :, None]), 0.0).astype(
            jnp.bfloat16
        )
        output = output + jnp.einsum(
            "hqk,khd->qhd",
            prob_low,
            value_rows[key_start : key_start + key_block],
            preferred_element_type=jnp.float32,
        )
    return (output.astype(jnp.bfloat16), log_total)


def attend_back(
    queries, key_rows, value_rows, grad_out, log_total, rel_bias, ids_all, q_start, score_scale
):
    stretch_len, head_count, head_dim = queries.shape
    seq_len = key_rows.shape[0]
    key_block = block_width(stretch_len, seq_len)
    ids_query = lax.dynamic_slice_in_dim(ids_all, q_start, stretch_len)
    pieces = seq_len // key_block

    def block_terms(piece_index):
        key_start = piece_index * key_block
        scores, visible = score_block(
            queries,
            key_rows[key_start : key_start + key_block],
            rel_bias,
            q_start - key_start,
            ids_query,
            ids_all[key_start : key_start + key_block],
            score_scale,
        )
        probs = jnp.where(visible[None], jnp.exp(scores - log_total[:, :, None]), 0.0)
        dprobs = jnp.einsum(
            "qhd,khd->hqk",
            grad_out,
            value_rows[key_start : key_start + key_block],
            preferred_element_type=jnp.float32,
        )
        return (key_start, probs, dprobs)

    row_delta = jnp.zeros((head_count, stretch_len), jnp.float32)
    for piece_index in range(pieces):
        key_start, probs, dprobs = block_terms(piece_index)
        row_delta = row_delta + jnp.sum(probs * dprobs, axis=-1)
    rel_grad = jnp.zeros(rel_bias.shape, jnp.float32)
    grad_query = jnp.zeros((stretch_len, head_count, head_dim), jnp.float32)
    key_grads = []
    value_grads = []
    for piece_index in range(pieces):
        key_start, probs, dprobs = block_terms(piece_index)
        dscores = probs * (dprobs - row_delta[:, :, None])
        rel_grad = diagonal_sums(dscores, q_start - key_start, rel_grad)
        dscores_low = dscores.astype(jnp.bfloat16)
        grad_query = (
            grad_query
            + jnp.einsum(
                "hqk,khd->qhd",
                dscores_low,
                key_rows[key_start : key_start + key_block],
                preferred_element_type=jnp.float32,
            )
            * score_scale
        )
        key_grads.append(
            jnp.einsum("hqk,qhd->khd", dscores_low, queries, preferred_element_type=jnp.float32)
            * score_scale
        )
        value_grads.append(
            jnp.einsum(
                "hqk,qhd->khd",
                probs.astype(jnp.bfloat16),
                grad_out,
                preferred_element_type=jnp.float32,
            )
        )
    return (
        grad_query,
        jnp.concatenate(key_grads, axis=0),
        jnp.concatenate(value_grads, axis=0),
        rel_grad,
    )


def to_experts(slots_out):
    return lax.all_to_all(slots_out, "dp", split_axis=0, concat_axis=2, tiled=True)[0]


def from_experts(slots_back):
    return lax.all_to_all(slots_back[None], "dp", split_axis=2, concat_axis=0, tiled=True)


def on_device(
    tokens_in,
    block_ids,
    rel_buckets,
    routes,
    attn_gain,
    w_qkv,
    w_attn_out,
    bias_table,
    moe_gain,
    w_router,
    w_expert_in,
    w_expert_out,
    cotangent,
):
    seq_count, stretch_len, model_width = tokens_in.shape
    row_count = seq_count * stretch_len
    layer_count = w_qkv.shape[0]
    expert_count = w_router.shape[2]
    local_experts = w_expert_in.shape[1]
    choice_count = routes.shape[2]
    dp_count = lax.axis_size("dp")
    slot_count = seq_count * max(2, 2 * stretch_len * choice_count // expert_count)
    head_dim = HD
    score_scale = HD ** (-0.5)
    q_start = lax.axis_index("ctx") * stretch_len
    bucket_table = (rel_buckets[:, None] == jnp.arange(NB, dtype=jnp.int32)[None, :]).astype(
        jnp.float32
    )
    flat_routes = routes.reshape(row_count * choice_count)
    route_hits = flat_routes[:, None] == jnp.arange(expert_count, dtype=jnp.int32)[None, :]
    hit_counts = route_hits.astype(jnp.int32)
    rank = jnp.sum(jnp.cumsum(hit_counts, axis=0) * hit_counts, axis=1) - 1
    slot = flat_routes * slot_count + rank
    source_row = jnp.arange(row_count * choice_count, dtype=jnp.int32) // choice_count
    pick = route_hits.reshape(row_count, choice_count, expert_count)
    residual = tokens_in.astype(jnp.float32).reshape(row_count, model_width)
    layer_index = 0
    gain_attn = lax.all_gather(attn_gain[layer_index], "dp", axis=0, tiled=True)
    wqkv_full = lax.all_gather(w_qkv[layer_index], "dp", axis=1, tiled=True)
    wout_full = lax.all_gather(w_attn_out[layer_index], "dp", axis=1, tiled=True)
    table_full = lax.all_gather(bias_table[layer_index], "dp", axis=0, tiled=True)
    gain_moe = lax.all_gather(moe_gain[layer_index], "dp", axis=0, tiled=True)
    router_full = lax.all_gather(w_router[layer_index], "dp", axis=0, tiled=True)
    gain_attn = gain_attn.astype(jnp.float32)
    gain_moe = gain_moe.astype(jnp.float32)
    normalized_input = norm_rows(residual, gain_attn).astype(jnp.bfloat16)
    output_projection = jnp.einsum(
        "rd,jde->jre", normalized_input, wqkv_full, preferred_element_type=jnp.float32
    ).astype(jnp.bfloat16)
    local_width = output_projection.shape[2]
    head_count = local_width // head_dim
    queries = output_projection[0].reshape(seq_count, stretch_len, head_count, head_dim)
    keys_all = lax.all_gather(
        output_projection[1].reshape(seq_count, stretch_len, local_width), "ctx", axis=1, tiled=True
    )
    values_all = lax.all_gather(
        output_projection[2].reshape(seq_count, stretch_len, local_width), "ctx", axis=1, tiled=True
    )
    seq_len = keys_all.shape[1]
    keys_all = keys_all.reshape(seq_count, seq_len, head_count, head_dim)
    values_all = values_all.reshape(seq_count, seq_len, head_count, head_dim)
    rel_bias = jnp.einsum(
        "rb,bh->hr", bucket_table, table_full.astype(jnp.float32), precision=FULL_PRECISION
    )
    attended_list = []
    lse_list = []
    for seq_index in range(seq_count):
        attended_seq, lse_seq = attend(
            queries[seq_index],
            keys_all[seq_index],
            values_all[seq_index],
            rel_bias,
            block_ids[seq_index],
            q_start,
            score_scale,
        )
        attended_list.append(attended_seq)
        lse_list.append(lse_seq)
    attention_output = jnp.stack(attended_list).reshape(row_count, local_width)
    attn_part = jnp.dot(attention_output, wout_full, preferred_element_type=jnp.float32)
    middle_activation = residual + lax.psum(attn_part, "tp")
    moe_in = norm_rows(middle_activation, gain_moe).astype(jnp.bfloat16)
    logits = jnp.dot(moe_in, router_full, preferred_element_type=jnp.float32)
    picked = jnp.sum(jnp.where(pick, logits[:, None, :], 0.0), axis=-1)
    gates = jax.nn.softmax(picked, axis=-1)
    outgoing = (
        jnp.zeros((expert_count * slot_count, model_width), jnp.bfloat16)
        .at[slot]
        .set(moe_in[source_row])
    )
    received = to_experts(outgoing.reshape(dp_count, local_experts, slot_count, model_width))
    expert_in = lax.all_gather(w_expert_in[layer_index], "ctx", axis=1, tiled=True)
    expert_out = lax.all_gather(w_expert_out[layer_index], "ctx", axis=2, tiled=True)
    pre_act = jnp.einsum("emd,edf->emf", received, expert_in, preferred_element_type=jnp.float32)
    hidden = jax.nn.gelu(pre_act).astype(jnp.bfloat16)
    partial_value = jnp.einsum(
        "emf,efd->emd", hidden, expert_out, preferred_element_type=jnp.float32
    ).astype(jnp.bfloat16)
    returned = from_experts(partial_value).reshape(expert_count * slot_count, model_width)
    routed = returned[slot].reshape(row_count, choice_count, model_width)
    combined = jnp.sum(gates[:, :, None] * routed.astype(jnp.float32), axis=1)
    saved = [
        (
            residual,
            normalized_input,
            queries,
            keys_all,
            values_all,
            rel_bias,
            attention_output,
            jnp.stack(lse_list),
            middle_activation,
            moe_in,
            gates,
            received,
            expert_in,
            expert_out,
            pre_act,
            routed,
            gain_attn,
            gain_moe,
            wqkv_full,
            wout_full,
            router_full,
        )
    ]
    residual = middle_activation + lax.psum(combined, "tp")
    tokens_out = residual.astype(jnp.bfloat16).reshape(seq_count, stretch_len, model_width)
    gradient = cotangent.astype(jnp.float32).reshape(row_count, model_width)
    layer_grads = [None] * layer_count
    for layer_index in reversed(range(layer_count)):
        (
            residual_in,
            normalized_input,
            queries,
            keys_all,
            values_all,
            rel_bias,
            attention_output,
            lse_all,
            middle_activation,
            moe_in,
            gates,
            received,
            expert_in,
            expert_out,
            pre_act,
            routed,
            gain_attn,
            gain_moe,
            wqkv_full,
            wout_full,
            router_full,
        ) = saved[layer_index]
        seq_len = keys_all.shape[1]
        head_count = queries.shape[2]
        local_width = head_count * head_dim
        grad_slots = (
            (gates[:, :, None] * gradient[:, None, :])
            .astype(jnp.bfloat16)
            .reshape(row_count * choice_count, model_width)
        )
        outgoing = (
            jnp.zeros((expert_count * slot_count, model_width), jnp.bfloat16)
            .at[slot]
            .set(grad_slots)
        )
        grad_received = to_experts(
            outgoing.reshape(dp_count, local_experts, slot_count, model_width)
        )
        hidden = jax.nn.gelu(pre_act).astype(jnp.bfloat16)
        grad_wexp_out = jnp.einsum(
            "emf,emd->efd", hidden, grad_received, preferred_element_type=jnp.float32
        )
        grad_hidden = jnp.einsum(
            "emd,efd->emf", grad_received, expert_out, preferred_element_type=jnp.float32
        )
        gelu_back = jax.vjp(jax.nn.gelu, pre_act)[1]
        grad_pre = gelu_back(grad_hidden)[0].astype(jnp.bfloat16)
        grad_wexp_in = jnp.einsum(
            "emd,emf->edf", received, grad_pre, preferred_element_type=jnp.float32
        )
        grad_inputs = jnp.einsum(
            "emf,edf->emd", grad_pre, expert_in, preferred_element_type=jnp.float32
        ).astype(jnp.bfloat16)
        came_back = from_experts(grad_inputs).reshape(expert_count * slot_count, model_width)
        grad_moe_part = jnp.sum(
            came_back[slot].reshape(row_count, choice_count, model_width).astype(jnp.float32),
            axis=1,
        )
        grad_gate_part = jnp.sum(gradient[:, None, :] * routed.astype(jnp.float32), axis=-1)
        grad_moe_in, grad_gates = lax.psum((grad_moe_part, grad_gate_part), "tp")
        grad_wexp_in, grad_wexp_out = (
            lax.psum_scatter(grad_wexp_in, "ctx", scatter_dimension=1, tiled=True),
            lax.psum_scatter(grad_wexp_out, "ctx", scatter_dimension=2, tiled=True),
        )
        grad_picked = gates * (grad_gates - jnp.sum(gates * grad_gates, axis=-1, keepdims=True))
        grad_logits = jnp.sum(jnp.where(pick, grad_picked[:, :, None], 0.0), axis=1)
        grad_moe_in = grad_moe_in + jnp.einsum(
            "re,de->rd", grad_logits, router_full.astype(jnp.float32), precision=FULL_PRECISION
        )
        grad_router = jnp.einsum(
            "rd,re->de", moe_in.astype(jnp.float32), grad_logits, precision=FULL_PRECISION
        )
        moe_norm_back = jax.vjp(norm_rows, middle_activation, gain_moe)[1]
        grad_middle, grad_gain_moe = moe_norm_back(grad_moe_in)
        gradient = gradient + grad_middle
        grad_low = gradient.astype(jnp.bfloat16)
        grad_wout = jnp.einsum(
            "re,rd->ed", attention_output, grad_low, preferred_element_type=jnp.float32
        )
        grad_attended = (
            jnp.einsum("rd,ed->re", grad_low, wout_full, preferred_element_type=jnp.float32)
            .astype(jnp.bfloat16)
            .reshape(seq_count, stretch_len, head_count, head_dim)
        )
        rel_grad = jnp.zeros(rel_bias.shape, jnp.float32)
        query_grads = []
        key_grads = []
        value_grads = []
        for seq_index in range(seq_count):
            grad_query, grad_key, grad_value, grad_rel = attend_back(
                queries[seq_index],
                keys_all[seq_index],
                values_all[seq_index],
                grad_attended[seq_index],
                lse_all[seq_index],
                rel_bias,
                block_ids[seq_index],
                q_start,
                score_scale,
            )
            query_grads.append(grad_query)
            key_grads.append(grad_key)
            value_grads.append(grad_value)
            rel_grad = rel_grad + grad_rel
        grad_keys_all = jnp.stack(key_grads).reshape(seq_count, seq_len, local_width)
        grad_values_all = jnp.stack(value_grads).reshape(seq_count, seq_len, local_width)
        grad_keys, grad_values = (
            lax.psum_scatter(grad_keys_all, "ctx", scatter_dimension=1, tiled=True),
            lax.psum_scatter(grad_values_all, "ctx", scatter_dimension=1, tiled=True),
        )
        grad_proj = jnp.stack(
            [
                jnp.stack(query_grads).reshape(row_count, local_width),
                grad_keys.reshape(row_count, local_width),
                grad_values.reshape(row_count, local_width),
            ]
        ).astype(jnp.bfloat16)
        grad_wqkv = jnp.einsum(
            "rd,jre->jde", normalized_input, grad_proj, preferred_element_type=jnp.float32
        )
        grad_normed = lax.psum(
            jnp.einsum("jre,jde->rd", grad_proj, wqkv_full, preferred_element_type=jnp.float32),
            "tp",
        )
        attn_norm_back = jax.vjp(norm_rows, residual_in, gain_attn)[1]
        grad_residual, grad_gain_attn = attn_norm_back(grad_normed)
        gradient = gradient + grad_residual
        grad_table = jnp.einsum("rb,hr->bh", bucket_table, rel_grad, precision=FULL_PRECISION)
        part_gain_attn, part_wqkv, part_wout, part_table, part_gain_moe, part_router = (
            lax.psum_scatter(grad_gain_attn, "dp", scatter_dimension=0, tiled=True),
            lax.psum_scatter(grad_wqkv, "dp", scatter_dimension=1, tiled=True),
            lax.psum_scatter(grad_wout, "dp", scatter_dimension=1, tiled=True),
            lax.psum_scatter(grad_table, "dp", scatter_dimension=0, tiled=True),
            lax.psum_scatter(grad_gain_moe, "dp", scatter_dimension=0, tiled=True),
            lax.psum_scatter(grad_router, "dp", scatter_dimension=0, tiled=True),
        )
        summed = lax.psum(
            (part_gain_attn, part_wqkv, part_wout, part_table, part_gain_moe, part_router), "ctx"
        )
        layer_grads[layer_index] = tuple(summed) + (grad_wexp_in, grad_wexp_out)
    stacked = [jnp.stack([layer_grads[0][member]]) for member in range(8)]
    grad_tokens = gradient.reshape(seq_count, stretch_len, model_width)
    return (
        tokens_out,
        grad_tokens,
        stacked[0],
        stacked[1],
        stacked[2],
        stacked[3],
        stacked[4],
        stacked[5],
        stacked[6],
        stacked[7],
    )


def solution(mesh):
    return jax.shard_map(
        on_device,
        mesh=mesh,
        in_specs=(
            P("dp", "ctx", None),
            P("dp", None),
            P(),
            P("dp", "ctx", None),
            P(None, "dp"),
            P(None, None, "dp", "tp"),
            P(None, "tp", "dp"),
            P(None, "dp", "tp"),
            P(None, "dp"),
            P(None, "dp", None),
            P(None, "dp", "ctx", "tp"),
            P(None, "dp", "tp", "ctx"),
            P("dp", "ctx", None),
        ),
        out_specs=(
            P("dp", "ctx", None),
            P("dp", "ctx", None),
            P(None, "dp"),
            P(None, None, "dp", "tp"),
            P(None, "tp", "dp"),
            P(None, "dp", "tp"),
            P(None, "dp"),
            P(None, "dp", None),
            P(None, "dp", "ctx", "tp"),
            P(None, "dp", "tp", "ctx"),
        ),
        check_vma=False,
    )
```

profile of v0, /device:TPU:0, one launch (start us, length us, event | category | flops | bytes accessed | tf_op | source)
XLA Modules:
  0.0 1509.3 jit_solution(3612196626915728315)
XLA Ops:
  11.8 13.7 all-reduce.17
  29.9 22.7 %all-gather.18.cloned.1.call-done = bf16[1,3,768,384]{3,2,1,0:T(8,128)(2,1)} async-done(((bf16[1,3,192,384]{3,2,1,0:T(8,128)(2,1)}), bf16[1,3,768,384]{3,2,1,0:T(8,128)(2,1)}) %all-gather.18.cloned.1.call-update) | async-done | bytes 1769488 | tf_op jit(solution)/shard_map/all_gather | solution.py:228
  59.3 12.1 all-gather.2
  74.7 8.9 reshape.707
  90.3 22.4 %rev.16 = f32[6,256,512]{2,1,0:T(8,128)S(1)} reverse(f32[6,256,512]{2,1,0:T(8,128)} %slice.367), dimensions={2} | reverse | bytes 6291456 | tf_op jit(solution)/shard_map/rev | solution.py:30
  115.2 8.9 reshape.709
  130.8 26.1 %rev.17 = f32[6,256,512]{2,1,0:T(8,128)} reverse(f32[6,256,512]{2,1,0:T(8,128)} %slice.369), dimensions={2} | reverse | bytes 6291456 | tf_op jit(solution)/shard_map/rev | solution.py:30
  156.9 16.1 %all-gather.3 = bf16[1,384,768]{1,2,0:T(8,128)(2,1)} all-gather(bf16[1,384,192]{1,2,0:T(8,128)(2,1)S(1)} %copy-done.116), channel_id=5, replica_groups=mesh['dp'=4,'ctx'=4,'tp'=2] {'dp'}, dimensions={2}, use_global_device_ids=true | all-gather | bytes 737280 | tf_op jit(solution)/shard_map/all_gather | solution.py:229
  234.0 63.3 %all-reduce.23.cloned.1.call-done = f32[768,768]{1,0:T(8,128)} async-done(((f32[768,768]{1,0:T(8,128)}), f32[768,768]{1,0:T(8,128)}) %all-reduce.23.cloned.1.call-update) | async-done | bytes 2359312 | tf_op jit(solution)/shard_map/psum | solution.py:270
  301.0 19.7 %scatter_custom_fusion = bf16[3072,768]{1,0:T(8,128)(2,1)} fusion(s32[1536]{0:T(1024)S(1)} %fusion.121, bf16[768,768]{1,0:T(8,128)(2,1)S(1)} %multiply_convert_fusion.3, s32[2048]{0:T(1024)S(1)} %pad_clamp_fusion.1, bf16[]{:T(256)} %constant.83.clone.1), kind=kCustom, calls=%fused_computation.89 | custom fusion | bytes 4718594 | tf_op jit(solution)/shard_map/scatter | solution.py:278
  320.7 5.1 all-to-all-start
  329.0 110.3 %all-gather.5 = bf16[1,768,8]{2,0,1:T(2,128)(2,1)S(1)} all-gather(bf16[1,192,8]{2,0,1:T(2,128)(2,1)S(1)} %copy.215), channel_id=7, replica_groups=mesh['dp'=4,'ctx'=4,'tp'=2] {'dp'}, dimensions={1}, use_global_device_ids=true | all-gather | bytes 15360 | tf_op jit(solution)/shard_map/all_gather | solution.py:232
  442.9 6.9 mul.403
  452.0 11.7 scatter_custom_fusion.1
  463.7 4.9 all-to-all-start.2
  469.2 12.7 copy.223
  481.9 4.8 copy.221
  486.7 83.6 %all-to-all-done.2 = bf16[4,2,384,768]{3,2,1,0:T(8,128)(2,1)} async-done(((bf16[4,2,384,768]{3,2,1,0:T(8,128)(2,1)}), bf16[4,2,384,768]{3,2,1,0:T(8,128)(2,1)}, u32[]{:S(2)}, u32[]{:S(2)}) %all-to-all-start.2) | async-done | bytes 4718624 | tf_op jit(solution)/shard_map/all_to_all | solution.py:182
  570.3 4.9 copy.227
  575.3 14.4 fusion.12
  589.7 21.2 %fusion.6 = bf16[2,1536,1536]{2,1,0:T(8,128)(2,1)} fusion(f32[2,1536,1536]{2,1,0:T(8,128)} %fusion.12, bf16[2,1536,768]{2,1,0:T(8,128)(2,1)S(1)} %bitcast.360, bf16[1,2,1536,768]{3,2,1,0:T(8,128)(2,1)S(1)} %bitcast.364), kind=kOutput, calls=%fused_computation.13 | convolution fusion | flops 7342129152 | bytes 37748736 | tf_op jit(solution)/shard_map/emd,efd->emf/dot_general | solution.py:364
  610.9 11.6 convert_bitcast_fusion
  622.6 34.0 %copy.228 = bf16[1,2,1536,768]{3,1,0,2:T(2,128)(2,1)} copy(bf16[1,2,1536,768]{3,2,1,0:T(8,128)(2,1)S(1)} %convert_bitcast_fusion) | data formatting | bytes 9437184 | tf_op jit(solution)/shard_map/broadcast_in_dim | solution.py:186
  656.6 5.0 all-to-all-start.3
  661.5 13.8 convert_bitcast_fusion.1
  675.4 33.8 %copy.224 = bf16[1,2,1536,768]{3,1,0,2:T(2,128)(2,1)} copy(bf16[1,2,1536,768]{3,2,1,0:T(8,128)(2,1)S(1)} %convert_bitcast_fusion.1) | data formatting | bytes 9437184 | tf_op jit(solution)/shard_map/broadcast_in_dim | solution.py:186
  709.2 56.4 %all-to-all-done.3 = bf16[1,2,1536,768]{3,1,0,2:T(2,128)(2,1)} async-done(((bf16[1,2,1536,768]{3,1,0,2:T(2,128)(2,1)}), bf16[1,2,1536,768]{3,1,0,2:T(2,128)(2,1)}, u32[]{:S(2)}, u32[]{:S(2)}) %all-to-all-start.3) | async-done | bytes 4718624 | tf_op jit(solution)/shard_map/all_to_all | solution.py:186
  765.5 5.4 all-to-all-start.1
  771.0 5.1 copy.229
  776.1 9.0 gather_fusion.1
  785.2 3.8 reshape.736
  789.0 9.4 reduce_sum.324
  800.2 74.7 %all-to-all-done.1 = bf16[1,2,1536,768]{3,1,0,2:T(2,128)(2,1)} async-done(((bf16[1,2,1536,768]{3,1,0,2:T(2,128)(2,1)}), bf16[1,2,1536,768]{3,1,0,2:T(2,128)(2,1)}, u32[]{:S(2)}, u32[]{:S(2)}) %all-to-all-start.1) | async-done | bytes 4718624 | tf_op jit(solution)/shard_map/all_to_all | solution.py:186
  874.9 5.2 copy.225
  880.1 9.0 gather_fusion
  889.2 3.9 reshape.733
  893.0 13.8 multiply_reduce_fusion
  908.6 5.9 psum.80
  917.3 3.9 multiply_reduce_fusion.8
  938.9 4.5 multiply_reduce_fusion.2
  995.0 37.9 %reduce-scatter.12.cloned.1.call-done = f32[3,256,384]{1,2,0:T(8,128)} async-done(((f32[3,1024,384]{1,2,0:T(8,128)}), f32[3,256,384]{1,2,0:T(8,128)}) %reduce-scatter.12.cloned.1.call-update) | async-done | bytes 1179664 | tf_op jit(solution)/shard_map/reduce_scatter | solution.py:429
  1037.2 5.3 convolution_bitcast_fusion
  1042.5 6.3 copy.248
  1048.8 4.4 copy.257
  1053.3 3.7 fusion.90
  1060.5 5.2 fusion.44
  1065.7 54.2 %reduce-scatter.22.cloned.1.call-done = f32[192,1152]{1,0:T(8,128)} async-done(((f32[768,1152]{1,0:T(8,128)}), f32[192,1152]{1,0:T(8,128)}) %reduce-scatter.22.cloned.1.call-update) | async-done | bytes 884752
  1124.6 27.7 %reduce-scatter.16.cloned.1.call-done = f32[384,192]{0,1:T(8,128)} async-done(((f32[384,768]{0,1:T(8,128)}), f32[384,192]{0,1:T(8,128)}) %reduce-scatter.16.cloned.1.call-update) | async-done | bytes 294928 | tf_op jit(solution)/shard_map/reduce_scatter | solution.py:453
  1152.5 14.3 fusion.156
  1166.9 17.1 %fusion.143 = f32[2,1536,768]{1,2,0:T(8,128)} fusion(bf16[2,1536,768]{2,1,0:T(8,128)(2,1)} %bitcast.359, f32[2,1536,1536]{2,1,0:T(8,128)} %fusion.12), kind=kOutput, calls=%fused_computation.271 | convolution fusion | flops 7290224640 | bytes 33030144 | tf_op jit(solution)/shard_map/emf,emd->efd/dot_general | solution.py:361
  1186.9 26.0 %rev.22 = f32[6,256,512]{2,1,0:T(8,128)} reverse(f32[6,256,512]{2,1,0:T(8,128)} %copy-done.23), dimensions={2} | reverse | bytes 6291456 | tf_op jit(solution)/shard_map/rev | solution.py:37
  1212.9 17.6 %rev.23 = f32[6,256,512]{2,1,0:T(8,128)} reverse(f32[6,256,512]{2,1,0:T(8,128)S(1)} %copy-done.22), dimensions={2} | reverse | bytes 6291456 | tf_op jit(solution)/shard_map/rev | solution.py:37
  1230.5 26.2 %rev.18 = f32[6,256,512]{2,1,0:T(8,128)} reverse(f32[6,256,512]{2,1,0:T(8,128)} %copy-done.32), dimensions={2} | reverse | bytes 6291456 | tf_op jit(solution)/shard_map/rev | solution.py:37
  1256.7 17.6 %rev.19 = f32[6,256,512]{2,1,0:T(8,128)} reverse(f32[6,256,512]{2,1,0:T(8,128)S(1)} %copy-done.31), dimensions={2} | reverse | bytes 6291456 | tf_op jit(solution)/shard_map/rev | solution.py:37
  1274.2 26.1 %rev.20 = f32[6,256,512]{2,1,0:T(8,128)} reverse(f32[6,256,512]{2,1,0:T(8,128)} %copy-done.27), dimensions={2} | reverse | bytes 6291456 | tf_op jit(solution)/shard_map/rev | solution.py:37
  1300.4 17.5 %rev.21 = f32[6,256,512]{2,1,0:T(8,128)} reverse(f32[6,256,512]{2,1,0:T(8,128)S(1)} %copy-done.26), dimensions={2} | reverse | bytes 6291456 | tf_op jit(solution)/shard_map/rev | solution.py:37
  1326.2 10.4 reshape.730
  1343.2 11.1 reshape.732
  1368.0 10.4 reshape.722
  1384.8 10.1 reshape.724
  1407.8 10.4 reshape.726
  1424.7 11.1 reshape.728
  1452.0 19.9 %all-reduce.15 = (f32[768]{0:T(1024)}, f32[32,6]{1,0:T(8,128)}, f32[768]{0:T(1024)}) all-reduce(f32[768]{0:T(1024)} %get-tuple-element.74, f32[32,6]{1,0:T(8,128)} %fusion.93, f32[768]{0:T(1024)} %get-tuple-element.70), channel_id=12, replica_groups=mesh['dp'=4,'ctx'=4,'tp'=2] {'dp'}, use_global_device_ids=true, to_apply=%region_43.44.clone | all-reduce | flops 1728 | bytes 13824
  1475.9 12.9 all-reduce.13
  (549 shorter events, 284.8 us)
Async XLA Ops:
  7.2 45.4 %all-gather.18.cloned.1.call-start = ((), (), s32[]{:S(2)}) async-start(), calls=%async_computation.20 | async-start | bytes 2211840 | tf_op jit(solution)/shard_map/all_gather | solution.py:228
  7.9 169.2 %all-gather.14.cloned.1.call-start = ((), (), s32[]{:S(2)}) async-start(), calls=%async_computation.11 | async-start | bytes 2949120 | tf_op jit(solution)/shard_map/all_gather | solution.py:245
  25.5 30.2 %copy-start.124 = (f32[768]{0:T(1024)}, f32[768]{0:T(1024)S(1)}, u32[]{:S(2)}) copy-start(f32[768]{0:T(1024)S(1)} %convert_element_type.209) | copy-start | bytes 9220
  29.9 22.7 %copy-start.104 = (bf16[768,768]{1,0:T(8,128)(2,1)}, bf16[768,768]{1,0:T(8,128)(2,1)S(1)}, u32[]{:S(2)}) copy-start(bf16[768,768]{1,0:T(8,128)(2,1)S(1)} %fusion.23) | copy-start | bytes 3538948
  56.9 14.5 copy-start.143
  58.1 124.0 %all-gather.16.cloned.1.call-start = ((), (), s32[]{:S(2)}) async-start(), calls=%async_computation.12 | async-start | bytes 2949120 | tf_op jit(solution)/shard_map/all_gather | solution.py:242
  59.2 238.1 %all-reduce.23.cloned.1.call-start = ((), (), s32[]{:S(2)}) async-start(), calls=%async_computation.13 | async-start | bytes 4718592 | tf_op jit(solution)/shard_map/psum | solution.py:270
  130.8 26.1 %copy-start.135 = (s32[3,1024]{1,0:T(4,128)S(1)}, s32[3,1024]{1,0:T(4,128)}, u32[]{:S(2)}) copy-start(s32[3,1024]{1,0:T(4,128)} %param.14) | copy-start | bytes 36868
  130.8 26.1 %copy-start.116 = (bf16[1,384,192]{1,2,0:T(8,128)(2,1)S(1)}, bf16[1,384,192]{1,2,0:T(8,128)(2,1)}, u32[]{:S(2)}) copy-start(bf16[1,384,192]{1,2,0:T(8,128)(2,1)} %param.19) | copy-start | bytes 442372
  174.9 43.3 %copy-start.53 = (pred[256,512]{1,0:T(8,128)(4,1)}, pred[256,512]{1,0:T(8,128)(4,1)S(1)}, u32[]{:S(2)}) copy-start(pred[256,512]{1,0:T(8,128)(4,1)S(1)} %get-tuple-element.142) | copy-start | bytes 393220
  175.1 49.0 %copy-start.49 = (pred[256,512]{1,0:T(8,128)(4,1)}, pred[256,512]{1,0:T(8,128)(4,1)S(1)}, u32[]{:S(2)}) copy-start(pred[256,512]{1,0:T(8,128)(4,1)S(1)} %get-tuple-element.140) | copy-start | bytes 393220
  175.1 49.8 %copy-start.51 = (pred[256,512]{1,0:T(8,128)(4,1)}, pred[256,512]{1,0:T(8,128)(4,1)S(1)}, u32[]{:S(2)}) copy-start(pred[256,512]{1,0:T(8,128)(4,1)S(1)} %get-tuple-element.141) | copy-start | bytes 393220
  229.6 67.6 %copy-start.36 = (bf16[3,256,768]{2,1,0:T(8,128)(2,1)S(1)}, bf16[3,256,768]{2,1,0:T(8,128)(2,1)}, u32[]{:S(2)}) copy-start(bf16[3,256,768]{2,1,0:T(8,128)(2,1)} %param.13) | copy-start | bytes 3538948
  233.5 67.4 %copy-start.128 = (f32[768]{0:T(1024)}, f32[768]{0:T(1024)S(1)}, u32[]{:S(2)}) copy-start(f32[768]{0:T(1024)S(1)} %convert_element_type.210) | copy-start | bytes 9220
  234.0 218.0 %copy-start.140 = (s32[1536]{0:T(1024)}, s32[1536]{0:T(1024)S(1)}, u32[]{:S(2)}) copy-start(s32[1536]{0:T(1024)S(1)} %fusion.121) | copy-start | bytes 18436
  299.3 21.4 %copy-start.133 = (f32[768]{0:T(1024)}, f32[768]{0:T(1024)S(1)}, u32[]{:S(2)}) copy-start(f32[768]{0:T(1024)S(1)} %get-tuple-element.95) | copy-start | bytes 9220
  299.3 21.4 %copy-start.130 = (f32[768]{0:T(1024)}, f32[768]{0:T(1024)S(1)}, u32[]{:S(2)}) copy-start(f32[768]{0:T(1024)S(1)} %fusion.123) | copy-start | bytes 9220
  301.0 148.8 %copy-start.47 = (bf16[768,768]{1,0:T(8,128)(2,1)}, bf16[768,768]{1,0:T(8,128)(2,1)S(1)}, u32[]{:S(2)}) copy-start(bf16[768,768]{1,0:T(8,128)(2,1)S(1)} %multiply_convert_fusion.3) | copy-start | bytes 3538948
  320.7 5.2 copy-start.103
  320.7 142.9 %all-to-all-start = ((bf16[4,2,384,768]{3,2,1,0:T(8,128)(2,1)}), bf16[4,2,384,768]{3,2,1,0:T(8,128)(2,1)}, u32[]{:S(2)}, u32[]{:S(2)}) async-start(bf16[4,2,384,768]{3,2,1,0:T(8,128)(2,1)} %bitcast.319), calls=%async_computation | async-start | bytes 9437184 | tf_op jit(solution)/shard_map/all_to_all | solution.py:182
  325.9 113.7 %copy-start.45 = (bf16[3,256,768]{2,1,0:T(8,128)(2,1)S(1)}, bf16[3,256,768]{2,1,0:T(8,128)(2,1)}, u32[]{:S(2)}) copy-start(bf16[3,256,768]{2,1,0:T(8,128)(2,1)} %param.25) | copy-start | bytes 3538948
  325.9 143.3 %all-gather.22.cloned.1.call-start = ((), (), s32[]{:S(2)}) async-start(), calls=%async_computation.22 | async-start | bytes 5898240 | tf_op jit(solution)/shard_map/all_gather | solution.py:282
  439.6 10.2 copy-start.120
  451.7 11.9 copy-start.85
  463.7 106.7 %all-to-all-start.2 = ((bf16[4,2,384,768]{3,2,1,0:T(8,128)(2,1)}), bf16[4,2,384,768]{3,2,1,0:T(8,128)(2,1)}, u32[]{:S(2)}, u32[]{:S(2)}) async-start(bf16[4,2,384,768]{3,2,1,0:T(8,128)(2,1)} %bitcast.320), calls=%async_computation.2 | async-start | bytes 9437184 | tf_op jit(solution)/shard_map/all_to_all | solution.py:182
  468.6 106.7 %all-gather.20.cloned.1.call-start = ((), (), s32[]{:S(2)}) async-start(), calls=%async_computation.21 | async-start | bytes 5898240 | tf_op jit(solution)/shard_map/all_gather | solution.py:281
  570.3 19.3 %slice-start = ((s8[4718592]{0:T(1024)(128)(4,1)}), s8[524288]{0:T(1024)(128)(4,1)S(1)}, s32[]{:S(2)}) async-start(s8[4718592]{0:T(1024)(128)(4,1)} %bitcast.363), calls=%async_computation.27 | async-start | bytes 1048576
  575.3 14.4 copy-start.79
  575.3 14.4 slice-start.1
  656.6 109.0 %all-to-all-start.3 = ((bf16[1,2,1536,768]{3,1,0,2:T(2,128)(2,1)}), bf16[1,2,1536,768]{3,1,0,2:T(2,128)(2,1)}, u32[]{:S(2)}, u32[]{:S(2)}) async-start(bf16[1,2,1536,768]{3,1,0,2:T(2,128)(2,1)} %copy.228), calls=%async_computation.3 | async-start | bytes 9437184 | tf_op jit(solution)/shard_map/all_to_all | solution.py:186
  709.2 61.8 %copy-start.141 = (s32[1536]{0:T(1024)S(1)}, s32[1536]{0:T(1024)}, u32[]{:S(2)}) copy-start(s32[1536]{0:T(1024)} %copy-done.140) | copy-start | bytes 18436
  765.5 109.4 %all-to-all-start.1 = ((bf16[1,2,1536,768]{3,1,0,2:T(2,128)(2,1)}), bf16[1,2,1536,768]{3,1,0,2:T(2,128)(2,1)}, u32[]{:S(2)}, u32[]{:S(2)}) async-start(bf16[1,2,1536,768]{3,1,0,2:T(2,128)(2,1)} %copy.224), calls=%async_computation.1 | async-start | bytes 9437184 | tf_op jit(solution)/shard_map/all_to_all | solution.py:186
  770.9 146.3 %all-reduce.25.cloned.1.call-start = ((), (), s32[]{:S(2)}) async-start(), calls=%async_computation.14 | async-start | bytes 4718592 | tf_op jit(solution)/shard_map/psum | solution.py:381
  789.0 9.7 copy-start.46
  798.4 192.1 %reduce-scatter.14.cloned.1.call-start = ((), (), s32[]{:S(2)}) async-start(), calls=%async_computation.16 | async-start | bytes 5898240 | tf_op jit(solution)/shard_map/reduce_scatter | solution.py:430
  893.0 21.4 %copy-start.115 = (f32[768,2]{0,1:T(2,128)S(1)}, f32[768,2]{0,1:T(2,128)}, u32[]{:S(2)}) copy-start(f32[768,2]{0,1:T(2,128)} %copy-done.114) | copy-start | bytes 18436
  893.0 21.4 %copy-start.122 = (f32[768]{0:T(1024)S(1)}, f32[768]{0:T(1024)}, u32[]{:S(2)}) copy-start(f32[768]{0:T(1024)} %copy-done.121) | copy-start | bytes 9220
  893.0 24.2 %copy-start.18 = (f32[768,768]{1,0:T(8,128)S(1)}, f32[768,768]{1,0:T(8,128)}, u32[]{:S(2)}) copy-start(f32[768,768]{1,0:T(8,128)} %copy-done.17) | copy-start | bytes 7077892
  893.0 24.2 %copy-start.129 = (f32[768]{0:T(1024)S(1)}, f32[768]{0:T(1024)}, u32[]{:S(2)}) copy-start(f32[768]{0:T(1024)} %copy-done.128) | copy-start | bytes 9220
  917.2 4.0 copy-start.131
  923.1 5.8 copy-start.75
  923.1 8.9 copy-start.73
  936.4 96.5 %reduce-scatter.12.cloned.1.call-start = ((), (), s32[]{:S(2)}) async-start(), calls=%async_computation.15 | async-start | bytes 5898240 | tf_op jit(solution)/shard_map/reduce_scatter | solution.py:429
  938.9 4.5 copy-start.76
  938.9 4.5 copy-start.90
  938.9 5.2 copy-start.10
  945.9 4.6 copy-start.16
  975.4 144.5 %reduce-scatter.22.cloned.1.call-start = ((), (), s32[]{:S(2)}) async-start(), calls=%async_computation.23 | async-start | bytes 4423680
  1053.2 99.1 %reduce-scatter.16.cloned.1.call-start = ((), (), s32[]{:S(2)}) async-start(), calls=%async_computation.17 | async-start | bytes 1474560 | tf_op jit(solution)/shard_map/reduce_scatter | solution.py:453
  1057.0 128.4 %reduce-scatter.24.cloned.1.call-start = ((), (), s32[]{:S(2)}) async-start(), calls=%async_computation.24 | async-start | bytes 491520
  1060.4 388.5 %all-reduce.29.cloned.1.call-start = ((), (), s32[]{:S(2)}) async-start(), calls=%async_computation.26 | async-start | bytes 9437184 | tf_op jit(solution)/shard_map/psum | solution.py:316
  1065.6 429.7 %all-reduce.27.cloned.1.call-start = ((), (), s32[]{:S(2)}) async-start(), calls=%async_computation.25 | async-start | bytes 2949120 | tf_op jit(solution)/shard_map/psum | solution.py:458
  1152.3 345.6 %reduce-scatter.18.cloned.1.call-start = ((), (), s32[]{:S(2)}) async-start(), calls=%async_computation.18 | async-start | bytes 11796480 | tf_op jit(solution)/shard_map/reduce_scatter | solution.py:383
  1166.9 333.6 %reduce-scatter.20.cloned.1.call-start = ((), (), s32[]{:S(2)}) async-start(), calls=%async_computation.19 | async-start | bytes 11796480 | tf_op jit(solution)/shard_map/reduce_scatter | solution.py:384
  1230.5 26.2 %copy-start.31 = (f32[6,256,512]{2,1,0:T(8,128)S(1)}, f32[6,256,512]{2,1,0:T(8,128)}, u32[]{:S(2)}) copy-start(f32[6,256,512]{2,1,0:T(8,128)} %copy-done.29) | copy-start | bytes 9437188
  1274.2 26.1 %copy-start.26 = (f32[6,256,512]{2,1,0:T(8,128)S(1)}, f32[6,256,512]{2,1,0:T(8,128)}, u32[]{:S(2)}) copy-start(f32[6,256,512]{2,1,0:T(8,128)} %copy-done.24) | copy-start | bytes 9437188
  1326.2 10.4 copy-start.42
  1368.0 10.4 copy-start.40
  1407.8 10.4 copy-start.38
  1439.0 9.9 copy-start.37
  1439.0 9.9 copy-start.125
  1439.0 9.9 copy-start.127
  1443.3 46.8 %copy-start.137 = (f32[768]{0:T(1024)S(1)}, f32[768]{0:T(1024)}, u32[]{:S(2)}) copy-start(f32[768]{0:T(1024)} %copy-done.136) | copy-start | bytes 9220
  1443.3 46.8 %copy-start.19 = (f32[768,768]{1,0:T(8,128)S(1)}, f32[768,768]{1,0:T(8,128)}, u32[]{:S(2)}) copy-start(f32[768,768]{1,0:T(8,128)} %copy-done.17) | copy-start | bytes 7077892
  (102 other events, 230.0 us)
Sparse Core Ops, SparseCore 0:
  9.6 43.0 all-gather.17
  58.2 22.8 all-gather.13
  83.2 24.0 all-gather.15
  229.8 67.4 all-reduce.22
  328.5 37.8 all-gather.21
  470.7 37.8 all-gather.19
  798.5 69.0 all-reduce.24
  936.6 45.9 reduce-scatter.13
  985.1 47.7 reduce-scatter.11
  1053.3 66.4 reduce-scatter.21
  1122.7 29.4 reduce-scatter.15
  1155.0 19.3 reduce-scatter.23
  1176.8 117.5 all-reduce.28
  1296.8 41.4 all-reduce.26
  1341.3 77.9 reduce-scatter.17
  1422.3 78.1 reduce-scatter.19
where the time goes:
time: 1520 us; the launch traced here: 1510 us
  local copies, waits for them, and re-layouts  586 us (39%)
  waiting for transfers between devices  424 us (28%)
  blocking collectives  191 us (13%)
  matrix products  162 us (11%)
  other arithmetic  106 us (7%)
  starting transfers between devices  22.3 us (1%)
  between operations  18.4 us (1%)
    all_to_all x2, waiting for transfers between devices, from_experts(): lax.all_to_all(slots_back[None], 'dp', split_axis=2, concat_axis=0, tiled...  131 us
    rev x6, local copies, waits for them, and re-layouts, diagonal_sums(): padded = jnp.pad(dscores[:, :, ::-1], ((0, 0), (0, 0), (0, row_count)))  131 us
    all_gather x1, blocking collectives, on_device(): lax.all_gather(w_router[layer_index], 'dp', axis=0, tiled=True)  110 us
    all_to_all x2, waiting for transfers between devices, to_experts(): lax.all_to_all(slots_out, 'dp', split_axis=0, concat_axis=2, tiled=True)[0]  83.6 us
    unnamed x325, local copies, waits for them, and re-layouts  82.2 us
    broadcast_in_dim x2, local copies, waits for them, and re-layouts, from_experts(): slots_back[None]  67.8 us
    reshape x6, local copies, waits for them, and re-layouts, diagonal_sums(): skewed = padded.reshape(head_count, row_count * (col_count + row_count))[...  63.4 us
    psum x1, waiting for transfers between devices, on_device(): middle_activation = residual + lax.psum(attn_part, 'tp')  63.3 us
  transfers between devices with their start and end apart: 20, of which 9 were waited for; matrix products, arithmetic and copies ran while one was open for 42% of the time, Pallas kernels for 0%

commit v1 on v0

v1 whole, which is shorter than its diff:
```python
import functools

import jax
import jax.numpy as jnp
from jax import lax
from jax.experimental import pallas as pl
from jax.experimental.pallas import tpu as pltpu
from jax.sharding import PartitionSpec as P

HD = 64
NB = 32
EPSILON = 1e-06
FULL_PRECISION = lax.Precision.HIGHEST
MASKED = -1e30
BF16 = jnp.bfloat16
F32 = jnp.float32
VMEM_BYTES = 60 * 1024 * 1024
GELU_C = 0.7978845608028654
GELU_A = 0.044715


def params():
    return pltpu.CompilerParams(vmem_limit_bytes=VMEM_BYTES)


def cost(flops, nbytes, trans=0):
    return pl.CostEstimate(flops=int(flops), bytes_accessed=int(nbytes), transcendentals=int(trans))


def dot(a, b):
    return lax.dot_general(a, b, (((1,), (0,)), ((), ())), preferred_element_type=F32)


def dot_nt(a, b):
    return lax.dot_general(a, b, (((1,), (1,)), ((), ())), preferred_element_type=F32)


def dot_tn(a, b):
    return lax.dot_general(a, b, (((0,), (0,)), ((), ())), preferred_element_type=F32)


def bias_kernel(win_ref, out_ref):
    for block in range(4):
        row = win_ref[0, block : block + 1, :]
        wide = jnp.broadcast_to(row, (256, 512))
        rolled = pltpu.roll(wide, 257, 1, stride=1, stride_axis=0)
        out_ref[0, block * 256 : (block + 1) * 256, :] = rolled[:, :256].astype(BF16)


def expand_bias(windows):
    heads = windows.shape[0]
    return pl.pallas_call(
        bias_kernel,
        name="expand_bias",
        grid=(heads,),
        in_specs=[pl.BlockSpec((1, 4, 512), lambda h: (h, 0, 0))],
        out_specs=pl.BlockSpec((1, 1024, 256), lambda h: (h, 0, 0)),
        out_shape=jax.ShapeDtypeStruct((heads, 1024, 256), BF16),
        compiler_params=params(),
        cost_estimate=cost(heads * 2 * 1024 * 512, heads * 1024 * 256 * 2),
    )(windows)


def attend_kernel(q_ref, k_ref, v_ref, bias_ref, idq_ref, idk_ref, out_ref, lse_ref, mask_ref):
    @pl.when(pl.program_id(0) == 0)
    def _():
        mask_ref[...] = jnp.where(idk_ref[...] <= idq_ref[...], 0.0, MASKED)

    queries = q_ref[...]
    keys = k_ref[...]
    values_t = v_ref[...].T
    low_half = lax.broadcasted_iota(jnp.int32, queries.shape, 1) < HD
    zero = jnp.zeros_like(queries)
    parts = []
    for head in range(2):
        own = jnp.where(low_half, queries, zero) if head == 0 else jnp.where(low_half, zero, queries)
        scores = dot_nt(keys, own) + bias_ref[head].astype(F32) + mask_ref[...]
        top = jnp.max(scores, axis=0, keepdims=True)
        weights = jnp.exp(scores - top)
        total = jnp.sum(weights, axis=0, keepdims=True)
        part = dot(values_t[head * HD : (head + 1) * HD], weights.astype(BF16)) * (1.0 / total)
        parts.append(part)
        lse_ref[0, head : head + 1, :] = top + jnp.log(total)
    out_ref[...] = jnp.concatenate(parts, axis=0).T.astype(BF16)


def attend(queries, keys, values, bias, ids_query, ids_key):
    rows, width = queries.shape
    length = keys.shape[0]
    pairs = width // (2 * HD)
    return pl.pallas_call(
        attend_kernel,
        name="attend",
        grid=(pairs,),
        in_specs=[
            pl.BlockSpec((rows, 128), lambda p: (0, p)),
            pl.BlockSpec((length, 128), lambda p: (0, p)),
            pl.BlockSpec((length, 128), lambda p: (0, p)),
            pl.BlockSpec((2, length, rows), lambda p: (p, 0, 0)),
            pl.BlockSpec((1, rows), lambda p: (0, 0)),
            pl.BlockSpec((length, 1), lambda p: (0, 0)),
        ],
        out_specs=[
            pl.BlockSpec((rows, 128), lambda p: (0, p)),
            pl.BlockSpec((1, 2, rows), lambda p: (p, 0, 0)),
        ],
        out_shape=[
            jax.ShapeDtypeStruct((rows, width), BF16),
            jax.ShapeDtypeStruct((pairs, 2, rows), F32),
        ],
        scratch_shapes=[pltpu.VMEM((length, rows), F32)],
        compiler_params=params(),
        cost_estimate=cost(pairs * 2 * 4 * rows * length * 128, 6 * rows * length * 2, pairs * 2 * rows * length),
    )(queries, keys, values, bias, ids_query, ids_key)


def attend_back_kernel(
    q_ref, k_ref, v_ref, do_ref, bias_ref, lse_ref, idq_ref, idk_ref, dq_ref, dk_ref, dv_ref, rel_ref, mask_ref
):
    @pl.when(pl.program_id(0) == 0)
    def _():
        mask_ref[...] = jnp.where(idk_ref[...] <= idq_ref[...], 0.0, MASKED)

    queries = q_ref[...]
    keys = k_ref[...]
    values = v_ref[...]
    grad_out = do_ref[...]
    keys_t = keys.T
    low_half = lax.broadcasted_iota(jnp.int32, queries.shape, 1) < HD
    zero = jnp.zeros_like(queries)
    dk = None
    dv = None
    dq_parts = []
    for head in range(2):
        own = (lambda a: jnp.where(low_half, a, zero)) if head == 0 else (lambda a: jnp.where(low_half, zero, a))
        q_own = own(queries)
        do_own = own(grad_out)
        scores = dot_nt(keys, q_own) + bias_ref[head].astype(F32) + mask_ref[...]
        probs = jnp.exp(scores - lse_ref[0, head : head + 1, :])
        dprobs = dot_nt(values, do_own)
        delta = jnp.sum(probs * dprobs, axis=0, keepdims=True)
        dscores = probs * (dprobs - delta)
        low = dscores.astype(BF16)
        dv_head = dot(probs.astype(BF16), do_own)
        dk_head = dot(low, q_own)
        dv = dv_head if dv is None else dv + dv_head
        dk = dk_head if dk is None else dk + dk_head
        dq_parts.append(dot(keys_t[head * HD : (head + 1) * HD], low))
        for block in range(4):
            tile = dscores[block * 256 : (block + 1) * 256]
            wide = jnp.concatenate([tile, jnp.zeros_like(tile)], axis=1)
            total = None
            for group in range(32):
                moved = pltpu.roll(wide[group * 8 : group * 8 + 8], 248 - 8 * group, 1)
                total = moved if total is None else total + moved
            row = lax.broadcasted_iota(jnp.int32, total.shape, 0)
            amount = 7 - row
            for bit in (1, 2, 4):
                total = jnp.where((amount & bit) != 0, pltpu.roll(total, bit, 1), total)
            rel_ref[0, head, block : block + 1, :] = jnp.sum(total, axis=0, keepdims=True)
    dq_ref[...] = (jnp.concatenate(dq_parts, axis=0).T * (HD ** (-0.5))).astype(BF16)
    dk_ref[...] = dk.astype(BF16)
    dv_ref[...] = dv.astype(BF16)


def attend_back(queries, keys, values, grad_out, bias, lse, ids_query, ids_key):
    rows, width = queries.shape
    length = keys.shape[0]
    pairs = width // (2 * HD)
    return pl.pallas_call(
        attend_back_kernel,
        name="attend_back",
        grid=(pairs,),
        in_specs=[
            pl.BlockSpec((rows, 128), lambda p: (0, p)),
            pl.BlockSpec((length, 128), lambda p: (0, p)),
            pl.BlockSpec((length, 128), lambda p: (0, p)),
            pl.BlockSpec((rows, 128), lambda p: (0, p)),
            pl.BlockSpec((2, length, rows), lambda p: (p, 0, 0)),
            pl.BlockSpec((1, 2, rows), lambda p: (p, 0, 0)),
            pl.BlockSpec((1, rows), lambda p: (0, 0)),
            pl.BlockSpec((length, 1), lambda p: (0, 0)),
        ],
        out_specs=[
            pl.BlockSpec((rows, 128), lambda p: (0, p)),
            pl.BlockSpec((length, 128), lambda p: (0, p)),
            pl.BlockSpec((length, 128), lambda p: (0, p)),
            pl.BlockSpec((1, 2, 4, 512), lambda p: (p, 0, 0, 0)),
        ],
        out_shape=[
            jax.ShapeDtypeStruct((rows, width), BF16),
            jax.ShapeDtypeStruct((length, width), BF16),
            jax.ShapeDtypeStruct((length, width), BF16),
            jax.ShapeDtypeStruct((pairs, 2, 4, 512), F32),
        ],
        scratch_shapes=[pltpu.VMEM((length, rows), F32)],
        compiler_params=params(),
        cost_estimate=cost(pairs * 2 * 10 * rows * length * 128, 8 * rows * length * 2, pairs * 2 * rows * length),
    )(queries, keys, values, grad_out, bias, lse, ids_query, ids_key)


def one_hot(place, cap):
    groups, rows = place.shape
    slots = lax.broadcasted_iota(jnp.int32, (cap, rows), 0).astype(F32)
    return [slots == place[group : group + 1, :] for group in range(groups)]


def diagonal(cap):
    return lax.broadcasted_iota(jnp.int32, (cap, cap), 0) == lax.broadcasted_iota(jnp.int32, (cap, cap), 1)


def dispatch_kernel(groups, cap, place_ref, rows_ref, out_ref):
    rows = rows_ref[0]
    picks = one_hot(place_ref[0], cap)
    pick = jnp.concatenate([jnp.where(p, 1.0, 0.0).astype(BF16) for p in picks], axis=0)
    out_ref[:, 0] = dot(pick, rows).astype(BF16).reshape(groups, cap, rows.shape[1])


def dispatch(place, rows, cap):
    seqs, groups, stretch = place.shape
    width = rows.shape[2]
    return pl.pallas_call(
        functools.partial(dispatch_kernel, groups, cap),
        name="dispatch_rows",
        grid=(seqs,),
        in_specs=[
            pl.BlockSpec((1, groups, stretch), lambda s: (s, 0, 0)),
            pl.BlockSpec((1, stretch, width), lambda s: (s, 0, 0)),
        ],
        out_specs=pl.BlockSpec((groups, 1, cap, width), lambda s: (0, s, 0, 0)),
        out_shape=jax.ShapeDtypeStruct((groups, seqs, cap, width), BF16),
        compiler_params=params(),
        cost_estimate=cost(seqs * 2 * groups * cap * stretch * width, seqs * 2 * (stretch + groups * cap) * width),
    )(place, rows)


def norm_factor(value):
    return lax.rsqrt(jnp.mean(value * value, axis=-1, keepdims=True) + EPSILON)


def middle_kernel(
    groups, cap, own_ref, other_ref, x_ref, wout_ref, gain_ref, router_ref, hits_ref, place_ref,
    middle_ref, moe_ref, gates_ref, send_ref, slot_gate_ref,
):
    mid = x_ref[...].astype(F32) + (dot(own_ref[...], wout_ref[0]) + dot(other_ref[...], wout_ref[1]))
    middle_ref[...] = mid
    moe_in = (mid * norm_factor(mid) * gain_ref[...].astype(F32)).astype(BF16)
    moe_ref[...] = moe_in
    logits = dot_nt(router_ref[...], moe_in)
    hit = hits_ref[...] > 0.5
    top = jnp.max(jnp.where(hit, logits, MASKED), axis=0, keepdims=True)
    raw = jnp.where(hit, jnp.exp(jnp.where(hit, logits, top) - top), 0.0)
    gates = raw / jnp.sum(raw, axis=0, keepdims=True)
    gates_ref[...] = gates
    picks = one_hot(place_ref[...], cap)
    pick = jnp.concatenate([jnp.where(p, 1.0, 0.0).astype(BF16) for p in picks], axis=0)
    send_ref[...] = dot(pick, moe_in).astype(BF16).reshape(groups, cap, moe_in.shape[1])
    eye = diagonal(cap)
    for group in range(groups):
        column = jnp.sum(jnp.where(picks[group], gates[group : group + 1, :], 0.0), axis=1, keepdims=True)
        slot_gate_ref[group] = jnp.sum(jnp.where(eye, column, 0.0), axis=0, keepdims=True)


def middle_stage(own, other, x, wout, gain, router, hits, place, cap):
    rows, width = x.shape
    experts = router.shape[0]
    groups = place.shape[0]
    return pl.pallas_call(
        functools.partial(middle_kernel, groups, cap),
        name="middle_stage",
        out_shape=[
            jax.ShapeDtypeStruct((rows, width), F32),
            jax.ShapeDtypeStruct((rows, width), BF16),
            jax.ShapeDtypeStruct((experts, rows), F32),
            jax.ShapeDtypeStruct((groups, cap, width), BF16),
            jax.ShapeDtypeStruct((groups, 1, cap), F32),
        ],
        compiler_params=params(),
        cost_estimate=cost(2 * rows * width * width + 2 * groups * cap * rows * width, rows * width * 16),
    )(own, other, x, wout, gain, router, hits, place)


def expert_kernel(
    first, final, tiles, groups, cap, x_ref, g_ref, gate_ref, w_ref, *refs
):
    if first:
        acc_in = None
    else:
        acc_in, refs = refs[0], refs[1:]
    part_out, din_out, h_out, acc_out, xt_ref, dy_ref, dyt_ref, part_ref, din_ref = refs
    step = pl.program_id(0)
    rows = groups * cap
    width = x_ref.shape[-1]
    slices = w_ref.shape[0]
    piece = width // slices

    @pl.when(step == 0)
    def _():
        eye = diagonal(cap)
        xt_ref[...] = x_ref[...].reshape(rows, width).T
        for group in range(groups):
            gate = jnp.sum(jnp.where(eye, gate_ref[group], 0.0), axis=1, keepdims=True)
            dy_ref[group * cap : (group + 1) * cap] = (g_ref[group, 0].astype(F32) * gate).astype(BF16)
        dyt_ref[...] = dy_ref[...].T

    x = x_ref[...].reshape(rows, width)
    w_in = w_ref[:, 0, 0].reshape(width, -1)
    w_out_t = w_ref[:, 1, 0].reshape(width, -1)
    dy = dy_ref[...]
    pre = dot(x, w_in)
    square = pre * pre
    inner = jnp.tanh(GELU_C * pre * (1.0 + GELU_A * square))
    half = 0.5 * (1.0 + inner)
    hidden = (pre * half).astype(BF16)
    slope = half + (0.5 * GELU_C) * pre * (1.0 - inner * inner) * (1.0 + (3.0 * GELU_A) * square)
    dhid = dot(dy, w_out_t)
    dpre = (dhid * slope).astype(BF16)
    part = dot_nt(hidden, w_out_t)
    din = dot_nt(dpre, w_in)
    dw_in = dot(xt_ref[...], dpre)
    dw_out_t = dot(dyt_ref[...], hidden)

    @pl.when(step == 0)
    def _():
        part_ref[...] = part
        din_ref[...] = din

    @pl.when(step > 0)
    def _():
        part_ref[...] += part
        din_ref[...] += din

    me = lax.axis_index("ctx")
    for index in range(slices):
        place = index ^ me
        grad_in = dw_in[index * piece : (index + 1) * piece]
        grad_out = dw_out_t[index * piece : (index + 1) * piece]
        if not first:
            grad_in += acc_in[0, place, 0]
            grad_out += acc_in[0, place, 1]
        acc_out[0, place, 0] = grad_in.astype(acc_out.dtype)
        acc_out[0, place, 1] = grad_out.astype(acc_out.dtype)

    @pl.when(step == tiles - 1)
    def _():
        eye = diagonal(cap)
        for group in range(groups):
            gate = jnp.sum(jnp.where(eye, gate_ref[group], 0.0), axis=1, keepdims=True)
            gated = part_ref[group * cap : (group + 1) * cap] * gate
            part_out[group] = gated.astype(BF16)
            din_out[group] = din_ref[group * cap : (group + 1) * cap].astype(BF16)
            h = jnp.sum(gated * g_ref[group, 0].astype(F32), axis=1, keepdims=True)
            h_out[group] = jnp.sum(jnp.where(eye, h, 0.0), axis=0, keepdims=True)


def experts(x, cot_slots, seq_index, gate, weights, acc, final, tile=512):
    groups, cap, width = x.shape
    slices, _, halves, piece, half_len = weights.shape
    per_half = half_len // tile
    tiles = halves * per_half
    rows = groups * cap
    first = acc is None
    acc_spec = pl.BlockSpec((1, slices, 2, piece, tile), lambda f: (f // per_half, 0, 0, 0, f % per_half))
    in_specs = [
        pl.BlockSpec((groups, cap, width), lambda f: (0, 0, 0)),
        pl.BlockSpec((groups, 1, cap, width), lambda f: (0, seq_index, 0, 0)),
        pl.BlockSpec((groups, 1, cap), lambda f: (0, 0, 0)),
        pl.BlockSpec((slices, 2, 1, piece, tile), lambda f: (0, 0, f // per_half, 0, f % per_half)),
    ]
    args = [x, cot_slots, gate, weights]
    aliases = {}
    if not first:
        in_specs.append(acc_spec)
        args.append(acc)
        if not final:
            aliases = {4: 3}
    acc_shape = (halves, slices, 2, piece, half_len)
    return pl.pallas_call(
        functools.partial(expert_kernel, first, final, tiles, groups, cap),
        name="experts",
        grid=(tiles,),
        in_specs=in_specs,
        out_specs=[
            pl.BlockSpec((groups, cap, width), lambda f: (0, 0, 0)),
            pl.BlockSpec((groups, cap, width), lambda f: (0, 0, 0)),
            pl.BlockSpec((groups, 1, cap), lambda f: (0, 0, 0)),
            acc_spec,
        ],
        out_shape=[
            jax.ShapeDtypeStruct((groups, cap, width), BF16),
            jax.ShapeDtypeStruct((groups, cap, width), BF16),
            jax.ShapeDtypeStruct((groups, 1, cap), F32),
            jax.ShapeDtypeStruct(acc_shape, BF16 if final else F32),
        ],
        scratch_shapes=[
            pltpu.VMEM((width, rows), BF16),
            pltpu.VMEM((rows, width), BF16),
            pltpu.VMEM((width, rows), BF16),
            pltpu.VMEM((rows, width), F32),
            pltpu.VMEM((rows, width), F32),
        ],
        input_output_aliases=aliases,
        compiler_params=params(),
        cost_estimate=cost(12 * rows * width * halves * half_len, 2 * width * halves * half_len * 10, rows * halves * half_len),
    )(*args)


def combine_kernel(groups, cap, place_ref, din_ref, h_ref, din_out, h_out):
    picks = one_hot(place_ref[...], cap)
    pick = jnp.concatenate([jnp.where(p, 1.0, 0.0).astype(BF16) for p in picks], axis=0)
    rows = groups * cap
    din_out[...] = dot_tn(pick, din_ref[...].reshape(rows, din_ref.shape[-1])).astype(BF16)
    eye = diagonal(cap)
    for group in range(groups):
        column = jnp.sum(jnp.where(eye, h_ref[group], 0.0), axis=1, keepdims=True)
        h_out[group : group + 1, :] = jnp.sum(jnp.where(picks[group], column, 0.0), axis=0, keepdims=True)


def combine(place, din, h, cap):
    groups, stretch = place.shape
    width = din.shape[-1]
    return pl.pallas_call(
        functools.partial(combine_kernel, groups, cap),
        name="combine_back",
        out_shape=[
            jax.ShapeDtypeStruct((stretch, width), BF16),
            jax.ShapeDtypeStruct((groups, stretch), F32),
        ],
        compiler_params=params(),
        cost_estimate=cost(2 * groups * cap * stretch * width, 4 * stretch * width * 2),
    )(place, din, h)


def combine_out_kernel(groups, cap, place_ref, part_ref, out_ref):
    picks = one_hot(place_ref[...], cap)
    pick = jnp.concatenate([jnp.where(p, 1.0, 0.0).astype(BF16) for p in picks], axis=0)
    out_ref[...] = dot_tn(pick, part_ref[...].reshape(groups * cap, part_ref.shape[-1])).astype(BF16)


def combine_out(place, part, cap):
    groups, stretch = place.shape
    width = part.shape[-1]
    return pl.pallas_call(
        functools.partial(combine_out_kernel, groups, cap),
        name="combine_out",
        out_shape=jax.ShapeDtypeStruct((stretch, width), BF16),
        compiler_params=params(),
        cost_estimate=cost(2 * groups * cap * stretch * width, 4 * stretch * width * 2),
    )(place, part)


def middle_back_kernel(
    own_ref, other_ref, h_ref, gates_ref, router_ref, moe_ref, mid_ref, gain_ref, cot_ref, att_ref, wout_ref,
    gmid_ref, datt_ref, gain_grad_ref, router_grad_ref, wout_grad_ref,
):
    h = h_ref[...]
    dlogits = h - gates_ref[...] * jnp.sum(h, axis=0, keepdims=True)
    router = router_ref[...]
    dmoe = own_ref[...].astype(F32) + other_ref[...].astype(F32)
    dmoe = dmoe + lax.dot_general(
        dlogits, router.astype(F32), (((0,), (0,)), ((), ())), precision=FULL_PRECISION, preferred_element_type=F32
    )
    router_grad_ref[...] = lax.dot_general(
        dlogits, moe_ref[...].astype(F32), (((1,), (0,)), ((), ())), precision=FULL_PRECISION, preferred_element_type=F32
    )
    mid = mid_ref[...]
    gain = gain_ref[...].astype(F32)
    factor = norm_factor(mid)
    normed = mid * factor
    gain_grad_ref[...] = jnp.sum(dmoe * normed, axis=0, keepdims=True)
    scaled = dmoe * gain
    dmid = factor * (scaled - normed * jnp.mean(scaled * normed, axis=-1, keepdims=True))
    gmid = cot_ref[...].astype(F32) + dmid
    gmid_ref[...] = gmid
    dattn = gmid.astype(BF16)
    datt_ref[...] = dot_nt(dattn, wout_ref[...]).astype(BF16)
    wout_grad_ref[...] = dot_tn(att_ref[...], dattn)


def middle_back(own, other, h, gates, router, moe_in, mid, gain, cot, attended, wout):
    rows, width = mid.shape
    local = attended.shape[1]
    return pl.pallas_call(
        middle_back_kernel,
        name="middle_back",
        out_shape=[
            jax.ShapeDtypeStruct((rows, width), F32),
            jax.ShapeDtypeStruct((rows, local), BF16),
            jax.ShapeDtypeStruct((1, width), F32),
            jax.ShapeDtypeStruct(router.shape, F32),
            jax.ShapeDtypeStruct((local, width), F32),
        ],
        compiler_params=params(),
        cost_estimate=cost(6 * rows * width * local, 30 * rows * width),
    )(own, other, h, gates, router, moe_in, mid, gain, cot, attended, wout)


def flip(value, axis, bit):
    count = lax.axis_size(axis)
    return lax.ppermute(value, axis, [(i, i ^ bit) for i in range(count)])


def all_to_all_dp(value):
    return lax.all_to_all(value, "dp", split_axis=0, concat_axis=0, tiled=True)


def on_device(
    tokens_in, block_ids, rel_buckets, routes, attn_gain, w_qkv, w_attn_out, bias_table, moe_gain, w_router,
    w_expert_in, w_expert_out, cotangent,
):
    seqs, stretch, width = tokens_in.shape
    dp = lax.axis_size("dp")
    ctx_count = lax.axis_size("ctx")
    tp_count = lax.axis_size("tp")
    expert_count = w_router.shape[2]
    assert w_expert_in.shape[1] == tp_count == 2 and ctx_count == 4
    cap = max(2, 2 * stretch * routes.shape[2] // expert_count)
    ctx = lax.axis_index("ctx")
    tp = lax.axis_index("tp")
    local = w_qkv.shape[3]
    heads = local // HD

    wqkv = lax.all_gather(w_qkv[0], "dp", axis=1, tiled=True)
    wout_own = lax.all_gather(w_attn_out[0], "dp", axis=1, tiled=True)
    wout_other = flip(wout_own, "tp", 1)
    table = lax.all_gather(bias_table[0], "dp", axis=0, tiled=True)
    gains = lax.all_gather(jnp.concatenate([attn_gain, moe_gain], axis=0), "dp", axis=1, tiled=True)
    gain_attn, gain_moe = gains[0:1], gains[1:2]
    router = lax.all_gather(w_router[0], "dp", axis=0, tiled=True).T.reshape(dp, 2, width).transpose(1, 0, 2)
    router = jnp.where(tp == 0, router, router[::-1]).reshape(expert_count, width)

    across = flip(tokens_in, "ctx", 2)
    beside, beyond = flip(jnp.stack([tokens_in, across]), "ctx", 1)
    pieces = jnp.stack([tokens_in, beside, across, beyond], axis=1)

    w_in = w_expert_in[0]
    w_out_t = w_expert_out[0].transpose(0, 2, 1)
    both = jnp.stack([w_in, w_out_t], axis=1)
    keep = lax.dynamic_index_in_dim(both, tp, 0, keepdims=False)
    give = lax.dynamic_index_in_dim(both, 1 - tp, 0, keepdims=False)
    got = flip(give, "tp", 1)
    weights = lax.all_gather(jnp.stack([keep, got], axis=1), "ctx", axis=0, tiled=False)

    e_order = jnp.arange(expert_count, dtype=jnp.int32).reshape(dp, 2).T
    e_order = jnp.where(tp == 0, e_order, e_order[::-1]).reshape(1, expert_count, 1)
    hits = ((routes[:, None, :, 0] == e_order) | (routes[:, None, :, 1] == e_order)).astype(F32)
    before = (
        lax.broadcasted_iota(jnp.int32, (stretch, stretch), 0) < lax.broadcasted_iota(jnp.int32, (stretch, stretch), 1)
    ).astype(BF16)
    ranks = jnp.einsum("set,tu->seu", hits.astype(BF16), before, preferred_element_type=F32)
    places = jnp.where(hits > 0.5, ranks, -1.0)[:, :dp]

    cot_slots = all_to_all_dp(dispatch(places, cotangent, cap))

    one_hot_bucket = (rel_buckets[:, None] == jnp.arange(NB, dtype=jnp.int32)[None, :]).astype(F32)
    one_hot_bucket = jnp.pad(one_hot_bucket, ((0, 1), (0, 0)))
    starts = [(ctx - (ctx ^ b)) * stretch + 3 * stretch for b in range(4)]
    hot_windows = jnp.stack([lax.dynamic_slice_in_dim(one_hot_bucket, s, 2 * stretch, 0) for s in starts])
    windows = jnp.einsum("bmn,nh->hbm", hot_windows, table.astype(F32), precision=FULL_PRECISION)
    bias = expand_bias(windows)

    x32 = pieces.astype(F32)
    normed = (x32 * norm_factor(x32) * gain_attn.astype(F32)[None, None]).astype(BF16)
    own_normed = normed[:, 0].reshape(seqs * stretch, width)
    queries = jnp.dot(own_normed, wqkv[0], preferred_element_type=F32).astype(BF16) * jnp.asarray(HD ** (-0.5), BF16)
    queries = queries.reshape(seqs, stretch, local)
    flat = normed.reshape(seqs * 4 * stretch, width)
    keys = jnp.dot(flat, wqkv[1], preferred_element_type=F32).astype(BF16).reshape(seqs, 4 * stretch, local)
    values = jnp.dot(flat, wqkv[2], preferred_element_type=F32).astype(BF16).reshape(seqs, 4 * stretch, local)

    ids = block_ids.reshape(seqs, 4, stretch)
    ids_pieces = [lax.dynamic_index_in_dim(ids, ctx ^ b, 1, keepdims=False) for b in range(4)]
    ids_query = ids_pieces[0].reshape(seqs, 1, stretch)
    ids_key = jnp.stack(ids_pieces, axis=1).reshape(seqs, 4 * stretch, 1)

    wout_pair = jnp.stack([wout_own, wout_other])
    attended, lse, mids, moes, gates, partials = [], [], [], [], [], []
    returned_din, returned_h = [], []
    acc = None
    for s in range(seqs):
        att, stat = attend(queries[s], keys[s], values[s], bias, ids_query[s], ids_key[s])
        attended.append(att)
        lse.append(stat)
        mid, moe_in, gate, send, slot_gate = middle_stage(
            att, flip(att, "tp", 1), tokens_in[s], wout_pair, gain_moe, router, hits[s], places[s], cap
        )
        mids.append(mid)
        moes.append(moe_in)
        gates.append(gate)
        received = all_to_all_dp(send)
        received_gate = all_to_all_dp(slot_gate)
        part, din, h, acc = experts(received, cot_slots, s, received_gate, weights, acc, s == seqs - 1)
        returned_din.append(all_to_all_dp(din))
        returned_h.append(all_to_all_dp(h))
        partials.append(all_to_all_dp(part))

    beside_sum = acc[:, 0::2].astype(F32) + flip(acc[:, 1::2], "ctx", 1).astype(F32)
    mine = beside_sum[:, 0] + flip(beside_sum[:, 1].astype(BF16), "ctx", 2).astype(F32)
    other = flip(mine[1].astype(BF16), "tp", 1).astype(F32)
    ordered = jnp.where(tp == 0, jnp.stack([mine[0], other]), jnp.stack([other, mine[0]]))
    grad_expert_in = ordered[:, 0]
    grad_expert_out = ordered[:, 1].transpose(0, 2, 1)

    tokens_out, gmids = [], []
    projections = []
    rel_grad = 0.0
    gain_moe_grad = 0.0
    router_grad = 0.0
    wout_grad = 0.0
    for s in range(seqs):
        out_own = combine_out(places[s], partials[s], cap)
        out_other = flip(out_own, "tp", 1)
        tokens_out.append((mids[s] + (out_own.astype(F32) + out_other.astype(F32))).astype(BF16))
        din_own, h_own = combine(places[s], returned_din[s], returned_h[s], cap)
        din_other = flip(din_own, "tp", 1)
        h_all = jnp.concatenate([h_own, flip(h_own, "tp", 1)], axis=0)
        gmid, datt, d_gain, d_router, d_wout = middle_back(
            din_own, din_other, h_all, gates[s], router, moes[s], mids[s], gain_moe, cotangent[s], attended[s], wout_own
        )
        gmids.append(gmid)
        gain_moe_grad += d_gain
        router_grad += d_router
        wout_grad += d_wout
        dq, dk, dv, rel = attend_back(
            queries[s], keys[s], values[s], datt, bias, lse[s], ids_query[s], ids_key[s]
        )
        rel_grad += rel
        dkv = jnp.stack([dk, dv]).reshape(2, 4, stretch, local)
        near = dkv[:, 0::2].astype(F32) + flip(dkv[:, 1::2], "ctx", 1).astype(F32)
        full = near[:, 0] + flip(near[:, 1].astype(BF16), "ctx", 2).astype(F32)
        projections.append(jnp.concatenate([dq[None], full.astype(BF16)], axis=0))
    grad_proj = jnp.concatenate(projections, axis=1)
    grad_wqkv = jnp.einsum("rd,jre->jde", own_normed, grad_proj, preferred_element_type=F32)
    dnormed_own = jnp.einsum("jre,jde->rd", grad_proj, wqkv, preferred_element_type=F32).astype(BF16)
    dnormed = dnormed_own.astype(F32) + flip(dnormed_own, "tp", 1).astype(F32)
    own_x = tokens_in.reshape(seqs * stretch, width).astype(F32)
    factor = norm_factor(own_x)
    unit = own_x * factor
    grad_gain_attn = jnp.sum(dnormed * unit, axis=0)
    scaled = dnormed * gain_attn.astype(F32)
    dres = factor * (scaled - unit * jnp.mean(scaled * unit, axis=-1, keepdims=True))
    grad_tokens = jnp.concatenate(gmids, axis=0) + dres

    rel_flat = rel_grad.reshape(heads, 4, 2 * stretch)
    grad_table = jnp.einsum("bmn,hbm->nh", hot_windows, rel_flat, precision=FULL_PRECISION)
    router_grad = router_grad.reshape(2, dp, width)
    router_grad = jnp.where(tp == 0, router_grad, router_grad[::-1]).transpose(1, 0, 2).reshape(expert_count, width).T

    def reduced(value, dim):
        return lax.psum(lax.psum_scatter(value, "dp", scatter_dimension=dim, tiled=True), "ctx")

    g_attn = reduced(grad_gain_attn, 0)
    g_qkv = reduced(grad_wqkv, 1)
    g_wout = reduced(wout_grad, 1)
    g_table = reduced(grad_table, 0)
    g_moe = reduced(gain_moe_grad[0], 0)
    g_router = reduced(router_grad, 0)
    return (
        jnp.stack(tokens_out),
        grad_tokens.reshape(seqs, stretch, width),
        g_attn[None],
        g_qkv[None],
        g_wout[None],
        g_table[None],
        g_moe[None],
        g_router[None],
        grad_expert_in[None],
        grad_expert_out[None],
    )


def solution(mesh):
    return jax.shard_map(
        on_device,
        mesh=mesh,
        in_specs=(
            P("dp", "ctx", None),
            P("dp", None),
            P(),
            P("dp", "ctx", None),
            P(None, "dp"),
            P(None, None, "dp", "tp"),
            P(None, "tp", "dp"),
            P(None, "dp", "tp"),
            P(None, "dp"),
            P(None, "dp", None),
            P(None, "dp", "ctx", "tp"),
            P(None, "dp", "tp", "ctx"),
            P("dp", "ctx", None),
        ),
        out_specs=(
            P("dp", "ctx", None),
            P("dp", "ctx", None),
            P(None, "dp"),
            P(None, None, "dp", "tp"),
            P(None, "tp", "dp"),
            P(None, "dp", "tp"),
            P(None, "dp"),
            P(None, "dp", None),
            P(None, "dp", "ctx", "tp"),
            P(None, "dp", "tp", "ctx"),
        ),
        check_vma=False,
    )
```

time: 1520 us -> 765 us (0.50)
  local copies, waits for them, and re-layouts: 586 us -> 88.8 us
  waiting for transfers between devices: 424 us -> 154 us
  Pallas kernels: 0 us -> 175 us
  matrix products: 162 us -> 19.4 us
  other arithmetic: 106 us -> 54 us
  starting transfers between devices: 22.3 us -> 69.1 us
    all_to_all x4 -> x10, waiting for transfers between devices: 215 us -> 20.4 us  [all_to_all_dp(): return lax.all_to_all(value, 'dp', split_axis=0, concat_axis=0, tiled=True)]
    rev x8 -> x3, local copies, waits for them, and re-layouts: 179 us -> 3.55 us  [the longest x1 3.3 us: on_device(): router_grad[::-1]]
    pallas_call x0 -> x23, Pallas kernels: none -> 175 us  [the longest x3 78.6 us: experts(): pl.pallas_call(functools.partial(expert_kernel, first, final, tiles, grou...]
    dot_general x52 -> x8, matrix products: 158 us -> 19.4 us  [the longest x1 5.57 us: on_device(): jnp.dot(flat, wqkv[2], preferred_element_type=F32).astype(BF16)]
    ppermute x0 -> x26, waiting for transfers between devices: none -> 94.4 us  [flip(): return lax.ppermute(value, axis, [(i, i ^ bit) for i in range(count)])]
    all_to_all x0 -> x6, blocking collectives: none -> 88.6 us  [all_to_all_dp(): return lax.all_to_all(value, 'dp', split_axis=0, concat_axis=0, tiled=True)]
    reshape x8 -> x6, local copies, waits for them, and re-layouts: 81.3 us -> 4.71 us  [the longest x2 2.71 us: on_device(): router_grad = router_grad.reshape(2, dp, width)]
    all_gather x3 -> x4, blocking collectives: 139 us -> 64.9 us  [the longest x1 21.3 us: on_device(): table = lax.all_gather(bias_table[0], 'dp', axis=0, tiled=True)]
  transfers between devices with their start and end apart: 20 -> 42, of which waited for: 9 -> 11; matrix products, arithmetic and copies ran while one was open for 42% -> 18% of each run, Pallas kernels for 0% -> 23%
where the time goes in v1:
time: 765 us; the launch traced here: 758 us
  blocking collectives  182 us (24%)
  Pallas kernels  175 us (23%)
  waiting for transfers between devices  154 us (20%)
  local copies, waits for them, and re-layouts  88.8 us (12%)
  starting transfers between devices  69.1 us (9%)
  other arithmetic  54 us (7%)
  matrix products  19.4 us (3%)
  between operations  16.9 us (2%)
    ppermute x26, waiting for transfers between devices, flip(): return lax.ppermute(value, axis, [(i, i ^ bit) for i in range(count)])  94.4 us
    all_to_all x6, blocking collectives, all_to_all_dp(): return lax.all_to_all(value, 'dp', split_axis=0, concat_axis=0, tiled=True)  88.6 us
    pallas_call x3, Pallas kernels, experts(): pl.pallas_call(functools.partial(expert_kernel, first, final, tiles, grou...  78.6 us
    unnamed x177, local copies, waits for them, and re-layouts  48.5 us
    all_to_all x10, starting transfers between devices, all_to_all_dp(): return lax.all_to_all(value, 'dp', split_axis=0, concat_axis=0, tiled=True)  44.9 us
    psum x1, waiting for transfers between devices, reduced(): lax.psum(lax.psum_scatter(value, 'dp', scatter_dimension=dim, tiled=True)...  37.9 us
    pallas_call x3, Pallas kernels, attend_back(): pl.pallas_call(attend_back_kernel, name='attend_back', grid=(pairs,), in_...  26 us
    ppermute x26, starting transfers between devices, flip(): return lax.ppermute(value, axis, [(i, i ^ bit) for i in range(count)])  23.8 us
  transfers between devices with their start and end apart: 42, of which 11 were waited for; matrix products, arithmetic and copies ran while one was open for 18% of the time, Pallas kernels for 23%

profile of v1, /device:TPU:0, one launch (start us, length us, event | category | flops | bytes accessed | tf_op | source)
XLA Modules:
  0.0 758.4 jit_solution(14488090134801295087)
XLA Ops:
  9.8 3.0 collective-permute-start.4
  12.8 26.0 %collective-permute-done.4 = bf16[2,192,1536]{2,1,0:T(8,128)(2,1)S(1)} collective-permute-done((bf16[2,192,1536]{2,1,0:T(8,128)(2,1)S(1)}, bf16[2,192,1536]{2,1,0:T(8,128)(2,1)S(1)}, u32[]{:S(2)}, u32[]{:S(2)}) %collective-permute-start.4) | collective-permute-done | bytes 1179680 | tf_op jit(solution)/shard_map/ppermute | solution.py:500
  41.3 20.9 %all-gather.2 = bf16[1,384,768]{1,2,0:T(8,128)(2,1)S(1)} all-gather(bf16[1,384,192]{1,2,0:T(8,128)(2,1)S(1)} %copy-done.39), channel_id=4, replica_groups=mesh['dp'=4,'ctx'=4,'tp'=2] {'dp'}, dimensions={2}, use_global_device_ids=true | all-gather | bytes 737280 | tf_op jit(solution)/shard_map/all_gather | solution.py:524
  66.4 4.1 dispatch_rows.1
  70.6 4.7 all-to-all-start.1
  75.4 36.2 %collective-permute-done = bf16[3,256,768]{2,1,0:T(8,128)(2,1)S(1)} collective-permute-done((bf16[3,256,768]{2,1,0:T(8,128)(2,1)S(1)}, bf16[3,256,768]{2,1,0:T(8,128)(2,1)S(1)}, u32[]{:S(2)}, u32[]{:S(2)}) %collective-permute-start) | collective-permute-done | bytes 1179680 | tf_op jit(solution)/shard_map/ppermute | solution.py:500
  113.3 7.9 %all-gather.5 = bf16[4,192,2]{1,2,0:T(2,128)(2,1)S(1)} all-gather(bf16[1,192,2]{1,2,0:T(2,128)(2,1)S(1)} %maximum_bitcast_fusion), channel_id=1, replica_groups=mesh['dp'=4,'ctx'=4,'tp'=2] {'dp'}, dimensions={0}, use_global_device_ids=true | all-gather | bytes 3840 | tf_op jit(solution)/shard_map/all_gather | solution.py:527
  121.9 21.3 %all-gather.1 = bf16[1,32,6]{2,0,1:T(2,128)(2,1)S(1)} all-gather(bf16[1,8,6]{2,0,1:T(2,128)(2,1)S(1)} %copy.100), channel_id=3, replica_groups=mesh['dp'=4,'ctx'=4,'tp'=2] {'dp'}, dimensions={1}, use_global_device_ids=true | all-gather | bytes 480 | tf_op jit(solution)/shard_map/all_gather | solution.py:526
  144.9 14.8 %all-gather.3 = bf16[1,768,8]{2,0,1:T(2,128)(2,1)S(1)} all-gather(bf16[1,192,8]{2,0,1:T(2,128)(2,1)S(1)} %copy.106), channel_id=5, replica_groups=mesh['dp'=4,'ctx'=4,'tp'=2] {'dp'}, dimensions={1}, use_global_device_ids=true | all-gather | bytes 15360 | tf_op jit(solution)/shard_map/all_gather | solution.py:529
  163.9 4.5 expand_bias.1.bias_ref
  181.0 5.6 convolution_convert_fusion
  186.6 2.9 convolution_convert_fusion.1
  191.8 7.4 attend.4
  199.6 7.4 attend.5
  208.7 7.8 %attend.3 = (bf16[256,384]{1,0:T(8,128)(2,1)}, f32[3,2,256]{2,1,0:T(2,128)}) custom-call(bf16[256,384]{1,0:T(8,128)(2,1)} %get-tuple-element.211.q_ref, bf16[1024,384]{1,0:T(8,128)(2,1)} %get-tuple-element.238.k_ref, bf16[1024,384]{1,0:T(8,128)(2,1)} %get-tuple-element.195.v_ref, bf16[6,1024,256]{2,1,0:T(8,128)(2,1)} %expand_bias.1.bias_ref, ...), custom_call_target="tpu_custom_call" | custom-call | flops 805306368 | bytes 3145728 | tf_op jit(solution)/shard_map/attend/pallas_call | solution.py:91
  219.9 3.8 middle_stage.5
  223.7 3.5 all-to-all-start.8
  227.9 3.8 middle_stage.4
  232.6 4.1 all-to-all-start.5
  237.5 3.8 middle_stage.3
  242.2 9.7 %all_to_all.80.gate_ref = f32[4,1,128]{2,1,0:T(1,128)} all-to-all(f32[4,1,128]{2,1,0:T(1,128)} %get-tuple-element.79), channel_id=1, replica_groups=mesh['dp'=4,'ctx'=4,'tp'=2] {'dp'}, dimensions={0} | all-to-all | bytes 4096 | tf_op jit(solution)/shard_map/all_to_all | solution.py:504
  251.9 23.8 %all_to_all.81.x_ref = bf16[4,128,768]{2,1,0:T(8,128)(2,1)} all-to-all(bf16[4,128,768]{2,1,0:T(8,128)(2,1)} %get-tuple-element.78), channel_id=1, replica_groups=mesh['dp'=4,'ctx'=4,'tp'=2] {'dp'}, dimensions={0} | all-to-all | bytes 1572864 | tf_op jit(solution)/shard_map/all_to_all | solution.py:504
  275.7 3.5 all-to-all-start.4
  279.3 25.1 %experts.3 = (bf16[4,128,768]{2,1,0:T(8,128)(2,1)}, bf16[4,128,768]{2,1,0:T(8,128)(2,1)}, f32[4,1,128]{2,1,0:T(1,128)}, f32[2,4,2,192,1536]{4,3,2,1,0:T(8,128)}) custom-call(bf16[4,128,768]{2,1,0:T(8,128)(2,1)} %all_to_all.81.x_ref, bf16[4,3,128,768]{3,2,1,0:T(8,128)(2,1)} %all-to-all-done.1.g_ref, f32[4,1,128]{2,1,0:T(1,128)} %all_to_all.80.gate_ref, ...), custom_call_target="tpu_custom_call" | custom-call | flops 14495514624 | bytes 47185920 | tf_op jit(solution)/shard_map/experts/pallas_call | solution.py:378
  304.4 5.0 all-to-all-start.7
  309.4 26.9 %experts.4 = (bf16[4,128,768]{2,1,0:T(8,128)(2,1)}, bf16[4,128,768]{2,1,0:T(8,128)(2,1)}, f32[4,1,128]{2,1,0:T(1,128)}, f32[2,4,2,192,1536]{4,3,2,1,0:T(8,128)}) custom-call(bf16[4,128,768]{2,1,0:T(8,128)(2,1)} %copy-done.27, bf16[4,3,128,768]{3,2,1,0:T(8,128)(2,1)} %all-to-all-done.1.g_ref, ...), custom_call_target="tpu_custom_call", output_to_operand_aliasing={{3}: (4, {})} | custom-call | flops 14495514624 | bytes 47185920 | tf_op jit(solution)/shard_map/experts/pallas_call | solution.py:378
  336.3 5.3 all-to-all-start.11
  341.6 26.6 %experts.5 = (bf16[4,128,768]{2,1,0:T(8,128)(2,1)}, bf16[4,128,768]{2,1,0:T(8,128)(2,1)}, f32[4,1,128]{2,1,0:T(1,128)}, bf16[2,4,2,192,1536]{4,3,2,1,0:T(8,128)(2,1)}) custom-call(bf16[4,128,768]{2,1,0:T(8,128)(2,1)} %copy-done.28, bf16[4,3,128,768]{3,2,1,0:T(8,128)(2,1)} %all-to-all-done.1.g_ref, f32[4,1,128]{2,1,0:T(1,128)} %copy-done.57, ...), custom_call_target="tpu_custom_call" | custom-call | flops 14495514624 | bytes 47185920 | tf_op jit(solution)/shard_map/experts/pallas_call | solution.py:378
  368.3 10.7 %all_to_all.82.h_ref = f32[4,1,128]{2,1,0:T(1,128)} all-to-all(f32[4,1,128]{2,1,0:T(1,128)} %get-tuple-element.108), channel_id=1, replica_groups=mesh['dp'=4,'ctx'=4,'tp'=2] {'dp'}, dimensions={0} | all-to-all | bytes 4096 | tf_op jit(solution)/shard_map/all_to_all | solution.py:504
  379.0 8.6 %all_to_all.83.h_ref = f32[4,1,128]{2,1,0:T(1,128)} all-to-all(f32[4,1,128]{2,1,0:T(1,128)S(1)} %copy-done.59), channel_id=1, replica_groups=mesh['dp'=4,'ctx'=4,'tp'=2] {'dp'}, dimensions={0} | all-to-all | bytes 4096 | tf_op jit(solution)/shard_map/all_to_all | solution.py:504
  387.5 16.8 %all_to_all.84.din_ref = bf16[4,128,768]{2,1,0:T(8,128)(2,1)} all-to-all(bf16[4,128,768]{2,1,0:T(8,128)(2,1)S(1)} %copy-done.25), channel_id=1, replica_groups=mesh['dp'=4,'ctx'=4,'tp'=2] {'dp'}, dimensions={0} | all-to-all | bytes 1572864 | tf_op jit(solution)/shard_map/all_to_all | solution.py:504
  404.4 19.0 %all_to_all.85.din_ref = bf16[4,128,768]{2,1,0:T(8,128)(2,1)} all-to-all(bf16[4,128,768]{2,1,0:T(8,128)(2,1)S(1)} %copy-done.26), channel_id=1, replica_groups=mesh['dp'=4,'ctx'=4,'tp'=2] {'dp'}, dimensions={0} | all-to-all | bytes 1572864 | tf_op jit(solution)/shard_map/all_to_all | solution.py:504
  423.3 3.5 all-to-all-start.14
  431.0 4.9 slice.260
  441.1 5.1 all-to-all-start.3
  454.2 4.6 middle_back.3
  458.8 8.6 %attend_back.3 = (bf16[256,384]{1,0:T(8,128)(2,1)}, bf16[1024,384]{1,0:T(8,128)(2,1)}, bf16[1024,384]{1,0:T(8,128)(2,1)}, f32[3,2,4,512]{3,2,1,0:T(4,128)}) custom-call(bf16[256,384]{1,0:T(8,128)(2,1)} %get-tuple-element.211.q_ref, bf16[1024,384]{1,0:T(8,128)(2,1)} %get-tuple-element.238.k_ref, bf16[1024,384]{1,0:T(8,128)(2,1)} %get-tuple-element.195.v_ref, ...), custom_call_target="tpu_custom_call" | custom-call | flops 2013265920 | bytes 4194304 | tf_op jit(solution)/shard_map/attend_back/pallas_call | solution.py:170
  469.9 4.6 middle_back.4
  475.2 4.6 middle_back.5
  483.9 3.3 rev.11
  491.6 8.8 %attend_back.4 = (bf16[256,384]{1,0:T(8,128)(2,1)}, bf16[1024,384]{1,0:T(8,128)(2,1)}, bf16[1024,384]{1,0:T(8,128)(2,1)}, f32[3,2,4,512]{3,2,1,0:T(4,128)}) custom-call(bf16[256,384]{1,0:T(8,128)(2,1)} %get-tuple-element.213.q_ref, bf16[1024,384]{1,0:T(8,128)(2,1)} %get-tuple-element.236.k_ref, bf16[1024,384]{1,0:T(8,128)(2,1)} %get-tuple-element.197.v_ref, ...), custom_call_target="tpu_custom_call" | custom-call | flops 2013265920 | bytes 4194304 | tf_op jit(solution)/shard_map/attend_back/pallas_call | solution.py:170
  505.0 8.6 %attend_back.5 = (bf16[256,384]{1,0:T(8,128)(2,1)}, bf16[1024,384]{1,0:T(8,128)(2,1)}, bf16[1024,384]{1,0:T(8,128)(2,1)}, f32[3,2,4,512]{3,2,1,0:T(4,128)}) custom-call(bf16[256,384]{1,0:T(8,128)(2,1)} %get-tuple-element.212.q_ref, bf16[1024,384]{1,0:T(8,128)(2,1)} %get-tuple-element.237.k_ref, bf16[1024,384]{1,0:T(8,128)(2,1)} %get-tuple-element.196.v_ref, ...), custom_call_target="tpu_custom_call" | custom-call | flops 2013265920 | bytes 4194304 | tf_op jit(solution)/shard_map/attend_back/pallas_call | solution.py:170
  513.6 2.7 pad_maximum_fusion.5
  516.3 2.7 copy.131
  531.2 5.1 all-to-all-start.6
  537.9 6.2 collective-permute-done.19
  545.2 6.9 collective-permute-done.21
  553.9 3.4 convolution_bitcast_fusion
  557.2 6.2 copy.129
  563.5 4.3 copy.144
  567.9 5.1 all-to-all-start.9
  573.2 5.9 convert_add_fusion
  579.2 3.7 copy-done.1
  594.7 18.5 %all-to-all-done.9.part_ref = bf16[4,128,768]{2,1,0:T(8,128)(2,1)S(1)} async-done(((bf16[4,128,768]{2,1,0:T(8,128)(2,1)}), bf16[4,128,768]{2,1,0:T(8,128)(2,1)S(1)}, u32[]{:S(2)}, u32[]{:S(2)}) %all-to-all-start.9) | async-done | bytes 786464 | tf_op jit(solution)/shard_map/all_to_all | solution.py:504
  625.7 3.0 bitcast_convert_fusion
  629.6 7.7 %collective-permute-done.24 = bf16[2,2,192,1536]{3,2,1,0:T(8,128)(2,1)} collective-permute-done((bf16[2,2,192,1536]{3,2,1,0:T(8,128)(2,1)}, bf16[2,2,192,1536]{3,2,1,0:T(8,128)(2,1)}, u32[]{:S(2)}, u32[]{:S(2)}) %collective-permute-start.24) | collective-permute-done | bytes 2359328 | tf_op jit(solution)/shard_map/ppermute | solution.py:500
  647.2 9.5 %collective-permute-done.22 = bf16[768,768]{1,0:T(8,128)(2,1)S(1)} collective-permute-done((bf16[768,768]{1,0:T(8,128)(2,1)S(1)}, bf16[768,768]{1,0:T(8,128)(2,1)S(1)}, u32[]{:S(2)}, u32[]{:S(2)}) %collective-permute-start.22) | collective-permute-done | bytes 1179680 | tf_op jit(solution)/shard_map/ppermute | solution.py:500
  658.3 16.9 %all-reduce.6 = (f32[768]{0:T(1024)}, f32[32,6]{1,0:T(8,128)}, f32[768]{0:T(1024)}) all-reduce(f32[768]{0:T(1024)} %get-tuple-element.182, f32[32,6]{1,0:T(8,128)} %convolution_bitcast_fusion.1, f32[768]{0:T(1024)} %add_reduce_fusion), channel_id=7, replica_groups=mesh['dp'=4,'ctx'=4,'tp'=2] {'dp'}, use_global_device_ids=true, to_apply=%region_4.5.clone | all-reduce | flops 1728 | bytes 13824
  679.1 11.3 %all-reduce.4 = (f32[1,192]{1,0:T(1,128)}, f32[1,8,6]{2,1,0:T(8,128)}, f32[1,192]{1,0:T(1,128)}, f32[1,192,8]{1,2,0:T(8,128)}) all-reduce(f32[1,192]{1,0:T(1,128)} %bitcast.290, f32[1,8,6]{2,1,0:T(8,128)} %dynamic-slice_bitcast_fusion, f32[1,192]{1,0:T(1,128)} %bitcast.291, ...), channel_id=1, replica_groups=mesh['dp'=4,'ctx'=4,'tp'=2] {'ctx'}, use_global_device_ids=true, to_apply=%region_5.6 | all-reduce | flops 1968 | bytes 15744 | tf_op jit(solution)/shard_map/psum | solution.py:650
  692.4 3.8 maximum_add_fusion
  698.2 2.7 maximum_select_fusion
  704.0 4.9 slice_bitcast_fusion.1
  708.9 37.9 %all-reduce.9.cloned.1.call-done = (f32[1,3,192,384]{2,3,1,0:T(8,128)}, f32[1,384,192]{2,1,0:T(8,128)}) async-done(((f32[1,3,192,384]{2,3,1,0:T(8,128)}, f32[1,384,192]{2,1,0:T(8,128)}), (f32[1,3,192,384]{2,3,1,0:T(8,128)}, f32[1,384,192]{2,1,0:T(8,128)})) %all-reduce.9.cloned.1.call-update) | async-done | bytes 1179664 | tf_op jit(solution)/shard_map/psum | solution.py:650
  746.8 2.5 copy.125
  (337 shorter events, 139.7 us)
Async XLA Ops:
  7.2 170.7 %all-gather.9.cloned.1.call-start = ((), (), s32[]{:S(2)}) async-start(), calls=%async_computation.19 | async-start | bytes 2211840 | tf_op jit(solution)/shard_map/all_gather | solution.py:523
  7.9 271.3 %all-gather.11.cloned.1.call-start = ((), (), s32[]{:S(2)}) async-start(), calls=%async_computation.20 | async-start | bytes 11796480 | tf_op jit(solution)/shard_map/all_gather | solution.py:542
  9.8 29.0 %collective-permute-start.4 = (bf16[2,192,1536]{2,1,0:T(8,128)(2,1)S(1)}, bf16[2,192,1536]{2,1,0:T(8,128)(2,1)S(1)}, u32[]{:S(2)}, u32[]{:S(2)}) collective-permute-start(bf16[2,192,1536]{2,1,0:T(8,128)(2,1)S(1)} %get-tuple-element.202), channel_id=1, source_target_pairs={{0,1},{1,0},{2,3},{3,2},{4,5},{5,4},{6,7},{7,6},{8,9},{9,8},{10,11... | collective-permute-start | bytes 3538952 | tf_op jit(solution)/shard_map/ppermute | solution.py:500
  40.4 23.6 %copy-start = (bf16[3,256,768]{2,1,0:T(8,128)(2,1)S(1)}, bf16[3,256,768]{2,1,0:T(8,128)(2,1)}, u32[]{:S(2)}) copy-start(bf16[3,256,768]{2,1,0:T(8,128)(2,1)} %param.13) | copy-start | bytes 3538948
  40.4 25.2 %copy-start.49 = (s32[3,256,2]{1,2,0:T(2,128)S(1)}, s32[3,256,2]{1,2,0:T(2,128)}, u32[]{:S(2)}) copy-start(s32[3,256,2]{1,2,0:T(2,128)} %param.16) | copy-start | bytes 18436
  62.5 154.5 %copy-start.2 = (bf16[1,384,768]{2,1,0:T(8,128)(2,1)}, bf16[1,384,768]{2,1,0:T(8,128)(2,1)S(1)}, u32[]{:S(2)}) copy-start(bf16[1,384,768]{2,1,0:T(8,128)(2,1)S(1)} %copy.105) | copy-start | bytes 1769476
  62.5 154.5 %collective-permute-start.3 = (bf16[384,768]{1,0:T(8,128)(2,1)S(1)}, bf16[384,768]{1,0:T(8,128)(2,1)}, u32[]{:S(2)}, u32[]{:S(2)}) collective-permute-start(bf16[384,768]{1,0:T(8,128)(2,1)S(1)} %bitcast.241), channel_id=1, source_target_pairs={{0,1},{1,0},{2,3},{3,2},{4,5},{5,4},{6,7},{7,6},{8,9},{9,8},{10,11... | collective-permute-start | bytes 1769480 | tf_op jit(solution)/shard_map/ppermute | solution.py:500
  64.0 47.6 %collective-permute-start = (bf16[3,256,768]{2,1,0:T(8,128)(2,1)S(1)}, bf16[3,256,768]{2,1,0:T(8,128)(2,1)S(1)}, u32[]{:S(2)}, u32[]{:S(2)}) collective-permute-start(bf16[3,256,768]{2,1,0:T(8,128)(2,1)S(1)} %copy-done), channel_id=1, source_target_pairs={{0,4},{2,6},{4,0},{6,2},{1,5},{3,7},{5,1},{7,3},{8,12},{10,14},{12... | collective-permute-start | bytes 3538952 | tf_op jit(solution)/shard_map/ppermute | solution.py:500
  70.6 153.1 %all-to-all-start.1 = ((bf16[4,3,128,768]{3,2,1,0:T(8,128)(2,1)}), bf16[4,3,128,768]{3,2,1,0:T(8,128)(2,1)}, u32[]{:S(2)}, u32[]{:S(2)}) async-start(bf16[4,3,128,768]{3,2,1,0:T(8,128)(2,1)} %dispatch_rows.1), calls=%async_computation.1 | async-start | bytes 4718592 | tf_op jit(solution)/shard_map/all_to_all | solution.py:504
  111.6 31.7 %copy-start.50 = (bf16[1,192,8]{1,2,0:T(8,128)(2,1)S(1)}, bf16[1,192,8]{1,2,0:T(8,128)(2,1)}, u32[]{:S(2)}) copy-start(bf16[1,192,8]{1,2,0:T(8,128)(2,1)} %param.22) | copy-start | bytes 9220
  111.6 31.8 %copy-start.48 = (s32[2047]{0:T(1024)S(1)}, s32[2047]{0:T(1024)}, u32[]{:S(2)}) copy-start(s32[2047]{0:T(1024)} %param.15) | copy-start | bytes 24568
  113.2 58.1 %collective-permute-start.1 = (bf16[2,3,256,768]{3,2,1,0:T(8,128)(2,1)}, bf16[2,3,256,768]{3,2,1,0:T(8,128)(2,1)}, u32[]{:S(2)}, u32[]{:S(2)}) collective-permute-start(bf16[2,3,256,768]{3,2,1,0:T(8,128)(2,1)} %pad_maximum_fusion.1), channel_id=1, source_target_pairs={{0,2},{2,0},{4,6},{6,4},{1,3},{3,1},{5,7},{7,5},{8,10},{10,8},{12,... | collective-permute-start | bytes 7077896 | tf_op jit(solution)/shard_map/ppermute | solution.py:500
  199.2 28.0 %collective-permute-start.6 = (bf16[256,384]{1,0:T(8,128)(2,1)}, bf16[256,384]{1,0:T(8,128)(2,1)S(1)}, u32[]{:S(2)}, u32[]{:S(2)}) collective-permute-start(bf16[256,384]{1,0:T(8,128)(2,1)} %get-tuple-element.81.own_ref.att_ref), channel_id=1, source_target_pairs={{0,1},{1,0},{2,3},{3,2},{4,5},{5,4},{6,7},{7,6},{8,9},{9,8},{10,11... | collective-permute-start | bytes 589832 | tf_op jit(solution)/shard_map/ppermute | solution.py:500
  207.1 12.1 %collective-permute-start.8 = (bf16[256,384]{1,0:T(8,128)(2,1)}, bf16[256,384]{1,0:T(8,128)(2,1)S(1)}, u32[]{:S(2)}, u32[]{:S(2)}) collective-permute-start(bf16[256,384]{1,0:T(8,128)(2,1)} %get-tuple-element.87.own_ref.att_ref), channel_id=1, source_target_pairs={{0,1},{1,0},{2,3},{3,2},{4,5},{5,4},{6,7},{7,6},{8,9},{9,8},{10,11... | collective-permute-start | bytes 589832 | tf_op jit(solution)/shard_map/ppermute | solution.py:500
  216.5 20.3 %collective-permute-start.2 = (bf16[256,384]{1,0:T(8,128)(2,1)}, bf16[256,384]{1,0:T(8,128)(2,1)S(1)}, u32[]{:S(2)}, u32[]{:S(2)}) collective-permute-start(bf16[256,384]{1,0:T(8,128)(2,1)} %get-tuple-element.76.own_ref.att_ref), channel_id=1, source_target_pairs={{0,1},{1,0},{2,3},{3,2},{4,5},{5,4},{6,7},{7,6},{8,9},{9,8},{10,11... | collective-permute-start | bytes 589832 | tf_op jit(solution)/shard_map/ppermute | solution.py:500
  223.7 8.9 %all-to-all-start.8 = ((f32[4,1,128]{2,1,0:T(1,128)}), f32[4,1,128]{2,1,0:T(1,128)S(1)}, u32[]{:S(2)}, u32[]{:S(2)}) async-start(f32[4,1,128]{2,1,0:T(1,128)} %get-tuple-element.90), calls=%async_computation.8 | async-start | bytes 4096 | tf_op jit(solution)/shard_map/all_to_all | solution.py:504
  232.6 43.1 %copy-start.57 = (f32[4,1,128]{2,1,0:T(1,128)}, f32[4,1,128]{2,1,0:T(1,128)S(1)}, u32[]{:S(2)}) copy-start(f32[4,1,128]{2,1,0:T(1,128)S(1)} %all-to-all-done.8.gate_ref) | copy-start | bytes 6148
  232.6 9.6 %all-to-all-start.5 = ((f32[4,1,128]{2,1,0:T(1,128)}), f32[4,1,128]{2,1,0:T(1,128)S(1)}, u32[]{:S(2)}, u32[]{:S(2)}) async-start(f32[4,1,128]{2,1,0:T(1,128)} %get-tuple-element.84), calls=%async_computation.5 | async-start | bytes 4096 | tf_op jit(solution)/shard_map/all_to_all | solution.py:504
  242.2 62.2 %copy-start.58 = (f32[4,1,128]{2,1,0:T(1,128)}, f32[4,1,128]{2,1,0:T(1,128)S(1)}, u32[]{:S(2)}) copy-start(f32[4,1,128]{2,1,0:T(1,128)S(1)} %all-to-all-done.5.gate_ref) | copy-start | bytes 6148
  275.7 28.6 %all-to-all-start.4 = ((bf16[4,128,768]{2,1,0:T(8,128)(2,1)}), bf16[4,128,768]{2,1,0:T(8,128)(2,1)S(1)}, u32[]{:S(2)}, u32[]{:S(2)}) async-start(bf16[4,128,768]{2,1,0:T(8,128)(2,1)} %get-tuple-element.83), calls=%async_computation.4 | async-start | bytes 1572864 | tf_op jit(solution)/shard_map/all_to_all | solution.py:504
  304.4 31.9 %all-to-all-start.7 = ((bf16[4,128,768]{2,1,0:T(8,128)(2,1)}), bf16[4,128,768]{2,1,0:T(8,128)(2,1)S(1)}, u32[]{:S(2)}, u32[]{:S(2)}) async-start(bf16[4,128,768]{2,1,0:T(8,128)(2,1)} %get-tuple-element.89), calls=%async_computation.7 | async-start | bytes 1572864 | tf_op jit(solution)/shard_map/all_to_all | solution.py:504
  336.3 32.0 %all-to-all-start.11 = ((f32[4,1,128]{2,1,0:T(1,128)}), f32[4,1,128]{2,1,0:T(1,128)S(1)}, u32[]{:S(2)}, u32[]{:S(2)}) async-start(f32[4,1,128]{2,1,0:T(1,128)} %get-tuple-element.94), calls=%async_computation.11 | async-start | bytes 4096 | tf_op jit(solution)/shard_map/all_to_all | solution.py:504
  341.6 37.4 %copy-start.59 = (f32[4,1,128]{2,1,0:T(1,128)S(1)}, f32[4,1,128]{2,1,0:T(1,128)}, u32[]{:S(2)}) copy-start(f32[4,1,128]{2,1,0:T(1,128)} %get-tuple-element.101) | copy-start | bytes 6148
  341.6 45.9 %copy-start.25 = (bf16[4,128,768]{2,1,0:T(8,128)(2,1)S(1)}, bf16[4,128,768]{2,1,0:T(8,128)(2,1)}, u32[]{:S(2)}) copy-start(bf16[4,128,768]{2,1,0:T(8,128)(2,1)} %get-tuple-element.93) | copy-start | bytes 2359300
  341.6 62.7 %copy-start.26 = (bf16[4,128,768]{2,1,0:T(8,128)(2,1)S(1)}, bf16[4,128,768]{2,1,0:T(8,128)(2,1)}, u32[]{:S(2)}) copy-start(bf16[4,128,768]{2,1,0:T(8,128)(2,1)} %get-tuple-element.100) | copy-start | bytes 2359300
  368.3 55.1 %copy-start.47 = (f32[4,1,128]{2,1,0:T(1,128)}, f32[4,1,128]{2,1,0:T(1,128)S(1)}, u32[]{:S(2)}) copy-start(f32[4,1,128]{2,1,0:T(1,128)S(1)} %all-to-all-done.11.h_ref) | copy-start | bytes 6148
  404.3 25.7 %copy-start.11 = (bf16[3,256,768]{2,1,0:T(8,128)(2,1)S(1)}, bf16[3,256,768]{2,1,0:T(8,128)(2,1)}, u32[]{:S(2)}) copy-start(bf16[3,256,768]{2,1,0:T(8,128)(2,1)} %rows_ref.1) | copy-start | bytes 3538948
  423.3 16.9 %all-to-all-start.14 = ((bf16[4,128,768]{2,1,0:T(8,128)(2,1)}), bf16[4,128,768]{2,1,0:T(8,128)(2,1)S(1)}, u32[]{:S(2)}, u32[]{:S(2)}) async-start(bf16[4,128,768]{2,1,0:T(8,128)(2,1)} %get-tuple-element.107), calls=%async_computation.14 | async-start | bytes 1572864 | tf_op jit(solution)/shard_map/all_to_all | solution.py:504
  429.2 25.0 %collective-permute-start.10 = (bf16[256,768]{1,0:T(8,128)(2,1)}, bf16[256,768]{1,0:T(8,128)(2,1)}, u32[]{:S(2)}, u32[]{:S(2)}) collective-permute-start(bf16[256,768]{1,0:T(8,128)(2,1)} %get-tuple-element.95.own_ref), channel_id=1, source_target_pairs={{0,1},{1,0},{2,3},{3,2},{4,5},{5,4},{6,7},{7,6},{8,9},{9,8},{10,11... | collective-permute-start | bytes 1179656 | tf_op jit(solution)/shard_map/ppermute | solution.py:500
  435.9 137.3 %collective-permute-start.23 = (bf16[2,2,2,192,1536]{4,3,2,1,0:T(8,128)(2,1)}, bf16[2,2,2,192,1536]{4,3,2,1,0:T(8,128)(2,1)}, u32[]{:S(2)}, u32[]{:S(2)}) collective-permute-start(bf16[2,2,2,192,1536]{4,3,2,1,0:T(8,128)(2,1)} %slice.260), channel_id=1, source_target_pairs={{0,2},{2,0},{4,6},{6,4},{1,3},{3,1},{5,7},{7,5},{8,10},{10,8},{12,... | collective-permute-start | bytes 14155784 | tf_op jit(solution)/shard_map/ppermute | solution.py:500
  435.9 13.8 %collective-permute-start.11 = (f32[4,256]{1,0:T(4,128)S(1)}, f32[4,256]{1,0:T(4,128)S(1)}, u32[]{:S(2)}, u32[]{:S(2)}) collective-permute-start(f32[4,256]{1,0:T(4,128)S(1)} %copy-done.51), channel_id=1, source_target_pairs={{0,1},{1,0},{2,3},{3,2},{4,5},{5,4},{6,7},{7,6},{8,9},{9,8},{10,11... | collective-permute-start | bytes 12296 | tf_op jit(solution)/shard_map/ppermute | solution.py:500
  439.4 12.9 %copy-start.52 = (f32[4,256]{1,0:T(4,128)S(1)}, f32[4,256]{1,0:T(4,128)}, u32[]{:S(2)}) copy-start(f32[4,256]{1,0:T(4,128)} %get-tuple-element.103) | copy-start | bytes 12292
  439.4 11.7 %collective-permute-start.13 = (f32[4,256]{1,0:T(4,128)}, f32[4,256]{1,0:T(4,128)S(1)}, u32[]{:S(2)}, u32[]{:S(2)}) collective-permute-start(f32[4,256]{1,0:T(4,128)} %get-tuple-element.103), channel_id=1, source_target_pairs={{0,1},{1,0},{2,3},{3,2},{4,5},{5,4},{6,7},{7,6},{8,9},{9,8},{10,11... | collective-permute-start | bytes 12296 | tf_op jit(solution)/shard_map/ppermute | solution.py:500
  441.1 90.1 %all-to-all-start.3 = ((bf16[4,128,768]{2,1,0:T(8,128)(2,1)}), bf16[4,128,768]{2,1,0:T(8,128)(2,1)S(1)}, u32[]{:S(2)}, u32[]{:S(2)}) async-start(bf16[4,128,768]{2,1,0:T(8,128)(2,1)} %get-tuple-element.80), calls=%async_computation.3 | async-start | bytes 1572864 | tf_op jit(solution)/shard_map/all_to_all | solution.py:504
  446.2 198.2 %reduce-scatter.14.cloned.1.call-start = ((), (), s32[]{:S(2)}) async-start(), calls=%async_computation.23 | async-start | bytes 491520
  448.5 4.4 collective-permute-start.15
  449.7 20.2 %collective-permute-start.12 = (bf16[256,768]{1,0:T(8,128)(2,1)}, bf16[256,768]{1,0:T(8,128)(2,1)}, u32[]{:S(2)}, u32[]{:S(2)}) collective-permute-start(bf16[256,768]{1,0:T(8,128)(2,1)} %get-tuple-element.102.own_ref), channel_id=1, source_target_pairs={{0,1},{1,0},{2,3},{3,2},{4,5},{5,4},{6,7},{7,6},{8,9},{9,8},{10,11... | collective-permute-start | bytes 1179656 | tf_op jit(solution)/shard_map/ppermute | solution.py:500
  451.1 23.3 %collective-permute-start.14 = (bf16[256,768]{1,0:T(8,128)(2,1)}, bf16[256,768]{1,0:T(8,128)(2,1)S(1)}, u32[]{:S(2)}, u32[]{:S(2)}) collective-permute-start(bf16[256,768]{1,0:T(8,128)(2,1)} %get-tuple-element.109.own_ref), channel_id=1, source_target_pairs={{0,1},{1,0},{2,3},{3,2},{4,5},{5,4},{6,7},{7,6},{8,9},{9,8},{10,11... | collective-permute-start | bytes 1179656 | tf_op jit(solution)/shard_map/ppermute | solution.py:500
  469.9 51.2 %collective-permute-start.16 = (bf16[2,2,256,384]{3,2,0,1:T(8,128)(2,1)}, bf16[2,2,256,384]{3,2,0,1:T(8,128)(2,1)}, u32[]{:S(2)}, u32[]{:S(2)}) collective-permute-start(bf16[2,2,256,384]{3,2,0,1:T(8,128)(2,1)} %slice.248), channel_id=1, source_target_pairs={{0,2},{2,0},{4,6},{6,4},{1,3},{3,1},{5,7},{7,5},{8,10},{10,8},{12,... | collective-permute-start | bytes 2359304 | tf_op jit(solution)/shard_map/ppermute | solution.py:500
  491.6 153.8 %reduce-scatter.12.cloned.1.call-start = ((), (), s32[]{:S(2)}) async-start(), calls=%async_computation.22 | async-start | bytes 1474560
  503.2 21.3 %collective-permute-start.18 = (bf16[2,2,256,384]{3,2,0,1:T(8,128)(2,1)}, bf16[2,2,256,384]{3,2,0,1:T(8,128)(2,1)}, u32[]{:S(2)}, u32[]{:S(2)}) collective-permute-start(bf16[2,2,256,384]{3,2,0,1:T(8,128)(2,1)} %slice.252), channel_id=1, source_target_pairs={{0,2},{2,0},{4,6},{6,4},{1,3},{3,1},{5,7},{7,5},{8,10},{10,8},{12,... | collective-permute-start | bytes 2359304 | tf_op jit(solution)/shard_map/ppermute | solution.py:500
  521.0 6.4 collective-permute-start.20
  523.3 13.1 %collective-permute-start.17 = (bf16[2,256,384]{2,1,0:T(8,128)(2,1)}, bf16[2,256,384]{2,1,0:T(8,128)(2,1)}, u32[]{:S(2)}, u32[]{:S(2)}) collective-permute-start(bf16[2,256,384]{2,1,0:T(8,128)(2,1)} %fusion.25), channel_id=1, source_target_pairs={{0,4},{2,6},{4,0},{6,2},{1,5},{3,7},{5,1},{7,3},{8,12},{10,14},{12... | collective-permute-start | bytes 1179656 | tf_op jit(solution)/shard_map/ppermute | solution.py:500
  526.6 17.4 %collective-permute-start.19 = (bf16[2,256,384]{2,1,0:T(8,128)(2,1)}, bf16[2,256,384]{2,1,0:T(8,128)(2,1)}, u32[]{:S(2)}, u32[]{:S(2)}) collective-permute-start(bf16[2,256,384]{2,1,0:T(8,128)(2,1)} %fusion.26), channel_id=1, source_target_pairs={{0,4},{2,6},{4,0},{6,2},{1,5},{3,7},{5,1},{7,3},{8,12},{10,14},{12... | collective-permute-start | bytes 1179656 | tf_op jit(solution)/shard_map/ppermute | solution.py:500
  530.1 21.9 %collective-permute-start.21 = (bf16[2,256,384]{2,1,0:T(8,128)(2,1)}, bf16[2,256,384]{2,1,0:T(8,128)(2,1)}, u32[]{:S(2)}, u32[]{:S(2)}) collective-permute-start(bf16[2,256,384]{2,1,0:T(8,128)(2,1)} %fusion.27), channel_id=1, source_target_pairs={{0,4},{2,6},{4,0},{6,2},{1,5},{3,7},{5,1},{7,3},{8,12},{10,14},{12... | collective-permute-start | bytes 1179656 | tf_op jit(solution)/shard_map/ppermute | solution.py:500
  531.2 13.9 %copy-start.12 = (bf16[4,128,768]{2,1,0:T(8,128)(2,1)}, bf16[4,128,768]{2,1,0:T(8,128)(2,1)S(1)}, u32[]{:S(2)}) copy-start(bf16[4,128,768]{2,1,0:T(8,128)(2,1)S(1)} %all-to-all-done.3.part_ref) | copy-start | bytes 2359300
  531.2 36.6 %all-to-all-start.6 = ((bf16[4,128,768]{2,1,0:T(8,128)(2,1)}), bf16[4,128,768]{2,1,0:T(8,128)(2,1)}, u32[]{:S(2)}, u32[]{:S(2)}) async-start(bf16[4,128,768]{2,1,0:T(8,128)(2,1)} %get-tuple-element.86), calls=%async_computation.6 | async-start | bytes 1572864 | tf_op jit(solution)/shard_map/all_to_all | solution.py:504
  536.4 164.5 %reduce-scatter.10.cloned.1.call-start = ((), (), s32[]{:S(2)}) async-start(), calls=%async_computation.21 | async-start | bytes 4423680
  536.4 15.6 %copy-start.10 = (f32[2,2,256,384]{3,2,0,1:T(8,128)S(1)}, f32[2,2,256,384]{3,2,0,1:T(8,128)}, u32[]{:S(2)}) copy-start(f32[2,2,256,384]{3,2,0,1:T(8,128)} %copy-done.9) | copy-start | bytes 4718596
  536.4 17.5 %copy-start.21 = (bf16[3,1,256,768]{3,2,1,0:T(8,128)(2,1)S(1)}, bf16[3,1,256,768]{3,2,1,0:T(8,128)(2,1)}, u32[]{:S(2)}) copy-start(bf16[3,1,256,768]{3,2,1,0:T(8,128)(2,1)} %copy-done.20) | copy-start | bytes 3538948
  536.4 17.5 %copy-start.64 = (bf16[256,384]{1,0:T(8,128)(2,1)S(1)}, bf16[256,384]{1,0:T(8,128)(2,1)}, u32[]{:S(2)}) copy-start(bf16[256,384]{1,0:T(8,128)(2,1)} %get-tuple-element.116) | copy-start | bytes 589828
  536.4 17.5 %copy-start.66 = (bf16[256,384]{1,0:T(8,128)(2,1)S(1)}, bf16[256,384]{1,0:T(8,128)(2,1)}, u32[]{:S(2)}) copy-start(bf16[256,384]{1,0:T(8,128)(2,1)} %get-tuple-element.121) | copy-start | bytes 589828
  536.4 17.5 %copy-start.68 = (bf16[256,384]{1,0:T(8,128)(2,1)S(1)}, bf16[256,384]{1,0:T(8,128)(2,1)}, u32[]{:S(2)}) copy-start(bf16[256,384]{1,0:T(8,128)(2,1)} %get-tuple-element.126) | copy-start | bytes 589828
  537.9 15.2 %copy-start.30 = (bf16[2,256,384]{2,1,0:T(8,128)(2,1)}, bf16[2,256,384]{2,1,0:T(8,128)(2,1)S(1)}, u32[]{:S(2)}) copy-start(bf16[2,256,384]{2,1,0:T(8,128)(2,1)S(1)} %fusion.21) | copy-start | bytes 1179652
  567.9 45.3 %all-to-all-start.9 = ((bf16[4,128,768]{2,1,0:T(8,128)(2,1)}), bf16[4,128,768]{2,1,0:T(8,128)(2,1)S(1)}, u32[]{:S(2)}, u32[]{:S(2)}) async-start(bf16[4,128,768]{2,1,0:T(8,128)(2,1)} %get-tuple-element.92), calls=%async_computation.9 | async-start | bytes 1572864 | tf_op jit(solution)/shard_map/all_to_all | solution.py:504
  573.0 173.8 %all-reduce.9.cloned.1.call-start = ((), (), s32[]{:S(2)}) async-start(), calls=%async_computation.24 | async-start | bytes 3145728 | tf_op jit(solution)/shard_map/psum | solution.py:650
  584.5 52.8 %collective-permute-start.24 = (bf16[2,2,192,1536]{3,2,1,0:T(8,128)(2,1)}, bf16[2,2,192,1536]{3,2,1,0:T(8,128)(2,1)}, u32[]{:S(2)}, u32[]{:S(2)}) collective-permute-start(bf16[2,2,192,1536]{3,2,1,0:T(8,128)(2,1)} %fusion.4), channel_id=1, source_target_pairs={{0,4},{2,6},{4,0},{6,2},{1,5},{3,7},{5,1},{7,3},{8,12},{10,14},{12... | collective-permute-start | bytes 7077896 | tf_op jit(solution)/shard_map/ppermute | solution.py:500
  587.6 30.5 %copy-start.17 = (f32[256,768]{1,0:T(8,128)S(1)}, f32[256,768]{1,0:T(8,128)}, u32[]{:S(2)}) copy-start(f32[256,768]{1,0:T(8,128)} %get-tuple-element.77.mid_ref) | copy-start | bytes 2359300
  590.2 27.9 %collective-permute-start.5 = (bf16[256,768]{1,0:T(8,128)(2,1)}, bf16[256,768]{1,0:T(8,128)(2,1)}, u32[]{:S(2)}, u32[]{:S(2)}) collective-permute-start(bf16[256,768]{1,0:T(8,128)(2,1)} %combine_out.3), channel_id=1, source_target_pairs={{0,1},{1,0},{2,3},{3,2},{4,5},{5,4},{6,7},{7,6},{8,9},{9,8},{10,11... | collective-permute-start | bytes 1179656 | tf_op jit(solution)/shard_map/ppermute | solution.py:500
  591.7 29.6 %copy-start.16 = (f32[256,768]{1,0:T(8,128)S(1)}, f32[256,768]{1,0:T(8,128)}, u32[]{:S(2)}) copy-start(f32[256,768]{1,0:T(8,128)} %get-tuple-element.82.mid_ref) | copy-start | bytes 2359300
  594.1 27.2 %collective-permute-start.7 = (bf16[256,768]{1,0:T(8,128)(2,1)}, bf16[256,768]{1,0:T(8,128)(2,1)}, u32[]{:S(2)}, u32[]{:S(2)}) collective-permute-start(bf16[256,768]{1,0:T(8,128)(2,1)} %combine_out.4), channel_id=1, source_target_pairs={{0,1},{1,0},{2,3},{3,2},{4,5},{5,4},{6,7},{7,6},{8,9},{9,8},{10,11... | collective-permute-start | bytes 1179656 | tf_op jit(solution)/shard_map/ppermute | solution.py:500
  616.4 8.0 %collective-permute-start.9 = (bf16[256,768]{1,0:T(8,128)(2,1)}, bf16[256,768]{1,0:T(8,128)(2,1)S(1)}, u32[]{:S(2)}, u32[]{:S(2)}) collective-permute-start(bf16[256,768]{1,0:T(8,128)(2,1)} %combine_out.5), channel_id=1, source_target_pairs={{0,1},{1,0},{2,3},{3,2},{4,5},{5,4},{6,7},{7,6},{8,9},{9,8},{10,11... | collective-permute-start | bytes 1179656 | tf_op jit(solution)/shard_map/ppermute | solution.py:500
  628.7 28.1 %collective-permute-start.22 = (bf16[768,768]{1,0:T(8,128)(2,1)S(1)}, bf16[768,768]{1,0:T(8,128)(2,1)S(1)}, u32[]{:S(2)}, u32[]{:S(2)}) collective-permute-start(bf16[768,768]{1,0:T(8,128)(2,1)S(1)} %bitcast_convert_fusion), channel_id=1, source_target_pairs={{0,1},{1,0},{2,3},{3,2},{4,5},{5,4},{6,7},{7,6},{8,9},{9,8},{10,11... | collective-permute-start | bytes 3538952 | tf_op jit(solution)/shard_map/ppermute | solution.py:500
  643.2 53.0 %collective-permute-start.25 = (bf16[2,192,1536]{2,1,0:T(8,128)(2,1)}, bf16[2,192,1536]{2,1,0:T(8,128)(2,1)}, u32[]{:S(2)}, u32[]{:S(2)}) collective-permute-start(bf16[2,192,1536]{2,1,0:T(8,128)(2,1)} %fusion.11), channel_id=1, source_target_pairs={{0,1},{1,0},{2,3},{3,2},{4,5},{5,4},{6,7},{7,6},{8,9},{9,8},{10,11... | collective-permute-start | bytes 3538952 | tf_op jit(solution)/shard_map/ppermute | solution.py:500
  (55 other events, 213.8 us)
Sparse Core Ops, SparseCore 0:
  9.6 48.9 all-gather.8
  60.7 82.2 all-gather.10
  491.7 22.0 reduce-scatter.13
  521.2 40.3 reduce-scatter.11
  568.0 77.9 reduce-scatter.9
  704.1 42.6 all-reduce.8

commit v2 on v1

--- a/solution.py
+++ b/solution.py
@@ -450,8 +450,8 @@
 
 
 def middle_back_kernel(
-    own_ref, other_ref, h_ref, gates_ref, router_ref, moe_ref, mid_ref, gain_ref, cot_ref, att_ref, wout_ref,
-    gmid_ref, datt_ref, gain_grad_ref, router_grad_ref, wout_grad_ref,
+    own_ref, other_ref, h_ref, gates_ref, router_ref, moe_ref, mid_ref, gain_ref, cot_ref, wout_ref,
+    gmid_ref, datt_ref, gain_grad_ref, router_grad_ref, low_ref,
 ):
     h = h_ref[...]
     dlogits = h - gates_ref[...] * jnp.sum(h, axis=0, keepdims=True)
@@ -474,12 +474,12 @@
     gmid_ref[...] = gmid
     dattn = gmid.astype(BF16)
     datt_ref[...] = dot_nt(dattn, wout_ref[...]).astype(BF16)
-    wout_grad_ref[...] = dot_tn(att_ref[...], dattn)
-
-
-def middle_back(own, other, h, gates, router, moe_in, mid, gain, cot, attended, wout):
+    low_ref[...] = dattn
+
+
+def middle_back(own, other, h, gates, router, moe_in, mid, gain, cot, wout):
     rows, width = mid.shape
-    local = attended.shape[1]
+    local = wout.shape[0]
     return pl.pallas_call(
         middle_back_kernel,
         name="middle_back",
@@ -488,11 +488,601 @@
             jax.ShapeDtypeStruct((rows, local), BF16),
             jax.ShapeDtypeStruct((1, width), F32),
             jax.ShapeDtypeStruct(router.shape, F32),
-            jax.ShapeDtypeStruct((local, width), F32),
+            jax.ShapeDtypeStruct((rows, width), BF16),
         ],
         compiler_params=params(),
-        cost_estimate=cost(6 * rows * width * local, 30 * rows * width),
-    )(own, other, h, gates, router, moe_in, mid, gain, cot, attended, wout)
+        cost_estimate=cost(2 * rows * width * local, 30 * rows * width),
+    )(own, other, h, gates, router, moe_in, mid, gain, cot, wout)
+
+
+MESH_ID = pl.DeviceIdType.MESH
+
+
+def remote(src, dst, send_sem, recv_sem, **where):
+    return pltpu.make_async_remote_copy(
+        src_ref=src, dst_ref=dst, send_sem=send_sem, recv_sem=recv_sem, device_id=where, device_id_type=MESH_ID
+    )
+
+
+def greet(peers):
+    barrier = pltpu.get_barrier_semaphore()
+    for where in peers:
+        pl.semaphore_signal(barrier, inc=1, device_id=where, device_id_type=MESH_ID)
+    pl.semaphore_wait(barrier, len(peers))
+
+
+def first_kernel(
+    seqs, tok_ref, wqkv_ref, wout_ref, table_ref, ga_ref, gm_ref, router_ref,
+    q_ref, k_ref, v_ref, normed_ref, wqkv_out, wout_out, table_out, gain_ref, gm_out, router_out,
+    tok_all, n_all, ga_all, gm_all, router_all,
+    z_send, z_recv, f_send, f_recv, t_send, t_recv, y_send, y_recv, l_sem,
+):
+    dp = lax.axis_index("dp")
+    ctx = lax.axis_index("ctx")
+    tp = lax.axis_index("tp")
+    core = ctx % 2
+    rows = wqkv_ref.shape[1]
+    half = rows // 2
+    orows = wout_ref.shape[0] // 2
+    greet([{"dp": dp ^ b} for b in (1, 2, 3)] + [{"ctx": ctx ^ 1}, {"ctx": ctx ^ 2}])
+
+    def w_rows(owner, side):
+        return pl.ds(pl.multiple_of(owner * rows + side * half, 16), half)
+
+    def o_rows(side):
+        return pl.ds(pl.multiple_of(side * orows, 16), orows)
+
+    def z_copies(b):
+        to = {"dp": dp ^ b}
+        return [
+            remote(ga_ref, ga_all.at[dp], z_send.at[0, b - 1], z_recv.at[0, b - 1], **to),
+            remote(gm_ref, gm_all.at[dp], z_send.at[1, b - 1], z_recv.at[1, b - 1], **to),
+            remote(table_ref, table_out.at[dp], z_send.at[2, b - 1], z_recv.at[2, b - 1], **to),
+            remote(router_ref, router_all.at[dp], z_send.at[3, b - 1], z_recv.at[3, b - 1], **to),
+            remote(
+                wqkv_ref.at[:, pl.ds(pl.multiple_of(core * half, 16), half)], wqkv_out.at[:, w_rows(dp, core)],
+                z_send.at[4, b - 1], z_recv.at[4, b - 1], **to,
+            ),
+            remote(
+                wout_ref.at[o_rows(core)], wout_out.at[dp, o_rows(core)],
+                z_send.at[5, b - 1], z_recv.at[5, b - 1], **to,
+            ),
+        ]
+
+    small = [z_copies(b) for b in (1, 2, 3)]
+    for kind in range(6):
+        for b in (3, 2, 1):
+            small[b - 1][kind].start()
+    beside = remote(tok_ref, tok_all.at[1], t_send.at[0], t_recv.at[0], ctx=ctx ^ 1)
+    beside.start()
+    across = [remote(tok_ref.at[s], tok_all.at[2, s], y_send.at[s], y_recv.at[s], ctx=ctx ^ 2) for s in range(seqs)]
+    for copy in across:
+        copy.start()
+    own = [
+        pltpu.make_async_copy(tok_ref, tok_all.at[0], l_sem.at[0]),
+        pltpu.make_async_copy(ga_ref, ga_all.at[dp], l_sem.at[1]),
+        pltpu.make_async_copy(gm_ref, gm_all.at[dp], l_sem.at[2]),
+        pltpu.make_async_copy(table_ref, table_out.at[dp], l_sem.at[3]),
+        pltpu.make_async_copy(router_ref, router_all.at[dp], l_sem.at[4]),
+        pltpu.make_async_copy(wqkv_ref, wqkv_out.at[:, pl.ds(pl.multiple_of(dp * rows, 16), rows)], l_sem.at[5]),
+        pltpu.make_async_copy(wout_ref, wout_out.at[dp], l_sem.at[6]),
+    ]
+    for copy in own:
+        copy.start()
+    for copy in own:
+        copy.wait()
+
+    for kind in range(4):
+        for b in (3, 2, 1):
+            small[b - 1][kind].wait_recv()
+    count = ga_all.shape[0]
+    piece = ga_all.shape[2]
+    width = count * piece
+    row = lax.broadcasted_iota(jnp.int32, (piece, width), 0)
+    col = lax.broadcasted_iota(jnp.int32, (piece, width), 1)
+    gain = 0.0
+    gain_m = 0.0
+    for d in range(count):
+        spread = jnp.where(col == row + d * piece, 1.0, 0.0).astype(BF16)
+        gain = gain + dot(ga_all[d], spread)
+        gain_m = gain_m + dot(gm_all[d], spread)
+    gain_ref[...] = gain
+    gm_out[...] = gain_m.astype(BF16)
+    experts_n = router_ref.shape[1]
+    slot_row = lax.broadcasted_iota(jnp.int32, (experts_n, experts_n), 0)
+    slot_col = lax.broadcasted_iota(jnp.int32, (experts_n, experts_n), 1)
+    side = slot_row // count
+    expert = (slot_row % count) * 2 + (side ^ tp)
+    order = jnp.where(slot_col == expert, 1.0, 0.0).astype(BF16)
+    router_out[...] = dot_nt(order, router_all[...].reshape(width, experts_n)).astype(BF16)
+
+    def norm_piece(b):
+        def body(s, carry):
+            value = tok_all[b, s].astype(F32)
+            out = (value * norm_factor(value) * gain_ref[...]).astype(BF16)
+            n_all[b, s] = out
+            return carry
+
+        lax.fori_loop(0, seqs, body, 0)
+
+    def project(b, s):
+        x = n_all[b, s]
+        k_ref[s, b] = dot(x, wqkv_out[1]).astype(BF16)
+        v_ref[s, b] = dot(x, wqkv_out[2]).astype(BF16)
+
+    norm_piece(0)
+    normed_ref[...] = n_all[0]
+    beside.wait_recv()
+    norm_piece(1)
+
+    forwards = []
+    for b in (1, 2, 3):
+        for kind, f in ((4, 0), (5, 1)):
+            small[b - 1][kind].wait_recv()
+            if f == 0:
+                ref = wqkv_out.at[:, w_rows(dp ^ b, core)]
+            else:
+                ref = wout_out.at[dp ^ b, o_rows(core)]
+            copy = remote(ref, ref, f_send.at[f, b - 1], f_recv.at[f, b - 1], ctx=ctx ^ 1)
+            copy.start()
+            forwards.append(copy)
+    for copy in forwards:
+        copy.wait_recv()
+
+    def own_q(s, carry):
+        q_ref[s] = (dot(n_all[0, s], wqkv_out[0]).astype(BF16) * (HD ** (-0.5))).astype(BF16)
+        project(0, s)
+        project(1, s)
+        return carry
+
+    lax.fori_loop(0, seqs, own_q, 0)
+    later = []
+    for s in range(seqs):
+        across[s].wait_recv()
+        copy = remote(tok_all.at[2, s], tok_all.at[3, s], t_send.at[1 + s], t_recv.at[1 + s], ctx=ctx ^ 1)
+        copy.start()
+        later.append(copy)
+    norm_piece(2)
+    for copy in later:
+        copy.wait_recv()
+    norm_piece(3)
+
+    def others(s, carry):
+        project(2, s)
+        project(3, s)
+        return carry
+
+    lax.fori_loop(0, seqs, others, 0)
+    for group in small:
+        for copy in group:
+            copy.wait_send()
+    for copy in forwards + later + across + [beside]:
+        copy.wait_send()
+
+
+def first_stage(tokens, wqkv, wout, table, gain_attn, gain_moe, router):
+    seqs, stretch, width = tokens.shape
+    count, rows, local = wqkv.shape
+    dp = width // rows
+    experts_n = router.shape[1]
+    any_spec = pl.BlockSpec(memory_space=pl.ANY)
+    vmem = pl.BlockSpec(memory_space=pltpu.VMEM)
+    dma = pltpu.SemaphoreType.DMA
+    return pl.pallas_call(
+        functools.partial(first_kernel, seqs),
+        name="first_stage",
+        in_specs=[any_spec] * 7,
+        out_specs=[vmem] * 10,
+        out_shape=[
+            jax.ShapeDtypeStruct((seqs, stretch, local), BF16),
+            jax.ShapeDtypeStruct((seqs, 4, stretch, local), BF16),
+            jax.ShapeDtypeStruct((seqs, 4, stretch, local), BF16),
+            jax.ShapeDtypeStruct((seqs, stretch, width), BF16),
+            jax.ShapeDtypeStruct((3, width, local), BF16),
+            jax.ShapeDtypeStruct((dp,) + wout.shape, BF16),
+            jax.ShapeDtypeStruct((dp,) + table.shape, BF16),
+            jax.ShapeDtypeStruct((1, width), F32),
+            jax.ShapeDtypeStruct((1, width), BF16),
+            jax.ShapeDtypeStruct((experts_n, width), BF16),
+        ],
+        scratch_shapes=[
+            pltpu.VMEM((4, seqs, stretch, width), BF16),
+            pltpu.VMEM((4, seqs, stretch, width), BF16),
+            pltpu.VMEM((dp, 1, rows), BF16),
+            pltpu.VMEM((dp, 1, rows), BF16),
+            pltpu.VMEM((dp, rows, experts_n), BF16),
+            dma((6, 3)), dma((6, 3)), dma((2, 3)), dma((2, 3)), dma((1 + seqs,)), dma((1 + seqs,)),
+            dma((seqs,)), dma((seqs,)), dma((7,)),
+        ],
+        compiler_params=pltpu.CompilerParams(vmem_limit_bytes=VMEM_BYTES, collective_id=0, has_side_effects=True),
+        cost_estimate=cost(40 * 10**9, 10**7),
+    )(tokens, wqkv, wout, table, gain_attn, gain_moe, router)
+
+
+def last_kernel(
+    normed_ref, proj_ref, datt_ref, att_ref, small_ref,
+    out_ref, router_out, gm_out, ga_out, table_out,
+    grads, core_send, core_got, y_out, y_got, z_out, z_got, wide, s_own, s_core, s_y, s_x, s_z,
+    c_sems, y_sems, z_sems, w_sems, s_sems,
+):
+    dp = lax.axis_index("dp")
+    ctx = lax.axis_index("ctx")
+    tp = lax.axis_index("tp")
+    core = ctx % 2
+    far = ctx // 2
+    greet([{"dp": dp ^ b} for b in (1, 2, 3)] + [{"ctx": ctx ^ b} for b in (1, 2, 3)] + [{"tp": tp ^ 1}])
+    count = z_got.shape[0] + 1
+    width = normed_ref.shape[1]
+    piece = width // count
+
+    x_copy = remote(small_ref, s_x, s_sems.at[0, 0], s_sems.at[1, 0], tp=tp ^ 1)
+    x_copy.start()
+    normed_t = normed_ref[...].T
+    for j in range(3):
+        grads[j] = dot(normed_t, proj_ref[j])
+    grads[3] = dot_tn(datt_ref[...], att_ref[...])
+    give = 1 - core
+    core_send[0] = grads[2 * give].astype(BF16)
+    core_send[1] = grads[2 * give + 1].astype(BF16)
+    c_copy = remote(core_send, core_got, c_sems.at[0], c_sems.at[1], ctx=ctx ^ 1)
+    c_copy.start()
+    x_copy.wait_recv()
+    lines = lax.broadcasted_iota(jnp.int32, small_ref.shape, 0)
+    s_own[...] = small_ref[...] + jnp.where(lines == 9, s_x[...], 0.0)
+    sc_copy = remote(s_own, s_core, s_sems.at[0, 1], s_sems.at[1, 1], ctx=ctx ^ 1)
+    sc_copy.start()
+    c_copy.wait_recv()
+    grads[2 * core] += core_got[0].astype(F32)
+    grads[2 * core + 1] += core_got[1].astype(F32)
+    y_out[...] = grads[2 * core + 1 - far].astype(BF16)
+    order = (3, 2, 1, 0)
+    y_copies = []
+    for b in order:
+        at = pl.ds(pl.multiple_of((dp ^ b) * piece, 16), piece)
+        copy = remote(y_out.at[at], y_got.at[b], y_sems.at[0, b], y_sems.at[1, b], ctx=ctx ^ 2)
+        copy.start()
+        y_copies.append(copy)
+    sc_copy.wait_recv()
+    y_small = s_own[...] + s_core[...]
+    s_y[0] = y_small
+    sy_copy = remote(s_y.at[0], s_y.at[1], s_sems.at[0, 2], s_sems.at[1, 2], ctx=ctx ^ 2)
+    sy_copy.start()
+    mine = 2 * core + far
+    z_copies = []
+    total = None
+    for copy, b in zip(y_copies, order):
+        copy.wait_recv()
+        at = pl.ds(pl.multiple_of((dp ^ b) * piece, 16), piece)
+        value = grads[mine, at] + y_got[b].astype(F32)
+        if b:
+            z_out[b - 1] = value.astype(BF16)
+            z_copy = remote(z_out.at[b - 1], z_got.at[b - 1], z_sems.at[0, b - 1], z_sems.at[1, b - 1], dp=dp ^ b)
+            z_copy.start()
+            z_copies.append((b, z_copy))
+        else:
+            total = value
+    sy_copy.wait_recv()
+    s_z[dp] = s_y[0] + s_y[1]
+    sz_copies = []
+    for b in (3, 2, 1):
+        copy = remote(s_z.at[dp], s_z.at[dp], s_sems.at[0, 2 + b], s_sems.at[1, 2 + b], dp=dp ^ b)
+        copy.start()
+        sz_copies.append(copy)
+    for b, copy in z_copies:
+        copy.wait_recv()
+        total = total + z_got[b - 1].astype(F32)
+    wide[mine] = total.astype(BF16)
+    w_copies = []
+    for b in (3, 2, 1):
+        copy = remote(wide.at[mine], wide.at[mine], w_sems.at[0, b - 1], w_sems.at[1, b - 1], ctx=ctx ^ b)
+        copy.start()
+        w_copies.append(copy)
+    for copy in sz_copies:
+        copy.wait_recv()
+    small = s_z[0]
+    for d in range(1, count):
+        small = small + s_z[d]
+
+    def exact(a, b, dims):
+        return lax.dot_general(a, b, (dims, ((), ())), precision=FULL_PRECISION, preferred_element_type=F32)
+
+    row = lax.broadcasted_iota(jnp.int32, (piece, width), 0)
+    col = lax.broadcasted_iota(jnp.int32, (piece, width), 1)
+    select = jnp.where(col == row + dp * piece, 1.0, 0.0)
+    experts_n = router_out.shape[1]
+    e_row = lax.broadcasted_iota(jnp.int32, (experts_n, experts_n), 0)
+    e_col = lax.broadcasted_iota(jnp.int32, (experts_n, experts_n), 1)
+    slot = ((e_row % 2) ^ tp) * count + e_row // 2
+    arranged = exact(jnp.where(e_col == slot, 1.0, 0.0), small[:experts_n], ((1,), (0,)))
+    router_out[...] = exact(select, arranged, ((1,), (1,)))
+    gains = exact(small[8:16], select, ((1,), (1,)))
+    gm_out[...] = gains[0:1]
+    ga_out[...] = gains[1:2]
+    t_rows, heads = table_out.shape
+    t_row = lax.broadcasted_iota(jnp.int32, (t_rows, width), 0)
+    t_col = lax.broadcasted_iota(jnp.int32, (t_rows, width), 1)
+    table_out[...] = exact(jnp.where(t_col == t_row + dp * t_rows, 1.0, 0.0), small[16:24], ((1,), (1,)))[:, :heads]
+    for copy in w_copies:
+        copy.wait_recv()
+    out_ref[...] = wide[...].astype(F32)
+    for copy in [x_copy, c_copy, sc_copy, sy_copy] + y_copies + [c for _, c in z_copies] + sz_copies + w_copies:
+        copy.wait_send()
+
+
+def last_stage(normed, proj, datt, att, small, dp, table_rows, heads, experts_n):
+    rows, width = normed.shape
+    local = att.shape[1]
+    piece = width // dp
+    vmem = pl.BlockSpec(memory_space=pltpu.VMEM)
+    dma = pltpu.SemaphoreType.DMA
+    return pl.pallas_call(
+        last_kernel,
+        name="last_stage",
+        in_specs=[vmem] * 5,
+        out_specs=[vmem] * 5,
+        out_shape=[
+            jax.ShapeDtypeStruct((4, piece, local), F32),
+            jax.ShapeDtypeStruct((piece, experts_n), F32),
+            jax.ShapeDtypeStruct((1, piece), F32),
+            jax.ShapeDtypeStruct((1, piece), F32),
+            jax.ShapeDtypeStruct((table_rows, heads), F32),
+        ],
+        scratch_shapes=[
+            pltpu.VMEM((4, width, local), F32),
+            pltpu.VMEM((2, width, local), BF16),
+            pltpu.VMEM((2, width, local), BF16),
+            pltpu.VMEM((width, local), BF16),
+            pltpu.VMEM((4, piece, local), BF16),
+            pltpu.VMEM((3, piece, local), BF16),
+            pltpu.VMEM((3, piece, local), BF16),
+            pltpu.VMEM((4, piece, local), BF16),
+            pltpu.VMEM(small.shape, F32),
+            pltpu.VMEM(small.shape, F32),
+            pltpu.VMEM((2,) + small.shape, F32),
+            pltpu.VMEM(small.shape, F32),
+            pltpu.VMEM((dp,) + small.shape, F32),
+            dma((2,)), dma((2, 4)), dma((2, 3)), dma((2, 3)), dma((2, 6)),
+        ],
+        compiler_params=pltpu.CompilerParams(vmem_limit_bytes=VMEM_BYTES, collective_id=1, has_side_effects=True),
+        cost_estimate=cost(8 * rows * width * local, 8 * rows * width),
+    )(normed, proj, datt, att, small)
+
+
+def moe_kernel(
+    seqs, groups, cap, tile, *refs,
+):
+    sends, refs = refs[:seqs], refs[seqs:]
+    slot_gates, refs = refs[:seqs], refs[seqs:]
+    cots, refs = refs[:groups], refs[groups:]
+    w_own, w_far, part_out, din_back, h_back, keep_out, give_out = refs[:7]
+    (
+        w_all, x_all, gate_all, g_all, xt_all, dyt_all, dy_ref, hid_all, dpre_all, part_acc, din_acc,
+        part_all, din_all, h_all, tile_ref,
+        x_sems, gate_sems, din_sems, h_sems, w_sems, own_sems, part_sems, out_sems,
+    ) = refs[7:]
+    dp = lax.axis_index("dp")
+    ctx = lax.axis_index("ctx")
+    greet([{"dp": dp ^ b} for b in range(1, groups)] + [{"ctx": ctx ^ 1}])
+    width = x_all.shape[-1]
+    rows = groups * cap
+    slices = w_all.shape[2]
+    piece = width // slices
+    half_len = w_all.shape[4]
+    per_half = half_len // tile
+    tiles = w_all.shape[1] * per_half
+    order = tuple(range(groups - 1, 0, -1))
+
+    sent = []
+    for s in range(seqs):
+        for b in order:
+            sent.append(
+                remote(sends[s].at[dp ^ b], x_all.at[s, dp], x_sems.at[0, s, b - 1], x_sems.at[1, s, b - 1], dp=dp ^ b)
+            )
+            sent.append(
+                remote(
+                    slot_gates[s].at[dp ^ b], gate_all.at[s, dp],
+                    gate_sems.at[0, s, b - 1], gate_sems.at[1, s, b - 1], dp=dp ^ b,
+                )
+            )
+    w_copies = [
+        remote(w_own, w_all.at[:, :, ctx], w_sems.at[0, 0], w_sems.at[1, 0], ctx=ctx ^ 1),
+        remote(w_far, w_all.at[:, :, ctx ^ 2], w_sems.at[0, 1], w_sems.at[1, 1], ctx=ctx ^ 1),
+    ]
+    for copy in w_copies + sent:
+        copy.start()
+    local = [
+        pltpu.make_async_copy(w_own, w_all.at[:, :, ctx], own_sems.at[0]),
+        pltpu.make_async_copy(w_far, w_all.at[:, :, ctx ^ 2], own_sems.at[1]),
+    ]
+    for s in range(seqs):
+        local.append(pltpu.make_async_copy(sends[s].at[dp], x_all.at[s, dp], own_sems.at[2 + 2 * s]))
+        local.append(pltpu.make_async_copy(slot_gates[s].at[dp], gate_all.at[s, dp], own_sems.at[3 + 2 * s]))
+    for b in range(groups):
+        local.append(pltpu.make_async_copy(cots[b], g_all.at[dp ^ b], own_sems.at[2 + 2 * seqs + b]))
+    for copy in local:
+        copy.start()
+    for copy in local:
+        copy.wait()
+    arrivals = [
+        remote(w_all.at[:, :, ctx ^ 1], w_all.at[:, :, ctx ^ 1], w_sems.at[0, 0], w_sems.at[1, 0], ctx=ctx ^ 1),
+        remote(w_all.at[:, :, ctx ^ 3], w_all.at[:, :, ctx ^ 3], w_sems.at[0, 1], w_sems.at[1, 1], ctx=ctx ^ 1),
+    ]
+    for copy in arrivals:
+        copy.wait_recv()
+    eye = diagonal(cap)
+
+    def weights(io, f):
+        lanes = pl.ds(pl.multiple_of((f % per_half) * tile, tile), tile)
+        return w_all[io, f // per_half, :, :, lanes].reshape(width, tile)
+
+    def gate_column(s, group):
+        return jnp.sum(jnp.where(eye, gate_all[s, group], 0.0), axis=1, keepdims=True)
+
+    def din_copy(s, b):
+        return remote(
+            din_all.at[s, dp ^ b], din_back.at[s, dp], din_sems.at[0, s, b - 1], din_sems.at[1, s, b - 1], dp=dp ^ b
+        )
+
+    def h_copy(s, b):
+        return remote(h_all.at[s, dp ^ b], h_back.at[s, dp], h_sems.at[0, s, b - 1], h_sems.at[1, s, b - 1], dp=dp ^ b)
+
+    def part_copy(s, b):
+        return pltpu.make_async_copy(part_all.at[s, dp ^ b], part_out.at[b, s], part_sems.at[s, b])
+
+    def own_copies(s):
+        return [
+            pltpu.make_async_copy(din_all.at[s, dp], din_back.at[s, dp], part_sems.at[s, groups]),
+            pltpu.make_async_copy(h_all.at[s, dp], h_back.at[s, dp], part_sems.at[s, groups + 1]),
+        ]
+
+    def chunk(s, carry):
+        for b in order:
+            there = x_all.at[s, dp ^ b]
+            remote(there, there, x_sems.at[0, s, b - 1], x_sems.at[1, s, b - 1], dp=dp ^ b).wait_recv()
+            there = gate_all.at[s, dp ^ b]
+            remote(there, there, gate_sems.at[0, s, b - 1], gate_sems.at[1, s, b - 1], dp=dp ^ b).wait_recv()
+        x = x_all[s].reshape(rows, width)
+        xt_all[s] = x.T
+        for group in range(groups):
+            dy_ref[group * cap : (group + 1) * cap] = (g_all[group, s].astype(F32) * gate_column(s, group)).astype(BF16)
+        dyt_all[s] = dy_ref[...].T
+        part_acc[...] = jnp.zeros_like(part_acc)
+        din_acc[...] = jnp.zeros_like(din_acc)
+
+        def step(f, carry):
+            x = x_all[s].reshape(rows, width)
+            w_in = weights(0, f)
+            w_out_t = weights(1, f)
+            pre = dot(x, w_in)
+            dhid = dot(dy_ref[...], w_out_t)
+            square = pre * pre
+            inner = jnp.tanh(GELU_C * pre * (1.0 + GELU_A * square))
+            half = 0.5 * (1.0 + inner)
+            hidden = (pre * half).astype(BF16)
+            slope = half + (0.5 * GELU_C) * pre * (1.0 - inner * inner) * (1.0 + (3.0 * GELU_A) * square)
+            dpre = (dhid * slope).astype(BF16)
+            hid_all[f, s] = hidden
+            dpre_all[f, s] = dpre
+            part_acc[...] += dot_nt(hidden, w_out_t)
+            din_acc[...] += dot_nt(dpre, w_in)
+            return carry
+
+        lax.fori_loop(0, tiles, step, 0)
+        for group in range(groups):
+            at = slice(group * cap, (group + 1) * cap)
+            din_all[s, group] = din_acc[at].astype(BF16)
+            gated = part_acc[at] * gate_column(s, group)
+            part_all[s, group] = gated.astype(BF16)
+            h = jnp.sum(gated * g_all[group, s].astype(F32), axis=1, keepdims=True)
+            h_all[s, group] = jnp.sum(jnp.where(eye, h, 0.0), axis=0, keepdims=True)
+        for b in order:
+            din_copy(s, b).start()
+            h_copy(s, b).start()
+        for copy in own_copies(s):
+            copy.start()
+        for b in range(groups):
+            part_copy(s, b).start()
+        return carry
+
+    lax.fori_loop(0, seqs, chunk, 0)
+
+    def out_copies(f, slot):
+        lanes = pl.ds(pl.multiple_of((f % per_half) * tile, tile), tile)
+        return [
+            pltpu.make_async_copy(
+                tile_ref.at[slot, 0], keep_out.at[f // per_half, :, :, :, lanes], out_sems.at[slot, 0]
+            ),
+            pltpu.make_async_copy(
+                tile_ref.at[slot, 1], give_out.at[f // per_half, :, :, :, lanes], out_sems.at[slot, 1]
+            ),
+        ]
+
+    def weight_grads(f, carry):
+        slot = f % 2
+
+        @pl.when(f >= 2)
+        def _():
+            for copy in out_copies(f - 2, slot):
+                copy.wait()
+
+        for io, (left, right) in enumerate(((xt_all, dpre_all), (dyt_all, hid_all))):
+            total = dot(left[0], right[f, 0])
+            for s in range(1, seqs):
+                total = total + dot(left[s], right[f, s])
+            for index in range(slices):
+                place = index ^ ctx
+                tile_ref[slot, place % 2, place // 2, io] = total[index * piece : (index + 1) * piece].astype(BF16)
+        for copy in out_copies(f, slot):
+            copy.start()
+        return carry
+
+    lax.fori_loop(0, tiles, weight_grads, 0)
+    for f in (tiles - 2, tiles - 1):
+        for copy in out_copies(f, f % 2):
+            copy.wait()
+    for s in range(seqs):
+        for b in order:
+            there = din_back.at[s, dp ^ b]
+            remote(there, there, din_sems.at[0, s, b - 1], din_sems.at[1, s, b - 1], dp=dp ^ b).wait_recv()
+            there = h_back.at[s, dp ^ b]
+            remote(there, there, h_sems.at[0, s, b - 1], h_sems.at[1, s, b - 1], dp=dp ^ b).wait_recv()
+            din_copy(s, b).wait_send()
+            h_copy(s, b).wait_send()
+        for copy in own_copies(s):
+            copy.wait()
+        for b in range(groups):
+            part_copy(s, b).wait()
+    for copy in w_copies + sent:
+        copy.wait_send()
+
+
+def moe_stage(sends, slot_gates, cots, w_own, w_far, tile=512):
+    seqs = len(sends)
+    groups, cap, width = sends[0].shape
+    _, halves, piece, half_len = w_own.shape
+    slices = width // piece
+    tiles = halves * half_len // tile
+    rows = groups * cap
+    any_spec = pl.BlockSpec(memory_space=pl.ANY)
+    vmem = pl.BlockSpec(memory_space=pltpu.VMEM)
+    dma = pltpu.SemaphoreType.DMA
+    return pl.pallas_call(
+        functools.partial(moe_kernel, seqs, groups, cap, tile),
+        name="moe_stage",
+        in_specs=[any_spec] * (2 * seqs + groups + 2),
+        out_specs=[any_spec, any_spec, vmem, any_spec, any_spec],
+        out_shape=[
+            jax.ShapeDtypeStruct((groups, seqs, cap, width), BF16),
+            jax.ShapeDtypeStruct((seqs, groups, cap, width), BF16),
+            jax.ShapeDtypeStruct((seqs, groups, 1, cap), F32),
+            jax.ShapeDtypeStruct((halves, slices // 2, 2, piece, half_len), BF16),
+            jax.ShapeDtypeStruct((halves, slices // 2, 2, piece, half_len), BF16),
+        ],
+        scratch_shapes=[
+            pltpu.VMEM((2, halves, slices, piece, half_len), BF16),
+            pltpu.VMEM((seqs, groups, cap, width), BF16),
+            pltpu.VMEM((seqs, groups, 1, cap), F32),
+            pltpu.VMEM((groups, seqs, cap, width), BF16),
+            pltpu.VMEM((seqs, width, rows), BF16),
+            pltpu.VMEM((seqs, width, rows), BF16),
+            pltpu.VMEM((rows, width), BF16),
+            pltpu.VMEM((tiles, seqs, rows, tile), BF16),
+            pltpu.VMEM((tiles, seqs, rows, tile), BF16),
+            pltpu.VMEM((rows, width), F32),
+            pltpu.VMEM((rows, width), F32),
+            pltpu.VMEM((seqs, groups, cap, width), BF16),
+            pltpu.VMEM((seqs, groups, cap, width), BF16),
+            pltpu.VMEM((seqs, groups, 1, cap), F32),
+            pltpu.VMEM((2, 2, slices // 2, 2, piece, tile), BF16),
+            dma((2, seqs, groups - 1)), dma((2, seqs, groups - 1)), dma((2, seqs, groups - 1)),
+            dma((2, seqs, groups - 1)), dma((2, 2)), dma((2 + 2 * seqs + groups,)), dma((seqs, groups + 2)),
+            dma((2, 2)),
+        ],
+        compiler_params=pltpu.CompilerParams(
+            vmem_limit_bytes=63 * 1024 * 1024, collective_id=2, has_side_effects=True
+        ),
+        cost_estimate=cost(20 * seqs * rows * width * halves * half_len, 40 * width * halves * half_len),
+    )(*sends, *slot_gates, *cots, w_own, w_far)
 
 
 def flip(value, axis, bit):
@@ -502,6 +1092,31 @@
 
 def all_to_all_dp(value):
     return lax.all_to_all(value, "dp", split_axis=0, concat_axis=0, tiled=True)
+
+
+def gathered(tokens, wqkv, wout, table, gain_attn, gain_moe, router):
+    seqs, stretch, width = tokens.shape
+    local = wqkv.shape[2]
+    dp = lax.axis_size("dp")
+    tp = lax.axis_index("tp")
+    experts_n = router.shape[1]
+    wqkv = lax.all_gather(wqkv, "dp", axis=1, tiled=True)
+    wout = lax.all_gather(wout, "dp", axis=1, tiled=True)
+    table = lax.all_gather(table, "dp", axis=0, tiled=True)
+    gains = lax.all_gather(jnp.concatenate([gain_attn, gain_moe], axis=0), "dp", axis=1, tiled=True)
+    gain_attn, gain_moe = gains[0:1].astype(F32), gains[1:2]
+    router = lax.all_gather(router, "dp", axis=0, tiled=True).T.reshape(dp, 2, width).transpose(1, 0, 2)
+    router = jnp.where(tp == 0, router, router[::-1]).reshape(experts_n, width)
+    across = flip(tokens, "ctx", 2)
+    beside, beyond = flip(jnp.stack([tokens, across]), "ctx", 1)
+    x32 = jnp.stack([tokens, beside, across, beyond], axis=1).astype(F32)
+    normed = (x32 * norm_factor(x32) * gain_attn[None, None]).astype(BF16)
+    own = normed[:, 0].reshape(seqs * stretch, width)
+    queries = jnp.dot(own, wqkv[0], preferred_element_type=F32).astype(BF16) * jnp.asarray(HD ** (-0.5), BF16)
+    flat = normed.reshape(seqs * 4 * stretch, width)
+    keys = jnp.dot(flat, wqkv[1], preferred_element_type=F32).astype(BF16).reshape(seqs, 4 * stretch, local)
+    values = jnp.dot(flat, wqkv[2], preferred_element_type=F32).astype(BF16).reshape(seqs, 4 * stretch, local)
+    return queries.reshape(seqs, stretch, local), keys, values, own, wqkv, wout, table, gain_attn, gain_moe, router
 
 
 def on_device(
@@ -520,18 +1135,21 @@
     local = w_qkv.shape[3]
     heads = local // HD
 
-    wqkv = lax.all_gather(w_qkv[0], "dp", axis=1, tiled=True)
-    wout_own = lax.all_gather(w_attn_out[0], "dp", axis=1, tiled=True)
+    fits = dp == 4
+    if fits:
+        queries, keys, values, own_normed, wqkv, wout_parts, table, gain_attn, gain_moe, router = first_stage(
+            tokens_in, w_qkv[0], w_attn_out[0], bias_table[0], attn_gain, moe_gain, w_router[0]
+        )
+        wout_own = wout_parts.transpose(1, 0, 2).reshape(local, width)
+        table = table.reshape(NB, heads)
+        keys = keys.reshape(seqs, 4 * stretch, local)
+        values = values.reshape(seqs, 4 * stretch, local)
+        own_normed = own_normed.reshape(seqs * stretch, width)
+    else:
+        queries, keys, values, own_normed, wqkv, wout_own, table, gain_attn, gain_moe, router = gathered(
+            tokens_in, w_qkv[0], w_attn_out[0], bias_table[0], attn_gain, moe_gain, w_router[0]
+        )
     wout_other = flip(wout_own, "tp", 1)
-    table = lax.all_gather(bias_table[0], "dp", axis=0, tiled=True)
-    gains = lax.all_gather(jnp.concatenate([attn_gain, moe_gain], axis=0), "dp", axis=1, tiled=True)
-    gain_attn, gain_moe = gains[0:1], gains[1:2]
-    router = lax.all_gather(w_router[0], "dp", axis=0, tiled=True).T.reshape(dp, 2, width).transpose(1, 0, 2)
-    router = jnp.where(tp == 0, router, router[::-1]).reshape(expert_count, width)
-
-    across = flip(tokens_in, "ctx", 2)
-    beside, beyond = flip(jnp.stack([tokens_in, across]), "ctx", 1)
-    pieces = jnp.stack([tokens_in, beside, across, beyond], axis=1)
 
     w_in = w_expert_in[0]
     w_out_t = w_expert_out[0].transpose(0, 2, 1)
@@ -539,7 +1157,11 @@
     keep = lax.dynamic_index_in_dim(both, tp, 0, keepdims=False)
     give = lax.dynamic_index_in_dim(both, 1 - tp, 0, keepdims=False)
     got = flip(give, "tp", 1)
-    weights = lax.all_gather(jnp.stack([keep, got], axis=1), "ctx", axis=0, tiled=False)
+    both = jnp.stack([keep, got], axis=1)
+    if fits:
+        far = flip(both, "ctx", 2)
+    else:
+        weights = lax.all_gather(both, "ctx", axis=0, tiled=False)
 
     e_order = jnp.arange(expert_count, dtype=jnp.int32).reshape(dp, 2).T
     e_order = jnp.where(tp == 0, e_order, e_order[::-1]).reshape(1, expert_count, 1)
@@ -550,7 +1172,13 @@
     ranks = jnp.einsum("set,tu->seu", hits.astype(BF16), before, preferred_element_type=F32)
     places = jnp.where(hits > 0.5, ranks, -1.0)[:, :dp]
 
-    cot_slots = all_to_all_dp(dispatch(places, cotangent, cap))
+    if fits:
+        me = lax.axis_index("dp")
+        near_places = jnp.stack([lax.dynamic_index_in_dim(places, me ^ b, 1, keepdims=False) for b in range(dp)], axis=1)
+        cot_slots = dispatch(near_places, cotangent, cap)
+        cot_slots = [cot_slots[0]] + [flip(cot_slots[b], "dp", b) for b in range(1, dp)]
+    else:
+        cot_slots = all_to_all_dp(dispatch(places, cotangent, cap))
 
     one_hot_bucket = (rel_buckets[:, None] == jnp.arange(NB, dtype=jnp.int32)[None, :]).astype(F32)
     one_hot_bucket = jnp.pad(one_hot_bucket, ((0, 1), (0, 0)))
@@ -559,24 +1187,13 @@
     windows = jnp.einsum("bmn,nh->hbm", hot_windows, table.astype(F32), precision=FULL_PRECISION)
     bias = expand_bias(windows)
 
-    x32 = pieces.astype(F32)
-    normed = (x32 * norm_factor(x32) * gain_attn.astype(F32)[None, None]).astype(BF16)
-    own_normed = normed[:, 0].reshape(seqs * stretch, width)
-    queries = jnp.dot(own_normed, wqkv[0], preferred_element_type=F32).astype(BF16) * jnp.asarray(HD ** (-0.5), BF16)
-    queries = queries.reshape(seqs, stretch, local)
-    flat = normed.reshape(seqs * 4 * stretch, width)
-    keys = jnp.dot(flat, wqkv[1], preferred_element_type=F32).astype(BF16).reshape(seqs, 4 * stretch, local)
-    values = jnp.dot(flat, wqkv[2], preferred_element_type=F32).astype(BF16).reshape(seqs, 4 * stretch, local)
-
     ids = block_ids.reshape(seqs, 4, stretch)
     ids_pieces = [lax.dynamic_index_in_dim(ids, ctx ^ b, 1, keepdims=False) for b in range(4)]
     ids_query = ids_pieces[0].reshape(seqs, 1, stretch)
     ids_key = jnp.stack(ids_pieces, axis=1).reshape(seqs, 4 * stretch, 1)
 
     wout_pair = jnp.stack([wout_own, wout_other])
-    attended, lse, mids, moes, gates, partials = [], [], [], [], [], []
-    returned_din, returned_h = [], []
-    acc = None
+    attended, lse, mids, moes, gates, sends, slot_gates = [], [], [], [], [], [], []
     for s in range(seqs):
         att, stat = attend(queries[s], keys[s], values[s], bias, ids_query[s], ids_key[s])
         attended.append(att)
@@ -587,14 +1204,27 @@
         mids.append(mid)
         moes.append(moe_in)
         gates.append(gate)
-        received = all_to_all_dp(send)
-        received_gate = all_to_all_dp(slot_gate)
-        part, din, h, acc = experts(received, cot_slots, s, received_gate, weights, acc, s == seqs - 1)
-        returned_din.append(all_to_all_dp(din))
-        returned_h.append(all_to_all_dp(h))
-        partials.append(all_to_all_dp(part))
-
-    beside_sum = acc[:, 0::2].astype(F32) + flip(acc[:, 1::2], "ctx", 1).astype(F32)
+        sends.append(send)
+        slot_gates.append(slot_gate)
+    if fits:
+        parts, returned_din, returned_h, kept, given = moe_stage(sends, slot_gates, cot_slots, both, far)
+        moved = [parts[0]] + [flip(parts[b], "dp", b) for b in range(1, dp)]
+        partials = [jnp.stack([piece[s] for piece in moved]) for s in range(seqs)]
+        out_places = near_places
+    else:
+        partials, returned_din, returned_h = [], [], []
+        out_places = places
+        acc = None
+        for s in range(seqs):
+            received = all_to_all_dp(sends[s])
+            received_gate = all_to_all_dp(slot_gates[s])
+            part, din, h, acc = experts(received, cot_slots, s, received_gate, weights, acc, s == seqs - 1)
+            returned_din.append(all_to_all_dp(din))
+            returned_h.append(all_to_all_dp(h))
+            partials.append(all_to_all_dp(part))
+        kept, given = acc[:, 0::2], acc[:, 1::2]
+
+    beside_sum = kept.astype(F32) + flip(given, "ctx", 1).astype(F32)
     mine = beside_sum[:, 0] + flip(beside_sum[:, 1].astype(BF16), "ctx", 2).astype(F32)
     other = flip(mine[1].astype(BF16), "tp", 1).astype(F32)
     ordered = jnp.where(tp == 0, jnp.stack([mine[0], other]), jnp.stack([other, mine[0]]))
@@ -606,21 +1236,21 @@
     rel_grad = 0.0
     gain_moe_grad = 0.0
     router_grad = 0.0
-    wout_grad = 0.0
+    datts = []
     for s in range(seqs):
-        out_own = combine_out(places[s], partials[s], cap)
+        out_own = combine_out(out_places[s], partials[s], cap)
         out_other = flip(out_own, "tp", 1)
         tokens_out.append((mids[s] + (out_own.astype(F32) + out_other.astype(F32))).astype(BF16))
         din_own, h_own = combine(places[s], returned_din[s], returned_h[s], cap)
         din_other = flip(din_own, "tp", 1)
         h_all = jnp.concatenate([h_own, flip(h_own, "tp", 1)], axis=0)
-        gmid, datt, d_gain, d_router, d_wout = middle_back(
-            din_own, din_other, h_all, gates[s], router, moes[s], mids[s], gain_moe, cotangent[s], attended[s], wout_own
+        gmid, datt, d_gain, d_router, dattn = middle_back(
+            din_own, din_other, h_all, gates[s], router, moes[s], mids[s], gain_moe, cotangent[s], wout_own
         )
+        datts.append(dattn)
         gmids.append(gmid)
         gain_moe_grad += d_gain
         router_grad += d_router
-        wout_grad += d_wout
         dq, dk, dv, rel = attend_back(
             queries[s], keys[s], values[s], datt, bias, lse[s], ids_query[s], ids_key[s]
         )
@@ -630,39 +1260,57 @@
         full = near[:, 0] + flip(near[:, 1].astype(BF16), "ctx", 2).astype(F32)
         projections.append(jnp.concatenate([dq[None], full.astype(BF16)], axis=0))
     grad_proj = jnp.concatenate(projections, axis=1)
-    grad_wqkv = jnp.einsum("rd,jre->jde", own_normed, grad_proj, preferred_element_type=F32)
-    dnormed_own = jnp.einsum("jre,jde->rd", grad_proj, wqkv, preferred_element_type=F32).astype(BF16)
+    dattn = jnp.concatenate(datts, axis=0)
+    attended = jnp.concatenate(attended, axis=0)
+    dnormed_part = jnp.einsum("jre,jde->rd", grad_proj, wqkv, preferred_element_type=F32)
+    dnormed_own = dnormed_part.astype(BF16)
     dnormed = dnormed_own.astype(F32) + flip(dnormed_own, "tp", 1).astype(F32)
     own_x = tokens_in.reshape(seqs * stretch, width).astype(F32)
     factor = norm_factor(own_x)
     unit = own_x * factor
-    grad_gain_attn = jnp.sum(dnormed * unit, axis=0)
-    scaled = dnormed * gain_attn.astype(F32)
+    scaled = dnormed * gain_attn
     dres = factor * (scaled - unit * jnp.mean(scaled * unit, axis=-1, keepdims=True))
     grad_tokens = jnp.concatenate(gmids, axis=0) + dres
 
     rel_flat = rel_grad.reshape(heads, 4, 2 * stretch)
     grad_table = jnp.einsum("bmn,hbm->nh", hot_windows, rel_flat, precision=FULL_PRECISION)
-    router_grad = router_grad.reshape(2, dp, width)
-    router_grad = jnp.where(tp == 0, router_grad, router_grad[::-1]).transpose(1, 0, 2).reshape(expert_count, width).T
-
-    def reduced(value, dim):
-        return lax.psum(lax.psum_scatter(value, "dp", scatter_dimension=dim, tiled=True), "ctx")
-
-    g_attn = reduced(grad_gain_attn, 0)
-    g_qkv = reduced(grad_wqkv, 1)
-    g_wout = reduced(wout_grad, 1)
-    g_table = reduced(grad_table, 0)
-    g_moe = reduced(gain_moe_grad[0], 0)
-    g_router = reduced(router_grad, 0)
+    if fits:
+        gain_rows = jnp.concatenate([gain_moe_grad, jnp.sum(dnormed_part * unit, axis=0)[None]], axis=0)
+        small = jnp.concatenate(
+            [
+                router_grad,
+                jnp.pad(gain_rows, ((0, 6), (0, 0))),
+                jnp.pad(grad_table.T, ((0, 8 - heads), (0, width - NB))),
+            ],
+            axis=0,
+        )
+        wide, g_router, g_moe, g_attn, g_table = last_stage(
+            own_normed, grad_proj, dattn, attended, small, dp, NB // dp, heads, expert_count
+        )
+        g_qkv = wide[:3]
+        g_wout = wide[3].T
+    else:
+        router_grad = router_grad.reshape(2, dp, width)
+        router_grad = jnp.where(tp == 0, router_grad, router_grad[::-1])
+        router_grad = router_grad.transpose(1, 0, 2).reshape(expert_count, width).T
+
+        def reduced(value, dim):
+            return lax.psum(lax.psum_scatter(value, "dp", scatter_dimension=dim, tiled=True), "ctx")
+
+        g_attn = reduced(jnp.sum(dnormed * unit, axis=0)[None], 1)
+        g_qkv = reduced(jnp.einsum("rd,jre->jde", own_normed, grad_proj, preferred_element_type=F32), 1)
+        g_wout = reduced(jnp.einsum("re,rd->ed", attended, dattn, preferred_element_type=F32), 1)
+        g_table = reduced(grad_table, 0)
+        g_moe = reduced(gain_moe_grad, 1)
+        g_router = reduced(router_grad, 0)
     return (
         jnp.stack(tokens_out),
         grad_tokens.reshape(seqs, stretch, width),
-        g_attn[None],
+        g_attn,
         g_qkv[None],
         g_wout[None],
         g_table[None],
-        g_moe[None],
+        g_moe,
         g_router[None],
         grad_expert_in[None],
         grad_expert_out[None],

time: 765 us -> 572 us (0.75)
  blocking collectives: 182 us -> 0 us
  Pallas kernels: 175 us -> 319 us
  waiting for transfers between devices: 154 us -> 103 us
  starting transfers between devices: 69.1 us -> 32.2 us
  local copies, waits for them, and re-layouts: 88.8 us -> 53.9 us
  between operations: 16.9 us -> 2.14 us
  matrix products: 19.4 us -> 5.23 us
  other arithmetic: 54 us -> 46.3 us
    pallas_call x3, Pallas kernels: 78.6 us -> 224 us  [the longest x1 117 us: moe_stage(): pl.pallas_call(functools.partial(moe_kernel, seqs, groups, cap, tile), na...]
    all_to_all x6 -> x0, blocking collectives: 88.6 us -> none  [all_to_all_dp(): return lax.all_to_all(value, 'dp', split_axis=0, concat_axis=0, tiled=True)]
    all_gather x4 -> x0, blocking collectives: 64.9 us -> none  [the longest x1 21.3 us: on_device(): table = lax.all_gather(bias_table[0], 'dp', axis=0, tiled=True)]
    all_to_all x10 -> x0, starting transfers between devices: 44.9 us -> none  [all_to_all_dp(): return lax.all_to_all(value, 'dp', split_axis=0, concat_axis=0, tiled=True)]
    psum x1 -> x0, waiting for transfers between devices: 37.9 us -> none  [reduced(): lax.psum(lax.psum_scatter(value, 'dp', scatter_dimension=dim, tiled=True)...]
    unnamed x177 -> x176, local copies, waits for them, and re-layouts: 48.5 us -> 17.5 us
    all_to_all x10 -> x0, waiting for transfers between devices: 20.4 us -> none  [all_to_all_dp(): return lax.all_to_all(value, 'dp', split_axis=0, concat_axis=0, tiled=True)]
    unnamed x1 -> x0, blocking collectives: 16.9 us -> none
  transfers between devices with their start and end apart: 42 -> 31, of which waited for: 11 -> 9; matrix products, arithmetic and copies ran while one was open for 18% -> 13% of each run, Pallas kernels for 23% -> 24%
where the time goes in v2:
time: 572 us; the launch traced here: 562 us
  Pallas kernels  319 us (56%)
  waiting for transfers between devices  103 us (18%)
  local copies, waits for them, and re-layouts  53.9 us (9%)
  other arithmetic  46.3 us (8%)
  starting transfers between devices  32.2 us (6%)
    pallas_call x1, Pallas kernels, moe_stage(): pl.pallas_call(functools.partial(moe_kernel, seqs, groups, cap, tile), na...  117 us
    ppermute x31, waiting for transfers between devices, flip(): return lax.ppermute(value, axis, [(i, i ^ bit) for i in range(count)])  103 us
    pallas_call x1, Pallas kernels, first_stage(): pl.pallas_call(functools.partial(first_kernel, seqs), name='first_stage',...  53.7 us
    pallas_call x1, Pallas kernels, last_stage(): pl.pallas_call(last_kernel, name='last_stage', in_specs=[vmem] * 5, out_s...  53.6 us
    ppermute x31, starting transfers between devices, flip(): return lax.ppermute(value, axis, [(i, i ^ bit) for i in range(count)])  32.2 us
    pallas_call x3, Pallas kernels, attend_back(): pl.pallas_call(attend_back_kernel, name='attend_back', grid=(pairs,), in_...  25.9 us
    pallas_call x3, Pallas kernels, attend(): pl.pallas_call(attend_kernel, name='attend', grid=(pairs,), in_specs=[pl....  22.8 us
    unnamed x176, local copies, waits for them, and re-layouts  17.5 us
  transfers between devices with their start and end apart: 31, of which 9 were waited for; matrix products, arithmetic and copies ran while one was open for 13% of the time, Pallas kernels for 24%

profile of v2, /device:TPU:0, one launch (start us, length us, event | category | flops | bytes accessed | tf_op | source)
XLA Modules:
  0.0 561.9 jit_solution(16580812775969426440)
XLA Ops:
  1.4 1.7 copy.36
  4.6 53.7 %first_stage.1 = (bf16[3,256,384]{2,1,0:T(8,128)(2,1)}, bf16[3,4,256,384]{3,2,1,0:T(8,128)(2,1)}, bf16[3,4,256,384]{3,2,1,0:T(8,128)(2,1)}, bf16[3,256,768]{2,1,...) custom-call(bf16[3,256,768]{2,1,0:T(8,128)(2,1)} %tok_ref.1, ...), custom_call_target="tpu_custom_call" | custom-call | flops 40000000000 | bytes 10000000 | tf_op jit(solution)/shard_map/first_stage/pallas_call | solution.py:671
  60.0 4.6 expand_bias.1.bias_ref
  67.2 3.9 fusion.39
  71.0 7.5 %attend.4 = (bf16[256,384]{1,0:T(8,128)(2,1)}, f32[3,2,256]{2,1,0:T(2,128)}) custom-call(bf16[256,384]{1,0:T(8,128)(2,1)} %get-tuple-element.218.q_ref, bf16[1024,384]{1,0:T(8,128)(2,1)} %bitcast.235, bf16[1024,384]{1,0:T(8,128)(2,1)} %bitcast.233, bf16[6,1024,256]{2,1,0:T(8,128)(2,1)} %expand_bias.1.bias_ref, s32[1,256]{1,0:T(1,128)} %get-tuple-element.237.idq_ref, ...), custom_call_target="tpu_custom_call" | custom-call | flops 805306368 | bytes 3145728 | tf_op jit(solution)/shard_map/attend/pallas_call | solution.py:91
  82.2 7.4 %attend.3 = (bf16[256,384]{1,0:T(8,128)(2,1)}, f32[3,2,256]{2,1,0:T(2,128)}) custom-call(bf16[256,384]{1,0:T(8,128)(2,1)} %get-tuple-element.220.q_ref, bf16[1024,384]{1,0:T(8,128)(2,1)} %bitcast.239, bf16[1024,384]{1,0:T(8,128)(2,1)} %bitcast.237, bf16[6,1024,256]{2,1,0:T(8,128)(2,1)} %expand_bias.1.bias_ref, s32[1,256]{1,0:T(1,128)} %get-tuple-element.239.idq_ref, ...), custom_call_target="tpu_custom_call" | custom-call | flops 805306368 | bytes 3145728 | tf_op jit(solution)/shard_map/attend/pallas_call | solution.py:91
  89.6 1.6 collective-permute-start
  91.2 2.8 fusion.7
  96.2 3.9 dispatch_rows.1
  100.1 26.4 %collective-permute-done.7 = bf16[2,192,1536]{2,1,0:T(8,128)(2,1)} collective-permute-done((bf16[2,192,1536]{2,1,0:T(8,128)(2,1)}, bf16[2,192,1536]{2,1,0:T(8,128)(2,1)}, u32[]{:S(2)}, u32[]{:S(2)}) %collective-permute-start.7) | collective-permute-done | bytes 1179680 | tf_op jit(solution)/shard_map/ppermute | solution.py:1090
  126.5 3.0 pad_maximum_fusion.refs_10_
  129.6 2.4 collective-permute-start.8
  134.5 7.9 %attend.5 = (bf16[256,384]{1,0:T(8,128)(2,1)}, f32[3,2,256]{2,1,0:T(2,128)}) custom-call(bf16[256,384]{1,0:T(8,128)(2,1)} %get-tuple-element.219.q_ref, bf16[1024,384]{1,0:T(8,128)(2,1)} %bitcast.231, bf16[1024,384]{1,0:T(8,128)(2,1)} %bitcast.229, bf16[6,1024,256]{2,1,0:T(8,128)(2,1)} %expand_bias.1.bias_ref, s32[1,256]{1,0:T(1,128)} %get-tuple-element.238.idq_ref, ...), custom_call_target="tpu_custom_call" | custom-call | flops 805306368 | bytes 3145728 | tf_op jit(solution)/shard_map/attend/pallas_call | solution.py:91
  145.8 2.5 collective-permute-start.5
  148.3 1.9 collective-permute-start.6
  155.1 2.2 pad_maximum_fusion.4.wout_ref
  157.3 3.8 middle_stage.4
  161.1 3.8 middle_stage.3
  165.6 3.8 middle_stage.5
  169.4 17.9 %collective-permute-done.5.refs_8_ = bf16[3,128,768]{2,1,0:T(8,128)(2,1)} collective-permute-done((bf16[3,128,768]{2,1,0:T(8,128)(2,1)}, bf16[3,128,768]{2,1,0:T(8,128)(2,1)}, u32[]{:S(2)}, u32[]{:S(2)}) %collective-permute-start.5) | collective-permute-done | bytes 589856 | tf_op jit(solution)/shard_map/ppermute | solution.py:1090
  187.3 116.7 %moe_stage.1 = (bf16[4,3,128,768]{3,2,1,0:T(8,128)(2,1)}, bf16[3,4,128,768]{3,2,1,0:T(8,128)(2,1)}, f32[3,4,1,128]{3,2,1,0:T(1,128)}, bf16[2,2,2,192,1536]{4,3,2,1,0:T(8,128)(2,1)}, bf16[2,2,2,192,1536]{4,3,2,1,0:T(8,128)(2,1)}) custom-call(bf16[4,128,768]{2,1,0:T(8,128)(2,1)} %get-tuple-element.93.refs_0_, bf16[4,128,768]{2,1,0:T(8,128)(2,1)} %get-tuple-element.95.refs_1_, ...), custom_call_target="tpu_custom_call" | custom-call | flops 72477573120 | bytes 94371840 | tf_op jit(solution)/shard_map/moe_stage/pallas_call | solution.py:1049
  304.0 3.2 slice_bitcast_fusion.9
  307.8 2.3 combine_back.3
  314.3 2.3 combine_back.4
  318.6 2.3 combine_back.5
  321.4 2.5 collective-permute-start.20
  325.8 4.5 collective-permute-done.20
  331.6 3.0 collective-permute-start.10
  334.7 4.2 middle_back.3
  338.9 8.6 %attend_back.3 = (bf16[256,384]{1,0:T(8,128)(2,1)}, bf16[1024,384]{1,0:T(8,128)(2,1)}, bf16[1024,384]{1,0:T(8,128)(2,1)}, f32[3,2,4,512]{3,2,1,0:T(4,128)}) custom-call(bf16[256,384]{1,0:T(8,128)(2,1)} %get-tuple-element.220.q_ref, bf16[1024,384]{1,0:T(8,128)(2,1)} %bitcast.240, bf16[1024,384]{1,0:T(8,128)(2,1)} %bitcast.238, ...), custom_call_target="tpu_custom_call" | custom-call | flops 2013265920 | bytes 4194304 | tf_op jit(solution)/shard_map/attend_back/pallas_call | solution.py:170
  350.5 4.2 middle_back.4
  354.7 8.6 %attend_back.4 = (bf16[256,384]{1,0:T(8,128)(2,1)}, bf16[1024,384]{1,0:T(8,128)(2,1)}, bf16[1024,384]{1,0:T(8,128)(2,1)}, f32[3,2,4,512]{3,2,1,0:T(4,128)}) custom-call(bf16[256,384]{1,0:T(8,128)(2,1)} %get-tuple-element.218.q_ref, bf16[1024,384]{1,0:T(8,128)(2,1)} %bitcast.236, bf16[1024,384]{1,0:T(8,128)(2,1)} %bitcast.234, ...), custom_call_target="tpu_custom_call" | custom-call | flops 2013265920 | bytes 4194304 | tf_op jit(solution)/shard_map/attend_back/pallas_call | solution.py:170
  365.0 4.2 middle_back.5
  369.2 8.8 %attend_back.5 = (bf16[256,384]{1,0:T(8,128)(2,1)}, bf16[1024,384]{1,0:T(8,128)(2,1)}, bf16[1024,384]{1,0:T(8,128)(2,1)}, f32[3,2,4,512]{3,2,1,0:T(4,128)}) custom-call(bf16[256,384]{1,0:T(8,128)(2,1)} %get-tuple-element.219.q_ref, bf16[1024,384]{1,0:T(8,128)(2,1)} %bitcast.232, bf16[1024,384]{1,0:T(8,128)(2,1)} %bitcast.230, ...), custom_call_target="tpu_custom_call" | custom-call | flops 2013265920 | bytes 4194304 | tf_op jit(solution)/shard_map/attend_back/pallas_call | solution.py:170
  378.0 1.6 pad_maximum_fusion.3
  385.6 1.9 fusion.41
  387.6 1.9 fusion.42
  389.5 1.9 fusion.43
  392.3 2.3 combine_out.3
  394.6 2.2 collective-permute-start.12
  400.2 1.7 collective-permute-start.24
  403.7 6.5 %collective-permute-done.22 = bf16[2,256,384]{2,1,0:T(8,128)(2,1)S(1)} collective-permute-done((bf16[2,256,384]{2,1,0:T(8,128)(2,1)S(1)}, bf16[2,256,384]{2,1,0:T(8,128)(2,1)S(1)}, u32[]{:S(2)}, u32[]{:S(2)}) %collective-permute-start.22) | collective-permute-done | bytes 393248 | tf_op jit(solution)/shard_map/ppermute | solution.py:1090
  410.3 8.3 %collective-permute-done.24 = bf16[2,256,384]{2,1,0:T(8,128)(2,1)S(1)} collective-permute-done((bf16[2,256,384]{2,1,0:T(8,128)(2,1)S(1)}, bf16[2,256,384]{2,1,0:T(8,128)(2,1)S(1)}, u32[]{:S(2)}, u32[]{:S(2)}) %collective-permute-start.24) | collective-permute-done | bytes 393248 | tf_op jit(solution)/shard_map/ppermute | solution.py:1090
  418.7 7.6 %collective-permute-done.26 = bf16[2,256,384]{2,1,0:T(8,128)(2,1)S(1)} collective-permute-done((bf16[2,256,384]{2,1,0:T(8,128)(2,1)S(1)}, bf16[2,256,384]{2,1,0:T(8,128)(2,1)S(1)}, u32[]{:S(2)}, u32[]{:S(2)}) %collective-permute-start.26) | collective-permute-done | bytes 393248 | tf_op jit(solution)/shard_map/ppermute | solution.py:1090
  426.4 3.7 convert_add_fusion
  430.2 1.7 fusion.1
  432.5 2.2 copy-done.78
  434.7 3.1 bitcast_convert_fusion
  439.1 2.4 combine_out.4
  441.5 1.7 collective-permute-start.13
  443.3 2.1 pad_maximum_fusion.9.part_ref
  445.4 2.3 combine_out.5
  449.2 26.0 %collective-permute-done.13 = bf16[256,768]{1,0:T(8,128)(2,1)} collective-permute-done((bf16[256,768]{1,0:T(8,128)(2,1)}, bf16[256,768]{1,0:T(8,128)(2,1)}, u32[]{:S(2)}, u32[]{:S(2)}) %collective-permute-start.13) | collective-permute-done | bytes 393248 | tf_op jit(solution)/shard_map/ppermute | solution.py:1090
  475.2 1.6 fusion.15
  476.8 5.1 collective-permute-done.14
  486.1 2.4 fusion
  488.6 2.2 copy-done.4
  492.5 53.6 %last_stage.1 = (f32[4,192,384]{2,1,0:T(8,128)}, f32[192,8]{1,0:T(8,128)}, f32[1,192]{1,0:T(1,128)}, f32[1,192]{1,0:T(1,128)}, f32[8,6]{1,0:T(8,128)}) custom-call(bf16[768,768]{1,0:T(8,128)(2,1)} %bitcast.277, bf16[3,768,384]{2,1,0:T(8,128)(2,1)} %copy-done.15, bf16[768,768]{1,0:T(8,128)(2,1)} %pad_maximum_fusion.6.datt_ref, ...), custom_call_target="tpu_custom_call" | custom-call | flops 1811939328 | bytes 4718592 | tf_op jit(solution)/shard_map/last_stage/pallas_call | solution.py:818
  546.0 1.6 copy.59
  548.9 1.8 slice_bitcast_fusion.23
  550.8 2.1 slice_bitcast_fusion.3
  552.9 2.2 maximum_add_fusion
  555.2 1.7 bitcast_convert_fusion.1
  557.7 2.6 slice_bitcast_fusion.1
  (291 shorter events, 63.5 us)
Async XLA Ops:
  4.6 53.8 %copy-start.42 = (f32[1,512,32]{1,2,0:T(8,128)}, f32[1,512,32]{1,2,0:T(8,128)S(1)}, u32[]{:S(2)}) copy-start(f32[1,512,32]{1,2,0:T(8,128)S(1)} %get-tuple-element.221) | copy-start | bytes 196612
  4.6 53.8 %copy-start.44 = (f32[1,512,32]{1,2,0:T(8,128)}, f32[1,512,32]{1,2,0:T(8,128)S(1)}, u32[]{:S(2)}) copy-start(f32[1,512,32]{1,2,0:T(8,128)S(1)} %get-tuple-element.222) | copy-start | bytes 196612
  4.6 53.8 %copy-start.46 = (f32[1,512,32]{1,2,0:T(8,128)}, f32[1,512,32]{1,2,0:T(8,128)S(1)}, u32[]{:S(2)}) copy-start(f32[1,512,32]{1,2,0:T(8,128)S(1)} %get-tuple-element.223) | copy-start | bytes 196612
  4.6 53.8 %copy-start.48 = (f32[1,512,32]{1,2,0:T(8,128)}, f32[1,512,32]{1,2,0:T(8,128)S(1)}, u32[]{:S(2)}) copy-start(f32[1,512,32]{1,2,0:T(8,128)S(1)} %get-tuple-element.224) | copy-start | bytes 196612
  58.3 6.3 %copy-start.60 = (s32[3,1024]{1,0:T(4,128)S(1)}, s32[3,1024]{1,0:T(4,128)}, u32[]{:S(2)}) copy-start(s32[3,1024]{1,0:T(4,128)} %param.14) | copy-start | bytes 36868
  58.3 7.5 %copy-start.30 = (bf16[3,256,384]{2,1,0:T(8,128)(2,1)S(1)}, bf16[3,256,384]{2,1,0:T(8,128)(2,1)}, u32[]{:S(2)}) copy-start(bf16[3,256,384]{2,1,0:T(8,128)(2,1)} %get-tuple-element.84) | copy-start | bytes 1769476
  60.0 7.2 %copy-start.13 = (bf16[3,4,256,384]{3,2,1,0:T(8,128)(2,1)S(1)}, bf16[3,4,256,384]{3,2,1,0:T(8,128)(2,1)}, u32[]{:S(2)}) copy-start(bf16[3,4,256,384]{3,2,1,0:T(8,128)(2,1)} %get-tuple-element.85) | copy-start | bytes 7077892
  71.0 9.0 %copy-start.29 = (bf16[4,384,192]{2,1,0:T(8,128)(2,1)S(1)}, bf16[4,384,192]{2,1,0:T(8,128)(2,1)}, u32[]{:S(2)}) copy-start(bf16[4,384,192]{2,1,0:T(8,128)(2,1)} %get-tuple-element.89) | copy-start | bytes 1769476
  78.5 67.2 %collective-permute-start.2 = (bf16[256,384]{1,0:T(8,128)(2,1)}, bf16[256,384]{1,0:T(8,128)(2,1)}, u32[]{:S(2)}, u32[]{:S(2)}) collective-permute-start(bf16[256,384]{1,0:T(8,128)(2,1)} %get-tuple-element.94.own_ref), channel_id=1, source_target_pairs={{0,1},{1,0},{2,3},{3,2},{4,5},{5,4},{6,7},{7,6},{8,9},{9,8},{10,11... | collective-permute-start | bytes 589832 | tf_op jit(solution)/shard_map/ppermute | solution.py:1090
  80.6 9.0 %copy-start.6 = (bf16[384,768]{1,0:T(8,128)(2,1)}, bf16[384,768]{1,0:T(8,128)(2,1)S(1)}, u32[]{:S(2)}) copy-start(bf16[384,768]{1,0:T(8,128)(2,1)S(1)} %copy.43.wout_ref) | copy-start | bytes 1769476
  80.6 73.0 %collective-permute-start.1 = (bf16[384,768]{1,0:T(8,128)(2,1)S(1)}, bf16[384,768]{1,0:T(8,128)(2,1)}, u32[]{:S(2)}, u32[]{:S(2)}) collective-permute-start(bf16[384,768]{1,0:T(8,128)(2,1)S(1)} %copy.43.wout_ref), channel_id=1, source_target_pairs={{0,1},{1,0},{2,3},{3,2},{4,5},{5,4},{6,7},{7,6},{8,9},{9,8},{10,11... | collective-permute-start | bytes 1769480 | tf_op jit(solution)/shard_map/ppermute | solution.py:1090
  89.6 58.6 %collective-permute-start = (bf16[256,384]{1,0:T(8,128)(2,1)}, bf16[256,384]{1,0:T(8,128)(2,1)}, u32[]{:S(2)}, u32[]{:S(2)}) collective-permute-start(bf16[256,384]{1,0:T(8,128)(2,1)} %get-tuple-element.88.own_ref), channel_id=1, source_target_pairs={{0,1},{1,0},{2,3},{3,2},{4,5},{5,4},{6,7},{7,6},{8,9},{9,8},{10,11... | collective-permute-start | bytes 589832 | tf_op jit(solution)/shard_map/ppermute | solution.py:1090
  94.0 32.5 %collective-permute-start.7 = (bf16[2,192,1536]{2,1,0:T(8,128)(2,1)}, bf16[2,192,1536]{2,1,0:T(8,128)(2,1)}, u32[]{:S(2)}, u32[]{:S(2)}) collective-permute-start(bf16[2,192,1536]{2,1,0:T(8,128)(2,1)} %get-tuple-element.192), channel_id=1, source_target_pairs={{0,1},{1,0},{2,3},{3,2},{4,5},{5,4},{6,7},{7,6},{8,9},{9,8},{10,11... | collective-permute-start | bytes 3538952 | tf_op jit(solution)/shard_map/ppermute | solution.py:1090
  95.5 34.1 %copy-start.55 = (f32[3,8,256]{2,1,0:T(8,128)}, f32[3,8,256]{2,1,0:T(8,128)S(1)}, u32[]{:S(2)}) copy-start(f32[3,8,256]{2,1,0:T(8,128)S(1)} %convolution_select_fusion) | copy-start | bytes 73732
  129.6 57.7 %collective-permute-start.8 = (bf16[2,2,192,1536]{3,2,1,0:T(8,128)(2,1)}, bf16[2,2,192,1536]{3,2,1,0:T(8,128)(2,1)}, u32[]{:S(2)}, u32[]{:S(2)}) collective-permute-start(bf16[2,2,192,1536]{3,2,1,0:T(8,128)(2,1)} %pad_maximum_fusion.refs_10_), channel_id=1, source_target_pairs={{0,4},{2,6},{4,0},{6,2},{1,5},{3,7},{5,1},{7,3},{8,12},{10,14},{12... | collective-permute-start | bytes 7077896 | tf_op jit(solution)/shard_map/ppermute | solution.py:1090
  133.4 36.0 %collective-permute-start.4 = (bf16[3,128,768]{2,1,0:T(8,128)(2,1)}, bf16[3,128,768]{2,1,0:T(8,128)(2,1)}, u32[]{:S(2)}, u32[]{:S(2)}) collective-permute-start(bf16[3,128,768]{2,1,0:T(8,128)(2,1)} %get-tuple-element.195), channel_id=1, source_target_pairs={{0,8},{8,0},{16,24},{24,16},{1,9},{9,1},{17,25},{25,17},{2,10},{10... | collective-permute-start | bytes 1769480 | tf_op jit(solution)/shard_map/ppermute | solution.py:1090
  134.4 8.0 %copy-start.2 = (bf16[3,256,768]{2,1,0:T(8,128)(2,1)S(1)}, bf16[3,256,768]{2,1,0:T(8,128)(2,1)}, u32[]{:S(2)}) copy-start(bf16[3,256,768]{2,1,0:T(8,128)(2,1)} %tok_ref.1) | copy-start | bytes 3538948
  134.5 8.3 %copy-start.40 = (f32[3,4,256]{2,1,0:T(4,128)S(1)}, f32[3,4,256]{2,1,0:T(4,128)}, u32[]{:S(2)}) copy-start(f32[3,4,256]{2,1,0:T(4,128)} %pad_maximum_fusion.14.place_ref) | copy-start | bytes 36868
  134.5 8.9 %copy-start.56 = (f32[3,8,256]{2,1,0:T(8,128)S(1)}, f32[3,8,256]{2,1,0:T(8,128)}, u32[]{:S(2)}) copy-start(f32[3,8,256]{2,1,0:T(8,128)} %copy-done.55) | copy-start | bytes 73732
  134.5 9.5 %copy-start.62 = (s32[3,256]{1,0:T(4,128)S(1)}, s32[3,256]{1,0:T(4,128)}, u32[]{:S(2)}) copy-start(s32[3,256]{1,0:T(4,128)} %copy-done.61) | copy-start | bytes 9220
  134.5 9.5 %copy-start.64 = (s32[3,256]{1,0:T(4,128)S(1)}, s32[3,256]{1,0:T(4,128)}, u32[]{:S(2)}) copy-start(s32[3,256]{1,0:T(4,128)} %copy-done.63) | copy-start | bytes 9220
  134.5 9.5 %copy-start.77 = (s32[8]{0:T(128)S(1)}, s32[8]{0:T(128)}, u32[]{:S(2)}) copy-start(s32[8]{0:T(128)} %copy-done.76) | copy-start | bytes 100
  142.4 7.8 %copy-start.23 = (bf16[256,384]{1,0:T(8,128)(2,1)S(1)}, bf16[256,384]{1,0:T(8,128)(2,1)}, u32[]{:S(2)}) copy-start(bf16[256,384]{1,0:T(8,128)(2,1)} %get-tuple-element.94.own_ref) | copy-start | bytes 589828
  142.4 7.8 %copy-start.24 = (bf16[256,384]{1,0:T(8,128)(2,1)S(1)}, bf16[256,384]{1,0:T(8,128)(2,1)}, u32[]{:S(2)}) copy-start(bf16[256,384]{1,0:T(8,128)(2,1)} %get-tuple-element.88.own_ref) | copy-start | bytes 589828
  142.4 7.8 %copy-start.28 = (bf16[256,384]{1,0:T(8,128)(2,1)S(1)}, bf16[256,384]{1,0:T(8,128)(2,1)}, u32[]{:S(2)}) copy-start(bf16[256,384]{1,0:T(8,128)(2,1)} %get-tuple-element.96.own_ref) | copy-start | bytes 589828
  144.7 7.9 %copy-start.9 = (bf16[3,256,768]{2,1,0:T(8,128)(2,1)S(1)}, bf16[3,256,768]{2,1,0:T(8,128)(2,1)}, u32[]{:S(2)}) copy-start(bf16[3,256,768]{2,1,0:T(8,128)(2,1)} %rows_ref.1) | copy-start | bytes 3538948
  145.7 6.2 %copy-start.70 = (f32[1,768]{1,0:T(1,128)S(1)}, f32[1,768]{1,0:T(1,128)}, u32[]{:S(2)}) copy-start(f32[1,768]{1,0:T(1,128)} %get-tuple-element.137) | copy-start | bytes 9220
  145.8 41.5 %collective-permute-start.5 = (bf16[3,128,768]{2,1,0:T(8,128)(2,1)}, bf16[3,128,768]{2,1,0:T(8,128)(2,1)}, u32[]{:S(2)}, u32[]{:S(2)}) collective-permute-start(bf16[3,128,768]{2,1,0:T(8,128)(2,1)} %get-tuple-element.194), channel_id=1, source_target_pairs={{0,16},{8,24},{16,0},{24,8},{1,17},{9,25},{17,1},{25,9},{2,18},{10... | collective-permute-start | bytes 1769480 | tf_op jit(solution)/shard_map/ppermute | solution.py:1090
  148.3 39.0 %collective-permute-start.6 = (bf16[3,128,768]{2,1,0:T(8,128)(2,1)}, bf16[3,128,768]{2,1,0:T(8,128)(2,1)}, u32[]{:S(2)}, u32[]{:S(2)}) collective-permute-start(bf16[3,128,768]{2,1,0:T(8,128)(2,1)} %get-tuple-element.193), channel_id=1, source_target_pairs={{0,24},{8,16},{16,8},{24,0},{1,25},{9,17},{17,9},{25,1},{2,26},{10... | collective-permute-start | bytes 1769480 | tf_op jit(solution)/shard_map/ppermute | solution.py:1090
  153.6 11.3 %collective-permute-start.3 = (bf16[256,384]{1,0:T(8,128)(2,1)S(1)}, bf16[256,384]{1,0:T(8,128)(2,1)S(1)}, u32[]{:S(2)}, u32[]{:S(2)}) collective-permute-start(bf16[256,384]{1,0:T(8,128)(2,1)S(1)} %copy-done.28), channel_id=1, source_target_pairs={{0,1},{1,0},{2,3},{3,2},{4,5},{5,4},{6,7},{7,6},{8,9},{9,8},{10,11... | collective-permute-start | bytes 589832 | tf_op jit(solution)/shard_map/ppermute | solution.py:1090
  304.0 7.6 %copy-start.12 = (bf16[4,3,128,768]{3,2,1,0:T(8,128)(2,1)S(1)}, bf16[4,3,128,768]{3,2,1,0:T(8,128)(2,1)}, u32[]{:S(2)}) copy-start(bf16[4,3,128,768]{3,2,1,0:T(8,128)(2,1)} %get-tuple-element.101) | copy-start | bytes 7077892
  310.1 21.5 %collective-permute-start.15 = (bf16[256,768]{1,0:T(8,128)(2,1)}, bf16[256,768]{1,0:T(8,128)(2,1)S(1)}, u32[]{:S(2)}, u32[]{:S(2)}) collective-permute-start(bf16[256,768]{1,0:T(8,128)(2,1)} %get-tuple-element.106.own_ref), channel_id=1, source_target_pairs={{0,1},{1,0},{2,3},{3,2},{4,5},{5,4},{6,7},{7,6},{8,9},{9,8},{10,11... | collective-permute-start | bytes 1179656 | tf_op jit(solution)/shard_map/ppermute | solution.py:1090
  313.7 112.7 %collective-permute-start.28 = (bf16[2,2,2,192,1536]{4,3,2,1,0:T(8,128)(2,1)}, bf16[2,2,2,192,1536]{4,3,2,1,0:T(8,128)(2,1)}, u32[]{:S(2)}, u32[]{:S(2)}) collective-permute-start(bf16[2,2,2,192,1536]{4,3,2,1,0:T(8,128)(2,1)} %get-tuple-element.157), channel_id=1, source_target_pairs={{0,2},{2,0},{4,6},{6,4},{1,3},{3,1},{5,7},{7,5},{8,10},{10,8},{12,... | collective-permute-start | bytes 14155784 | tf_op jit(solution)/shard_map/ppermute | solution.py:1090
  313.7 7.7 %collective-permute-start.16 = (f32[4,256]{1,0:T(4,128)S(1)}, f32[4,256]{1,0:T(4,128)S(1)}, u32[]{:S(2)}, u32[]{:S(2)}) collective-permute-start(f32[4,256]{1,0:T(4,128)S(1)} %copy-done.69), channel_id=1, source_target_pairs={{0,1},{1,0},{2,3},{3,2},{4,5},{5,4},{6,7},{7,6},{8,9},{9,8},{10,11... | collective-permute-start | bytes 12296 | tf_op jit(solution)/shard_map/ppermute | solution.py:1090
  316.6 8.0 %collective-permute-start.18 = (f32[4,256]{1,0:T(4,128)}, f32[4,256]{1,0:T(4,128)S(1)}, u32[]{:S(2)}, u32[]{:S(2)}) collective-permute-start(f32[4,256]{1,0:T(4,128)} %get-tuple-element.112), channel_id=1, source_target_pairs={{0,1},{1,0},{2,3},{3,2},{4,5},{5,4},{6,7},{7,6},{8,9},{9,8},{10,11... | collective-permute-start | bytes 12296 | tf_op jit(solution)/shard_map/ppermute | solution.py:1090
  318.1 31.0 %collective-permute-start.17 = (bf16[256,768]{1,0:T(8,128)(2,1)}, bf16[256,768]{1,0:T(8,128)(2,1)S(1)}, u32[]{:S(2)}, u32[]{:S(2)}) collective-permute-start(bf16[256,768]{1,0:T(8,128)(2,1)} %get-tuple-element.111.own_ref), channel_id=1, source_target_pairs={{0,1},{1,0},{2,3},{3,2},{4,5},{5,4},{6,7},{7,6},{8,9},{9,8},{10,11... | collective-permute-start | bytes 1179656 | tf_op jit(solution)/shard_map/ppermute | solution.py:1090
  321.4 8.9 %collective-permute-start.20 = (f32[4,256]{1,0:T(4,128)}, f32[4,256]{1,0:T(4,128)S(1)}, u32[]{:S(2)}, u32[]{:S(2)}) collective-permute-start(f32[4,256]{1,0:T(4,128)} %get-tuple-element.117), channel_id=1, source_target_pairs={{0,1},{1,0},{2,3},{3,2},{4,5},{5,4},{6,7},{7,6},{8,9},{9,8},{10,11... | collective-permute-start | bytes 12296 | tf_op jit(solution)/shard_map/ppermute | solution.py:1090
  324.5 40.4 %collective-permute-start.19 = (bf16[256,768]{1,0:T(8,128)(2,1)}, bf16[256,768]{1,0:T(8,128)(2,1)}, u32[]{:S(2)}, u32[]{:S(2)}) collective-permute-start(bf16[256,768]{1,0:T(8,128)(2,1)} %get-tuple-element.116.own_ref), channel_id=1, source_target_pairs={{0,1},{1,0},{2,3},{3,2},{4,5},{5,4},{6,7},{7,6},{8,9},{9,8},{10,11... | collective-permute-start | bytes 1179656 | tf_op jit(solution)/shard_map/ppermute | solution.py:1090
  330.3 54.8 %collective-permute-start.9 = (bf16[3,128,768]{2,1,0:T(8,128)(2,1)}, bf16[3,128,768]{2,1,0:T(8,128)(2,1)}, u32[]{:S(2)}, u32[]{:S(2)}) collective-permute-start(bf16[3,128,768]{2,1,0:T(8,128)(2,1)} %get-tuple-element.188), channel_id=1, source_target_pairs={{0,8},{8,0},{16,24},{24,16},{1,9},{9,1},{17,25},{25,17},{2,10},{10... | collective-permute-start | bytes 1769480 | tf_op jit(solution)/shard_map/ppermute | solution.py:1090
  331.6 55.9 %collective-permute-start.10 = (bf16[3,128,768]{2,1,0:T(8,128)(2,1)}, bf16[3,128,768]{2,1,0:T(8,128)(2,1)}, u32[]{:S(2)}, u32[]{:S(2)}) collective-permute-start(bf16[3,128,768]{2,1,0:T(8,128)(2,1)} %get-tuple-element.190), channel_id=1, source_target_pairs={{0,16},{8,24},{16,0},{24,8},{1,17},{9,25},{17,1},{25,9},{2,18},{10... | collective-permute-start | bytes 1769480 | tf_op jit(solution)/shard_map/ppermute | solution.py:1090
  349.1 40.4 %collective-permute-start.11 = (bf16[3,128,768]{2,1,0:T(8,128)(2,1)}, bf16[3,128,768]{2,1,0:T(8,128)(2,1)}, u32[]{:S(2)}, u32[]{:S(2)}) collective-permute-start(bf16[3,128,768]{2,1,0:T(8,128)(2,1)} %get-tuple-element.189), channel_id=1, source_target_pairs={{0,24},{8,16},{16,8},{24,0},{1,25},{9,17},{17,9},{25,1},{2,26},{10... | collective-permute-start | bytes 1769480 | tf_op jit(solution)/shard_map/ppermute | solution.py:1090
  364.9 31.9 %collective-permute-start.21 = (bf16[2,2,256,384]{3,2,0,1:T(8,128)(2,1)S(1)}, bf16[2,2,256,384]{3,2,0,1:T(8,128)(2,1)}, u32[]{:S(2)}, u32[]{:S(2)}) collective-permute-start(bf16[2,2,256,384]{3,2,0,1:T(8,128)(2,1)S(1)} %slice.346), channel_id=1, source_target_pairs={{0,2},{2,0},{4,6},{6,4},{1,3},{3,1},{5,7},{7,5},{8,10},{10,8},{12,... | collective-permute-start | bytes 2359304 | tf_op jit(solution)/shard_map/ppermute | solution.py:1090
  385.1 13.6 %collective-permute-start.23 = (bf16[2,2,256,384]{3,2,0,1:T(8,128)(2,1)}, bf16[2,2,256,384]{3,2,0,1:T(8,128)(2,1)}, u32[]{:S(2)}, u32[]{:S(2)}) collective-permute-start(bf16[2,2,256,384]{3,2,0,1:T(8,128)(2,1)} %slice.350), channel_id=1, source_target_pairs={{0,2},{2,0},{4,6},{6,4},{1,3},{3,1},{5,7},{7,5},{8,10},{10,8},{12,... | collective-permute-start | bytes 2359304 | tf_op jit(solution)/shard_map/ppermute | solution.py:1090
  387.5 14.3 %collective-permute-start.25 = (bf16[2,2,256,384]{3,2,0,1:T(8,128)(2,1)}, bf16[2,2,256,384]{3,2,0,1:T(8,128)(2,1)}, u32[]{:S(2)}, u32[]{:S(2)}) collective-permute-start(bf16[2,2,256,384]{3,2,0,1:T(8,128)(2,1)} %slice.354), channel_id=1, source_target_pairs={{0,2},{2,0},{4,6},{6,4},{1,3},{3,1},{5,7},{7,5},{8,10},{10,8},{12,... | collective-permute-start | bytes 2359304 | tf_op jit(solution)/shard_map/ppermute | solution.py:1090
  394.6 53.3 %collective-permute-start.12 = (bf16[256,768]{1,0:T(8,128)(2,1)}, bf16[256,768]{1,0:T(8,128)(2,1)}, u32[]{:S(2)}, u32[]{:S(2)}) collective-permute-start(bf16[256,768]{1,0:T(8,128)(2,1)} %combine_out.3), channel_id=1, source_target_pairs={{0,1},{1,0},{2,3},{3,2},{4,5},{5,4},{6,7},{7,6},{8,9},{9,8},{10,11... | collective-permute-start | bytes 1179656 | tf_op jit(solution)/shard_map/ppermute | solution.py:1090
  398.2 12.1 %collective-permute-start.22 = (bf16[2,256,384]{2,1,0:T(8,128)(2,1)S(1)}, bf16[2,256,384]{2,1,0:T(8,128)(2,1)S(1)}, u32[]{:S(2)}, u32[]{:S(2)}) collective-permute-start(bf16[2,256,384]{2,1,0:T(8,128)(2,1)S(1)} %fusion.17), channel_id=1, source_target_pairs={{0,4},{2,6},{4,0},{6,2},{1,5},{3,7},{5,1},{7,3},{8,12},{10,14},{12... | collective-permute-start | bytes 1179656 | tf_op jit(solution)/shard_map/ppermute | solution.py:1090
  398.7 27.7 %slice-start.1 = ((s8[4718592]{0:T(1024)(128)(4,1)}), s8[4194304]{0:T(1024)(128)(4,1)S(1)}, s32[]{:S(2)}) async-start(s8[4718592]{0:T(1024)(128)(4,1)} %bitcast.227), calls=%async_computation.1 | async-start | bytes 8388608
  400.2 26.2 %slice-start.2 = ((s8[4718592]{0:T(1024)(128)(4,1)}), s8[524288]{0:T(1024)(128)(4,1)S(1)}, s32[]{:S(2)}) async-start(s8[4718592]{0:T(1024)(128)(4,1)} %bitcast.227), calls=%async_computation.2 | async-start | bytes 1048576
  400.2 18.5 %collective-permute-start.24 = (bf16[2,256,384]{2,1,0:T(8,128)(2,1)S(1)}, bf16[2,256,384]{2,1,0:T(8,128)(2,1)S(1)}, u32[]{:S(2)}, u32[]{:S(2)}) collective-permute-start(bf16[2,256,384]{2,1,0:T(8,128)(2,1)S(1)} %fusion.18), channel_id=1, source_target_pairs={{0,4},{2,6},{4,0},{6,2},{1,5},{3,7},{5,1},{7,3},{8,12},{10,14},{12... | collective-permute-start | bytes 1179656 | tf_op jit(solution)/shard_map/ppermute | solution.py:1090
  403.2 23.1 %collective-permute-start.26 = (bf16[2,256,384]{2,1,0:T(8,128)(2,1)S(1)}, bf16[2,256,384]{2,1,0:T(8,128)(2,1)S(1)}, u32[]{:S(2)}, u32[]{:S(2)}) collective-permute-start(bf16[2,256,384]{2,1,0:T(8,128)(2,1)S(1)} %fusion.19), channel_id=1, source_target_pairs={{0,4},{2,6},{4,0},{6,2},{1,5},{3,7},{5,1},{7,3},{8,12},{10,14},{12... | collective-permute-start | bytes 1179656 | tf_op jit(solution)/shard_map/ppermute | solution.py:1090
  430.1 7.7 %copy-start = (f32[2,2,2,192,1536]{4,3,2,1,0:T(8,128)}, f32[2,2,2,192,1536]{4,3,2,1,0:T(8,128)S(1)}, u32[]{:S(2)}) copy-start(f32[2,2,2,192,1536]{4,3,2,1,0:T(8,128)S(1)} %convert_add_fusion) | copy-start | bytes 28311556
  431.8 53.5 %collective-permute-start.29 = (bf16[2,2,192,1536]{3,2,1,0:T(8,128)(2,1)}, bf16[2,2,192,1536]{3,2,1,0:T(8,128)(2,1)}, u32[]{:S(2)}, u32[]{:S(2)}) collective-permute-start(bf16[2,2,192,1536]{3,2,1,0:T(8,128)(2,1)} %fusion.1), channel_id=1, source_target_pairs={{0,4},{2,6},{4,0},{6,2},{1,5},{3,7},{5,1},{7,3},{8,12},{10,14},{12... | collective-permute-start | bytes 7077896 | tf_op jit(solution)/shard_map/ppermute | solution.py:1090
  437.8 45.4 %collective-permute-start.27 = (bf16[768,768]{1,0:T(8,128)(2,1)S(1)}, bf16[768,768]{1,0:T(8,128)(2,1)S(1)}, u32[]{:S(2)}, u32[]{:S(2)}) collective-permute-start(bf16[768,768]{1,0:T(8,128)(2,1)S(1)} %get-tuple-element.253), channel_id=1, source_target_pairs={{0,1},{1,0},{2,3},{3,2},{4,5},{5,4},{6,7},{7,6},{8,9},{9,8},{10,11... | collective-permute-start | bytes 3538952 | tf_op jit(solution)/shard_map/ppermute | solution.py:1090
  439.1 8.8 %copy-start.10 = (f32[256,768]{1,0:T(8,128)S(1)}, f32[256,768]{1,0:T(8,128)}, u32[]{:S(2)}) copy-start(f32[256,768]{1,0:T(8,128)} %get-tuple-element.92.mid_ref) | copy-start | bytes 2359300
  439.1 8.8 %copy-start.16 = (bf16[256,768]{1,0:T(8,128)(2,1)S(1)}, bf16[256,768]{1,0:T(8,128)(2,1)}, u32[]{:S(2)}) copy-start(bf16[256,768]{1,0:T(8,128)(2,1)} %combine_out.3) | copy-start | bytes 1179652
  441.5 33.7 %collective-permute-start.13 = (bf16[256,768]{1,0:T(8,128)(2,1)}, bf16[256,768]{1,0:T(8,128)(2,1)}, u32[]{:S(2)}, u32[]{:S(2)}) collective-permute-start(bf16[256,768]{1,0:T(8,128)(2,1)} %combine_out.4), channel_id=1, source_target_pairs={{0,1},{1,0},{2,3},{3,2},{4,5},{5,4},{6,7},{7,6},{8,9},{9,8},{10,11... | collective-permute-start | bytes 1179656 | tf_op jit(solution)/shard_map/ppermute | solution.py:1090
  447.7 34.3 %copy-start.11 = (f32[256,768]{1,0:T(8,128)S(1)}, f32[256,768]{1,0:T(8,128)}, u32[]{:S(2)}) copy-start(f32[256,768]{1,0:T(8,128)} %get-tuple-element.103.mid_ref) | copy-start | bytes 2359300
  447.7 34.3 %copy-start.17 = (bf16[256,768]{1,0:T(8,128)(2,1)S(1)}, bf16[256,768]{1,0:T(8,128)(2,1)}, u32[]{:S(2)}) copy-start(bf16[256,768]{1,0:T(8,128)(2,1)} %combine_out.5) | copy-start | bytes 1179652
  447.7 34.2 %collective-permute-start.14 = (bf16[256,768]{1,0:T(8,128)(2,1)}, bf16[256,768]{1,0:T(8,128)(2,1)S(1)}, u32[]{:S(2)}, u32[]{:S(2)}) collective-permute-start(bf16[256,768]{1,0:T(8,128)(2,1)} %combine_out.5), channel_id=1, source_target_pairs={{0,1},{1,0},{2,3},{3,2},{4,5},{5,4},{6,7},{7,6},{8,9},{9,8},{10,11... | collective-permute-start | bytes 1179656 | tf_op jit(solution)/shard_map/ppermute | solution.py:1090
  448.0 35.3 %copy-start.14 = (f32[768,768,1]{1,0,2:T(8,128)S(1)}, f32[768,768,1]{1,0,2:T(8,128)}, u32[]{:S(2)}) copy-start(f32[768,768,1]{1,0,2:T(8,128)} %get-tuple-element.254) | copy-start | bytes 7077892
  475.2 8.0 %copy-start.3 = (bf16[3,256,768]{2,1,0:T(8,128)(2,1)S(1)}, bf16[3,256,768]{2,1,0:T(8,128)(2,1)}, u32[]{:S(2)}) copy-start(bf16[3,256,768]{2,1,0:T(8,128)(2,1)} %tok_ref.1) | copy-start | bytes 3538948
  476.8 6.5 %copy-start.53 = (f32[768]{0:T(1024)S(1)}, f32[768]{0:T(1024)}, u32[]{:S(2)}) copy-start(f32[768]{0:T(1024)} %rsqrt.12) | copy-start | bytes 9220
  476.8 6.5 %copy-start.54 = (f32[768]{0:T(1024)S(1)}, f32[768]{0:T(1024)}, u32[]{:S(2)}) copy-start(f32[768]{0:T(1024)} %reduce.1) | copy-start | bytes 9220
  491.9 63.3 %collective-permute-start.30 = (bf16[2,192,1536]{2,1,0:T(8,128)(2,1)}, bf16[2,192,1536]{2,1,0:T(8,128)(2,1)}, u32[]{:S(2)}, u32[]{:S(2)}) collective-permute-start(bf16[2,192,1536]{2,1,0:T(8,128)(2,1)} %fusion.3), channel_id=1, source_target_pairs={{0,1},{1,0},{2,3},{3,2},{4,5},{5,4},{6,7},{7,6},{8,9},{9,8},{10,11... | collective-permute-start | bytes 3538952 | tf_op jit(solution)/shard_map/ppermute | solution.py:1090
  (49 other events, 140.0 us)

commit v3 on v2

--- a/solution.py
+++ b/solution.py
@@ -14,6 +14,7 @@
 MASKED = -1e30
 BF16 = jnp.bfloat16
 F32 = jnp.float32
+EARLY = 50
 VMEM_BYTES = 60 * 1024 * 1024
 GELU_C = 0.7978845608028654
 GELU_A = 0.044715
@@ -23,8 +24,10 @@
     return pltpu.CompilerParams(vmem_limit_bytes=VMEM_BYTES)
 
 
-def cost(flops, nbytes, trans=0):
-    return pl.CostEstimate(flops=int(flops), bytes_accessed=int(nbytes), transcendentals=int(trans))
+def cost(flops, nbytes, trans=0, scale=1):
+    return pl.CostEstimate(
+        flops=int(flops) // scale, bytes_accessed=int(nbytes) // scale, transcendentals=int(trans) // scale
+    )
 
 
 def dot(a, b):
@@ -57,7 +60,7 @@
         out_specs=pl.BlockSpec((1, 1024, 256), lambda h: (h, 0, 0)),
         out_shape=jax.ShapeDtypeStruct((heads, 1024, 256), BF16),
         compiler_params=params(),
-        cost_estimate=cost(heads * 2 * 1024 * 512, heads * 1024 * 256 * 2),
+        cost_estimate=cost(heads * 2 * 1024 * 512, heads * 1024 * 256 * 2, scale=EARLY),
     )(windows)
 
 
@@ -110,7 +113,7 @@
         ],
         scratch_shapes=[pltpu.VMEM((length, rows), F32)],
         compiler_params=params(),
-        cost_estimate=cost(pairs * 2 * 4 * rows * length * 128, 6 * rows * length * 2, pairs * 2 * rows * length),
+        cost_estimate=cost(pairs * 2 * 4 * rows * length * 128, 6 * rows * length * 2, pairs * 2 * rows * length, scale=EARLY),
     )(queries, keys, values, bias, ids_query, ids_key)
 
 
@@ -276,7 +279,7 @@
             jax.ShapeDtypeStruct((groups, 1, cap), F32),
         ],
         compiler_params=params(),
-        cost_estimate=cost(2 * rows * width * width + 2 * groups * cap * rows * width, rows * width * 16),
+        cost_estimate=cost(2 * rows * width * width + 2 * groups * cap * rows * width, rows * width * 16, scale=EARLY),
     )(own, other, x, wout, gain, router, hits, place)
 
 
@@ -512,10 +515,10 @@
 
 
 def first_kernel(
-    seqs, tok_ref, wqkv_ref, wout_ref, table_ref, ga_ref, gm_ref, router_ref,
-    q_ref, k_ref, v_ref, normed_ref, wqkv_out, wout_out, table_out, gain_ref, gm_out, router_out,
+    seqs, tok_ref, wqkv_ref, wout_ref, table_ref, ga_ref, gm_ref, router_ref, pair_ref,
+    q_ref, k_ref, v_ref, normed_ref, wqkv_out, wout_out, table_out, gain_ref, gm_out, router_out, got_out, far_out,
     tok_all, n_all, ga_all, gm_all, router_all,
-    z_send, z_recv, f_send, f_recv, t_send, t_recv, y_send, y_recv, l_sem,
+    z_send, z_recv, f_send, f_recv, t_send, t_recv, y_send, y_recv, l_sem, e_sems,
 ):
     dp = lax.axis_index("dp")
     ctx = lax.axis_index("ctx")
@@ -524,7 +527,7 @@
     rows = wqkv_ref.shape[1]
     half = rows // 2
     orows = wout_ref.shape[0] // 2
-    greet([{"dp": dp ^ b} for b in (1, 2, 3)] + [{"ctx": ctx ^ 1}, {"ctx": ctx ^ 2}])
+    greet([{"dp": dp ^ b} for b in (1, 2, 3)] + [{"ctx": ctx ^ 1}, {"ctx": ctx ^ 2}, {"tp": tp ^ 1}])
 
     def w_rows(owner, side):
         return pl.ds(pl.multiple_of(owner * rows + side * half, 16), half)
@@ -556,7 +559,11 @@
     beside = remote(tok_ref, tok_all.at[1], t_send.at[0], t_recv.at[0], ctx=ctx ^ 1)
     beside.start()
     across = [remote(tok_ref.at[s], tok_all.at[2, s], y_send.at[s], y_recv.at[s], ctx=ctx ^ 2) for s in range(seqs)]
-    for copy in across:
+    expert_copies = [
+        remote(pair_ref.at[1 - tp], got_out, e_sems.at[0, 0], e_sems.at[1, 0], tp=tp ^ 1),
+        remote(pair_ref.at[tp], far_out, e_sems.at[0, 1], e_sems.at[1, 1], ctx=ctx ^ 2),
+    ]
+    for copy in across + expert_copies:
         copy.start()
     own = [
         pltpu.make_async_copy(tok_ref, tok_all.at[0], l_sem.at[0]),
@@ -653,6 +660,8 @@
         return carry
 
     lax.fori_loop(0, seqs, others, 0)
+    for copy in expert_copies:
+        copy.wait()
     for group in small:
         for copy in group:
             copy.wait_send()
@@ -660,7 +669,7 @@
         copy.wait_send()
 
 
-def first_stage(tokens, wqkv, wout, table, gain_attn, gain_moe, router):
+def first_stage(tokens, wqkv, wout, table, gain_attn, gain_moe, router, expert_pair):
     seqs, stretch, width = tokens.shape
     count, rows, local = wqkv.shape
     dp = width // rows
@@ -671,8 +680,8 @@
     return pl.pallas_call(
         functools.partial(first_kernel, seqs),
         name="first_stage",
-        in_specs=[any_spec] * 7,
-        out_specs=[vmem] * 10,
+        in_specs=[any_spec] * 8,
+        out_specs=[vmem] * 10 + [any_spec] * 2,
         out_shape=[
             jax.ShapeDtypeStruct((seqs, stretch, local), BF16),
             jax.ShapeDtypeStruct((seqs, 4, stretch, local), BF16),
@@ -684,6 +693,8 @@
             jax.ShapeDtypeStruct((1, width), F32),
             jax.ShapeDtypeStruct((1, width), BF16),
             jax.ShapeDtypeStruct((experts_n, width), BF16),
+            jax.ShapeDtypeStruct(expert_pair.shape[1:], BF16),
+            jax.ShapeDtypeStruct(expert_pair.shape[1:], BF16),
         ],
         scratch_shapes=[
             pltpu.VMEM((4, seqs, stretch, width), BF16),
@@ -692,17 +703,287 @@
             pltpu.VMEM((dp, 1, rows), BF16),
             pltpu.VMEM((dp, rows, experts_n), BF16),
             dma((6, 3)), dma((6, 3)), dma((2, 3)), dma((2, 3)), dma((1 + seqs,)), dma((1 + seqs,)),
-            dma((seqs,)), dma((seqs,)), dma((7,)),
+            dma((seqs,)), dma((seqs,)), dma((7,)), dma((2, 2)),
         ],
         compiler_params=pltpu.CompilerParams(vmem_limit_bytes=VMEM_BYTES, collective_id=0, has_side_effects=True),
         cost_estimate=cost(40 * 10**9, 10**7),
-    )(tokens, wqkv, wout, table, gain_attn, gain_moe, router)
+    )(tokens, wqkv, wout, table, gain_attn, gain_moe, router, expert_pair)
+
+
+def back_kernel(seqs, groups, cap, *refs):
+    mid_refs, moe_refs, gate_refs, lse_refs = (refs[i * seqs : (i + 1) * seqs] for i in range(4))
+    refs = refs[4 * seqs :]
+    din_ref, part_ref, q_ref, k_ref, v_ref, bias_ref, cot_ref, wout_ref = refs[:8]
+    h_ref, place_ref, near_ref, idq_ref, idk_ref, router_ref, gain_ref = refs[8:15]
+    out_ref, gmid_ref, low_ref, proj_ref, gain_grad_ref, router_grad_ref, rel_ref = refs[15:22]
+    (
+        mid_v, moe_v, gate_v, lse_v, din_v, part_v, q_v, k_v, v_v, bias_v, cot_v, wout_v,
+        din_own, din_other, h_own, h_other, out_own, out_other, datt_v, mask_v, keep_v, give_v, core_v, y_v, far_v,
+        load_sems, seq_sems, part_sems, x_sems, c_sems, y_sems,
+    ) = refs[22:]
+    dp = lax.axis_index("dp")
+    ctx = lax.axis_index("ctx")
+    tp = lax.axis_index("tp")
+    greet([{"dp": dp ^ b} for b in range(1, groups)] + [{"ctx": ctx ^ 1}, {"ctx": ctx ^ 2}, {"tp": tp ^ 1}])
+    rows = groups * cap
+    stretch, width = mid_v.shape[1:]
+    local = q_v.shape[2]
+    pairs = local // (2 * HD)
+
+    def part_copy(s, b):
+        return remote(part_ref.at[b, s], part_v.at[b, s], part_sems.at[0, s, b], part_sems.at[1, s, b], dp=dp ^ b)
+
+    for s in range(seqs):
+        for b in range(groups - 1, 0, -1):
+            part_copy(s, b).start()
+    din_load = pltpu.make_async_copy(din_ref, din_v, load_sems.at[0])
+    loads = [
+        pltpu.make_async_copy(src, dst, load_sems.at[i + 1])
+        for i, (src, dst) in enumerate(
+            ((wout_ref, wout_v), (cot_ref, cot_v), (q_ref, q_v), (k_ref, k_v), (v_ref, v_v), (bias_ref, bias_v),
+             (part_ref.at[0], part_v.at[0]))
+        )
+    ]
+    for s in range(seqs):
+        for i, (src, dst) in enumerate(((mid_refs, mid_v), (moe_refs, moe_v), (gate_refs, gate_v), (lse_refs, lse_v))):
+            loads.append(pltpu.make_async_copy(src[s], dst.at[s], seq_sems.at[s, i]))
+    din_load.start()
+    for copy in loads:
+        copy.start()
+    gain_grad_ref[...] = jnp.zeros_like(gain_grad_ref)
+    router_grad_ref[...] = jnp.zeros_like(router_grad_ref)
+    rel_ref[...] = jnp.zeros_like(rel_ref)
+
+    def din_copy(s):
+        return remote(din_own.at[s], din_other.at[s], x_sems.at[0, 0, s], x_sems.at[1, 0, s], tp=tp ^ 1)
+
+    def h_copy(s):
+        return remote(h_own.at[s], h_other.at[s], x_sems.at[0, 1, s], x_sems.at[1, 1, s], tp=tp ^ 1)
+
+    def out_copy(s):
+        return remote(out_own.at[s], out_other.at[s], x_sems.at[0, 2, s], x_sems.at[1, 2, s], tp=tp ^ 1)
+
+    def core_copy(s):
+        return remote(give_v.at[s], core_v.at[s], c_sems.at[0, s], c_sems.at[1, s], ctx=ctx ^ 1)
+
+    def y_copy(s):
+        return remote(y_v.at[s], far_v.at[s], y_sems.at[0, s], y_sems.at[1, s], ctx=ctx ^ 2)
+
+    def chosen(place):
+        picks = one_hot(place, cap)
+        return picks, jnp.concatenate([jnp.where(p, 1.0, 0.0).astype(BF16) for p in picks], axis=0)
+
+    din_load.wait()
+
+    def gather_back(s, carry):
+        picks, pick = chosen(place_ref[s])
+        din_own[s] = dot_tn(pick, din_v[s].reshape(rows, width)).astype(BF16)
+        eye = diagonal(cap)
+        for group in range(groups):
+            column = jnp.sum(jnp.where(eye, h_ref[s, group], 0.0), axis=1, keepdims=True)
+            h_own[s, group : group + 1, :] = jnp.sum(jnp.where(picks[group], column, 0.0), axis=0, keepdims=True)
+        h_copy(s).start()
+        din_copy(s).start()
+        return carry
+
+    lax.fori_loop(0, seqs, gather_back, 0)
+    for copy in loads:
+        copy.wait()
+
+    def middle_back(s):
+        h = jnp.concatenate([h_own[s], h_other[s]], axis=0)
+        dlogits = h - gate_v[s] * jnp.sum(h, axis=0, keepdims=True)
+        dmoe = din_own[s].astype(F32) + din_other[s].astype(F32)
+        dmoe = dmoe + lax.dot_general(
+            dlogits, router_ref[...].astype(F32), (((0,), (0,)), ((), ())),
+            precision=FULL_PRECISION, preferred_element_type=F32,
+        )
+        router_grad_ref[...] += lax.dot_general(
+            dlogits, moe_v[s].astype(F32), (((1,), (0,)), ((), ())),
+            precision=FULL_PRECISION, preferred_element_type=F32,
+        )
+        mid = mid_v[s]
+        factor = norm_factor(mid)
+        normed = mid * factor
+        gain_grad_ref[...] += jnp.sum(dmoe * normed, axis=0, keepdims=True)
+        scaled = dmoe * gain_ref[...].astype(F32)
+        dmid = factor * (scaled - normed * jnp.mean(scaled * normed, axis=-1, keepdims=True))
+        gmid = cot_v[s].astype(F32) + dmid
+        gmid_ref[s] = gmid
+        dattn = gmid.astype(BF16)
+        low_ref[s] = dattn
+        datt_v[...] = dot_nt(dattn, wout_v[...]).astype(BF16)
+
+    def core_sum(s):
+        core_copy(s).wait_recv()
+        for kind in range(2):
+            keep_v[s, kind, 0] += core_v[s, kind, 0].astype(F32)
+            y_v[s, kind] = (keep_v[s, kind, 1] + core_v[s, kind, 1].astype(F32)).astype(BF16)
+        y_copy(s).start()
+
+    def out_sum(s):
+        for b in range(1, groups):
+            part_copy(s, b).wait_recv()
+        pick = chosen(near_ref[s])[1]
+        out_own[s] = dot_tn(pick, part_v[:, s].reshape(rows, width)).astype(BF16)
+        out_copy(s).start()
+
+    def attention_back(s):
+        mask_v[...] = jnp.where(idk_ref[s] <= idq_ref[s], 0.0, MASKED)
+
+        def pair(p, carry):
+            lanes = pl.ds(pl.multiple_of(p * 2 * HD, 2 * HD), 2 * HD)
+            queries = q_v[s, :, lanes]
+            keys = k_v[s, :, lanes]
+            values = v_v[s, :, lanes]
+            grad_out = datt_v[:, lanes]
+            keys_t = keys.T
+            low_half = lax.broadcasted_iota(jnp.int32, queries.shape, 1) < HD
+            zero = jnp.zeros_like(queries)
+            dk = None
+            dv = None
+            dq_parts = []
+            for head in range(2):
+                own = (lambda a: jnp.where(low_half, a, zero)) if head == 0 else (
+                    lambda a: jnp.where(low_half, zero, a)
+                )
+                q_own = own(queries)
+                do_own = own(grad_out)
+                scores = dot_nt(keys, q_own) + bias_v[2 * p + head].astype(F32) + mask_v[...]
+                probs = jnp.exp(scores - lse_v[s, p, head : head + 1, :])
+                dprobs = dot_nt(values, do_own)
+                delta = jnp.sum(probs * dprobs, axis=0, keepdims=True)
+                dscores = probs * (dprobs - delta)
+                low = dscores.astype(BF16)
+                dv_head = dot(probs.astype(BF16), do_own)
+                dk_head = dot(low, q_own)
+                dv = dv_head if dv is None else dv + dv_head
+                dk = dk_head if dk is None else dk + dk_head
+                dq_parts.append(dot(keys_t[head * HD : (head + 1) * HD], low))
+                for block in range(4):
+                    tile = dscores[block * 256 : (block + 1) * 256]
+                    wide = jnp.concatenate([tile, jnp.zeros_like(tile)], axis=1)
+                    total = None
+                    for group in range(32):
+                        moved = pltpu.roll(wide[group * 8 : group * 8 + 8], 248 - 8 * group, 1)
+                        total = moved if total is None else total + moved
+                    row = lax.broadcasted_iota(jnp.int32, total.shape, 0)
+                    amount = 7 - row
+                    for bit in (1, 2, 4):
+                        total = jnp.where((amount & bit) != 0, pltpu.roll(total, bit, 1), total)
+                    rel_ref[p, head, block : block + 1, :] += jnp.sum(total, axis=0, keepdims=True)
+            proj_ref[0, s, :, lanes] = (jnp.concatenate(dq_parts, axis=0).T * (HD ** (-0.5))).astype(BF16)
+            for kind, value in enumerate((dk, dv)):
+                for index in range(2):
+                    at = 2 * index * stretch
+                    keep_v[s, kind, index, :, lanes] = value[at : at + stretch]
+                    give_v[s, kind, index, :, lanes] = value[at + stretch : at + 2 * stretch].astype(BF16)
+            return carry
+
+        lax.fori_loop(0, pairs, pair, 0)
+        core_copy(s).start()
+
+    def main(s, carry):
+        h_copy(s).wait_recv()
+        din_copy(s).wait_recv()
+        middle_back(s)
+        attention_back(s)
+
+        @pl.when(s > 0)
+        def _():
+            core_sum(s - 1)
+            out_sum(s - 1)
+
+        return carry
+
+    lax.fori_loop(0, seqs, main, 0)
+    core_sum(seqs - 1)
+    out_sum(seqs - 1)
+
+    def finish_keys(s, carry):
+        y_copy(s).wait_recv()
+        for kind in range(2):
+            proj_ref[1 + kind, s] = (keep_v[s, kind, 0] + far_v[s, kind].astype(F32)).astype(BF16)
+        return carry
+
+    def finish_out(s, carry):
+        out_copy(s).wait_recv()
+        out_ref[s] = (mid_v[s] + (out_own[s].astype(F32) + out_other[s].astype(F32))).astype(BF16)
+        return carry
+
+    lax.fori_loop(0, seqs, finish_keys, 0)
+    lax.fori_loop(0, seqs, finish_out, 0)
+    for s in range(seqs):
+        for b in range(1, groups):
+            part_copy(s, b).wait_send()
+        for copy in (h_copy(s), din_copy(s), out_copy(s), core_copy(s), y_copy(s)):
+            copy.wait_send()
+
+
+def back_stage(mids, moes, gates, lse, din, parts, q, k, v, bias, cot, wout, h, places, near, ids_query, ids_key, router, gain):
+    seqs = len(mids)
+    groups, _, cap, width = parts.shape
+    stretch = mids[0].shape[0]
+    local = wout.shape[0]
+    length = k.shape[1]
+    pairs = local // (2 * HD)
+    experts_n = router.shape[0]
+    any_spec = pl.BlockSpec(memory_space=pl.ANY)
+    vmem = pl.BlockSpec(memory_space=pltpu.VMEM)
+    dma = pltpu.SemaphoreType.DMA
+    return pl.pallas_call(
+        functools.partial(back_kernel, seqs, groups, cap),
+        name="back_stage",
+        in_specs=[any_spec] * (4 * seqs + 8) + [vmem] * 7,
+        out_specs=[vmem] * 7,
+        out_shape=[
+            jax.ShapeDtypeStruct((seqs, stretch, width), BF16),
+            jax.ShapeDtypeStruct((seqs, stretch, width), F32),
+            jax.ShapeDtypeStruct((seqs, stretch, width), BF16),
+            jax.ShapeDtypeStruct((3, seqs, stretch, local), BF16),
+            jax.ShapeDtypeStruct((1, width), F32),
+            jax.ShapeDtypeStruct((experts_n, width), F32),
+            jax.ShapeDtypeStruct((pairs, 2, 4, 2 * stretch), F32),
+        ],
+        scratch_shapes=[
+            pltpu.VMEM((seqs, stretch, width), F32),
+            pltpu.VMEM((seqs, stretch, width), BF16),
+            pltpu.VMEM((seqs, experts_n, stretch), F32),
+            pltpu.VMEM((seqs, pairs, 2, stretch), F32),
+            pltpu.VMEM((seqs, groups, cap, width), BF16),
+            pltpu.VMEM((groups, seqs, cap, width), BF16),
+            pltpu.VMEM((seqs, stretch, local), BF16),
+            pltpu.VMEM((seqs, length, local), BF16),
+            pltpu.VMEM((seqs, length, local), BF16),
+            pltpu.VMEM((2 * pairs, length, stretch), BF16),
+            pltpu.VMEM((seqs, stretch, width), BF16),
+            pltpu.VMEM((local, width), BF16),
+            pltpu.VMEM((seqs, stretch, width), BF16),
+            pltpu.VMEM((seqs, stretch, width), BF16),
+            pltpu.VMEM((seqs, groups, stretch), F32),
+            pltpu.VMEM((seqs, groups, stretch), F32),
+            pltpu.VMEM((seqs, stretch, width), BF16),
+            pltpu.VMEM((seqs, stretch, width), BF16),
+            pltpu.VMEM((stretch, local), BF16),
+            pltpu.VMEM((length, stretch), F32),
+            pltpu.VMEM((seqs, 2, 2, stretch, local), F32),
+            pltpu.VMEM((seqs, 2, 2, stretch, local), BF16),
+            pltpu.VMEM((seqs, 2, 2, stretch, local), BF16),
+            pltpu.VMEM((seqs, 2, stretch, local), BF16),
+            pltpu.VMEM((seqs, 2, stretch, local), BF16),
+            dma((8,)), dma((seqs, 4)), dma((2, seqs, groups)), dma((2, 3, seqs)), dma((2, seqs)), dma((2, seqs)),
+        ],
+        compiler_params=pltpu.CompilerParams(
+            vmem_limit_bytes=63 * 1024 * 1024, collective_id=3, has_side_effects=True
+        ),
+        cost_estimate=cost(6 * 10**10, 10**7),
+    )(*mids, *moes, *gates, *lse, din, parts, q, k, v, bias, cot, wout, h, places, near, ids_query, ids_key, router, gain)
 
 
 def last_kernel(
-    normed_ref, proj_ref, datt_ref, att_ref, small_ref,
-    out_ref, router_out, gm_out, ga_out, table_out,
-    grads, core_send, core_got, y_out, y_got, z_out, z_got, wide, s_own, s_core, s_y, s_x, s_z,
+    normed_ref, proj_ref, datt_ref, att_ref, small_ref, wqkv_ref, gmid_ref, x_ref, gain_ref,
+    out_ref, router_out, gm_out, ga_out, table_out, gx_ref,
+    dn_own, dn_other, ga_own, dn_sems, grads, core_send, core_got, y_out, y_got, z_out, z_got, wide, s_own, s_core, s_y, s_x, s_z,
     c_sems, y_sems, z_sems, w_sems, s_sems,
 ):
     dp = lax.axis_index("dp")
@@ -715,8 +996,33 @@
     width = normed_ref.shape[1]
     piece = width // count
 
-    x_copy = remote(small_ref, s_x, s_sems.at[0, 0], s_sems.at[1, 0], tp=tp ^ 1)
+    seqs, stretch = x_ref.shape[:2]
+
+    def unit_of(s):
+        value = x_ref[s].astype(F32)
+        factor = norm_factor(value)
+        return factor, value * factor
+
+    def rows_of(s):
+        return pl.ds(pl.multiple_of(s * stretch, stretch), stretch)
+
+    def input_grad(s, total):
+        part = dot_nt(proj_ref[0, rows_of(s)], wqkv_ref[0])
+        part = part + dot_nt(proj_ref[1, rows_of(s)], wqkv_ref[1])
+        part = part + dot_nt(proj_ref[2, rows_of(s)], wqkv_ref[2])
+        dn_own[s] = part.astype(BF16)
+        return total + jnp.sum(part * unit_of(s)[1], axis=0, keepdims=True)
+
+    own_gain = lax.fori_loop(0, seqs, input_grad, jnp.zeros((1, width), F32))
+    lines = lax.broadcasted_iota(jnp.int32, small_ref.shape, 0)
+    ga_own[...] = small_ref[...] + jnp.where(lines == 9, own_gain, 0.0)
+    x_copy = remote(ga_own, s_x, s_sems.at[0, 0], s_sems.at[1, 0], tp=tp ^ 1)
     x_copy.start()
+    dn_copies = [
+        remote(dn_own.at[s], dn_other.at[s], dn_sems.at[0, s], dn_sems.at[1, s], tp=tp ^ 1) for s in range(seqs)
+    ]
+    for copy in dn_copies:
+        copy.start()
     normed_t = normed_ref[...].T
     for j in range(3):
         grads[j] = dot(normed_t, proj_ref[j])
@@ -727,8 +1033,7 @@
     c_copy = remote(core_send, core_got, c_sems.at[0], c_sems.at[1], ctx=ctx ^ 1)
     c_copy.start()
     x_copy.wait_recv()
-    lines = lax.broadcasted_iota(jnp.int32, small_ref.shape, 0)
-    s_own[...] = small_ref[...] + jnp.where(lines == 9, s_x[...], 0.0)
+    s_own[...] = ga_own[...] + jnp.where(lines == 9, s_x[...], 0.0)
     sc_copy = remote(s_own, s_core, s_sems.at[0, 1], s_sems.at[1, 1], ctx=ctx ^ 1)
     sc_copy.start()
     c_copy.wait_recv()
@@ -777,6 +1082,17 @@
         copy = remote(wide.at[mine], wide.at[mine], w_sems.at[0, b - 1], w_sems.at[1, b - 1], ctx=ctx ^ b)
         copy.start()
         w_copies.append(copy)
+    for copy in dn_copies:
+        copy.wait_recv()
+
+    def input_norm(s, carry):
+        factor, unit = unit_of(s)
+        scaled = (dn_own[s].astype(F32) + dn_other[s].astype(F32)) * gain_ref[...]
+        dres = factor * (scaled - unit * jnp.mean(scaled * unit, axis=-1, keepdims=True))
+        gx_ref[s] = gmid_ref[s] + dres
+        return carry
+
+    lax.fori_loop(0, seqs, input_norm, 0)
     for copy in sz_copies:
         copy.wait_recv()
     small = s_z[0]
@@ -805,11 +1121,11 @@
     for copy in w_copies:
         copy.wait_recv()
     out_ref[...] = wide[...].astype(F32)
-    for copy in [x_copy, c_copy, sc_copy, sy_copy] + y_copies + [c for _, c in z_copies] + sz_copies + w_copies:
+    for copy in [x_copy, c_copy, sc_copy, sy_copy] + dn_copies + y_copies + [c for _, c in z_copies] + sz_copies + w_copies:
         copy.wait_send()
 
 
-def last_stage(normed, proj, datt, att, small, dp, table_rows, heads, experts_n):
+def last_stage(normed, proj, datt, att, small, wqkv, gmid, x, gain, dp, table_rows, heads, experts_n):
     rows, width = normed.shape
     local = att.shape[1]
     piece = width // dp
@@ -818,16 +1134,21 @@
     return pl.pallas_call(
         last_kernel,
         name="last_stage",
-        in_specs=[vmem] * 5,
-        out_specs=[vmem] * 5,
+        in_specs=[vmem] * 9,
+        out_specs=[vmem] * 6,
         out_shape=[
             jax.ShapeDtypeStruct((4, piece, local), F32),
             jax.ShapeDtypeStruct((piece, experts_n), F32),
             jax.ShapeDtypeStruct((1, piece), F32),
             jax.ShapeDtypeStruct((1, piece), F32),
             jax.ShapeDtypeStruct((table_rows, heads), F32),
+            jax.ShapeDtypeStruct(x.shape, F32),
         ],
         scratch_shapes=[
+            pltpu.VMEM(x.shape, BF16),
+            pltpu.VMEM(x.shape, BF16),
+            pltpu.VMEM(small.shape, F32),
+            dma((2, x.shape[0])),
             pltpu.VMEM((4, width, local), F32),
             pltpu.VMEM((2, width, local), BF16),
             pltpu.VMEM((2, width, local), BF16),
@@ -845,7 +1166,7 @@
         ],
         compiler_params=pltpu.CompilerParams(vmem_limit_bytes=VMEM_BYTES, collective_id=1, has_side_effects=True),
         cost_estimate=cost(8 * rows * width * local, 8 * rows * width),
-    )(normed, proj, datt, att, small)
+    )(normed, proj, datt, att, small, wqkv, gmid, x, gain)
 
 
 def moe_kernel(
@@ -854,12 +1175,12 @@
     sends, refs = refs[:seqs], refs[seqs:]
     slot_gates, refs = refs[:seqs], refs[seqs:]
     cots, refs = refs[:groups], refs[groups:]
-    w_own, w_far, part_out, din_back, h_back, keep_out, give_out = refs[:7]
+    w_own, w_far, part_out, din_back, h_back, keep_out, give_out = (refs[:2], refs[2:4]) + refs[4:9]
     (
         w_all, x_all, gate_all, g_all, xt_all, dyt_all, dy_ref, hid_all, dpre_all, part_acc, din_acc,
         part_all, din_all, h_all, tile_ref,
-        x_sems, gate_sems, din_sems, h_sems, w_sems, own_sems, part_sems, out_sems,
-    ) = refs[7:]
+        x_sems, gate_sems, din_sems, h_sems, w_sems, own_sems, part_sems, out_sems, core_sems,
+    ) = refs[9:]
     dp = lax.axis_index("dp")
     ctx = lax.axis_index("ctx")
     greet([{"dp": dp ^ b} for b in range(1, groups)] + [{"ctx": ctx ^ 1}])
@@ -884,29 +1205,27 @@
                     gate_sems.at[0, s, b - 1], gate_sems.at[1, s, b - 1], dp=dp ^ b,
                 )
             )
-    w_copies = [
-        remote(w_own, w_all.at[:, :, ctx], w_sems.at[0, 0], w_sems.at[1, 0], ctx=ctx ^ 1),
-        remote(w_far, w_all.at[:, :, ctx ^ 2], w_sems.at[0, 1], w_sems.at[1, 1], ctx=ctx ^ 1),
-    ]
+    w_copies = []
+    local = []
+    arrivals = []
+    for half in range(2):
+        for index, (ref, place) in enumerate(((w_own[half], ctx), (w_far[half], ctx ^ 2))):
+            sems = (w_sems.at[0, half, index], w_sems.at[1, half, index])
+            w_copies.append(remote(ref, w_all.at[:, half, place], *sems, ctx=ctx ^ 1))
+            there = w_all.at[:, half, place ^ 1]
+            arrivals.append(remote(there, there, *sems, ctx=ctx ^ 1))
+            local.append(pltpu.make_async_copy(ref, w_all.at[:, half, place], w_sems.at[2, half, index]))
     for copy in w_copies + sent:
         copy.start()
-    local = [
-        pltpu.make_async_copy(w_own, w_all.at[:, :, ctx], own_sems.at[0]),
-        pltpu.make_async_copy(w_far, w_all.at[:, :, ctx ^ 2], own_sems.at[1]),
-    ]
     for s in range(seqs):
-        local.append(pltpu.make_async_copy(sends[s].at[dp], x_all.at[s, dp], own_sems.at[2 + 2 * s]))
-        local.append(pltpu.make_async_copy(slot_gates[s].at[dp], gate_all.at[s, dp], own_sems.at[3 + 2 * s]))
+        local.append(pltpu.make_async_copy(sends[s].at[dp], x_all.at[s, dp], own_sems.at[2 * s]))
+        local.append(pltpu.make_async_copy(slot_gates[s].at[dp], gate_all.at[s, dp], own_sems.at[1 + 2 * s]))
     for b in range(groups):
-        local.append(pltpu.make_async_copy(cots[b], g_all.at[dp ^ b], own_sems.at[2 + 2 * seqs + b]))
+        local.append(pltpu.make_async_copy(cots[b], g_all.at[dp ^ b], own_sems.at[2 * seqs + b]))
     for copy in local:
         copy.start()
     for copy in local:
         copy.wait()
-    arrivals = [
-        remote(w_all.at[:, :, ctx ^ 1], w_all.at[:, :, ctx ^ 1], w_sems.at[0, 0], w_sems.at[1, 0], ctx=ctx ^ 1),
-        remote(w_all.at[:, :, ctx ^ 3], w_all.at[:, :, ctx ^ 3], w_sems.at[0, 1], w_sems.at[1, 1], ctx=ctx ^ 1),
-    ]
     for copy in arrivals:
         copy.wait_recv()
     eye = diagonal(cap)
@@ -986,24 +1305,25 @@
 
     lax.fori_loop(0, seqs, chunk, 0)
 
-    def out_copies(f, slot):
+    def tile_of(ref, f):
         lanes = pl.ds(pl.multiple_of((f % per_half) * tile, tile), tile)
-        return [
-            pltpu.make_async_copy(
-                tile_ref.at[slot, 0], keep_out.at[f // per_half, :, :, :, lanes], out_sems.at[slot, 0]
-            ),
-            pltpu.make_async_copy(
-                tile_ref.at[slot, 1], give_out.at[f // per_half, :, :, :, lanes], out_sems.at[slot, 1]
-            ),
-        ]
+        return ref.at[f // per_half, :, :, :, lanes]
+
+    def keep_copy(f, slot):
+        return pltpu.make_async_copy(tile_ref.at[slot, 0], tile_of(keep_out, f), out_sems.at[slot, 0])
+
+    def give_copy(f, slot):
+        return remote(
+            tile_ref.at[slot, 1], tile_of(give_out, f), out_sems.at[slot, 1], core_sems.at[f], ctx=ctx ^ 1
+        )
 
     def weight_grads(f, carry):
         slot = f % 2
 
         @pl.when(f >= 2)
         def _():
-            for copy in out_copies(f - 2, slot):
-                copy.wait()
+            keep_copy(f - 2, slot).wait()
+            give_copy(f - 2, slot).wait_send()
 
         for io, (left, right) in enumerate(((xt_all, dpre_all), (dyt_all, hid_all))):
             total = dot(left[0], right[f, 0])
@@ -1012,14 +1332,16 @@
             for index in range(slices):
                 place = index ^ ctx
                 tile_ref[slot, place % 2, place // 2, io] = total[index * piece : (index + 1) * piece].astype(BF16)
-        for copy in out_copies(f, slot):
-            copy.start()
+        keep_copy(f, slot).start()
+        give_copy(f, slot).start()
         return carry
 
     lax.fori_loop(0, tiles, weight_grads, 0)
     for f in (tiles - 2, tiles - 1):
-        for copy in out_copies(f, f % 2):
-            copy.wait()
+        keep_copy(f, f % 2).wait()
+        give_copy(f, f % 2).wait_send()
+    for f in range(tiles):
+        give_copy(f, f % 2).wait_recv()
     for s in range(seqs):
         for b in order:
             there = din_back.at[s, dp ^ b]
@@ -1036,10 +1358,11 @@
         copy.wait_send()
 
 
-def moe_stage(sends, slot_gates, cots, w_own, w_far, tile=512):
+def moe_stage(sends, slot_gates, cots, keep, got, far_keep, far_got, tile=512):
     seqs = len(sends)
     groups, cap, width = sends[0].shape
-    _, halves, piece, half_len = w_own.shape
+    _, piece, half_len = keep.shape
+    halves = 2
     slices = width // piece
     tiles = halves * half_len // tile
     rows = groups * cap
@@ -1049,7 +1372,7 @@
     return pl.pallas_call(
         functools.partial(moe_kernel, seqs, groups, cap, tile),
         name="moe_stage",
-        in_specs=[any_spec] * (2 * seqs + groups + 2),
+        in_specs=[any_spec] * (2 * seqs + groups + 4),
         out_specs=[any_spec, any_spec, vmem, any_spec, any_spec],
         out_shape=[
             jax.ShapeDtypeStruct((groups, seqs, cap, width), BF16),
@@ -1075,14 +1398,14 @@
             pltpu.VMEM((seqs, groups, 1, cap), F32),
             pltpu.VMEM((2, 2, slices // 2, 2, piece, tile), BF16),
             dma((2, seqs, groups - 1)), dma((2, seqs, groups - 1)), dma((2, seqs, groups - 1)),
-            dma((2, seqs, groups - 1)), dma((2, 2)), dma((2 + 2 * seqs + groups,)), dma((seqs, groups + 2)),
-            dma((2, 2)),
+            dma((2, seqs, groups - 1)), dma((3, 2, 2)), dma((2 * seqs + groups,)), dma((seqs, groups + 2)),
+            dma((2, 2)), dma((tiles,)),
         ],
         compiler_params=pltpu.CompilerParams(
             vmem_limit_bytes=63 * 1024 * 1024, collective_id=2, has_side_effects=True
         ),
         cost_estimate=cost(20 * seqs * rows * width * halves * half_len, 40 * width * halves * half_len),
-    )(*sends, *slot_gates, *cots, w_own, w_far)
+    )(*sends, *slot_gates, *cots, keep, got, far_keep, far_got)
 
 
 def flip(value, axis, bit):
@@ -1136,10 +1459,30 @@
     heads = local // HD
 
     fits = dp == 4
+    e_order = jnp.arange(expert_count, dtype=jnp.int32).reshape(dp, 2).T
+    e_order = jnp.where(tp == 0, e_order, e_order[::-1]).reshape(1, expert_count, 1)
+    hits = ((routes[:, None, :, 0] == e_order) | (routes[:, None, :, 1] == e_order)).astype(F32)
+    before = (
+        lax.broadcasted_iota(jnp.int32, (stretch, stretch), 0) < lax.broadcasted_iota(jnp.int32, (stretch, stretch), 1)
+    ).astype(BF16)
+    ranks = jnp.einsum("set,tu->seu", hits.astype(BF16), before, preferred_element_type=F32)
+    places = jnp.where(hits > 0.5, ranks, -1.0)[:, :dp]
+
+    pair = jnp.stack([w_expert_in[0], w_expert_out[0].transpose(0, 2, 1)], axis=1)
+
     if fits:
-        queries, keys, values, own_normed, wqkv, wout_parts, table, gain_attn, gain_moe, router = first_stage(
-            tokens_in, w_qkv[0], w_attn_out[0], bias_table[0], attn_gain, moe_gain, w_router[0]
+        me = lax.axis_index("dp")
+        near_places = jnp.stack([lax.dynamic_index_in_dim(places, me ^ b, 1, keepdims=False) for b in range(dp)], axis=1)
+        cot_slots = dispatch(near_places, cotangent, cap)
+        cot_slots, tokens_first, pair = lax.optimization_barrier((cot_slots, tokens_in, pair))
+        cot_slots = [cot_slots[0]] + [flip(cot_slots[b], "dp", b) for b in range(1, dp)]
+        (
+            queries, keys, values, own_normed, wqkv, wout_parts, table, gain_attn, gain_moe, router, got, far_keep,
+        ) = first_stage(
+            tokens_first, w_qkv[0], w_attn_out[0], bias_table[0], attn_gain, moe_gain, w_router[0], pair
         )
+        keep = lax.dynamic_index_in_dim(pair, tp, 0, keepdims=False)
+        far_got = flip(got, "ctx", 2)
         wout_own = wout_parts.transpose(1, 0, 2).reshape(local, width)
         table = table.reshape(NB, heads)
         keys = keys.reshape(seqs, 4 * stretch, local)
@@ -1149,36 +1492,11 @@
         queries, keys, values, own_normed, wqkv, wout_own, table, gain_attn, gain_moe, router = gathered(
             tokens_in, w_qkv[0], w_attn_out[0], bias_table[0], attn_gain, moe_gain, w_router[0]
         )
+        keep = lax.dynamic_index_in_dim(pair, tp, 0, keepdims=False)
+        got = flip(lax.dynamic_index_in_dim(pair, 1 - tp, 0, keepdims=False), "tp", 1)
+        weights = lax.all_gather(jnp.stack([keep, got], axis=1), "ctx", axis=0, tiled=False)
+        cot_slots = all_to_all_dp(dispatch(places, cotangent, cap))
     wout_other = flip(wout_own, "tp", 1)
-
-    w_in = w_expert_in[0]
-    w_out_t = w_expert_out[0].transpose(0, 2, 1)
-    both = jnp.stack([w_in, w_out_t], axis=1)
-    keep = lax.dynamic_index_in_dim(both, tp, 0, keepdims=False)
-    give = lax.dynamic_index_in_dim(both, 1 - tp, 0, keepdims=False)
-    got = flip(give, "tp", 1)
-    both = jnp.stack([keep, got], axis=1)
-    if fits:
-        far = flip(both, "ctx", 2)
-    else:
-        weights = lax.all_gather(both, "ctx", axis=0, tiled=False)
-
-    e_order = jnp.arange(expert_count, dtype=jnp.int32).reshape(dp, 2).T
-    e_order = jnp.where(tp == 0, e_order, e_order[::-1]).reshape(1, expert_count, 1)
-    hits = ((routes[:, None, :, 0] == e_order) | (routes[:, None, :, 1] == e_order)).astype(F32)
-    before = (
-        lax.broadcasted_iota(jnp.int32, (stretch, stretch), 0) < lax.broadcasted_iota(jnp.int32, (stretch, stretch), 1)
-    ).astype(BF16)
-    ranks = jnp.einsum("set,tu->seu", hits.astype(BF16), before, preferred_element_type=F32)
-    places = jnp.where(hits > 0.5, ranks, -1.0)[:, :dp]
-
-    if fits:
-        me = lax.axis_index("dp")
-        near_places = jnp.stack([lax.dynamic_index_in_dim(places, me ^ b, 1, keepdims=False) for b in range(dp)], axis=1)
-        cot_slots = dispatch(near_places, cotangent, cap)
-        cot_slots = [cot_slots[0]] + [flip(cot_slots[b], "dp", b) for b in range(1, dp)]
-    else:
-        cot_slots = all_to_all_dp(dispatch(places, cotangent, cap))
 
     one_hot_bucket = (rel_buckets[:, None] == jnp.arange(NB, dtype=jnp.int32)[None, :]).astype(F32)
     one_hot_bucket = jnp.pad(one_hot_bucket, ((0, 1), (0, 0)))
@@ -1207,13 +1525,9 @@
         sends.append(send)
         slot_gates.append(slot_gate)
     if fits:
-        parts, returned_din, returned_h, kept, given = moe_stage(sends, slot_gates, cot_slots, both, far)
-        moved = [parts[0]] + [flip(parts[b], "dp", b) for b in range(1, dp)]
-        partials = [jnp.stack([piece[s] for piece in moved]) for s in range(seqs)]
-        out_places = near_places
+        parts, returned_din, returned_h, kept, given = moe_stage(sends, slot_gates, cot_slots, keep, got, far_keep, far_got)
     else:
         partials, returned_din, returned_h = [], [], []
-        out_places = places
         acc = None
         for s in range(seqs):
             received = all_to_all_dp(sends[s])
@@ -1222,74 +1536,82 @@
             returned_din.append(all_to_all_dp(din))
             returned_h.append(all_to_all_dp(h))
             partials.append(all_to_all_dp(part))
-        kept, given = acc[:, 0::2], acc[:, 1::2]
-
-    beside_sum = kept.astype(F32) + flip(given, "ctx", 1).astype(F32)
-    mine = beside_sum[:, 0] + flip(beside_sum[:, 1].astype(BF16), "ctx", 2).astype(F32)
-    other = flip(mine[1].astype(BF16), "tp", 1).astype(F32)
-    ordered = jnp.where(tp == 0, jnp.stack([mine[0], other]), jnp.stack([other, mine[0]]))
-    grad_expert_in = ordered[:, 0]
-    grad_expert_out = ordered[:, 1].transpose(0, 2, 1)
-
-    tokens_out, gmids = [], []
-    projections = []
-    rel_grad = 0.0
-    gain_moe_grad = 0.0
-    router_grad = 0.0
-    datts = []
-    for s in range(seqs):
-        out_own = combine_out(out_places[s], partials[s], cap)
-        out_other = flip(out_own, "tp", 1)
-        tokens_out.append((mids[s] + (out_own.astype(F32) + out_other.astype(F32))).astype(BF16))
-        din_own, h_own = combine(places[s], returned_din[s], returned_h[s], cap)
-        din_other = flip(din_own, "tp", 1)
-        h_all = jnp.concatenate([h_own, flip(h_own, "tp", 1)], axis=0)
-        gmid, datt, d_gain, d_router, dattn = middle_back(
-            din_own, din_other, h_all, gates[s], router, moes[s], mids[s], gain_moe, cotangent[s], wout_own
+        kept, given = acc[:, 0::2], flip(acc[:, 1::2], "ctx", 1)
+
+    beside_sum = kept.astype(F32) + given.astype(F32)
+    far_sum = flip(beside_sum[:, 1].astype(BF16), "ctx", 2)
+
+    hits_of = (heads, 4, 2 * stretch)
+    if fits:
+        tokens_out, gmid, dattn, grad_proj, gain_moe_grad, router_grad, rel_grad = back_stage(
+            mids, moes, gates, lse, returned_din, parts, queries, keys, values, bias, cotangent, wout_own,
+            returned_h, places, near_places, ids_query, ids_key, router, gain_moe,
         )
-        datts.append(dattn)
-        gmids.append(gmid)
-        gain_moe_grad += d_gain
-        router_grad += d_router
-        dq, dk, dv, rel = attend_back(
-            queries[s], keys[s], values[s], datt, bias, lse[s], ids_query[s], ids_key[s]
-        )
-        rel_grad += rel
-        dkv = jnp.stack([dk, dv]).reshape(2, 4, stretch, local)
-        near = dkv[:, 0::2].astype(F32) + flip(dkv[:, 1::2], "ctx", 1).astype(F32)
-        full = near[:, 0] + flip(near[:, 1].astype(BF16), "ctx", 2).astype(F32)
-        projections.append(jnp.concatenate([dq[None], full.astype(BF16)], axis=0))
-    grad_proj = jnp.concatenate(projections, axis=1)
-    dattn = jnp.concatenate(datts, axis=0)
-    attended = jnp.concatenate(attended, axis=0)
-    dnormed_part = jnp.einsum("jre,jde->rd", grad_proj, wqkv, preferred_element_type=F32)
-    dnormed_own = dnormed_part.astype(BF16)
-    dnormed = dnormed_own.astype(F32) + flip(dnormed_own, "tp", 1).astype(F32)
-    own_x = tokens_in.reshape(seqs * stretch, width).astype(F32)
-    factor = norm_factor(own_x)
-    unit = own_x * factor
-    scaled = dnormed * gain_attn
-    dres = factor * (scaled - unit * jnp.mean(scaled * unit, axis=-1, keepdims=True))
-    grad_tokens = jnp.concatenate(gmids, axis=0) + dres
-
-    rel_flat = rel_grad.reshape(heads, 4, 2 * stretch)
-    grad_table = jnp.einsum("bmn,hbm->nh", hot_windows, rel_flat, precision=FULL_PRECISION)
-    if fits:
-        gain_rows = jnp.concatenate([gain_moe_grad, jnp.sum(dnormed_part * unit, axis=0)[None]], axis=0)
+        far_sum, grad_proj = lax.optimization_barrier((far_sum, grad_proj))
+        mine = beside_sum[:, 0] + far_sum.astype(F32)
+        other = flip(mine[1].astype(BF16), "tp", 1)
+        grad_proj = grad_proj.reshape(3, seqs * stretch, local)
+        dattn = dattn.reshape(seqs * stretch, width)
+        grad_table = jnp.einsum("bmn,hbm->nh", hot_windows, rel_grad.reshape(hits_of), precision=FULL_PRECISION)
         small = jnp.concatenate(
             [
                 router_grad,
-                jnp.pad(gain_rows, ((0, 6), (0, 0))),
+                jnp.pad(gain_moe_grad, ((0, 7), (0, 0))),
                 jnp.pad(grad_table.T, ((0, 8 - heads), (0, width - NB))),
             ],
             axis=0,
         )
-        wide, g_router, g_moe, g_attn, g_table = last_stage(
-            own_normed, grad_proj, dattn, attended, small, dp, NB // dp, heads, expert_count
+        wide, g_router, g_moe, g_attn, g_table, grad_tokens = last_stage(
+            own_normed, grad_proj, dattn, jnp.concatenate(attended, axis=0), small, wqkv, gmid, tokens_in, gain_attn,
+            dp, NB // dp, heads, expert_count,
         )
+        other, wide = lax.optimization_barrier((other, wide))
         g_qkv = wide[:3]
         g_wout = wide[3].T
     else:
+        mine = beside_sum[:, 0] + far_sum.astype(F32)
+        other = flip(mine[1].astype(BF16), "tp", 1)
+        tokens_out, gmids = [], []
+        projections = []
+        rel_grad = 0.0
+        gain_moe_grad = 0.0
+        router_grad = 0.0
+        datts = []
+        for s in range(seqs):
+            out_own = combine_out(places[s], partials[s], cap)
+            out_other = flip(out_own, "tp", 1)
+            tokens_out.append((mids[s] + (out_own.astype(F32) + out_other.astype(F32))).astype(BF16))
+            din_own, h_own = combine(places[s], returned_din[s], returned_h[s], cap)
+            din_other = flip(din_own, "tp", 1)
+            h_all = jnp.concatenate([h_own, flip(h_own, "tp", 1)], axis=0)
+            gmid, datt, d_gain, d_router, dattn = middle_back(
+                din_own, din_other, h_all, gates[s], router, moes[s], mids[s], gain_moe, cotangent[s], wout_own
+            )
+            datts.append(dattn)
+            gmids.append(gmid)
+            gain_moe_grad += d_gain
+            router_grad += d_router
+            dq, dk, dv, rel = attend_back(
+                queries[s], keys[s], values[s], datt, bias, lse[s], ids_query[s], ids_key[s]
+            )
+            rel_grad += rel
+            dkv = jnp.stack([dk, dv]).reshape(2, 4, stretch, local)
+            near = dkv[:, 0::2].astype(F32) + flip(dkv[:, 1::2], "ctx", 1).astype(F32)
+            full = near[:, 0] + flip(near[:, 1].astype(BF16), "ctx", 2).astype(F32)
+            projections.append(jnp.concatenate([dq[None], full.astype(BF16)], axis=0))
+        grad_proj = jnp.concatenate(projections, axis=1)
+        dattn = jnp.concatenate(datts, axis=0)
+        attended = jnp.concatenate(attended, axis=0)
+        dnormed_part = jnp.einsum("jre,jde->rd", grad_proj, wqkv, preferred_element_type=F32)
+        dnormed_own = dnormed_part.astype(BF16)
+        dnormed = dnormed_own.astype(F32) + flip(dnormed_own, "tp", 1).astype(F32)
+        own_x = tokens_in.reshape(seqs * stretch, width).astype(F32)
+        factor = norm_factor(own_x)
+        unit = own_x * factor
+        scaled = dnormed * gain_attn
+        dres = factor * (scaled - unit * jnp.mean(scaled * unit, axis=-1, keepdims=True))
+        grad_tokens = jnp.concatenate(gmids, axis=0) + dres
+        grad_table = jnp.einsum("bmn,hbm->nh", hot_windows, rel_grad.reshape(hits_of), precision=FULL_PRECISION)
         router_grad = router_grad.reshape(2, dp, width)
         router_grad = jnp.where(tp == 0, router_grad, router_grad[::-1])
         router_grad = router_grad.transpose(1, 0, 2).reshape(expert_count, width).T
@@ -1303,8 +1625,13 @@
         g_table = reduced(grad_table, 0)
         g_moe = reduced(gain_moe_grad, 1)
         g_router = reduced(router_grad, 0)
+        tokens_out = jnp.stack(tokens_out)
+    other = other.astype(F32)
+    ordered = jnp.where(tp == 0, jnp.stack([mine[0], other]), jnp.stack([other, mine[0]]))
+    grad_expert_in = ordered[:, 0]
+    grad_expert_out = ordered[:, 1].transpose(0, 2, 1)
     return (
-        jnp.stack(tokens_out),
+        tokens_out,
         grad_tokens.reshape(seqs, stretch, width),
         g_attn,
         g_qkv[None],

time: 572 us -> 450 us (0.79); the launches traced: 562 us -> 449 us
  waiting for transfers between devices: 103 us -> 16.8 us
  Pallas kernels: 319 us -> 356 us
  other arithmetic: 46.3 us -> 15.9 us
  starting transfers between devices: 32.2 us -> 11.2 us
  local copies, waits for them, and re-layouts: 53.9 us -> 47.7 us
    ppermute x31 -> x10, waiting for transfers between devices: 103 us -> 16.8 us  [flip(): return lax.ppermute(value, axis, [(i, i ^ bit) for i in range(count)])]
    pallas_call x13 -> x2, Pallas kernels: 106 us -> 135 us  [the longest x1 80.4 us: back_stage(): pl.pallas_call(functools.partial(back_kernel, seqs, groups, cap), name='b...]
    ppermute x31 -> x10, starting transfers between devices: 32.2 us -> 11.2 us  [flip(): return lax.ppermute(value, axis, [(i, i ^ bit) for i in range(count)])]
    another operation x12 -> x1, other arithmetic: 18.8 us -> 1.62 us  [on_device(): jnp.stack([w_expert_in[0], w_expert_out[0].transpose(0, 2, 1)], axis=1)]
    pallas_call x1, Pallas kernels: 53.7 us -> 62.2 us  [first_stage(): pl.pallas_call(functools.partial(first_kernel, seqs), name='first_stage',...]
    slice x8 -> x1, local copies, waits for them, and re-layouts: 9.12 us -> 3.23 us  [on_device(): keys[s]]
    add x9 -> x2, other arithmetic: 13.6 us -> 9.03 us  [the longest x1 5.23 us: on_device(): beside_sum = kept.astype(F32) + given.astype(F32)]
    unnamed x176 -> x112, local copies, waits for them, and re-layouts: 17.5 us -> 20.8 us
  transfers between devices with their start and end apart: 31 -> 10, of which waited for: 9 -> 1; matrix products, arithmetic and copies ran while one was open for 13% -> 4% of each run, Pallas kernels for 24% -> 36%
where the time goes in v3:
time: 450 us; the launch traced here: 449 us
  Pallas kernels  356 us (79%)
  local copies, waits for them, and re-layouts  47.7 us (11%)
  waiting for transfers between devices  16.8 us (4%)
  other arithmetic  15.9 us (4%)
  starting transfers between devices  11.2 us (2%)
    pallas_call x1, Pallas kernels, moe_stage(): pl.pallas_call(functools.partial(moe_kernel, seqs, groups, cap, tile), na...  116 us
    pallas_call x1, Pallas kernels, back_stage(): pl.pallas_call(functools.partial(back_kernel, seqs, groups, cap), name='b...  80.4 us
    pallas_call x1, Pallas kernels, first_stage(): pl.pallas_call(functools.partial(first_kernel, seqs), name='first_stage',...  62.2 us
    pallas_call x1, Pallas kernels, last_stage(): pl.pallas_call(last_kernel, name='last_stage', in_specs=[vmem] * 9, out_s...  54.7 us
    pallas_call x3, Pallas kernels, attend(): pl.pallas_call(attend_kernel, name='attend', grid=(pairs,), in_specs=[pl....  22.6 us
    unnamed x112, local copies, waits for them, and re-layouts  20.8 us
    ppermute x10, waiting for transfers between devices, flip(): return lax.ppermute(value, axis, [(i, i ^ bit) for i in range(count)])  16.8 us
    pallas_call x3, Pallas kernels, middle_stage(): pl.pallas_call(functools.partial(middle_kernel, groups, cap), name='middl...  11.4 us
  transfers between devices with their start and end apart: 10, of which 1 were waited for; matrix products, arithmetic and copies ran while one was open for 4% of the time, Pallas kernels for 36%

profile of v3, /device:TPU:0, one launch (start us, length us, event | category | flops | bytes accessed | tf_op | source)
XLA Modules:
  0.0 449.5 jit_solution(9752771171187012682)
XLA Ops:
  0.7 0.9 fusion.25
  2.5 0.6 copy-done.29
  3.1 0.6 pad_maximum_fusion.6.place_ref.refs_22_
  3.7 3.9 dispatch_rows.1
  7.7 1.6 pad_maximum_fusion.pair_ref
  9.3 0.8 copy.36
  10.2 0.7 copy.37
  10.9 62.2 %first_stage.1 = (bf16[3,256,384]{2,1,0:T(8,128)(2,1)}, bf16[3,4,256,384]{3,2,1,0:T(8,128)(2,1)}, bf16[3,4,256,384]{3,2,1,0:T(8,128)(2,1)}, bf16[3,256,768]{2,1,...) custom-call(bf16[3,256,768]{2,1,0:T(8,128)(2,1)} %x_ref.1, ...), custom_call_target="tpu_custom_call" | custom-call | flops 40000000000 | bytes 10000000 | tf_op jit(solution)/shard_map/first_stage/pallas_call | solution.py:680
  73.1 1.9 slice_bitcast_fusion.12
  75.0 3.2 fusion.24
  78.2 1.5 fusion.23
  79.8 0.6 copy-done.20
  80.7 0.6 copy.39.win_ref
  81.3 4.4 expand_bias.1.bias_ref.refs_17_
  85.9 0.6 copy-done.19
  86.5 1.0 copy.59
  87.5 0.6 fusion.19
  88.1 7.5 %attend.3 = (bf16[256,384]{1,0:T(8,128)(2,1)}, f32[3,2,256]{2,1,0:T(2,128)}) custom-call(bf16[256,384]{1,0:T(8,128)(2,1)} %get-tuple-element.163.q_ref, bf16[1024,384]{1,0:T(8,128)(2,1)} %bitcast.135, bf16[1024,384]{1,0:T(8,128)(2,1)} %bitcast.136, bf16[6,1024,256]{2,1,0:T(8,128)(2,1)} %expand_bias.1.bias_ref.refs_17_, s32[1,256]{1,0:T(1,128)} %get-tuple-element.179.idq_ref, ...), custom_call_target="tpu_custom_call" | custom-call | flops 16106127 | bytes 62914 | tf_op jit(solution)/shard_map/attend/pallas_call | solution.py:94
  95.6 1.5 collective-permute-start
  97.4 1.1 copy.43.refs_19_
  98.5 0.5 collective-permute-start.1
  99.0 1.0 copy.61
  100.1 7.5 %attend.4 = (bf16[256,384]{1,0:T(8,128)(2,1)}, f32[3,2,256]{2,1,0:T(2,128)}) custom-call(bf16[256,384]{1,0:T(8,128)(2,1)} %get-tuple-element.162.q_ref, bf16[1024,384]{1,0:T(8,128)(2,1)} %bitcast.133, bf16[1024,384]{1,0:T(8,128)(2,1)} %bitcast.134, bf16[6,1024,256]{2,1,0:T(8,128)(2,1)} %expand_bias.1.bias_ref.refs_17_, s32[1,256]{1,0:T(1,128)} %get-tuple-element.178.idq_ref, ...), custom_call_target="tpu_custom_call" | custom-call | flops 16106127 | bytes 62914 | tf_op jit(solution)/shard_map/attend/pallas_call | solution.py:94
  107.6 1.6 collective-permute-start.2
  109.2 1.3 slice_bitcast_fusion.4
  110.5 0.6 collective-permute-start.4
  111.5 1.0 slice_bitcast_fusion.8
  112.6 1.0 copy.63
  113.6 7.5 %attend.5 = (bf16[256,384]{1,0:T(8,128)(2,1)}, f32[3,2,256]{2,1,0:T(2,128)}) custom-call(bf16[256,384]{1,0:T(8,128)(2,1)} %get-tuple-element.161.q_ref, bf16[1024,384]{1,0:T(8,128)(2,1)} %bitcast.131, bf16[1024,384]{1,0:T(8,128)(2,1)} %bitcast.132, bf16[6,1024,256]{2,1,0:T(8,128)(2,1)} %expand_bias.1.bias_ref.refs_17_, s32[1,256]{1,0:T(1,128)} %get-tuple-element.177.idq_ref, ...), custom_call_target="tpu_custom_call" | custom-call | flops 16106127 | bytes 62914 | tf_op jit(solution)/shard_map/attend/pallas_call | solution.py:94
  121.2 1.1 dynamic-slice_bitcast_fusion.refs_10_
  122.4 1.6 collective-permute-start.5
  124.0 2.3 collective-permute-start.6
  126.3 0.6 slice_bitcast_fusion.16
  126.9 0.5 collective-permute-start.3
  127.4 0.6 slice_bitcast_fusion.19
  128.0 3.3 reshape.104.refs_24_
  131.6 2.2 pad_maximum_fusion.1.wout_ref
  133.8 3.8 middle_stage.3
  137.6 3.9 middle_stage.4
  141.5 0.7 copy-done.17
  142.1 3.8 middle_stage.5
  145.9 16.7 %collective-permute-done.5.refs_8_ = bf16[3,128,768]{2,1,0:T(8,128)(2,1)S(1)} collective-permute-done((bf16[3,128,768]{2,1,0:T(8,128)(2,1)}, bf16[3,128,768]{2,1,0:T(8,128)(2,1)S(1)}, u32[]{:S(2)}, u32[]{:S(2)}) %collective-permute-start.5) | collective-permute-done | bytes 589856 | tf_op jit(solution)/shard_map/ppermute | solution.py:1413
  162.7 0.8 copy-done.45
  163.5 116.4 %moe_stage.1 = (bf16[4,3,128,768]{3,2,1,0:T(8,128)(2,1)}, bf16[3,4,128,768]{3,2,1,0:T(8,128)(2,1)}, f32[3,4,1,128]{3,2,1,0:T(1,128)}, bf16[2,2,2,192,1536]{4,3,2,1,0:T(8,128)(2,1)}, bf16[2,2,2,192,1536]{4,3,2,1,0:T(8,128)(2,1)}) custom-call(bf16[4,128,768]{2,1,0:T(8,128)(2,1)} %get-tuple-element.92.refs_0_, bf16[4,128,768]{2,1,0:T(8,128)(2,1)} %get-tuple-element.93.refs_1_, ...), custom_call_target="tpu_custom_call" | custom-call | flops 72477573120 | bytes 94371840 | tf_op jit(solution)/shard_map/moe_stage/pallas_call | solution.py:1372
  279.9 5.2 %convert_add_fusion = f32[2,2,2,192,1536]{4,3,2,1,0:T(8,128)S(1)} fusion(bf16[2,2,2,192,1536]{4,3,2,1,0:T(8,128)(2,1)} %get-tuple-element.107, bf16[2,2,2,192,1536]{4,3,2,1,0:T(8,128)(2,1)} %get-tuple-element.106), kind=kLoop, calls=%fused_computation | loop fusion | flops 7077888 | bytes 18874368 | tf_op jit(solution)/shard_map/add | solution.py:1541
  285.1 3.7 copy-done
  288.8 1.7 fusion.1
  290.5 1.5 collective-permute-start.8
  292.0 80.4 %back_stage.1 = (bf16[3,256,768]{2,1,0:T(8,128)(2,1)}, f32[3,256,768]{2,1,0:T(8,128)}, bf16[3,256,768]{2,1,0:T(8,128)(2,1)}, bf16[3,3,256,384]{3,2,1,0:T(8,128)(...) custom-call(f32[256,768]{1,0:T(8,128)} %get-tuple-element.78.refs_0_, ...), custom_call_target="tpu_custom_call" | custom-call | flops 60000002048 | bytes 10000000 | tf_op jit(solution)/shard_map/back_stage/pallas_call | solution.py:934
  372.4 3.8 fusion
  376.4 0.6 collective-permute-start.9
  378.0 0.9 pad_maximum_fusion.2.att_ref
  379.2 0.7 select_maximum_fusion.small_ref
  379.9 54.7 %last_stage.1 = (f32[4,192,384]{2,1,0:T(8,128)}, f32[192,8]{1,0:T(8,128)}, f32[1,192]{1,0:T(1,128)}, f32[1,192]{1,0:T(1,128)}, f32[8,6]{1,0:T(8,128)}, /*index=5*/f32[3,256,768]{2,1,0:T(8,128)}) custom-call(bf16[768,768]{1,0:T(8,128)(2,1)} %bitcast.143, bf16[3,768,384]{2,1,0:T(8,128)(2,1)} %bitcast.142, bf16[768,768]{1,0:T(8,128)(2,1)} %bitcast.144, ...), custom_call_target="tpu_custom_call" | custom-call | flops 1811939328 | bytes 4718592 | tf_op jit(solution)/shard_map/last_stage/pallas_call | solution.py:1134
  434.5 1.3 copy.51
  435.9 1.6 copy.52
  437.4 2.1 slice_bitcast_fusion.3
  439.6 1.8 slice_bitcast_fusion.11
  442.2 2.6 slice_bitcast_fusion.1
  444.8 1.0 copy.75
  445.9 1.1 copy-done.6
  446.9 1.4 copy.76
  448.3 0.6 copy.77
  448.9 0.6 copy.78
  (126 shorter events, 4.8 us)
Async XLA Ops:
  0.6 7.0 %copy-start.8 = (bf16[1,2,1536,192]{2,3,1,0:T(8,128)(2,1)S(1)}, bf16[1,2,1536,192]{2,3,1,0:T(8,128)(2,1)}, u32[]{:S(2)}) copy-start(bf16[1,2,1536,192]{2,3,1,0:T(8,128)(2,1)} %param.24) | copy-start | bytes 3538948
  0.7 7.0 %copy-start.9 = (bf16[1,2,192,1536]{3,2,1,0:T(8,128)(2,1)S(1)}, bf16[1,2,192,1536]{3,2,1,0:T(8,128)(2,1)}, u32[]{:S(2)}) copy-start(bf16[1,2,192,1536]{3,2,1,0:T(8,128)(2,1)} %param.23) | copy-start | bytes 3538948
  1.7 0.5 copy-start.43
  1.7 0.6 copy-start.33
  1.7 0.8 copy-start.35
  2.5 0.6 copy-start.29
  3.1 4.6 %copy-start.28 = (f32[3,4,256]{2,1,0:T(4,128)}, f32[3,4,256]{2,1,0:T(4,128)S(1)}, u32[]{:S(2)}) copy-start(f32[3,4,256]{2,1,0:T(4,128)S(1)} %slice.172.refs_21_) | copy-start | bytes 36868
  7.7 1.6 copy-start.18
  7.7 2.5 copy-start.39
  75.0 3.2 copy-start.5
  78.2 1.5 copy-start.38
  78.2 2.2 copy-start.47
  79.7 6.1 %copy-start.32 = (s32[3,1024]{1,0:T(4,128)S(1)}, s32[3,1024]{1,0:T(4,128)}, u32[]{:S(2)}) copy-start(s32[3,1024]{1,0:T(4,128)} %param.14) | copy-start | bytes 36868
  79.8 0.6 copy-start.20
  79.8 0.8 copy-start.22
  79.8 0.8 copy-start.24
  79.8 0.8 copy-start.26
  85.8 0.6 copy-start.37
  85.9 0.6 copy-start.19
  88.1 9.0 %copy-start.14 = (bf16[4,384,192]{2,1,0:T(8,128)(2,1)S(1)}, bf16[4,384,192]{2,1,0:T(8,128)(2,1)}, u32[]{:S(2)}) copy-start(bf16[4,384,192]{2,1,0:T(8,128)(2,1)} %get-tuple-element.75) | copy-start | bytes 1769476
  95.6 26.8 %collective-permute-start = (bf16[256,384]{1,0:T(8,128)(2,1)}, bf16[256,384]{1,0:T(8,128)(2,1)S(1)}, u32[]{:S(2)}, u32[]{:S(2)}) collective-permute-start(bf16[256,384]{1,0:T(8,128)(2,1)} %get-tuple-element.74.own_ref), channel_id=1, source_target_pairs={{0,1},{1,0},{2,3},{3,2},{4,5},{5,4},{6,7},{7,6},{8,9},{9,8},{10,11... | collective-permute-start | bytes 589832 | tf_op jit(solution)/shard_map/ppermute | solution.py:1413
  98.5 28.4 %collective-permute-start.1 = (bf16[384,768]{1,0:T(8,128)(2,1)}, bf16[384,768]{1,0:T(8,128)(2,1)}, u32[]{:S(2)}, u32[]{:S(2)}) collective-permute-start(bf16[384,768]{1,0:T(8,128)(2,1)} %copy.43.refs_19_), channel_id=1, source_target_pairs={{0,1},{1,0},{2,3},{3,2},{4,5},{5,4},{6,7},{7,6},{8,9},{9,8},{10,11... | collective-permute-start | bytes 1769480 | tf_op jit(solution)/shard_map/ppermute | solution.py:1413
  100.1 9.1 %copy-start.2 = (bf16[4,3,128,768]{3,2,1,0:T(8,128)(2,1)S(1)}, bf16[4,3,128,768]{3,2,1,0:T(8,128)(2,1)}, u32[]{:S(2)}) copy-start(bf16[4,3,128,768]{3,2,1,0:T(8,128)(2,1)} %dispatch_rows.1) | copy-start | bytes 7077892
  107.6 3.9 copy-start.4
  107.6 16.4 %collective-permute-start.2 = (bf16[256,384]{1,0:T(8,128)(2,1)}, bf16[256,384]{1,0:T(8,128)(2,1)S(1)}, u32[]{:S(2)}, u32[]{:S(2)}) collective-permute-start(bf16[256,384]{1,0:T(8,128)(2,1)} %get-tuple-element.79.own_ref), channel_id=1, source_target_pairs={{0,1},{1,0},{2,3},{3,2},{4,5},{5,4},{6,7},{7,6},{8,9},{9,8},{10,11... | collective-permute-start | bytes 589832 | tf_op jit(solution)/shard_map/ppermute | solution.py:1413
  110.5 35.5 %collective-permute-start.4 = (bf16[3,128,768]{2,1,0:T(8,128)(2,1)}, bf16[3,128,768]{2,1,0:T(8,128)(2,1)}, u32[]{:S(2)}, u32[]{:S(2)}) collective-permute-start(bf16[3,128,768]{2,1,0:T(8,128)(2,1)} %get-tuple-element.150), channel_id=1, source_target_pairs={{0,8},{8,0},{16,24},{24,16},{1,9},{9,1},{17,25},{25,17},{2,10},{10... | collective-permute-start | bytes 1769480 | tf_op jit(solution)/shard_map/ppermute | solution.py:1413
  111.0 52.4 %collective-permute-start.7 = (bf16[2,192,1536]{2,1,0:T(8,128)(2,1)}, bf16[2,192,1536]{2,1,0:T(8,128)(2,1)}, u32[]{:S(2)}, u32[]{:S(2)}) collective-permute-start(bf16[2,192,1536]{2,1,0:T(8,128)(2,1)} %get-tuple-element.99.refs_11_), channel_id=1, source_target_pairs={{0,4},{2,6},{4,0},{6,2},{1,5},{3,7},{5,1},{7,3},{8,12},{10,14},{12... | collective-permute-start | bytes 3538952 | tf_op jit(solution)/shard_map/ppermute | solution.py:1413
  113.6 7.5 %copy-start.3 = (bf16[2,2,192,1536]{3,2,1,0:T(8,128)(2,1)S(1)}, bf16[2,2,192,1536]{3,2,1,0:T(8,128)(2,1)}, u32[]{:S(2)}) copy-start(bf16[2,2,192,1536]{3,2,1,0:T(8,128)(2,1)} %pad_maximum_fusion.pair_ref) | copy-start | bytes 7077892
  121.2 1.2 copy-start.34
  121.2 1.1 copy-start.36
  121.2 1.1 copy-start.44
  121.2 5.7 %copy-start.12 = (bf16[256,384]{1,0:T(8,128)(2,1)S(1)}, bf16[256,384]{1,0:T(8,128)(2,1)}, u32[]{:S(2)}) copy-start(bf16[256,384]{1,0:T(8,128)(2,1)} %get-tuple-element.81.own_ref) | copy-start | bytes 589828
  121.2 6.2 %copy-start.30 = (f32[3,8,256]{2,1,0:T(8,128)S(1)}, f32[3,8,256]{2,1,0:T(8,128)}, u32[]{:S(2)}) copy-start(f32[3,8,256]{2,1,0:T(8,128)} %copy-done.29) | copy-start | bytes 73732
  122.4 11.4 %copy-start.15 = (bf16[256,384]{1,0:T(8,128)(2,1)}, bf16[256,384]{1,0:T(8,128)(2,1)S(1)}, u32[]{:S(2)}) copy-start(bf16[256,384]{1,0:T(8,128)(2,1)S(1)} %collective-permute-done.other_ref) | copy-start | bytes 589828
  122.4 40.3 %collective-permute-start.5 = (bf16[3,128,768]{2,1,0:T(8,128)(2,1)}, bf16[3,128,768]{2,1,0:T(8,128)(2,1)S(1)}, u32[]{:S(2)}, u32[]{:S(2)}) collective-permute-start(bf16[3,128,768]{2,1,0:T(8,128)(2,1)} %get-tuple-element.149), channel_id=1, source_target_pairs={{0,16},{8,24},{16,0},{24,8},{1,17},{9,25},{17,1},{25,9},{2,18},{10... | collective-permute-start | bytes 1769480 | tf_op jit(solution)/shard_map/ppermute | solution.py:1413
  124.0 9.8 %copy-start.16 = (bf16[256,384]{1,0:T(8,128)(2,1)}, bf16[256,384]{1,0:T(8,128)(2,1)S(1)}, u32[]{:S(2)}) copy-start(bf16[256,384]{1,0:T(8,128)(2,1)S(1)} %collective-permute-done.2.other_ref) | copy-start | bytes 589828
  124.0 38.7 %collective-permute-start.6 = (bf16[3,128,768]{2,1,0:T(8,128)(2,1)S(1)}, bf16[3,128,768]{2,1,0:T(8,128)(2,1)}, u32[]{:S(2)}, u32[]{:S(2)}) collective-permute-start(bf16[3,128,768]{2,1,0:T(8,128)(2,1)S(1)} %get-tuple-element.148), channel_id=1, source_target_pairs={{0,24},{8,16},{16,8},{24,0},{1,25},{9,17},{17,9},{25,1},{2,26},{10... | collective-permute-start | bytes 1769480 | tf_op jit(solution)/shard_map/ppermute | solution.py:1413
  126.9 14.6 %collective-permute-start.3 = (bf16[256,384]{1,0:T(8,128)(2,1)S(1)}, bf16[256,384]{1,0:T(8,128)(2,1)S(1)}, u32[]{:S(2)}, u32[]{:S(2)}) collective-permute-start(bf16[256,384]{1,0:T(8,128)(2,1)S(1)} %copy-done.12), channel_id=1, source_target_pairs={{0,1},{1,0},{2,3},{3,2},{4,5},{5,4},{6,7},{7,6},{8,9},{9,8},{10,11... | collective-permute-start | bytes 589832 | tf_op jit(solution)/shard_map/ppermute | solution.py:1413
  141.5 0.7 copy-start.17
  162.7 0.8 copy-start.45
  285.1 3.7 copy-start
  290.5 81.9 %collective-permute-start.8 = (bf16[2,2,192,1536]{3,2,1,0:T(8,128)(2,1)}, bf16[2,2,192,1536]{3,2,1,0:T(8,128)(2,1)}, u32[]{:S(2)}, u32[]{:S(2)}) collective-permute-start(bf16[2,2,192,1536]{3,2,1,0:T(8,128)(2,1)} %fusion.1), channel_id=1, source_target_pairs={{0,4},{2,6},{4,0},{6,2},{1,5},{3,7},{5,1},{7,3},{8,12},{10,14},{12... | collective-permute-start | bytes 7077896 | tf_op jit(solution)/shard_map/ppermute | solution.py:1413
  376.2 3.7 copy-start.1
  376.2 1.1 copy-start.10
  376.2 1.5 copy-start.11
  376.2 1.8 copy-start.13
  376.2 2.6 copy-start.21
  376.2 2.6 copy-start.23
  376.2 2.6 copy-start.25
  376.2 2.6 copy-start.27
  376.3 2.6 copy-start.46
  376.3 2.9 copy-start.31
  376.3 2.9 copy-start.40
  376.4 61.0 %collective-permute-start.9 = (bf16[2,192,1536]{2,1,0:T(8,128)(2,1)S(1)}, bf16[2,192,1536]{2,1,0:T(8,128)(2,1)S(1)}, u32[]{:S(2)}, u32[]{:S(2)}) collective-permute-start(bf16[2,192,1536]{2,1,0:T(8,128)(2,1)S(1)} %fusion.2), channel_id=1, source_target_pairs={{0,1},{1,0},{2,3},{3,2},{4,5},{5,4},{6,7},{7,6},{8,9},{9,8},{10,11... | collective-permute-start | bytes 3538952 | tf_op jit(solution)/shard_map/ppermute | solution.py:1413
  439.6 2.1 slice-start
  442.2 2.6 copy-start.7
  444.8 2.1 copy-start.6
  446.9 1.4 copy-start.42
  446.9 2.0 copy-start.41

commit v4 on v3

--- a/solution.py
+++ b/solution.py
@@ -515,10 +515,11 @@
 
 
 def first_kernel(
-    seqs, tok_ref, wqkv_ref, wout_ref, table_ref, ga_ref, gm_ref, router_ref, pair_ref,
+    seqs, cap, tok_ref, wqkv_ref, wout_ref, table_ref, ga_ref, gm_ref, router_ref, pair_ref, near_ref, cot_ref,
     q_ref, k_ref, v_ref, normed_ref, wqkv_out, wout_out, table_out, gain_ref, gm_out, router_out, got_out, far_out,
+    slots_ref, cot_out,
     tok_all, n_all, ga_all, gm_all, router_all,
-    z_send, z_recv, f_send, f_recv, t_send, t_recv, y_send, y_recv, l_sem, e_sems,
+    z_send, z_recv, f_send, f_recv, t_send, t_recv, y_send, y_recv, l_sem, e_sems, c_sems,
 ):
     dp = lax.axis_index("dp")
     ctx = lax.axis_index("ctx")
@@ -576,6 +577,27 @@
     ]
     for copy in own:
         copy.start()
+
+    groups = slots_ref.shape[0]
+
+    def cot_copy(s, b):
+        return remote(
+            slots_ref.at[b, s], cot_out.at[b - 1, s], c_sems.at[0, s, b - 1], c_sems.at[1, s, b - 1], dp=dp ^ b
+        )
+
+    def dispatch_cot(s, carry):
+        picks = one_hot(near_ref[s], cap)
+        pick = jnp.concatenate([jnp.where(p, 1.0, 0.0).astype(BF16) for p in picks], axis=0)
+        slots_ref[:, s] = dot(pick, cot_ref[s]).astype(BF16).reshape(groups, cap, cot_ref.shape[2])
+
+        @pl.when(s < seqs - 1)
+        def _():
+            for b in (3, 2, 1):
+                cot_copy(s, b).start()
+
+        return carry
+
+    lax.fori_loop(0, seqs, dispatch_cot, 0)
     for copy in own:
         copy.wait()
 
@@ -662,6 +684,9 @@
     lax.fori_loop(0, seqs, others, 0)
     for copy in expert_copies:
         copy.wait()
+    for s in range(seqs - 1):
+        for b in (3, 2, 1):
+            cot_copy(s, b).wait()
     for group in small:
         for copy in group:
             copy.wait_send()
@@ -669,7 +694,7 @@
         copy.wait_send()
 
 
-def first_stage(tokens, wqkv, wout, table, gain_attn, gain_moe, router, expert_pair):
+def first_stage(tokens, wqkv, wout, table, gain_attn, gain_moe, router, expert_pair, near, cot, cap):
     seqs, stretch, width = tokens.shape
     count, rows, local = wqkv.shape
     dp = width // rows
@@ -678,10 +703,10 @@
     vmem = pl.BlockSpec(memory_space=pltpu.VMEM)
     dma = pltpu.SemaphoreType.DMA
     return pl.pallas_call(
-        functools.partial(first_kernel, seqs),
+        functools.partial(first_kernel, seqs, cap),
         name="first_stage",
-        in_specs=[any_spec] * 8,
-        out_specs=[vmem] * 10 + [any_spec] * 2,
+        in_specs=[any_spec] * 8 + [vmem] * 2,
+        out_specs=[vmem] * 10 + [any_spec] * 2 + [vmem, any_spec],
         out_shape=[
             jax.ShapeDtypeStruct((seqs, stretch, local), BF16),
             jax.ShapeDtypeStruct((seqs, 4, stretch, local), BF16),
@@ -695,6 +720,8 @@
             jax.ShapeDtypeStruct((experts_n, width), BF16),
             jax.ShapeDtypeStruct(expert_pair.shape[1:], BF16),
             jax.ShapeDtypeStruct(expert_pair.shape[1:], BF16),
+            jax.ShapeDtypeStruct((dp, seqs, cap, width), BF16),
+            jax.ShapeDtypeStruct((dp - 1, seqs - 1, cap, width), BF16),
         ],
         scratch_shapes=[
             pltpu.VMEM((4, seqs, stretch, width), BF16),
@@ -703,16 +730,15 @@
             pltpu.VMEM((dp, 1, rows), BF16),
             pltpu.VMEM((dp, rows, experts_n), BF16),
             dma((6, 3)), dma((6, 3)), dma((2, 3)), dma((2, 3)), dma((1 + seqs,)), dma((1 + seqs,)),
-            dma((seqs,)), dma((seqs,)), dma((7,)), dma((2, 2)),
+            dma((seqs,)), dma((seqs,)), dma((7,)), dma((2, 2)), dma((2, seqs - 1, 3)),
         ],
         compiler_params=pltpu.CompilerParams(vmem_limit_bytes=VMEM_BYTES, collective_id=0, has_side_effects=True),
         cost_estimate=cost(40 * 10**9, 10**7),
-    )(tokens, wqkv, wout, table, gain_attn, gain_moe, router, expert_pair)
+    )(tokens, wqkv, wout, table, gain_attn, gain_moe, router, expert_pair, near, cot)
 
 
 def back_kernel(seqs, groups, cap, *refs):
-    mid_refs, moe_refs, gate_refs, lse_refs = (refs[i * seqs : (i + 1) * seqs] for i in range(4))
-    refs = refs[4 * seqs :]
+    seq_refs, refs = refs[:4], refs[4:]
     din_ref, part_ref, q_ref, k_ref, v_ref, bias_ref, cot_ref, wout_ref = refs[:8]
     h_ref, place_ref, near_ref, idq_ref, idk_ref, router_ref, gain_ref = refs[8:15]
     out_ref, gmid_ref, low_ref, proj_ref, gain_grad_ref, router_grad_ref, rel_ref = refs[15:22]
@@ -744,9 +770,8 @@
              (part_ref.at[0], part_v.at[0]))
         )
     ]
-    for s in range(seqs):
-        for i, (src, dst) in enumerate(((mid_refs, mid_v), (moe_refs, moe_v), (gate_refs, gate_v), (lse_refs, lse_v))):
-            loads.append(pltpu.make_async_copy(src[s], dst.at[s], seq_sems.at[s, i]))
+    for i, (src, dst) in enumerate(zip(seq_refs, (mid_v, moe_v, gate_v, lse_v))):
+        loads.append(pltpu.make_async_copy(src, dst, seq_sems.at[i]))
     din_load.start()
     for copy in loads:
         copy.start()
@@ -921,9 +946,8 @@
 
 
 def back_stage(mids, moes, gates, lse, din, parts, q, k, v, bias, cot, wout, h, places, near, ids_query, ids_key, router, gain):
-    seqs = len(mids)
     groups, _, cap, width = parts.shape
-    stretch = mids[0].shape[0]
+    seqs, stretch = mids.shape[:2]
     local = wout.shape[0]
     length = k.shape[1]
     pairs = local // (2 * HD)
@@ -934,7 +958,7 @@
     return pl.pallas_call(
         functools.partial(back_kernel, seqs, groups, cap),
         name="back_stage",
-        in_specs=[any_spec] * (4 * seqs + 8) + [vmem] * 7,
+        in_specs=[any_spec] * 12 + [vmem] * 7,
         out_specs=[vmem] * 7,
         out_shape=[
             jax.ShapeDtypeStruct((seqs, stretch, width), BF16),
@@ -971,13 +995,13 @@
             pltpu.VMEM((seqs, 2, 2, stretch, local), BF16),
             pltpu.VMEM((seqs, 2, stretch, local), BF16),
             pltpu.VMEM((seqs, 2, stretch, local), BF16),
-            dma((8,)), dma((seqs, 4)), dma((2, seqs, groups)), dma((2, 3, seqs)), dma((2, seqs)), dma((2, seqs)),
+            dma((8,)), dma((4,)), dma((2, seqs, groups)), dma((2, 3, seqs)), dma((2, seqs)), dma((2, seqs)),
         ],
         compiler_params=pltpu.CompilerParams(
             vmem_limit_bytes=63 * 1024 * 1024, collective_id=3, has_side_effects=True
         ),
         cost_estimate=cost(6 * 10**10, 10**7),
-    )(*mids, *moes, *gates, *lse, din, parts, q, k, v, bias, cot, wout, h, places, near, ids_query, ids_key, router, gain)
+    )(mids, moes, gates, lse, din, parts, q, k, v, bias, cot, wout, h, places, near, ids_query, ids_key, router, gain)
 
 
 def last_kernel(
@@ -1169,17 +1193,186 @@
     )(normed, proj, datt, att, small, wqkv, gmid, x, gain)
 
 
+def front_kernel(
+    seqs, groups, cap,
+    got_ref, cot_ref, q_ref, k_ref, v_ref, win_ref, idq_ref, idk_ref, x_ref, wout_ref, gain_ref, router_ref,
+    hits_ref, place_ref,
+    far_out, cot_out, row_out, gate_out, bias_ref, att_ref, lse_ref, mid_ref, moe_ref, gates_ref, send_ref, slot_ref,
+    wout_other, att_other, mask_ref, w_sems, x_sems, z_sems, r_sems, g_sems, own_sems,
+):
+    dp = lax.axis_index("dp")
+    ctx = lax.axis_index("ctx")
+    tp = lax.axis_index("tp")
+    greet([{"dp": dp ^ b} for b in range(1, groups)] + [{"ctx": ctx ^ 2}, {"tp": tp ^ 1}])
+    width = x_ref.shape[2]
+    local = q_ref.shape[2]
+    pairs = local // (2 * HD)
+    far_copy = remote(got_ref, far_out, w_sems.at[0, 0], w_sems.at[1, 0], ctx=ctx ^ 2)
+    wout_copy = remote(wout_ref, wout_other, w_sems.at[0, 1], w_sems.at[1, 1], tp=tp ^ 1)
+    order = tuple(range(groups - 1, 0, -1))
+    cot_copies = [
+        remote(cot_ref.at[b, seqs - 1], cot_out.at[b - 1], z_sems.at[0, b - 1], z_sems.at[1, b - 1], dp=dp ^ b)
+        for b in order
+    ]
+    for copy in [far_copy, wout_copy] + cot_copies:
+        copy.start()
+
+    def expand(head, carry):
+        for block in range(4):
+            row = win_ref[head, block : block + 1, :]
+            wide = jnp.broadcast_to(row, (256, 512))
+            rolled = pltpu.roll(wide, 257, 1, stride=1, stride_axis=0)
+            bias_ref[head, block * 256 : (block + 1) * 256, :] = rolled[:, :256].astype(BF16)
+        return carry
+
+    lax.fori_loop(0, 2 * pairs, expand, 0)
+
+    def att_copy(s):
+        return remote(att_ref.at[s], att_other.at[s], x_sems.at[0, s], x_sems.at[1, s], tp=tp ^ 1)
+
+    def row_copy(b):
+        return remote(send_ref.at[0, dp ^ b], row_out.at[dp], r_sems.at[0, b - 1], r_sems.at[1, b - 1], dp=dp ^ b)
+
+    def gate_copy(b):
+        return remote(slot_ref.at[0, dp ^ b], gate_out.at[dp], g_sems.at[0, b - 1], g_sems.at[1, b - 1], dp=dp ^ b)
+
+    def own_row():
+        return pltpu.make_async_copy(send_ref.at[0, dp], row_out.at[dp], own_sems.at[0])
+
+    def own_gate():
+        return pltpu.make_async_copy(slot_ref.at[0, dp], gate_out.at[dp], own_sems.at[1])
+
+    def attention(s):
+        mask_ref[...] = jnp.where(idk_ref[s] <= idq_ref[s], 0.0, MASKED)
+
+        def pair(p, carry):
+            lanes = pl.ds(pl.multiple_of(p * 2 * HD, 2 * HD), 2 * HD)
+            queries = q_ref[s, :, lanes]
+            keys = k_ref[s, :, lanes]
+            values_t = v_ref[s, :, lanes].T
+            low_half = lax.broadcasted_iota(jnp.int32, queries.shape, 1) < HD
+            zero = jnp.zeros_like(queries)
+            parts = []
+            for head in range(2):
+                own = jnp.where(low_half, queries, zero) if head == 0 else jnp.where(low_half, zero, queries)
+                scores = dot_nt(keys, own) + bias_ref[2 * p + head].astype(F32) + mask_ref[...]
+                top = jnp.max(scores, axis=0, keepdims=True)
+                weights = jnp.exp(scores - top)
+                total = jnp.sum(weights, axis=0, keepdims=True)
+                part = dot(values_t[head * HD : (head + 1) * HD], weights.astype(BF16)) * (1.0 / total)
+                parts.append(part)
+                lse_ref[s, p, head : head + 1, :] = top + jnp.log(total)
+            att_ref[s, :, lanes] = jnp.concatenate(parts, axis=0).T.astype(BF16)
+            return carry
+
+        lax.fori_loop(0, pairs, pair, 0)
+        att_copy(s).start()
+
+    def middle(s):
+        att_copy(s).wait_recv()
+        mid = x_ref[s].astype(F32) + (dot(att_ref[s], wout_ref[...]) + dot(att_other[s], wout_other[...]))
+        mid_ref[s] = mid
+        moe_in = (mid * norm_factor(mid) * gain_ref[...].astype(F32)).astype(BF16)
+        moe_ref[s] = moe_in
+        logits = dot_nt(router_ref[...], moe_in)
+        hit = hits_ref[s] > 0.5
+        top = jnp.max(jnp.where(hit, logits, MASKED), axis=0, keepdims=True)
+        raw = jnp.where(hit, jnp.exp(jnp.where(hit, logits, top) - top), 0.0)
+        gates = raw / jnp.sum(raw, axis=0, keepdims=True)
+        gates_ref[s] = gates
+        picks = one_hot(place_ref[s], cap)
+        pick = jnp.concatenate([jnp.where(p, 1.0, 0.0).astype(BF16) for p in picks], axis=0)
+        send_ref[s] = dot(pick, moe_in).astype(BF16).reshape(groups, cap, width)
+        eye = diagonal(cap)
+        for group in range(groups):
+            column = jnp.sum(jnp.where(picks[group], gates[group : group + 1, :], 0.0), axis=1, keepdims=True)
+            slot_ref[s, group] = jnp.sum(jnp.where(eye, column, 0.0), axis=0, keepdims=True)
+
+    def main(s, carry):
+        attention(s)
+
+        @pl.when(s == 1)
+        def _():
+            wout_copy.wait_recv()
+
+        @pl.when(s > 0)
+        def _():
+            middle(s - 1)
+
+        @pl.when(s == 1)
+        def _():
+            for b in order:
+                gate_copy(b).start()
+                row_copy(b).start()
+            own_row().start()
+            own_gate().start()
+
+        return carry
+
+    lax.fori_loop(0, seqs, main, 0)
+    middle(seqs - 1)
+    for b in order:
+        gate_copy(b).wait()
+        row_copy(b).wait()
+    own_row().wait()
+    own_gate().wait()
+    for copy in [far_copy] + cot_copies:
+        copy.wait()
+    wout_copy.wait_send()
+    for s in range(seqs):
+        att_copy(s).wait_send()
+
+
+def front_stage(got, cot, q, k, v, windows, ids_query, ids_key, x, wout, gain, router, hits, places, cap):
+    seqs, stretch, width = x.shape
+    groups = places.shape[1]
+    local = q.shape[2]
+    length = k.shape[1]
+    pairs = local // (2 * HD)
+    experts_n = router.shape[0]
+    any_spec = pl.BlockSpec(memory_space=pl.ANY)
+    vmem = pl.BlockSpec(memory_space=pltpu.VMEM)
+    dma = pltpu.SemaphoreType.DMA
+    return pl.pallas_call(
+        functools.partial(front_kernel, seqs, groups, cap),
+        name="front_stage",
+        in_specs=[any_spec] * 2 + [vmem] * 12,
+        out_specs=[any_spec] * 3 + [vmem] * 9,
+        out_shape=[
+            jax.ShapeDtypeStruct(got.shape, BF16),
+            jax.ShapeDtypeStruct((groups - 1, cap, width), BF16),
+            jax.ShapeDtypeStruct((groups, cap, width), BF16),
+            jax.ShapeDtypeStruct((groups, 1, cap), F32),
+            jax.ShapeDtypeStruct((2 * pairs, length, stretch), BF16),
+            jax.ShapeDtypeStruct((seqs, stretch, local), BF16),
+            jax.ShapeDtypeStruct((seqs, pairs, 2, stretch), F32),
+            jax.ShapeDtypeStruct((seqs, stretch, width), F32),
+            jax.ShapeDtypeStruct((seqs, stretch, width), BF16),
+            jax.ShapeDtypeStruct((seqs, experts_n, stretch), F32),
+            jax.ShapeDtypeStruct((seqs, groups, cap, width), BF16),
+            jax.ShapeDtypeStruct((seqs, groups, 1, cap), F32),
+        ],
+        scratch_shapes=[
+            pltpu.VMEM((local, width), BF16),
+            pltpu.VMEM((seqs, stretch, local), BF16),
+            pltpu.VMEM((length, stretch), F32),
+            dma((2, 2)), dma((2, seqs)), dma((2, groups - 1)), dma((2, groups - 1)), dma((2, groups - 1)), dma((2,)),
+        ],
+        compiler_params=pltpu.CompilerParams(vmem_limit_bytes=VMEM_BYTES, collective_id=4, has_side_effects=True),
+        cost_estimate=cost(4 * 10**10, 10**7),
+    )(got, cot, q, k, v, windows, ids_query, ids_key, x, wout, gain, router, hits, places)
+
+
 def moe_kernel(
     seqs, groups, cap, tile, *refs,
 ):
-    sends, refs = refs[:seqs], refs[seqs:]
-    slot_gates, refs = refs[:seqs], refs[seqs:]
-    cots, refs = refs[:groups], refs[groups:]
+    send_ref, slot_ref, row_ref, gate_ref, slots_ref, cot_ref, last_ref = refs[:7]
+    refs = refs[7:]
     w_own, w_far, part_out, din_back, h_back, keep_out, give_out = (refs[:2], refs[2:4]) + refs[4:9]
     (
         w_all, x_all, gate_all, g_all, xt_all, dyt_all, dy_ref, hid_all, dpre_all, part_acc, din_acc,
         part_all, din_all, h_all, tile_ref,
-        x_sems, gate_sems, din_sems, h_sems, w_sems, own_sems, part_sems, out_sems, core_sems,
+        x_sems, gate_sems, din_sems, h_sems, w_sems, own_sems, cot_sems, part_sems, out_sems, core_sems,
     ) = refs[9:]
     dp = lax.axis_index("dp")
     ctx = lax.axis_index("ctx")
@@ -1194,14 +1387,14 @@
     order = tuple(range(groups - 1, 0, -1))
 
     sent = []
-    for s in range(seqs):
+    for s in range(1, seqs):
         for b in order:
             sent.append(
-                remote(sends[s].at[dp ^ b], x_all.at[s, dp], x_sems.at[0, s, b - 1], x_sems.at[1, s, b - 1], dp=dp ^ b)
+                remote(send_ref.at[s, dp ^ b], x_all.at[s, dp], x_sems.at[0, s, b - 1], x_sems.at[1, s, b - 1], dp=dp ^ b)
             )
             sent.append(
                 remote(
-                    slot_gates[s].at[dp ^ b], gate_all.at[s, dp],
+                    slot_ref.at[s, dp ^ b], gate_all.at[s, dp],
                     gate_sems.at[0, s, b - 1], gate_sems.at[1, s, b - 1], dp=dp ^ b,
                 )
             )
@@ -1217,11 +1410,17 @@
             local.append(pltpu.make_async_copy(ref, w_all.at[:, half, place], w_sems.at[2, half, index]))
     for copy in w_copies + sent:
         copy.start()
-    for s in range(seqs):
-        local.append(pltpu.make_async_copy(sends[s].at[dp], x_all.at[s, dp], own_sems.at[2 * s]))
-        local.append(pltpu.make_async_copy(slot_gates[s].at[dp], gate_all.at[s, dp], own_sems.at[1 + 2 * s]))
-    for b in range(groups):
-        local.append(pltpu.make_async_copy(cots[b], g_all.at[dp ^ b], own_sems.at[2 * seqs + b]))
+    local.append(pltpu.make_async_copy(row_ref, x_all.at[0], own_sems.at[0]))
+    local.append(pltpu.make_async_copy(gate_ref, gate_all.at[0], own_sems.at[1]))
+    for s in range(1, seqs):
+        local.append(pltpu.make_async_copy(send_ref.at[s, dp], x_all.at[s, dp], own_sems.at[2 * s]))
+        local.append(pltpu.make_async_copy(slot_ref.at[s, dp], gate_all.at[s, dp], own_sems.at[1 + 2 * s]))
+    local.append(pltpu.make_async_copy(slots_ref.at[0], g_all.at[dp], cot_sems.at[0, 0]))
+    for b in range(1, groups):
+        local.append(
+            pltpu.make_async_copy(cot_ref.at[b - 1], g_all.at[dp ^ b, pl.ds(0, seqs - 1)], cot_sems.at[0, b])
+        )
+        local.append(pltpu.make_async_copy(last_ref.at[b - 1], g_all.at[dp ^ b, seqs - 1], cot_sems.at[1, b]))
     for copy in local:
         copy.start()
     for copy in local:
@@ -1255,11 +1454,14 @@
         ]
 
     def chunk(s, carry):
-        for b in order:
-            there = x_all.at[s, dp ^ b]
-            remote(there, there, x_sems.at[0, s, b - 1], x_sems.at[1, s, b - 1], dp=dp ^ b).wait_recv()
-            there = gate_all.at[s, dp ^ b]
-            remote(there, there, gate_sems.at[0, s, b - 1], gate_sems.at[1, s, b - 1], dp=dp ^ b).wait_recv()
+        @pl.when(s > 0)
+        def _():
+            for b in order:
+                there = x_all.at[s, dp ^ b]
+                remote(there, there, x_sems.at[0, s, b - 1], x_sems.at[1, s, b - 1], dp=dp ^ b).wait_recv()
+                there = gate_all.at[s, dp ^ b]
+                remote(there, there, gate_sems.at[0, s, b - 1], gate_sems.at[1, s, b - 1], dp=dp ^ b).wait_recv()
+
         x = x_all[s].reshape(rows, width)
         xt_all[s] = x.T
         for group in range(groups):
@@ -1358,9 +1560,8 @@
         copy.wait_send()
 
 
-def moe_stage(sends, slot_gates, cots, keep, got, far_keep, far_got, tile=512):
-    seqs = len(sends)
-    groups, cap, width = sends[0].shape
+def moe_stage(send, slot_gate, row, row_gate, slots, cot, last, keep, got, far_keep, far_got, tile=512):
+    seqs, groups, cap, width = send.shape
     _, piece, half_len = keep.shape
     halves = 2
     slices = width // piece
@@ -1372,7 +1573,7 @@
     return pl.pallas_call(
         functools.partial(moe_kernel, seqs, groups, cap, tile),
         name="moe_stage",
-        in_specs=[any_spec] * (2 * seqs + groups + 4),
+        in_specs=[any_spec] * 11,
         out_specs=[any_spec, any_spec, vmem, any_spec, any_spec],
         out_shape=[
             jax.ShapeDtypeStruct((groups, seqs, cap, width), BF16),
@@ -1398,14 +1599,14 @@
             pltpu.VMEM((seqs, groups, 1, cap), F32),
             pltpu.VMEM((2, 2, slices // 2, 2, piece, tile), BF16),
             dma((2, seqs, groups - 1)), dma((2, seqs, groups - 1)), dma((2, seqs, groups - 1)),
-            dma((2, seqs, groups - 1)), dma((3, 2, 2)), dma((2 * seqs + groups,)), dma((seqs, groups + 2)),
+            dma((2, seqs, groups - 1)), dma((3, 2, 2)), dma((2 * seqs,)), dma((2, groups)), dma((seqs, groups + 2)),
             dma((2, 2)), dma((tiles,)),
         ],
         compiler_params=pltpu.CompilerParams(
             vmem_limit_bytes=63 * 1024 * 1024, collective_id=2, has_side_effects=True
         ),
         cost_estimate=cost(20 * seqs * rows * width * halves * half_len, 40 * width * halves * half_len),
-    )(*sends, *slot_gates, *cots, keep, got, far_keep, far_got)
+    )(send, slot_gate, row, row_gate, slots, cot, last, keep, got, far_keep, far_got)
 
 
 def flip(value, axis, bit):
@@ -1473,16 +1674,14 @@
     if fits:
         me = lax.axis_index("dp")
         near_places = jnp.stack([lax.dynamic_index_in_dim(places, me ^ b, 1, keepdims=False) for b in range(dp)], axis=1)
-        cot_slots = dispatch(near_places, cotangent, cap)
-        cot_slots, tokens_first, pair = lax.optimization_barrier((cot_slots, tokens_in, pair))
-        cot_slots = [cot_slots[0]] + [flip(cot_slots[b], "dp", b) for b in range(1, dp)]
         (
             queries, keys, values, own_normed, wqkv, wout_parts, table, gain_attn, gain_moe, router, got, far_keep,
+            cot_slots, cot_in,
         ) = first_stage(
-            tokens_first, w_qkv[0], w_attn_out[0], bias_table[0], attn_gain, moe_gain, w_router[0], pair
+            tokens_in, w_qkv[0], w_attn_out[0], bias_table[0], attn_gain, moe_gain, w_router[0], pair,
+            near_places, cotangent, cap,
         )
         keep = lax.dynamic_index_in_dim(pair, tp, 0, keepdims=False)
-        far_got = flip(got, "ctx", 2)
         wout_own = wout_parts.transpose(1, 0, 2).reshape(local, width)
         table = table.reshape(NB, heads)
         keys = keys.reshape(seqs, 4 * stretch, local)
@@ -1496,37 +1695,45 @@
         got = flip(lax.dynamic_index_in_dim(pair, 1 - tp, 0, keepdims=False), "tp", 1)
         weights = lax.all_gather(jnp.stack([keep, got], axis=1), "ctx", axis=0, tiled=False)
         cot_slots = all_to_all_dp(dispatch(places, cotangent, cap))
-    wout_other = flip(wout_own, "tp", 1)
 
     one_hot_bucket = (rel_buckets[:, None] == jnp.arange(NB, dtype=jnp.int32)[None, :]).astype(F32)
     one_hot_bucket = jnp.pad(one_hot_bucket, ((0, 1), (0, 0)))
     starts = [(ctx - (ctx ^ b)) * stretch + 3 * stretch for b in range(4)]
     hot_windows = jnp.stack([lax.dynamic_slice_in_dim(one_hot_bucket, s, 2 * stretch, 0) for s in starts])
     windows = jnp.einsum("bmn,nh->hbm", hot_windows, table.astype(F32), precision=FULL_PRECISION)
-    bias = expand_bias(windows)
 
     ids = block_ids.reshape(seqs, 4, stretch)
     ids_pieces = [lax.dynamic_index_in_dim(ids, ctx ^ b, 1, keepdims=False) for b in range(4)]
     ids_query = ids_pieces[0].reshape(seqs, 1, stretch)
     ids_key = jnp.stack(ids_pieces, axis=1).reshape(seqs, 4 * stretch, 1)
 
-    wout_pair = jnp.stack([wout_own, wout_other])
-    attended, lse, mids, moes, gates, sends, slot_gates = [], [], [], [], [], [], []
-    for s in range(seqs):
-        att, stat = attend(queries[s], keys[s], values[s], bias, ids_query[s], ids_key[s])
-        attended.append(att)
-        lse.append(stat)
-        mid, moe_in, gate, send, slot_gate = middle_stage(
-            att, flip(att, "tp", 1), tokens_in[s], wout_pair, gain_moe, router, hits[s], places[s], cap
+    if fits:
+        (
+            far_got, cot_last, row, row_gate, bias, attended, lse, mids, moes, gates, send, slot_gate,
+        ) = front_stage(
+            got, cot_slots, queries, keys, values, windows, ids_query, ids_key, tokens_in, wout_own, gain_moe, router,
+            hits, places, cap,
         )
-        mids.append(mid)
-        moes.append(moe_in)
-        gates.append(gate)
-        sends.append(send)
-        slot_gates.append(slot_gate)
-    if fits:
-        parts, returned_din, returned_h, kept, given = moe_stage(sends, slot_gates, cot_slots, keep, got, far_keep, far_got)
+        parts, returned_din, returned_h, kept, given = moe_stage(
+            send, slot_gate, row, row_gate, cot_slots, cot_in, cot_last, keep, got, far_keep, far_got
+        )
     else:
+        bias = expand_bias(windows)
+        wout_pair = jnp.stack([wout_own, flip(wout_own, "tp", 1)])
+        attended, lse, mids, moes, gates, sends, slot_gates = [], [], [], [], [], [], []
+        for s in range(seqs):
+            att, stat = attend(queries[s], keys[s], values[s], bias, ids_query[s], ids_key[s])
+            attended.append(att)
+            lse.append(stat)
+            mid, moe_in, gate, send, slot_gate = middle_stage(
+                att, flip(att, "tp", 1), tokens_in[s], wout_pair, gain_moe, router, hits[s], places[s], cap
+            )
+            mids.append(mid)
+            moes.append(moe_in)
+            gates.append(gate)
+            sends.append(send)
+            slot_gates.append(slot_gate)
+        attended = jnp.stack(attended)
         partials, returned_din, returned_h = [], [], []
         acc = None
         for s in range(seqs):
@@ -1562,7 +1769,7 @@
             axis=0,
         )
         wide, g_router, g_moe, g_attn, g_table, grad_tokens = last_stage(
-            own_normed, grad_proj, dattn, jnp.concatenate(attended, axis=0), small, wqkv, gmid, tokens_in, gain_attn,
+            own_normed, grad_proj, dattn, attended.reshape(seqs * stretch, local), small, wqkv, gmid, tokens_in, gain_attn,
             dp, NB // dp, heads, expert_count,
         )
         other, wide = lax.optimization_barrier((other, wide))
@@ -1601,7 +1808,7 @@
             projections.append(jnp.concatenate([dq[None], full.astype(BF16)], axis=0))
         grad_proj = jnp.concatenate(projections, axis=1)
         dattn = jnp.concatenate(datts, axis=0)
-        attended = jnp.concatenate(attended, axis=0)
+        attended = attended.reshape(seqs * stretch, local)
         dnormed_part = jnp.einsum("jre,jde->rd", grad_proj, wqkv, preferred_element_type=F32)
         dnormed_own = dnormed_part.astype(BF16)
         dnormed = dnormed_own.astype(F32) + flip(dnormed_own, "tp", 1).astype(F32)

time: 450 us -> 404 us (0.90)
  waiting for transfers between devices: 16.8 us -> 0.01 us
  local copies, waits for them, and re-layouts: 47.7 us -> 31.3 us
  starting transfers between devices: 11.2 us -> 2.65 us
  Pallas kernels: 356 us -> 350 us
    pallas_call x1, Pallas kernels: 116 us -> 89.3 us  [moe_stage(): pl.pallas_call(functools.partial(moe_kernel, seqs, groups, cap, tile), na...]
    pallas_call x9 -> x2, Pallas kernels: 105 us -> 125 us  [the longest x1 78.4 us: first_stage(): pl.pallas_call(functools.partial(first_kernel, seqs, cap), name='first_st...]
    ppermute x10 -> x2, waiting for transfers between devices: 16.8 us -> 0.01 us  [flip(): return lax.ppermute(value, axis, [(i, i ^ bit) for i in range(count)])]
    ppermute x10 -> x2, starting transfers between devices: 11.2 us -> 2.65 us  [flip(): return lax.ppermute(value, axis, [(i, i ^ bit) for i in range(count)])]
    squeeze x7 -> x0, local copies, waits for them, and re-layouts: 7.14 us -> none  [the longest x1 1.93 us: on_device(): queries[s]]
    unnamed x112 -> x53, local copies, waits for them, and re-layouts: 20.8 us -> 15.4 us
    slice x3 -> x0, local copies, waits for them, and re-layouts: 4.71 us -> none  [the longest x1 3.23 us: on_device(): keys[s]]
  transfers between devices with their start and end apart: 10 -> 2, of which waited for: 1 -> 0; matrix products, arithmetic and copies ran while one was open for 4% -> 1% of each run, Pallas kernels for 36% -> 34%
where the time goes in v4:
time: 404 us; the launch traced here: 403 us
  Pallas kernels  350 us (87%)
  local copies, waits for them, and re-layouts  31.3 us (8%)
  other arithmetic  16.5 us (4%)
    pallas_call x1, Pallas kernels, moe_stage(): pl.pallas_call(functools.partial(moe_kernel, seqs, groups, cap, tile), na...  89.3 us
    pallas_call x1, Pallas kernels, back_stage(): pl.pallas_call(functools.partial(back_kernel, seqs, groups, cap), name='b...  80.2 us
    pallas_call x1, Pallas kernels, first_stage(): pl.pallas_call(functools.partial(first_kernel, seqs, cap), name='first_st...  78.4 us
    pallas_call x1, Pallas kernels, last_stage(): pl.pallas_call(last_kernel, name='last_stage', in_specs=[vmem] * 9, out_s...  56.3 us
    pallas_call x1, Pallas kernels, front_stage(): pl.pallas_call(functools.partial(front_kernel, seqs, groups, cap), name='...  46.1 us
    unnamed x53, local copies, waits for them, and re-layouts  15.4 us
  transfers between devices with their start and end apart: 2, of which 0 were waited for; matrix products, arithmetic and copies ran while one was open for 1% of the time, Pallas kernels for 34%

profile of v4, /device:TPU:0, one launch (start us, length us, event | category | flops | bytes accessed | tf_op | source)
XLA Modules:
  0.0 403.1 jit_solution(2400252356064786222)
XLA Ops:
  0.7 0.1 eq.50
  0.8 0.8 fusion.19
  1.6 0.1 or_convert_fusion.hits_ref
  1.7 0.2 fusion.7
  1.9 0.7 reshape.78
  2.6 1.4 copy.33
  4.0 1.7 copy.32
  5.7 0.7 fusion.6
  6.5 0.0 copy-start.2
  6.5 0.0 copy-start.3
  6.5 3.4 pad_maximum_fusion.pair_ref
  9.9 0.0 copy-done.3
  9.9 1.1 fusion.4.refs_7_
  11.0 0.0 copy-start.17
  11.1 2.6 reshape.90.idk_ref.refs_16_
  13.7 0.6 pad_maximum_fusion.4.near_ref.refs_14_
  14.4 0.0 copy-start.6
  14.4 0.0 copy-start.8
  14.4 0.0 copy-start.10
  14.4 78.4 %first_stage.1 = (bf16[3,256,384]{2,1,0:T(8,128)(2,1)}, bf16[3,4,256,384]{3,2,1,0:T(8,128)(2,1)}, bf16[3,4,256,384]{3,2,1,0:T(8,128)(2,1)}, bf16[3,256,768]{2,1,...) custom-call(bf16[3,256,768]{2,1,0:T(8,128)(2,1)} %x_ref.3, ...), custom_call_target="tpu_custom_call" | custom-call | flops 40000000000 | bytes 10000000 | tf_op jit(solution)/shard_map/first_stage/pallas_call | solution.py:705
  92.8 0.0 copy-done.17
  92.9 0.0 copy-done.15
  92.9 0.0 copy-done.6
  92.9 0.0 copy-done.8
  92.9 0.0 copy-done.10
  92.9 0.0 copy-done.12
  92.9 0.9 fusion.9
  93.8 0.7 copy.36.win_ref
  94.5 1.5 copy.35
  96.0 1.1 copy.38.wout_ref.refs_11_
  97.0 46.1 %front_stage.1 = (bf16[2,192,1536]{2,1,0:T(8,128)(2,1)}, bf16[3,128,768]{2,1,0:T(8,128)(2,1)}, bf16[4,128,768]{2,1,0:T(8,128)(2,1)}, f32[4,1,128]{2,1,0:T(1,128)...) custom-call(bf16[2,192,1536]{2,1,0:T(8,128)(2,1)} %get-tuple-element, ...), custom_call_target="tpu_custom_call" | custom-call | flops 40000000000 | bytes 10000000 | tf_op jit(solution)/shard_map/front_stage/pallas_call | solution.py:1336
  143.2 89.3 %moe_stage.1 = (bf16[4,3,128,768]{3,2,1,0:T(8,128)(2,1)}, bf16[3,4,128,768]{3,2,1,0:T(8,128)(2,1)}, f32[3,4,1,128]{3,2,1,0:T(1,128)}, bf16[2,2,2,192,1536]{4,3,2,1,0:T(8,128)(2,1)}, bf16[2,2,2,192,1536]{4,3,2,1,0:T(8,128)(2,1)}) custom-call(bf16[3,4,128,768]{3,2,1,0:T(8,128)(2,1)} %get-tuple-element.71.refs_0_, f32[3,4,1,128]{3,2,1,0:T(1,128)} %get-tuple-element.72.refs_1_, ...), custom_call_target="tpu_custom_call" | custom-call | flops 72477573120 | bytes 94371840 | tf_op jit(solution)/shard_map/moe_stage/pallas_call | solution.py:1573
  232.5 5.2 %convert_add_fusion = f32[2,2,2,192,1536]{4,3,2,1,0:T(8,128)S(1)} fusion(bf16[2,2,2,192,1536]{4,3,2,1,0:T(8,128)(2,1)} %get-tuple-element.86, bf16[2,2,2,192,1536]{4,3,2,1,0:T(8,128)(2,1)} %get-tuple-element.85), kind=kLoop, calls=%fused_computation | loop fusion | flops 7077888 | bytes 18874368 | tf_op jit(solution)/shard_map/add | solution.py:1748
  237.7 0.0 copy-start
  237.7 3.7 copy-done
  241.4 1.7 fusion.1
  243.1 2.6 collective-permute-start
  245.7 80.2 %back_stage.1 = (bf16[3,256,768]{2,1,0:T(8,128)(2,1)}, f32[3,256,768]{2,1,0:T(8,128)}, bf16[3,256,768]{2,1,0:T(8,128)(2,1)}, bf16[3,3,256,384]{3,2,1,0:T(8,128)(...) custom-call(f32[3,256,768]{2,1,0:T(8,128)} %get-tuple-element.67.refs_0_, ...), custom_call_target="tpu_custom_call" | custom-call | flops 60000002048 | bytes 10000000 | tf_op jit(solution)/shard_map/back_stage/pallas_call | solution.py:958
  325.8 0.0 collective-permute-done
  325.8 3.8 fusion
  329.7 0.0 copy-start.11
  329.7 0.1 fusion.2
  329.9 0.1 collective-permute-start.1
  329.9 0.6 copy-done.7
  330.6 0.1 copy-done.9
  330.7 0.1 copy-done.11
  330.8 0.1 copy-done.13
  330.9 0.1 copy-done.21
  330.9 0.3 convolution_bitcast_fusion
  331.2 0.7 select_maximum_fusion.small_ref
  331.9 56.3 %last_stage.1 = (f32[4,192,384]{2,1,0:T(8,128)}, f32[192,8]{1,0:T(8,128)}, f32[1,192]{1,0:T(1,128)}, f32[1,192]{1,0:T(1,128)}, f32[8,6]{1,0:T(8,128)}, /*index=5*/f32[3,256,768]{2,1,0:T(8,128)}) custom-call(bf16[768,768]{1,0:T(8,128)(2,1)} %bitcast.78, bf16[3,768,384]{2,1,0:T(8,128)(2,1)} %bitcast.77, bf16[768,768]{1,0:T(8,128)(2,1)} %bitcast.79, ...), custom_call_target="tpu_custom_call" | custom-call | flops 1811939328 | bytes 4718592 | tf_op jit(solution)/shard_map/last_stage/pallas_call | solution.py:1158
  388.2 1.3 copy.43
  389.5 1.6 copy.44
  391.1 0.0 collective-permute-done.1
  391.1 1.7 slice_bitcast_fusion.4
  392.8 2.3 slice_bitcast_fusion.3
  395.1 0.3 bitcast_convert_fusion
  395.3 0.5 maximum_select_fusion
  395.9 2.6 slice_bitcast_fusion.1
  398.5 1.0 copy.61
  399.5 1.1 copy-done.4
  400.6 1.4 copy.62
  402.0 0.6 copy.63
  402.5 0.6 copy.64
  (33 shorter events, 0.2 us)
Async XLA Ops:
  1.7 12.0 %copy-start.14 = (f32[3,8,256]{2,1,0:T(8,128)}, f32[3,8,256]{2,1,0:T(8,128)S(1)}, u32[]{:S(2)}) copy-start(f32[3,8,256]{2,1,0:T(8,128)S(1)} %or_convert_fusion.hits_ref) | copy-start | bytes 73732
  6.5 3.4 copy-start.2
  6.5 3.4 copy-start.3
  11.0 81.8 %copy-start.17 = (s32[3,1,256]{2,1,0:T(1,128)}, s32[3,1,256]{2,1,0:T(1,128)S(1)}, u32[]{:S(2)}) copy-start(s32[3,1,256]{2,1,0:T(1,128)S(1)} %get-tuple-element.135.idq_ref.refs_15_) | copy-start | bytes 9220
  13.7 79.2 %copy-start.15 = (f32[3,4,256]{2,1,0:T(4,128)}, f32[3,4,256]{2,1,0:T(4,128)S(1)}, u32[]{:S(2)}) copy-start(f32[3,4,256]{2,1,0:T(4,128)S(1)} %slice_select_fusion.place_ref.refs_13_) | copy-start | bytes 36868
  14.4 78.5 %copy-start.6 = (f32[1,512,32]{1,2,0:T(8,128)}, f32[1,512,32]{1,2,0:T(8,128)S(1)}, u32[]{:S(2)}) copy-start(f32[1,512,32]{1,2,0:T(8,128)S(1)} %get-tuple-element.128) | copy-start | bytes 196612
  14.4 78.5 %copy-start.8 = (f32[1,512,32]{1,2,0:T(8,128)}, f32[1,512,32]{1,2,0:T(8,128)S(1)}, u32[]{:S(2)}) copy-start(f32[1,512,32]{1,2,0:T(8,128)S(1)} %get-tuple-element.129) | copy-start | bytes 196612
  14.4 78.5 %copy-start.10 = (f32[1,512,32]{1,2,0:T(8,128)}, f32[1,512,32]{1,2,0:T(8,128)S(1)}, u32[]{:S(2)}) copy-start(f32[1,512,32]{1,2,0:T(8,128)S(1)} %get-tuple-element.130) | copy-start | bytes 196612
  14.4 78.5 %copy-start.12 = (f32[1,512,32]{1,2,0:T(8,128)}, f32[1,512,32]{1,2,0:T(8,128)S(1)}, u32[]{:S(2)}) copy-start(f32[1,512,32]{1,2,0:T(8,128)S(1)} %get-tuple-element.131) | copy-start | bytes 196612
  237.7 3.7 copy-start
  243.1 82.7 %collective-permute-start = (bf16[2,2,192,1536]{3,2,1,0:T(8,128)(2,1)}, bf16[2,2,192,1536]{3,2,1,0:T(8,128)(2,1)}, u32[]{:S(2)}, u32[]{:S(2)}) collective-permute-start(bf16[2,2,192,1536]{3,2,1,0:T(8,128)(2,1)} %fusion.1), channel_id=1, source_target_pairs={{0,4},{2,6},{4,0},{6,2},{1,5},{3,7},{5,1},{7,3},{8,12},{10,14},{12... | collective-permute-start | bytes 7077896 | tf_op jit(solution)/shard_map/ppermute | solution.py:1614
  329.6 2.3 copy-start.1
  329.6 0.9 copy-start.7
  329.7 1.0 copy-start.9
  329.7 1.1 copy-start.11
  329.7 1.2 copy-start.13
  329.7 1.2 copy-start.21
  329.7 1.5 copy-start.16
  329.7 1.5 copy-start.18
  329.9 61.2 %collective-permute-start.1 = (bf16[2,192,1536]{2,1,0:T(8,128)(2,1)S(1)}, bf16[2,192,1536]{2,1,0:T(8,128)(2,1)S(1)}, u32[]{:S(2)}, u32[]{:S(2)}) collective-permute-start(bf16[2,192,1536]{2,1,0:T(8,128)(2,1)S(1)} %fusion.2), channel_id=1, source_target_pairs={{0,1},{1,0},{2,3},{3,2},{4,5},{5,4},{6,7},{7,6},{8,9},{9,8},{10,11... | collective-permute-start | bytes 3538952 | tf_op jit(solution)/shard_map/ppermute | solution.py:1614
  392.8 2.6 slice-start
  395.9 2.6 copy-start.5
  398.5 2.1 copy-start.4
  400.6 1.4 copy-start.20
  400.6 2.0 copy-start.19

commit v5 on v4

--- a/solution.py
+++ b/solution.py
@@ -15,6 +15,7 @@
 BF16 = jnp.bfloat16
 F32 = jnp.float32
 EARLY = 50
+FIRST = 1
 VMEM_BYTES = 60 * 1024 * 1024
 GELU_C = 0.7978845608028654
 GELU_A = 0.044715
@@ -516,10 +517,10 @@
 
 def first_kernel(
     seqs, cap, tok_ref, wqkv_ref, wout_ref, table_ref, ga_ref, gm_ref, router_ref, pair_ref, near_ref, cot_ref,
-    q_ref, k_ref, v_ref, normed_ref, wqkv_out, wout_out, table_out, gain_ref, gm_out, router_out, got_out, far_out,
+    q_ref, k_ref, v_ref, normed_ref, wqkv_out, wout_out, table_out, gain_ref, gm_out, router_out, got_out,
     slots_ref, cot_out,
     tok_all, n_all, ga_all, gm_all, router_all,
-    z_send, z_recv, f_send, f_recv, t_send, t_recv, y_send, y_recv, l_sem, e_sems, c_sems,
+    z_send, z_recv, f_send, f_recv, t_send, t_recv, y_send, y_recv, l_sem, e_sems, c_sems, wout_all,
 ):
     dp = lax.axis_index("dp")
     ctx = lax.axis_index("ctx")
@@ -548,7 +549,7 @@
                 z_send.at[4, b - 1], z_recv.at[4, b - 1], **to,
             ),
             remote(
-                wout_ref.at[o_rows(core)], wout_out.at[dp, o_rows(core)],
+                wout_ref.at[o_rows(core)], wout_all.at[dp, o_rows(core)],
                 z_send.at[5, b - 1], z_recv.at[5, b - 1], **to,
             ),
         ]
@@ -561,8 +562,7 @@
     beside.start()
     across = [remote(tok_ref.at[s], tok_all.at[2, s], y_send.at[s], y_recv.at[s], ctx=ctx ^ 2) for s in range(seqs)]
     expert_copies = [
-        remote(pair_ref.at[1 - tp], got_out, e_sems.at[0, 0], e_sems.at[1, 0], tp=tp ^ 1),
-        remote(pair_ref.at[tp], far_out, e_sems.at[0, 1], e_sems.at[1, 1], ctx=ctx ^ 2),
+        remote(pair_ref.at[1 - tp], got_out, e_sems.at[0], e_sems.at[1], tp=tp ^ 1),
     ]
     for copy in across + expert_copies:
         copy.start()
@@ -573,7 +573,7 @@
         pltpu.make_async_copy(table_ref, table_out.at[dp], l_sem.at[3]),
         pltpu.make_async_copy(router_ref, router_all.at[dp], l_sem.at[4]),
         pltpu.make_async_copy(wqkv_ref, wqkv_out.at[:, pl.ds(pl.multiple_of(dp * rows, 16), rows)], l_sem.at[5]),
-        pltpu.make_async_copy(wout_ref, wout_out.at[dp], l_sem.at[6]),
+        pltpu.make_async_copy(wout_ref, wout_all.at[dp], l_sem.at[6]),
     ]
     for copy in own:
         copy.start()
@@ -590,7 +590,7 @@
         pick = jnp.concatenate([jnp.where(p, 1.0, 0.0).astype(BF16) for p in picks], axis=0)
         slots_ref[:, s] = dot(pick, cot_ref[s]).astype(BF16).reshape(groups, cap, cot_ref.shape[2])
 
-        @pl.when(s < seqs - 1)
+        @pl.when(s < FIRST)
         def _():
             for b in (3, 2, 1):
                 cot_copy(s, b).start()
@@ -651,12 +651,13 @@
             if f == 0:
                 ref = wqkv_out.at[:, w_rows(dp ^ b, core)]
             else:
-                ref = wout_out.at[dp ^ b, o_rows(core)]
+                ref = wout_all.at[dp ^ b, o_rows(core)]
             copy = remote(ref, ref, f_send.at[f, b - 1], f_recv.at[f, b - 1], ctx=ctx ^ 1)
             copy.start()
             forwards.append(copy)
     for copy in forwards:
         copy.wait_recv()
+    wout_out[...] = jnp.concatenate([wout_all[d] for d in range(wout_all.shape[0])], axis=1)
 
     def own_q(s, carry):
         q_ref[s] = (dot(n_all[0, s], wqkv_out[0]).astype(BF16) * (HD ** (-0.5))).astype(BF16)
@@ -684,7 +685,7 @@
     lax.fori_loop(0, seqs, others, 0)
     for copy in expert_copies:
         copy.wait()
-    for s in range(seqs - 1):
+    for s in range(FIRST):
         for b in (3, 2, 1):
             cot_copy(s, b).wait()
     for group in small:
@@ -706,22 +707,21 @@
         functools.partial(first_kernel, seqs, cap),
         name="first_stage",
         in_specs=[any_spec] * 8 + [vmem] * 2,
-        out_specs=[vmem] * 10 + [any_spec] * 2 + [vmem, any_spec],
+        out_specs=[vmem] * 10 + [any_spec, vmem, any_spec],
         out_shape=[
             jax.ShapeDtypeStruct((seqs, stretch, local), BF16),
             jax.ShapeDtypeStruct((seqs, 4, stretch, local), BF16),
             jax.ShapeDtypeStruct((seqs, 4, stretch, local), BF16),
             jax.ShapeDtypeStruct((seqs, stretch, width), BF16),
             jax.ShapeDtypeStruct((3, width, local), BF16),
-            jax.ShapeDtypeStruct((dp,) + wout.shape, BF16),
+            jax.ShapeDtypeStruct((wout.shape[0], width), BF16),
             jax.ShapeDtypeStruct((dp,) + table.shape, BF16),
             jax.ShapeDtypeStruct((1, width), F32),
             jax.ShapeDtypeStruct((1, width), BF16),
             jax.ShapeDtypeStruct((experts_n, width), BF16),
             jax.ShapeDtypeStruct(expert_pair.shape[1:], BF16),
-            jax.ShapeDtypeStruct(expert_pair.shape[1:], BF16),
             jax.ShapeDtypeStruct((dp, seqs, cap, width), BF16),
-            jax.ShapeDtypeStruct((dp - 1, seqs - 1, cap, width), BF16),
+            jax.ShapeDtypeStruct((dp - 1, FIRST, cap, width), BF16),
         ],
         scratch_shapes=[
             pltpu.VMEM((4, seqs, stretch, width), BF16),
@@ -730,11 +730,18 @@
             pltpu.VMEM((dp, 1, rows), BF16),
             pltpu.VMEM((dp, rows, experts_n), BF16),
             dma((6, 3)), dma((6, 3)), dma((2, 3)), dma((2, 3)), dma((1 + seqs,)), dma((1 + seqs,)),
-            dma((seqs,)), dma((seqs,)), dma((7,)), dma((2, 2)), dma((2, seqs - 1, 3)),
+            dma((seqs,)), dma((seqs,)), dma((7,)), dma((2,)), dma((2, FIRST, 3)),
+            pltpu.VMEM((dp,) + wout.shape, BF16),
         ],
         compiler_params=pltpu.CompilerParams(vmem_limit_bytes=VMEM_BYTES, collective_id=0, has_side_effects=True),
         cost_estimate=cost(40 * 10**9, 10**7),
     )(tokens, wqkv, wout, table, gain_attn, gain_moe, router, expert_pair, near, cot)
+
+
+def block_mask(keys, queries):
+    ones = jnp.ones(queries.shape, BF16)
+    spread = lax.dot_general(keys, ones, (((0,), (0,)), ((), ())), preferred_element_type=F32)
+    return jnp.where(spread <= queries, 0.0, MASKED)
 
 
 def back_kernel(seqs, groups, cap, *refs):
@@ -854,7 +861,7 @@
         out_copy(s).start()
 
     def attention_back(s):
-        mask_v[...] = jnp.where(idk_ref[s] <= idq_ref[s], 0.0, MASKED)
+        mask_v[...] = block_mask(idk_ref[s], idq_ref[s])
 
         def pair(p, carry):
             lanes = pl.ds(pl.multiple_of(p * 2 * HD, 2 * HD), 2 * HD)
@@ -1195,9 +1202,9 @@
 
 def front_kernel(
     seqs, groups, cap,
-    got_ref, cot_ref, q_ref, k_ref, v_ref, win_ref, idq_ref, idk_ref, x_ref, wout_ref, gain_ref, router_ref,
+    pair_ref, got_ref, cot_ref, q_ref, k_ref, v_ref, win_ref, idq_ref, idk_ref, x_ref, wout_ref, gain_ref, router_ref,
     hits_ref, place_ref,
-    far_out, cot_out, row_out, gate_out, bias_ref, att_ref, lse_ref, mid_ref, moe_ref, gates_ref, send_ref, slot_ref,
+    near_out, far_out, cot_out, row_out, gate_out, bias_ref, att_ref, lse_ref, mid_ref, moe_ref, gates_ref, send_ref, slot_ref,
     wout_other, att_other, mask_ref, w_sems, x_sems, z_sems, r_sems, g_sems, own_sems,
 ):
     dp = lax.axis_index("dp")
@@ -1207,14 +1214,21 @@
     width = x_ref.shape[2]
     local = q_ref.shape[2]
     pairs = local // (2 * HD)
-    far_copy = remote(got_ref, far_out, w_sems.at[0, 0], w_sems.at[1, 0], ctx=ctx ^ 2)
+    far_copies = [
+        remote(pair_ref.at[tp], near_out, w_sems.at[0, 2], w_sems.at[1, 2], ctx=ctx ^ 2),
+        remote(got_ref, far_out, w_sems.at[0, 0], w_sems.at[1, 0], ctx=ctx ^ 2),
+    ]
     wout_copy = remote(wout_ref, wout_other, w_sems.at[0, 1], w_sems.at[1, 1], tp=tp ^ 1)
     order = tuple(range(groups - 1, 0, -1))
     cot_copies = [
-        remote(cot_ref.at[b, seqs - 1], cot_out.at[b - 1], z_sems.at[0, b - 1], z_sems.at[1, b - 1], dp=dp ^ b)
+        remote(
+            cot_ref.at[b, s], cot_out.at[b - 1, s - FIRST],
+            z_sems.at[0, s - FIRST, b - 1], z_sems.at[1, s - FIRST, b - 1], dp=dp ^ b,
+        )
+        for s in range(FIRST, seqs)
         for b in order
     ]
-    for copy in [far_copy, wout_copy] + cot_copies:
+    for copy in [wout_copy] + far_copies + cot_copies:
         copy.start()
 
     def expand(head, carry):
@@ -1243,7 +1257,7 @@
         return pltpu.make_async_copy(slot_ref.at[0, dp], gate_out.at[dp], own_sems.at[1])
 
     def attention(s):
-        mask_ref[...] = jnp.where(idk_ref[s] <= idq_ref[s], 0.0, MASKED)
+        mask_ref[...] = block_mask(idk_ref[s], idq_ref[s])
 
         def pair(p, carry):
             lanes = pl.ds(pl.multiple_of(p * 2 * HD, 2 * HD), 2 * HD)
@@ -1316,14 +1330,14 @@
         row_copy(b).wait()
     own_row().wait()
     own_gate().wait()
-    for copy in [far_copy] + cot_copies:
+    for copy in far_copies + cot_copies:
         copy.wait()
     wout_copy.wait_send()
     for s in range(seqs):
         att_copy(s).wait_send()
 
 
-def front_stage(got, cot, q, k, v, windows, ids_query, ids_key, x, wout, gain, router, hits, places, cap):
+def front_stage(pair, got, cot, q, k, v, windows, ids_query, ids_key, x, wout, gain, router, hits, places, cap):
     seqs, stretch, width = x.shape
     groups = places.shape[1]
     local = q.shape[2]
@@ -1336,11 +1350,12 @@
     return pl.pallas_call(
         functools.partial(front_kernel, seqs, groups, cap),
         name="front_stage",
-        in_specs=[any_spec] * 2 + [vmem] * 12,
-        out_specs=[any_spec] * 3 + [vmem] * 9,
+        in_specs=[any_spec] * 3 + [vmem] * 12,
+        out_specs=[any_spec] * 4 + [vmem] * 9,
         out_shape=[
             jax.ShapeDtypeStruct(got.shape, BF16),
-            jax.ShapeDtypeStruct((groups - 1, cap, width), BF16),
+            jax.ShapeDtypeStruct(got.shape, BF16),
+            jax.ShapeDtypeStruct((groups - 1, seqs - FIRST, cap, width), BF16),
             jax.ShapeDtypeStruct((groups, cap, width), BF16),
             jax.ShapeDtypeStruct((groups, 1, cap), F32),
             jax.ShapeDtypeStruct((2 * pairs, length, stretch), BF16),
@@ -1356,11 +1371,12 @@
             pltpu.VMEM((local, width), BF16),
             pltpu.VMEM((seqs, stretch, local), BF16),
             pltpu.VMEM((length, stretch), F32),
-            dma((2, 2)), dma((2, seqs)), dma((2, groups - 1)), dma((2, groups - 1)), dma((2, groups - 1)), dma((2,)),
+            dma((2, 3)), dma((2, seqs)), dma((2, seqs - FIRST, groups - 1)), dma((2, groups - 1)), dma((2, groups - 1)),
+            dma((2,)),
         ],
         compiler_params=pltpu.CompilerParams(vmem_limit_bytes=VMEM_BYTES, collective_id=4, has_side_effects=True),
         cost_estimate=cost(4 * 10**10, 10**7),
-    )(got, cot, q, k, v, windows, ids_query, ids_key, x, wout, gain, router, hits, places)
+    )(pair, got, cot, q, k, v, windows, ids_query, ids_key, x, wout, gain, router, hits, places)
 
 
 def moe_kernel(
@@ -1418,9 +1434,11 @@
     local.append(pltpu.make_async_copy(slots_ref.at[0], g_all.at[dp], cot_sems.at[0, 0]))
     for b in range(1, groups):
         local.append(
-            pltpu.make_async_copy(cot_ref.at[b - 1], g_all.at[dp ^ b, pl.ds(0, seqs - 1)], cot_sems.at[0, b])
+            pltpu.make_async_copy(cot_ref.at[b - 1], g_all.at[dp ^ b, pl.ds(0, FIRST)], cot_sems.at[0, b])
         )
-        local.append(pltpu.make_async_copy(last_ref.at[b - 1], g_all.at[dp ^ b, seqs - 1], cot_sems.at[1, b]))
+        local.append(
+            pltpu.make_async_copy(last_ref.at[b - 1], g_all.at[dp ^ b, pl.ds(FIRST, seqs - FIRST)], cot_sems.at[1, b])
+        )
     for copy in local:
         copy.start()
     for copy in local:
@@ -1675,14 +1693,13 @@
         me = lax.axis_index("dp")
         near_places = jnp.stack([lax.dynamic_index_in_dim(places, me ^ b, 1, keepdims=False) for b in range(dp)], axis=1)
         (
-            queries, keys, values, own_normed, wqkv, wout_parts, table, gain_attn, gain_moe, router, got, far_keep,
+            queries, keys, values, own_normed, wqkv, wout_own, table, gain_attn, gain_moe, router, got,
             cot_slots, cot_in,
         ) = first_stage(
             tokens_in, w_qkv[0], w_attn_out[0], bias_table[0], attn_gain, moe_gain, w_router[0], pair,
             near_places, cotangent, cap,
         )
         keep = lax.dynamic_index_in_dim(pair, tp, 0, keepdims=False)
-        wout_own = wout_parts.transpose(1, 0, 2).reshape(local, width)
         table = table.reshape(NB, heads)
         keys = keys.reshape(seqs, 4 * stretch, local)
         values = values.reshape(seqs, 4 * stretch, local)
@@ -1705,13 +1722,18 @@
     ids = block_ids.reshape(seqs, 4, stretch)
     ids_pieces = [lax.dynamic_index_in_dim(ids, ctx ^ b, 1, keepdims=False) for b in range(4)]
     ids_query = ids_pieces[0].reshape(seqs, 1, stretch)
-    ids_key = jnp.stack(ids_pieces, axis=1).reshape(seqs, 4 * stretch, 1)
+    ids_key = jnp.stack(ids_pieces, axis=1)
+    if fits:
+        ids_query = ids_query.astype(F32)
+        ids_key = ids_key.astype(BF16).reshape(seqs, 1, 4 * stretch)
+    else:
+        ids_key = ids_key.reshape(seqs, 4 * stretch, 1)
 
     if fits:
         (
-            far_got, cot_last, row, row_gate, bias, attended, lse, mids, moes, gates, send, slot_gate,
+            far_keep, far_got, cot_last, row, row_gate, bias, attended, lse, mids, moes, gates, send, slot_gate,
         ) = front_stage(
-            got, cot_slots, queries, keys, values, windows, ids_query, ids_key, tokens_in, wout_own, gain_moe, router,
+            pair, got, cot_slots, queries, keys, values, windows, ids_query, ids_key, tokens_in, wout_own, gain_moe, router,
             hits, places, cap,
         )
         parts, returned_din, returned_h, kept, given = moe_stage(
@@ -1745,8 +1767,11 @@
             partials.append(all_to_all_dp(part))
         kept, given = acc[:, 0::2], flip(acc[:, 1::2], "ctx", 1)
 
-    beside_sum = kept.astype(F32) + given.astype(F32)
-    far_sum = flip(beside_sum[:, 1].astype(BF16), "ctx", 2)
+    far_other = flip((kept[1, 1].astype(F32) + given[1, 1].astype(F32)).astype(BF16), "ctx", 2)
+    far_send = (kept[0, 1].astype(F32) + given[0, 1].astype(F32)).astype(BF16)
+
+    def summed(half, far):
+        return (kept[half, 0].astype(F32) + given[half, 0].astype(F32)) + far.astype(F32)
 
     hits_of = (heads, 4, 2 * stretch)
     if fits:
@@ -1754,9 +1779,9 @@
             mids, moes, gates, lse, returned_din, parts, queries, keys, values, bias, cotangent, wout_own,
             returned_h, places, near_places, ids_query, ids_key, router, gain_moe,
         )
-        far_sum, grad_proj = lax.optimization_barrier((far_sum, grad_proj))
-        mine = beside_sum[:, 0] + far_sum.astype(F32)
-        other = flip(mine[1].astype(BF16), "tp", 1)
+        far_other, far_send, grad_proj = lax.optimization_barrier((far_other, far_send, grad_proj))
+        far_mine = flip(far_send, "ctx", 2)
+        other = flip(summed(1, far_other).astype(BF16), "tp", 1)
         grad_proj = grad_proj.reshape(3, seqs * stretch, local)
         dattn = dattn.reshape(seqs * stretch, width)
         grad_table = jnp.einsum("bmn,hbm->nh", hot_windows, rel_grad.reshape(hits_of), precision=FULL_PRECISION)
@@ -1772,12 +1797,12 @@
             own_normed, grad_proj, dattn, attended.reshape(seqs * stretch, local), small, wqkv, gmid, tokens_in, gain_attn,
             dp, NB // dp, heads, expert_count,
         )
-        other, wide = lax.optimization_barrier((other, wide))
+        other, far_mine, wide = lax.optimization_barrier((other, far_mine, wide))
         g_qkv = wide[:3]
         g_wout = wide[3].T
     else:
-        mine = beside_sum[:, 0] + far_sum.astype(F32)
-        other = flip(mine[1].astype(BF16), "tp", 1)
+        far_mine = flip(far_send, "ctx", 2)
+        other = flip(summed(1, far_other).astype(BF16), "tp", 1)
         tokens_out, gmids = [], []
         projections = []
         rel_grad = 0.0
@@ -1833,10 +1858,16 @@
         g_moe = reduced(gain_moe_grad, 1)
         g_router = reduced(router_grad, 0)
         tokens_out = jnp.stack(tokens_out)
+    mine = summed(0, far_mine)
     other = other.astype(F32)
-    ordered = jnp.where(tp == 0, jnp.stack([mine[0], other]), jnp.stack([other, mine[0]]))
-    grad_expert_in = ordered[:, 0]
-    grad_expert_out = ordered[:, 1].transpose(0, 2, 1)
+
+    def by_expert(index):
+        return jnp.where(
+            tp == 0, jnp.stack([mine[index], other[index]]), jnp.stack([other[index], mine[index]])
+        )
+
+    grad_expert_in = by_expert(0)
+    grad_expert_out = by_expert(1).transpose(0, 2, 1)
     return (
         tokens_out,
         grad_tokens.reshape(seqs, stretch, width),

time: 404 us -> 382 us (0.946)
  local copies, waits for them, and re-layouts: 31.3 us -> 17.9 us
  Pallas kernels: 350 us -> 338 us
  other arithmetic: 16.5 us -> 20.6 us
    pallas_call x1, Pallas kernels: 46.1 us -> 61.2 us  [front_stage(): pl.pallas_call(functools.partial(front_kernel, seqs, groups, cap), name='...]
    pallas_call x1, Pallas kernels: 78.4 us -> 65.2 us  [first_stage(): pl.pallas_call(functools.partial(first_kernel, seqs, cap), name='first_st...]
    pallas_call x1, Pallas kernels: 80.2 us -> 67.5 us  [back_stage(): pl.pallas_call(functools.partial(back_kernel, seqs, groups, cap), name='b...]
    convert_element_type x0 -> x3, other arithmetic: none -> 8.16 us  [the longest x1 4.36 us: on_device(): far_send = (kept[0, 1].astype(F32) + given[0, 1].astype(F32)).astype(BF16)]
    add x2 -> x1, other arithmetic: 9.03 us -> 2.05 us  [summed(): kept[half, 0].astype(F32) + given[half, 0].astype(F32) + far.astype(F32)]
    unnamed x53 -> x49, local copies, waits for them, and re-layouts: 15.4 us -> 10.8 us
  transfers between devices with their start and end apart: 2 -> 3, of which waited for: 0 -> 0; matrix products, arithmetic and copies ran while one was open for 1% -> 1% of each run, Pallas kernels for 34% -> 32%
where the time goes in v5:
time: 382 us
  Pallas kernels  338 us (88%)
  other arithmetic  20.6 us (5%)
  local copies, waits for them, and re-layouts  17.9 us (5%)
    pallas_call x1, Pallas kernels, moe_stage(): pl.pallas_call(functools.partial(moe_kernel, seqs, groups, cap, tile), na...  88.7 us
    pallas_call x1, Pallas kernels, back_stage(): pl.pallas_call(functools.partial(back_kernel, seqs, groups, cap), name='b...  67.5 us
    pallas_call x1, Pallas kernels, first_stage(): pl.pallas_call(functools.partial(first_kernel, seqs, cap), name='first_st...  65.2 us
    pallas_call x1, Pallas kernels, front_stage(): pl.pallas_call(functools.partial(front_kernel, seqs, groups, cap), name='...  61.2 us
    pallas_call x1, Pallas kernels, last_stage(): pl.pallas_call(last_kernel, name='last_stage', in_specs=[vmem] * 9, out_s...  55.9 us
    unnamed x49, local copies, waits for them, and re-layouts  10.8 us
  transfers between devices with their start and end apart: 3, of which 0 were waited for; matrix products, arithmetic and copies ran while one was open for 1% of the time, Pallas kernels for 32%

profile of v5, /device:TPU:0, one launch (start us, length us, event | category | flops | bytes accessed | tf_op | source)
XLA Modules:
  0.0 381.7 jit_solution(15924835789466817576)
XLA Ops:
  0.7 0.1 eq.51
  0.8 0.8 fusion.26
  1.6 0.1 or_convert_fusion.hits_ref
  1.7 0.2 fusion.8
  1.9 0.7 reshape.151
  2.6 0.6 fusion.21
  3.2 0.6 convert_element_type.108.idk_ref.refs_16_
  3.8 1.4 copy.31
  5.3 1.7 copy.30
  7.0 0.7 fusion.7
  7.7 0.0 copy-start
  7.7 0.0 copy-start.1
  7.7 3.4 pad_maximum_fusion.pair_ref
  11.1 1.1 fusion.5.refs_7_
  12.3 0.0 copy-done.13
  12.3 0.6 pad_maximum_fusion.4.near_ref.refs_14_
  12.9 0.0 copy-start.5
  13.0 0.0 copy-start.7
  13.0 0.0 copy-start.9
  13.0 0.0 copy-start.11
  13.0 65.2 %first_stage.1 = (bf16[3,256,384]{2,1,0:T(8,128)(2,1)}, bf16[3,4,256,384]{3,2,1,0:T(8,128)(2,1)}, bf16[3,4,256,384]{3,2,1,0:T(8,128)(2,1)}, bf16[3,256,768]{2,1,...) custom-call(bf16[3,256,768]{2,1,0:T(8,128)(2,1)} %x_ref.3, ...), custom_call_target="tpu_custom_call" | custom-call | flops 40000000000 | bytes 10000000 | tf_op jit(solution)/shard_map/first_stage/pallas_call | solution.py:706
  78.3 0.9 fusion.10
  79.2 0.7 copy.33.win_ref
  79.9 61.2 %front_stage.1 = (bf16[2,192,1536]{2,1,0:T(8,128)(2,1)}, bf16[2,192,1536]{2,1,0:T(8,128)(2,1)}, bf16[3,2,128,768]{3,2,1,0:T(8,128)(2,1)}, bf16[4,128,768]{2,1,0:...) custom-call(bf16[2,2,192,1536]{3,2,1,0:T(8,128)(2,1)} %pad_maximum_f, ...), custom_call_target="tpu_custom_call" | custom-call | flops 40000000000 | bytes 10000000 | tf_op jit(solution)/shard_map/front_stage/pallas_call | solution.py:1350
  141.0 88.7 %moe_stage.1 = (bf16[4,3,128,768]{3,2,1,0:T(8,128)(2,1)}, bf16[3,4,128,768]{3,2,1,0:T(8,128)(2,1)}, f32[3,4,1,128]{3,2,1,0:T(1,128)}, bf16[2,2,2,192,1536]{4,3,2,1,0:T(8,128)(2,1)}, bf16[2,2,2,192,1536]{4,3,2,1,0:T(8,128)(2,1)}) custom-call(bf16[3,4,128,768]{3,2,1,0:T(8,128)(2,1)} %get-tuple-element.73.refs_0_, f32[3,4,1,128]{3,2,1,0:T(1,128)} %get-tuple-element.74.refs_1_, ...), custom_call_target="tpu_custom_call" | custom-call | flops 72477573120 | bytes 94371840 | tf_op jit(solution)/shard_map/moe_stage/pallas_call | solution.py:1591
  229.7 4.4 %fusion.3 = (bf16[2,192,1536]{2,1,0:T(8,128)(2,1)}, bf16[2,192,1536]{2,1,0:T(8,128)(2,1)}) fusion(bf16[2,2,2,192,1536]{4,3,2,1,0:T(8,128)(2,1)} %get-tuple-element.88, bf16[2,2,2,192,1536]{4,3,2,1,0:T(8,128)(2,1)} %get-tuple-element.87), kind=kLoop, calls=%fused_computation.12 | loop fusion | flops 4718592 | bytes 7077888 | tf_op jit(solution)/shard_map/convert_element_type | solution.py:1771
  234.1 1.3 collective-permute-start
  235.4 67.5 %back_stage.1 = (bf16[3,256,768]{2,1,0:T(8,128)(2,1)}, f32[3,256,768]{2,1,0:T(8,128)}, bf16[3,256,768]{2,1,0:T(8,128)(2,1)}, bf16[3,3,256,384]{3,2,1,0:T(8,128)(...) custom-call(f32[3,256,768]{2,1,0:T(8,128)} %get-tuple-element.69.refs_0_, ...), custom_call_target="tpu_custom_call" | custom-call | flops 60000002048 | bytes 10000000 | tf_op jit(solution)/shard_map/back_stage/pallas_call | solution.py:965
  302.9 0.0 collective-permute-done
  302.9 0.0 copy-start.3
  302.9 0.0 copy-start.8
  302.9 0.0 copy-start.10
  302.9 0.0 copy-start.12
  302.9 0.0 copy-start.19
  302.9 0.0 copy-start.15
  302.9 0.0 copy-start.16
  303.0 3.5 fusion.1
  306.5 0.5 collective-permute-start.1
  307.0 0.0 copy-done.3
  307.0 0.5 collective-permute-start.2
  307.5 0.0 copy-done.6
  307.5 0.0 copy-done.19
  307.5 0.3 convolution_bitcast_fusion
  307.8 0.7 select_maximum_fusion.small_ref
  308.5 55.9 %last_stage.1 = (f32[4,192,384]{2,1,0:T(8,128)}, f32[192,8]{1,0:T(8,128)}, f32[1,192]{1,0:T(1,128)}, f32[1,192]{1,0:T(1,128)}, f32[8,6]{1,0:T(8,128)}, /*index=5*/f32[3,256,768]{2,1,0:T(8,128)}) custom-call(bf16[768,768]{1,0:T(8,128)(2,1)} %bitcast.74, bf16[3,768,384]{2,1,0:T(8,128)(2,1)} %bitcast.73, bf16[768,768]{1,0:T(8,128)(2,1)} %bitcast.75, ...), custom_call_target="tpu_custom_call" | custom-call | flops 1811939328 | bytes 4718592 | tf_op jit(solution)/shard_map/last_stage/pallas_call | solution.py:1165
  364.4 1.3 copy.37
  365.8 1.6 copy.38
  367.3 0.0 collective-permute-done.1
  367.3 0.0 collective-permute-done.2
  367.3 1.7 slice_bitcast_fusion.3
  369.0 2.1 slice_bitcast_fusion.2
  371.1 0.1 slice.78
  371.3 0.3 convert_element_type.107
  371.6 2.0 bitcast_add_fusion
  373.6 0.2 fusion.25
  373.8 0.1 slice_bitcast_fusion
  373.9 1.6 fusion
  375.5 1.6 maximum_select_fusion
  377.0 0.1 copy-done.4
  377.1 1.0 copy.51
  378.1 1.1 copy-done.2
  379.2 1.4 copy.52
  380.6 0.6 copy.53
  381.2 0.6 copy.54
  (29 shorter events, 0.2 us)
Async XLA Ops:
  1.7 10.6 %copy-start.13 = (f32[3,8,256]{2,1,0:T(8,128)}, f32[3,8,256]{2,1,0:T(8,128)S(1)}, u32[]{:S(2)}) copy-start(f32[3,8,256]{2,1,0:T(8,128)S(1)} %or_convert_fusion.hits_ref) | copy-start | bytes 73732
  7.7 3.4 copy-start
  7.7 3.4 copy-start.1
  12.3 66.0 %copy-start.14 = (f32[3,4,256]{2,1,0:T(4,128)}, f32[3,4,256]{2,1,0:T(4,128)S(1)}, u32[]{:S(2)}) copy-start(f32[3,4,256]{2,1,0:T(4,128)S(1)} %slice_select_fusion.place_ref.refs_13_) | copy-start | bytes 36868
  12.9 65.3 %copy-start.5 = (f32[1,512,32]{1,2,0:T(8,128)}, f32[1,512,32]{1,2,0:T(8,128)S(1)}, u32[]{:S(2)}) copy-start(f32[1,512,32]{1,2,0:T(8,128)S(1)} %get-tuple-element.134) | copy-start | bytes 196612
  13.0 65.3 %copy-start.7 = (f32[1,512,32]{1,2,0:T(8,128)}, f32[1,512,32]{1,2,0:T(8,128)S(1)}, u32[]{:S(2)}) copy-start(f32[1,512,32]{1,2,0:T(8,128)S(1)} %get-tuple-element.135) | copy-start | bytes 196612
  13.0 65.3 %copy-start.9 = (f32[1,512,32]{1,2,0:T(8,128)}, f32[1,512,32]{1,2,0:T(8,128)S(1)}, u32[]{:S(2)}) copy-start(f32[1,512,32]{1,2,0:T(8,128)S(1)} %get-tuple-element.136) | copy-start | bytes 196612
  13.0 65.3 %copy-start.11 = (f32[1,512,32]{1,2,0:T(8,128)}, f32[1,512,32]{1,2,0:T(8,128)S(1)}, u32[]{:S(2)}) copy-start(f32[1,512,32]{1,2,0:T(8,128)S(1)} %get-tuple-element.137) | copy-start | bytes 196612
  234.1 68.8 %collective-permute-start = (bf16[2,192,1536]{2,1,0:T(8,128)(2,1)}, bf16[2,192,1536]{2,1,0:T(8,128)(2,1)}, u32[]{:S(2)}, u32[]{:S(2)}) collective-permute-start(bf16[2,192,1536]{2,1,0:T(8,128)(2,1)} %get-tuple-element.131), channel_id=1, source_target_pairs={{0,4},{2,6},{4,0},{6,2},{1,5},{3,7},{5,1},{7,3},{8,12},{10,14},{12... | collective-permute-start | bytes 3538952 | tf_op jit(solution)/shard_map/ppermute | solution.py:1632
  302.9 4.2 %copy-start.3 = (bf16[2,192,1536]{2,1,0:T(8,128)(2,1)S(1)}, bf16[2,192,1536]{2,1,0:T(8,128)(2,1)}, u32[]{:S(2)}) copy-start(bf16[2,192,1536]{2,1,0:T(8,128)(2,1)} %get-tuple-element.102) | copy-start | bytes 3538948
  302.9 4.6 %copy-start.6 = (f32[1,512,32]{1,2,0:T(8,128)S(1)}, f32[1,512,32]{1,2,0:T(8,128)}, u32[]{:S(2)}) copy-start(f32[1,512,32]{1,2,0:T(8,128)} %copy-done.5) | copy-start | bytes 196612
  302.9 4.6 %copy-start.8 = (f32[1,512,32]{1,2,0:T(8,128)S(1)}, f32[1,512,32]{1,2,0:T(8,128)}, u32[]{:S(2)}) copy-start(f32[1,512,32]{1,2,0:T(8,128)} %copy-done.7) | copy-start | bytes 196612
  302.9 4.6 %copy-start.10 = (f32[1,512,32]{1,2,0:T(8,128)S(1)}, f32[1,512,32]{1,2,0:T(8,128)}, u32[]{:S(2)}) copy-start(f32[1,512,32]{1,2,0:T(8,128)} %copy-done.9) | copy-start | bytes 196612
  302.9 4.6 %copy-start.12 = (f32[1,512,32]{1,2,0:T(8,128)S(1)}, f32[1,512,32]{1,2,0:T(8,128)}, u32[]{:S(2)}) copy-start(f32[1,512,32]{1,2,0:T(8,128)} %copy-done.11) | copy-start | bytes 196612
  302.9 4.6 %copy-start.19 = (f32[3,2,4,512]{3,2,1,0:T(4,128)S(1)}, f32[3,2,4,512]{3,2,1,0:T(4,128)}, u32[]{:S(2)}) copy-start(f32[3,2,4,512]{3,2,1,0:T(4,128)} %get-tuple-element.95) | copy-start | bytes 147460
  302.9 4.9 %copy-start.15 = (f32[8,768]{1,0:T(8,128)S(1)}, f32[8,768]{1,0:T(8,128)}, u32[]{:S(2)}) copy-start(f32[8,768]{1,0:T(8,128)} %get-tuple-element.93) | copy-start | bytes 73732
  302.9 4.9 %copy-start.16 = (f32[1,768]{1,0:T(1,128)S(1)}, f32[1,768]{1,0:T(1,128)}, u32[]{:S(2)}) copy-start(f32[1,768]{1,0:T(1,128)} %get-tuple-element.94) | copy-start | bytes 9220
  306.5 60.8 %collective-permute-start.1 = (bf16[2,192,1536]{2,1,0:T(8,128)(2,1)}, bf16[2,192,1536]{2,1,0:T(8,128)(2,1)S(1)}, u32[]{:S(2)}, u32[]{:S(2)}) collective-permute-start(bf16[2,192,1536]{2,1,0:T(8,128)(2,1)} %fusion.1), channel_id=1, source_target_pairs={{0,1},{1,0},{2,3},{3,2},{4,5},{5,4},{6,7},{7,6},{8,9},{9,8},{10,11... | collective-permute-start | bytes 3538952 | tf_op jit(solution)/shard_map/ppermute | solution.py:1632
  307.0 60.3 %collective-permute-start.2 = (bf16[2,192,1536]{2,1,0:T(8,128)(2,1)S(1)}, bf16[2,192,1536]{2,1,0:T(8,128)(2,1)S(1)}, u32[]{:S(2)}, u32[]{:S(2)}) collective-permute-start(bf16[2,192,1536]{2,1,0:T(8,128)(2,1)S(1)} %copy-done.3), channel_id=1, source_target_pairs={{0,4},{2,6},{4,0},{6,2},{1,5},{3,7},{5,1},{7,3},{8,12},{10,14},{12... | collective-permute-start | bytes 3538952 | tf_op jit(solution)/shard_map/ppermute | solution.py:1632
  375.5 1.6 copy-start.4
  377.1 2.1 copy-start.2
  379.2 1.4 copy-start.18
  379.2 2.0 copy-start.17

commit v6 on v5

--- a/solution.py
+++ b/solution.py
@@ -516,11 +516,11 @@
 
 
 def first_kernel(
-    seqs, cap, tok_ref, wqkv_ref, wout_ref, table_ref, ga_ref, gm_ref, router_ref, pair_ref, near_ref, cot_ref,
+    seqs, cap, tok_ref, wqkv_ref, wout_ref, table_ref, ga_ref, gm_ref, router_ref, win_ref, wot_ref, near_ref, cot_ref,
     q_ref, k_ref, v_ref, normed_ref, wqkv_out, wout_out, table_out, gain_ref, gm_out, router_out, got_out,
     slots_ref, cot_out,
     tok_all, n_all, ga_all, gm_all, router_all,
-    z_send, z_recv, f_send, f_recv, t_send, t_recv, y_send, y_recv, l_sem, e_sems, c_sems, wout_all,
+    z_send, z_recv, f_send, f_recv, t_send, t_recv, y_send, y_recv, l_sem, e_sems, c_sems,
 ):
     dp = lax.axis_index("dp")
     ctx = lax.axis_index("ctx")
@@ -528,14 +528,10 @@
     core = ctx % 2
     rows = wqkv_ref.shape[1]
     half = rows // 2
-    orows = wout_ref.shape[0] // 2
     greet([{"dp": dp ^ b} for b in (1, 2, 3)] + [{"ctx": ctx ^ 1}, {"ctx": ctx ^ 2}, {"tp": tp ^ 1}])
 
     def w_rows(owner, side):
         return pl.ds(pl.multiple_of(owner * rows + side * half, 16), half)
-
-    def o_rows(side):
-        return pl.ds(pl.multiple_of(side * orows, 16), orows)
 
     def z_copies(b):
         to = {"dp": dp ^ b}
@@ -549,7 +545,7 @@
                 z_send.at[4, b - 1], z_recv.at[4, b - 1], **to,
             ),
             remote(
-                wout_ref.at[o_rows(core)], wout_all.at[dp, o_rows(core)],
+                wout_ref.at[pl.ds(pl.multiple_of(core * half, 16), half)], wout_out.at[w_rows(dp, core)],
                 z_send.at[5, b - 1], z_recv.at[5, b - 1], **to,
             ),
         ]
@@ -562,7 +558,8 @@
     beside.start()
     across = [remote(tok_ref.at[s], tok_all.at[2, s], y_send.at[s], y_recv.at[s], ctx=ctx ^ 2) for s in range(seqs)]
     expert_copies = [
-        remote(pair_ref.at[1 - tp], got_out, e_sems.at[0], e_sems.at[1], tp=tp ^ 1),
+        remote(win_ref.at[1 - tp], got_out.at[0], e_sems.at[0, 0], e_sems.at[1, 0], tp=tp ^ 1),
+        remote(wot_ref.at[1 - tp], got_out.at[1], e_sems.at[0, 1], e_sems.at[1, 1], tp=tp ^ 1),
     ]
     for copy in across + expert_copies:
         copy.start()
@@ -573,7 +570,7 @@
         pltpu.make_async_copy(table_ref, table_out.at[dp], l_sem.at[3]),
         pltpu.make_async_copy(router_ref, router_all.at[dp], l_sem.at[4]),
         pltpu.make_async_copy(wqkv_ref, wqkv_out.at[:, pl.ds(pl.multiple_of(dp * rows, 16), rows)], l_sem.at[5]),
-        pltpu.make_async_copy(wout_ref, wout_all.at[dp], l_sem.at[6]),
+        pltpu.make_async_copy(wout_ref, wout_out.at[pl.ds(pl.multiple_of(dp * rows, 16), rows)], l_sem.at[6]),
     ]
     for copy in own:
         copy.start()
@@ -617,13 +614,13 @@
         gain_m = gain_m + dot(gm_all[d], spread)
     gain_ref[...] = gain
     gm_out[...] = gain_m.astype(BF16)
-    experts_n = router_ref.shape[1]
+    experts_n = router_ref.shape[0]
     slot_row = lax.broadcasted_iota(jnp.int32, (experts_n, experts_n), 0)
     slot_col = lax.broadcasted_iota(jnp.int32, (experts_n, experts_n), 1)
     side = slot_row // count
     expert = (slot_row % count) * 2 + (side ^ tp)
     order = jnp.where(slot_col == expert, 1.0, 0.0).astype(BF16)
-    router_out[...] = dot_nt(order, router_all[...].reshape(width, experts_n)).astype(BF16)
+    router_out[...] = dot(order, jnp.concatenate([router_all[d] for d in range(count)], axis=1)).astype(BF16)
 
     def norm_piece(b):
         def body(s, carry):
@@ -645,19 +642,17 @@
     norm_piece(1)
 
     forwards = []
+
+    def forward(kind, ref, b):
+        small[b - 1][kind + 4].wait_recv()
+        copy = remote(ref, ref, f_send.at[kind, b - 1], f_recv.at[kind, b - 1], ctx=ctx ^ 1)
+        copy.start()
+        forwards.append(copy)
+
     for b in (1, 2, 3):
-        for kind, f in ((4, 0), (5, 1)):
-            small[b - 1][kind].wait_recv()
-            if f == 0:
-                ref = wqkv_out.at[:, w_rows(dp ^ b, core)]
-            else:
-                ref = wout_all.at[dp ^ b, o_rows(core)]
-            copy = remote(ref, ref, f_send.at[f, b - 1], f_recv.at[f, b - 1], ctx=ctx ^ 1)
-            copy.start()
-            forwards.append(copy)
+        forward(0, wqkv_out.at[:, w_rows(dp ^ b, core)], b)
     for copy in forwards:
         copy.wait_recv()
-    wout_out[...] = jnp.concatenate([wout_all[d] for d in range(wout_all.shape[0])], axis=1)
 
     def own_q(s, carry):
         q_ref[s] = (dot(n_all[0, s], wqkv_out[0]).astype(BF16) * (HD ** (-0.5))).astype(BF16)
@@ -666,6 +661,8 @@
         return carry
 
     lax.fori_loop(0, seqs, own_q, 0)
+    for b in (1, 2, 3):
+        forward(1, wout_out.at[w_rows(dp ^ b, core)], b)
     later = []
     for s in range(seqs):
         across[s].wait_recv()
@@ -683,6 +680,8 @@
         return carry
 
     lax.fori_loop(0, seqs, others, 0)
+    for copy in forwards[3:]:
+        copy.wait_recv()
     for copy in expert_copies:
         copy.wait()
     for s in range(FIRST):
@@ -695,18 +694,18 @@
         copy.wait_send()
 
 
-def first_stage(tokens, wqkv, wout, table, gain_attn, gain_moe, router, expert_pair, near, cot, cap):
+def first_stage(tokens, wqkv, wout, table, gain_attn, gain_moe, router, w_in, w_out, near, cot, cap):
     seqs, stretch, width = tokens.shape
     count, rows, local = wqkv.shape
     dp = width // rows
-    experts_n = router.shape[1]
+    experts_n = router.shape[0]
     any_spec = pl.BlockSpec(memory_space=pl.ANY)
     vmem = pl.BlockSpec(memory_space=pltpu.VMEM)
     dma = pltpu.SemaphoreType.DMA
     return pl.pallas_call(
         functools.partial(first_kernel, seqs, cap),
         name="first_stage",
-        in_specs=[any_spec] * 8 + [vmem] * 2,
+        in_specs=[any_spec] * 9 + [vmem] * 2,
         out_specs=[vmem] * 10 + [any_spec, vmem, any_spec],
         out_shape=[
             jax.ShapeDtypeStruct((seqs, stretch, local), BF16),
@@ -714,12 +713,12 @@
             jax.ShapeDtypeStruct((seqs, 4, stretch, local), BF16),
             jax.ShapeDtypeStruct((seqs, stretch, width), BF16),
             jax.ShapeDtypeStruct((3, width, local), BF16),
-            jax.ShapeDtypeStruct((wout.shape[0], width), BF16),
+            jax.ShapeDtypeStruct((width, local), BF16),
             jax.ShapeDtypeStruct((dp,) + table.shape, BF16),
             jax.ShapeDtypeStruct((1, width), F32),
             jax.ShapeDtypeStruct((1, width), BF16),
             jax.ShapeDtypeStruct((experts_n, width), BF16),
-            jax.ShapeDtypeStruct(expert_pair.shape[1:], BF16),
+            jax.ShapeDtypeStruct(w_in.shape, BF16),
             jax.ShapeDtypeStruct((dp, seqs, cap, width), BF16),
             jax.ShapeDtypeStruct((dp - 1, FIRST, cap, width), BF16),
         ],
@@ -728,14 +727,13 @@
             pltpu.VMEM((4, seqs, stretch, width), BF16),
             pltpu.VMEM((dp, 1, rows), BF16),
             pltpu.VMEM((dp, 1, rows), BF16),
-            pltpu.VMEM((dp, rows, experts_n), BF16),
+            pltpu.VMEM((dp, experts_n, rows), BF16),
             dma((6, 3)), dma((6, 3)), dma((2, 3)), dma((2, 3)), dma((1 + seqs,)), dma((1 + seqs,)),
-            dma((seqs,)), dma((seqs,)), dma((7,)), dma((2,)), dma((2, FIRST, 3)),
-            pltpu.VMEM((dp,) + wout.shape, BF16),
+            dma((seqs,)), dma((seqs,)), dma((7,)), dma((2, 2)), dma((2, FIRST, 3)),
         ],
         compiler_params=pltpu.CompilerParams(vmem_limit_bytes=VMEM_BYTES, collective_id=0, has_side_effects=True),
         cost_estimate=cost(40 * 10**9, 10**7),
-    )(tokens, wqkv, wout, table, gain_attn, gain_moe, router, expert_pair, near, cot)
+    )(tokens, wqkv, wout, table, gain_attn, gain_moe, router, w_in, w_out, near, cot)
 
 
 def block_mask(keys, queries):
@@ -844,7 +842,7 @@
         gmid_ref[s] = gmid
         dattn = gmid.astype(BF16)
         low_ref[s] = dattn
-        datt_v[...] = dot_nt(dattn, wout_v[...]).astype(BF16)
+        datt_v[...] = dot(dattn, wout_v[...]).astype(BF16)
 
     def core_sum(s):
         core_copy(s).wait_recv()
@@ -955,7 +953,7 @@
 def back_stage(mids, moes, gates, lse, din, parts, q, k, v, bias, cot, wout, h, places, near, ids_query, ids_key, router, gain):
     groups, _, cap, width = parts.shape
     seqs, stretch = mids.shape[:2]
-    local = wout.shape[0]
+    local = wout.shape[1]
     length = k.shape[1]
     pairs = local // (2 * HD)
     experts_n = router.shape[0]
@@ -988,7 +986,7 @@
             pltpu.VMEM((seqs, length, local), BF16),
             pltpu.VMEM((2 * pairs, length, stretch), BF16),
             pltpu.VMEM((seqs, stretch, width), BF16),
-            pltpu.VMEM((local, width), BF16),
+            pltpu.VMEM((width, local), BF16),
             pltpu.VMEM((seqs, stretch, width), BF16),
             pltpu.VMEM((seqs, stretch, width), BF16),
             pltpu.VMEM((seqs, groups, stretch), F32),
@@ -1136,19 +1134,19 @@
     row = lax.broadcasted_iota(jnp.int32, (piece, width), 0)
     col = lax.broadcasted_iota(jnp.int32, (piece, width), 1)
     select = jnp.where(col == row + dp * piece, 1.0, 0.0)
-    experts_n = router_out.shape[1]
+    experts_n = router_out.shape[0]
     e_row = lax.broadcasted_iota(jnp.int32, (experts_n, experts_n), 0)
     e_col = lax.broadcasted_iota(jnp.int32, (experts_n, experts_n), 1)
     slot = ((e_row % 2) ^ tp) * count + e_row // 2
     arranged = exact(jnp.where(e_col == slot, 1.0, 0.0), small[:experts_n], ((1,), (0,)))
-    router_out[...] = exact(select, arranged, ((1,), (1,)))
+    router_out[...] = exact(arranged, select, ((1,), (1,)))
     gains = exact(small[8:16], select, ((1,), (1,)))
     gm_out[...] = gains[0:1]
     ga_out[...] = gains[1:2]
-    t_rows, heads = table_out.shape
+    heads, t_rows = table_out.shape
     t_row = lax.broadcasted_iota(jnp.int32, (t_rows, width), 0)
     t_col = lax.broadcasted_iota(jnp.int32, (t_rows, width), 1)
-    table_out[...] = exact(jnp.where(t_col == t_row + dp * t_rows, 1.0, 0.0), small[16:24], ((1,), (1,)))[:, :heads]
+    table_out[...] = exact(small[16:24], jnp.where(t_col == t_row + dp * t_rows, 1.0, 0.0), ((1,), (1,)))[:heads]
     for copy in w_copies:
         copy.wait_recv()
     out_ref[...] = wide[...].astype(F32)
@@ -1169,10 +1167,10 @@
         out_specs=[vmem] * 6,
         out_shape=[
             jax.ShapeDtypeStruct((4, piece, local), F32),
-            jax.ShapeDtypeStruct((piece, experts_n), F32),
+            jax.ShapeDtypeStruct((experts_n, piece), F32),
             jax.ShapeDtypeStruct((1, piece), F32),
             jax.ShapeDtypeStruct((1, piece), F32),
-            jax.ShapeDtypeStruct((table_rows, heads), F32),
+            jax.ShapeDtypeStruct((heads, table_rows), F32),
             jax.ShapeDtypeStruct(x.shape, F32),
         ],
         scratch_shapes=[
@@ -1202,7 +1200,7 @@
 
 def front_kernel(
     seqs, groups, cap,
-    pair_ref, got_ref, cot_ref, q_ref, k_ref, v_ref, win_ref, idq_ref, idk_ref, x_ref, wout_ref, gain_ref, router_ref,
+    ein_ref, eot_ref, got_ref, cot_ref, q_ref, k_ref, v_ref, win_ref, idq_ref, idk_ref, x_ref, wout_ref, gain_ref, router_ref,
     hits_ref, place_ref,
     near_out, far_out, cot_out, row_out, gate_out, bias_ref, att_ref, lse_ref, mid_ref, moe_ref, gates_ref, send_ref, slot_ref,
     wout_other, att_other, mask_ref, w_sems, x_sems, z_sems, r_sems, g_sems, own_sems,
@@ -1215,7 +1213,8 @@
     local = q_ref.shape[2]
     pairs = local // (2 * HD)
     far_copies = [
-        remote(pair_ref.at[tp], near_out, w_sems.at[0, 2], w_sems.at[1, 2], ctx=ctx ^ 2),
+        remote(ein_ref.at[tp], near_out.at[0], w_sems.at[0, 2], w_sems.at[1, 2], ctx=ctx ^ 2),
+        remote(eot_ref.at[tp], near_out.at[1], w_sems.at[0, 3], w_sems.at[1, 3], ctx=ctx ^ 2),
         remote(got_ref, far_out, w_sems.at[0, 0], w_sems.at[1, 0], ctx=ctx ^ 2),
     ]
     wout_copy = remote(wout_ref, wout_other, w_sems.at[0, 1], w_sems.at[1, 1], tp=tp ^ 1)
@@ -1284,7 +1283,7 @@
 
     def middle(s):
         att_copy(s).wait_recv()
-        mid = x_ref[s].astype(F32) + (dot(att_ref[s], wout_ref[...]) + dot(att_other[s], wout_other[...]))
+        mid = x_ref[s].astype(F32) + (dot_nt(att_ref[s], wout_ref[...]) + dot_nt(att_other[s], wout_other[...]))
         mid_ref[s] = mid
         moe_in = (mid * norm_factor(mid) * gain_ref[...].astype(F32)).astype(BF16)
         moe_ref[s] = moe_in
@@ -1337,7 +1336,7 @@
         att_copy(s).wait_send()
 
 
-def front_stage(pair, got, cot, q, k, v, windows, ids_query, ids_key, x, wout, gain, router, hits, places, cap):
+def front_stage(w_in, w_out, got, cot, q, k, v, windows, ids_query, ids_key, x, wout, gain, router, hits, places, cap):
     seqs, stretch, width = x.shape
     groups = places.shape[1]
     local = q.shape[2]
@@ -1350,7 +1349,7 @@
     return pl.pallas_call(
         functools.partial(front_kernel, seqs, groups, cap),
         name="front_stage",
-        in_specs=[any_spec] * 3 + [vmem] * 12,
+        in_specs=[any_spec] * 4 + [vmem] * 12,
         out_specs=[any_spec] * 4 + [vmem] * 9,
         out_shape=[
             jax.ShapeDtypeStruct(got.shape, BF16),
@@ -1368,15 +1367,15 @@
             jax.ShapeDtypeStruct((seqs, groups, 1, cap), F32),
         ],
         scratch_shapes=[
-            pltpu.VMEM((local, width), BF16),
+            pltpu.VMEM((width, local), BF16),
             pltpu.VMEM((seqs, stretch, local), BF16),
             pltpu.VMEM((length, stretch), F32),
-            dma((2, 3)), dma((2, seqs)), dma((2, seqs - FIRST, groups - 1)), dma((2, groups - 1)), dma((2, groups - 1)),
+            dma((2, 4)), dma((2, seqs)), dma((2, seqs - FIRST, groups - 1)), dma((2, groups - 1)), dma((2, groups - 1)),
             dma((2,)),
         ],
         compiler_params=pltpu.CompilerParams(vmem_limit_bytes=VMEM_BYTES, collective_id=4, has_side_effects=True),
         cost_estimate=cost(4 * 10**10, 10**7),
-    )(pair, got, cot, q, k, v, windows, ids_query, ids_key, x, wout, gain, router, hits, places)
+    )(w_in, w_out, got, cot, q, k, v, windows, ids_query, ids_key, x, wout, gain, router, hits, places)
 
 
 def moe_kernel(
@@ -1384,14 +1383,15 @@
 ):
     send_ref, slot_ref, row_ref, gate_ref, slots_ref, cot_ref, last_ref = refs[:7]
     refs = refs[7:]
-    w_own, w_far, part_out, din_back, h_back, keep_out, give_out = (refs[:2], refs[2:4]) + refs[4:9]
+    ein_ref, eot_ref, got_ref, near_ref, far_ref, part_out, din_back, h_back, keep_out, give_out = refs[:10]
     (
         w_all, x_all, gate_all, g_all, xt_all, dyt_all, dy_ref, hid_all, dpre_all, part_acc, din_acc,
         part_all, din_all, h_all, tile_ref,
         x_sems, gate_sems, din_sems, h_sems, w_sems, own_sems, cot_sems, part_sems, out_sems, core_sems,
-    ) = refs[9:]
+    ) = refs[10:]
     dp = lax.axis_index("dp")
     ctx = lax.axis_index("ctx")
+    tp = lax.axis_index("tp")
     greet([{"dp": dp ^ b} for b in range(1, groups)] + [{"ctx": ctx ^ 1}])
     width = x_all.shape[-1]
     rows = groups * cap
@@ -1417,13 +1417,17 @@
     w_copies = []
     local = []
     arrivals = []
-    for half in range(2):
-        for index, (ref, place) in enumerate(((w_own[half], ctx), (w_far[half], ctx ^ 2))):
-            sems = (w_sems.at[0, half, index], w_sems.at[1, half, index])
-            w_copies.append(remote(ref, w_all.at[:, half, place], *sems, ctx=ctx ^ 1))
-            there = w_all.at[:, half, place ^ 1]
-            arrivals.append(remote(there, there, *sems, ctx=ctx ^ 1))
-            local.append(pltpu.make_async_copy(ref, w_all.at[:, half, place], w_sems.at[2, half, index]))
+    both = slice(None)
+    sources = (
+        (ein_ref.at[tp], 0, 0, ctx), (eot_ref.at[tp], 1, 0, ctx), (near_ref, both, 0, ctx ^ 2),
+        (got_ref, both, 1, ctx), (far_ref, both, 1, ctx ^ 2),
+    )
+    for index, (ref, io, half, place) in enumerate(sources):
+        here = w_all.at[io, half, place]
+        there = w_all.at[io, half, place ^ 1]
+        w_copies.append(remote(ref, here, w_sems.at[0, index], w_sems.at[1, index], ctx=ctx ^ 1))
+        arrivals.append(remote(there, there, w_sems.at[0, index], w_sems.at[1, index], ctx=ctx ^ 1))
+        local.append(pltpu.make_async_copy(ref, here, w_sems.at[2, index]))
     for copy in w_copies + sent:
         copy.start()
     local.append(pltpu.make_async_copy(row_ref, x_all.at[0], own_sems.at[0]))
@@ -1578,9 +1582,9 @@
         copy.wait_send()
 
 
-def moe_stage(send, slot_gate, row, row_gate, slots, cot, last, keep, got, far_keep, far_got, tile=512):
+def moe_stage(send, slot_gate, row, row_gate, slots, cot, last, w_in, w_out, got, far_keep, far_got, tile=512):
     seqs, groups, cap, width = send.shape
-    _, piece, half_len = keep.shape
+    _, piece, half_len = got.shape
     halves = 2
     slices = width // piece
     tiles = halves * half_len // tile
@@ -1591,7 +1595,7 @@
     return pl.pallas_call(
         functools.partial(moe_kernel, seqs, groups, cap, tile),
         name="moe_stage",
-        in_specs=[any_spec] * 11,
+        in_specs=[any_spec] * 12,
         out_specs=[any_spec, any_spec, vmem, any_spec, any_spec],
         out_shape=[
             jax.ShapeDtypeStruct((groups, seqs, cap, width), BF16),
@@ -1617,14 +1621,14 @@
             pltpu.VMEM((seqs, groups, 1, cap), F32),
             pltpu.VMEM((2, 2, slices // 2, 2, piece, tile), BF16),
             dma((2, seqs, groups - 1)), dma((2, seqs, groups - 1)), dma((2, seqs, groups - 1)),
-            dma((2, seqs, groups - 1)), dma((3, 2, 2)), dma((2 * seqs,)), dma((2, groups)), dma((seqs, groups + 2)),
+            dma((2, seqs, groups - 1)), dma((3, 5)), dma((2 * seqs,)), dma((2, groups)), dma((seqs, groups + 2)),
             dma((2, 2)), dma((tiles,)),
         ],
         compiler_params=pltpu.CompilerParams(
             vmem_limit_bytes=63 * 1024 * 1024, collective_id=2, has_side_effects=True
         ),
         cost_estimate=cost(20 * seqs * rows * width * halves * half_len, 40 * width * halves * half_len),
-    )(send, slot_gate, row, row_gate, slots, cot, last, keep, got, far_keep, far_got)
+    )(send, slot_gate, row, row_gate, slots, cot, last, w_in, w_out, got, far_keep, far_got)
 
 
 def flip(value, axis, bit):
@@ -1687,7 +1691,7 @@
     ranks = jnp.einsum("set,tu->seu", hits.astype(BF16), before, preferred_element_type=F32)
     places = jnp.where(hits > 0.5, ranks, -1.0)[:, :dp]
 
-    pair = jnp.stack([w_expert_in[0], w_expert_out[0].transpose(0, 2, 1)], axis=1)
+    w_in, w_out = w_expert_in[0], w_expert_out[0].transpose(0, 2, 1)
 
     if fits:
         me = lax.axis_index("dp")
@@ -1696,10 +1700,9 @@
             queries, keys, values, own_normed, wqkv, wout_own, table, gain_attn, gain_moe, router, got,
             cot_slots, cot_in,
         ) = first_stage(
-            tokens_in, w_qkv[0], w_attn_out[0], bias_table[0], attn_gain, moe_gain, w_router[0], pair,
+            tokens_in, w_qkv[0], w_attn_out[0].T, bias_table[0], attn_gain, moe_gain, w_router[0].T, w_in, w_out,
             near_places, cotangent, cap,
         )
-        keep = lax.dynamic_index_in_dim(pair, tp, 0, keepdims=False)
         table = table.reshape(NB, heads)
         keys = keys.reshape(seqs, 4 * stretch, local)
         values = values.reshape(seqs, 4 * stretch, local)
@@ -1708,6 +1711,7 @@
         queries, keys, values, own_normed, wqkv, wout_own, table, gain_attn, gain_moe, router = gathered(
             tokens_in, w_qkv[0], w_attn_out[0], bias_table[0], attn_gain, moe_gain, w_router[0]
         )
+        pair = jnp.stack([w_in, w_out], axis=1)
         keep = lax.dynamic_index_in_dim(pair, tp, 0, keepdims=False)
         got = flip(lax.dynamic_index_in_dim(pair, 1 - tp, 0, keepdims=False), "tp", 1)
         weights = lax.all_gather(jnp.stack([keep, got], axis=1), "ctx", axis=0, tiled=False)
@@ -1733,11 +1737,11 @@
         (
             far_keep, far_got, cot_last, row, row_gate, bias, attended, lse, mids, moes, gates, send, slot_gate,
         ) = front_stage(
-            pair, got, cot_slots, queries, keys, values, windows, ids_query, ids_key, tokens_in, wout_own, gain_moe, router,
+            w_in, w_out, got, cot_slots, queries, keys, values, windows, ids_query, ids_key, tokens_in, wout_own, gain_moe, router,
             hits, places, cap,
         )
         parts, returned_din, returned_h, kept, given = moe_stage(
-            send, slot_gate, row, row_gate, cot_slots, cot_in, cot_last, keep, got, far_keep, far_got
+            send, slot_gate, row, row_gate, cot_slots, cot_in, cot_last, w_in, w_out, got, far_keep, far_got
         )
     else:
         bias = expand_bias(windows)
@@ -1800,6 +1804,7 @@
         other, far_mine, wide = lax.optimization_barrier((other, far_mine, wide))
         g_qkv = wide[:3]
         g_wout = wide[3].T
+        g_router, g_table = g_router.T, g_table.T
     else:
         far_mine = flip(far_send, "ctx", 2)
         other = flip(summed(1, far_other).astype(BF16), "tp", 1)

time: 382 us -> 365 us (0.955)
  Pallas kernels: 338 us -> 329 us
  other arithmetic: 20.6 us -> 16.1 us
  local copies, waits for them, and re-layouts: 17.9 us -> 13.7 us
    pallas_call x1, Pallas kernels: 65.2 us -> 56.3 us  [first_stage(): pl.pallas_call(functools.partial(first_kernel, seqs, cap), name='first_st...]
    unnamed x49 -> x45, local copies, waits for them, and re-layouts: 10.8 us -> 6.63 us
  transfers between devices with their start and end apart: 3 -> 3, of which waited for: 0 -> 0; matrix products, arithmetic and copies ran while one was open for 1% -> 1% of each run, Pallas kernels for 32% -> 34%
where the time goes in v6:
time: 365 us; the launch traced here: 364 us
  Pallas kernels  329 us (90%)
  other arithmetic  16.1 us (4%)
  local copies, waits for them, and re-layouts  13.7 us (4%)
    pallas_call x1, Pallas kernels, moe_stage(): pl.pallas_call(functools.partial(moe_kernel, seqs, groups, cap, tile), na...  88.7 us
    pallas_call x1, Pallas kernels, back_stage(): pl.pallas_call(functools.partial(back_kernel, seqs, groups, cap), name='b...  67.4 us
    pallas_call x1, Pallas kernels, front_stage(): pl.pallas_call(functools.partial(front_kernel, seqs, groups, cap), name='...  61.2 us
    pallas_call x1, Pallas kernels, first_stage(): pl.pallas_call(functools.partial(first_kernel, seqs, cap), name='first_st...  56.3 us
    pallas_call x1, Pallas kernels, last_stage(): pl.pallas_call(last_kernel, name='last_stage', in_specs=[vmem] * 9, out_s...  55.8 us
  transfers between devices with their start and end apart: 3, of which 0 were waited for; matrix products, arithmetic and copies ran while one was open for 1% of the time, Pallas kernels for 34%

profile of v6, /device:TPU:0, one launch (start us, length us, event | category | flops | bytes accessed | tf_op | source)
XLA Modules:
  0.0 364.2 jit_solution(6360825203288802231)
XLA Ops:
  0.7 0.1 eq.51
  0.8 0.8 fusion.21
  1.6 0.1 or_convert_fusion.hits_ref
  1.7 0.2 fusion.6
  1.9 0.7 reshape.151
  2.6 0.6 fusion.16
  3.2 0.6 convert_element_type.108.idk_ref.refs_16_
  3.8 0.7 fusion.5
  4.6 0.0 copy-start.12
  4.7 0.6 pad_maximum_fusion.3.near_ref.refs_14_
  5.3 0.0 copy-start.3
  5.3 0.0 copy-start.5
  5.3 0.0 copy-start.7
  5.3 0.0 copy-start.9
  5.3 56.3 %first_stage.1 = (bf16[3,256,384]{2,1,0:T(8,128)(2,1)}, bf16[3,4,256,384]{3,2,1,0:T(8,128)(2,1)}, bf16[3,4,256,384]{3,2,1,0:T(8,128)(2,1)}, bf16[3,256,768]{2,1,...) custom-call(bf16[3,256,768]{2,1,0:T(8,128)(2,1)} %x_ref.3, ...), custom_call_target="tpu_custom_call" | custom-call | flops 40000000000 | bytes 10000000 | tf_op jit(solution)/shard_map/first_stage/pallas_call | solution.py:705
  61.7 0.0 copy-done.11
  61.7 0.0 copy-done.12
  61.7 0.0 copy-done.3
  61.7 0.0 copy-done.5
  61.7 0.0 copy-done.7
  61.7 0.0 copy-done.9
  61.7 0.9 fusion.8
  62.7 0.7 copy.29.win_ref
  63.3 61.2 %front_stage.1 = (bf16[2,192,1536]{2,1,0:T(8,128)(2,1)}, bf16[2,192,1536]{2,1,0:T(8,128)(2,1)}, bf16[3,2,128,768]{3,2,1,0:T(8,128)(2,1)}, bf16[4,128,768]{2,1,0:...) custom-call(bf16[2,192,1536]{2,1,0:T(8,128)(2,1)} %bitcast.80, ...), custom_call_target="tpu_custom_call" | custom-call | flops 40000000000 | bytes 10000000 | tf_op jit(solution)/shard_map/front_stage/pallas_call | solution.py:1349
  124.5 88.7 %moe_stage.1 = (bf16[4,3,128,768]{3,2,1,0:T(8,128)(2,1)}, bf16[3,4,128,768]{3,2,1,0:T(8,128)(2,1)}, f32[3,4,1,128]{3,2,1,0:T(1,128)}, bf16[2,2,2,192,1536]{4,3,2,1,0:T(8,128)(2,1)}, bf16[2,2,2,192,1536]{4,3,2,1,0:T(8,128)(2,1)}) custom-call(bf16[3,4,128,768]{3,2,1,0:T(8,128)(2,1)} %get-tuple-element.73.refs_0_, f32[3,4,1,128]{3,2,1,0:T(1,128)} %get-tuple-element.74.refs_1_, ...), custom_call_target="tpu_custom_call" | custom-call | flops 72477573120 | bytes 94371840 | tf_op jit(solution)/shard_map/moe_stage/pallas_call | solution.py:1595
  213.2 4.4 %fusion.3 = (bf16[2,192,1536]{2,1,0:T(8,128)(2,1)}, bf16[2,192,1536]{2,1,0:T(8,128)(2,1)}) fusion(bf16[2,2,2,192,1536]{4,3,2,1,0:T(8,128)(2,1)} %get-tuple-element.88, bf16[2,2,2,192,1536]{4,3,2,1,0:T(8,128)(2,1)} %get-tuple-element.87), kind=kLoop, calls=%fused_computation.9 | loop fusion | flops 4718592 | bytes 7077888 | tf_op jit(solution)/shard_map/convert_element_type | solution.py:1775
  217.6 1.3 collective-permute-start
  218.9 67.4 %back_stage.1 = (bf16[3,256,768]{2,1,0:T(8,128)(2,1)}, f32[3,256,768]{2,1,0:T(8,128)}, bf16[3,256,768]{2,1,0:T(8,128)(2,1)}, bf16[3,3,256,384]{3,2,1,0:T(8,128)(...) custom-call(f32[3,256,768]{2,1,0:T(8,128)} %get-tuple-element.69.refs_0_, ...), custom_call_target="tpu_custom_call" | custom-call | flops 60000002048 | bytes 10000000 | tf_op jit(solution)/shard_map/back_stage/pallas_call | solution.py:963
  286.3 0.0 collective-permute-done
  286.4 0.0 copy-start.1
  286.4 0.0 copy-start.4
  286.4 0.0 copy-start.6
  286.4 0.0 copy-start.8
  286.4 0.0 copy-start.10
  286.4 0.0 copy-start.18
  286.4 0.0 copy-start.13
  286.4 0.0 copy-start.15
  286.4 3.5 fusion.1
  290.0 0.6 collective-permute-start.1
  290.5 0.5 collective-permute-start.2
  291.0 0.0 copy-done.4
  291.0 0.0 copy-done.8
  291.1 0.3 convolution_bitcast_fusion
  291.3 0.7 select_maximum_fusion.small_ref
  292.0 55.8 %last_stage.1 = (f32[4,192,384]{2,1,0:T(8,128)}, f32[8,192]{1,0:T(8,128)}, f32[1,192]{1,0:T(1,128)}, f32[1,192]{1,0:T(1,128)}, f32[6,8]{1,0:T(8,128)}, /*index=5*/f32[3,256,768]{2,1,0:T(8,128)}) custom-call(bf16[768,768]{1,0:T(8,128)(2,1)} %bitcast.74, bf16[3,768,384]{2,1,0:T(8,128)(2,1)} %bitcast.73, bf16[768,768]{1,0:T(8,128)(2,1)} %bitcast.75, ...), custom_call_target="tpu_custom_call" | custom-call | flops 1811939328 | bytes 4718592 | tf_op jit(solution)/shard_map/last_stage/pallas_call | solution.py:1163
  347.9 1.3 copy.34
  349.1 0.0 collective-permute-done.1
  349.1 0.0 collective-permute-done.2
  349.1 1.7 slice_bitcast_fusion.3
  350.8 2.1 slice_bitcast_fusion.2
  353.0 0.1 slice.78
  353.1 0.3 convert_element_type.107
  353.4 2.1 bitcast_add_fusion
  355.5 0.2 fusion.20
  355.6 0.1 slice_bitcast_fusion
  355.7 1.6 fusion
  357.3 1.6 maximum_select_fusion
  358.9 0.1 copy-done.2
  358.9 1.0 copy.50
  360.0 1.1 copy-done
  361.0 1.4 copy.51
  362.4 0.6 copy.52
  363.0 0.6 copy.53
  363.6 0.6 copy.54
  (23 shorter events, 0.1 us)
Async XLA Ops:
  1.7 60.0 %copy-start.11 = (f32[3,8,256]{2,1,0:T(8,128)}, f32[3,8,256]{2,1,0:T(8,128)S(1)}, u32[]{:S(2)}) copy-start(f32[3,8,256]{2,1,0:T(8,128)S(1)} %or_convert_fusion.hits_ref) | copy-start | bytes 73732
  4.6 57.1 %copy-start.12 = (f32[3,4,256]{2,1,0:T(4,128)}, f32[3,4,256]{2,1,0:T(4,128)S(1)}, u32[]{:S(2)}) copy-start(f32[3,4,256]{2,1,0:T(4,128)S(1)} %slice_select_fusion.place_ref.refs_13_) | copy-start | bytes 36868
  5.3 56.4 %copy-start.3 = (f32[1,512,32]{1,2,0:T(8,128)}, f32[1,512,32]{1,2,0:T(8,128)S(1)}, u32[]{:S(2)}) copy-start(f32[1,512,32]{1,2,0:T(8,128)S(1)} %get-tuple-element.134) | copy-start | bytes 196612
  5.3 56.4 %copy-start.5 = (f32[1,512,32]{1,2,0:T(8,128)}, f32[1,512,32]{1,2,0:T(8,128)S(1)}, u32[]{:S(2)}) copy-start(f32[1,512,32]{1,2,0:T(8,128)S(1)} %get-tuple-element.135) | copy-start | bytes 196612
  5.3 56.4 %copy-start.7 = (f32[1,512,32]{1,2,0:T(8,128)}, f32[1,512,32]{1,2,0:T(8,128)S(1)}, u32[]{:S(2)}) copy-start(f32[1,512,32]{1,2,0:T(8,128)S(1)} %get-tuple-element.136) | copy-start | bytes 196612
  5.3 56.4 %copy-start.9 = (f32[1,512,32]{1,2,0:T(8,128)}, f32[1,512,32]{1,2,0:T(8,128)S(1)}, u32[]{:S(2)}) copy-start(f32[1,512,32]{1,2,0:T(8,128)S(1)} %get-tuple-element.137) | copy-start | bytes 196612
  217.6 68.7 %collective-permute-start = (bf16[2,192,1536]{2,1,0:T(8,128)(2,1)}, bf16[2,192,1536]{2,1,0:T(8,128)(2,1)}, u32[]{:S(2)}, u32[]{:S(2)}) collective-permute-start(bf16[2,192,1536]{2,1,0:T(8,128)(2,1)} %get-tuple-element.131), channel_id=1, source_target_pairs={{0,4},{2,6},{4,0},{6,2},{1,5},{3,7},{5,1},{7,3},{8,12},{10,14},{12... | collective-permute-start | bytes 3538952 | tf_op jit(solution)/shard_map/ppermute | solution.py:1636
  286.4 4.2 %copy-start.1 = (bf16[2,192,1536]{2,1,0:T(8,128)(2,1)S(1)}, bf16[2,192,1536]{2,1,0:T(8,128)(2,1)}, u32[]{:S(2)}) copy-start(bf16[2,192,1536]{2,1,0:T(8,128)(2,1)} %get-tuple-element.102) | copy-start | bytes 3538948
  286.4 4.7 %copy-start.4 = (f32[1,512,32]{1,2,0:T(8,128)S(1)}, f32[1,512,32]{1,2,0:T(8,128)}, u32[]{:S(2)}) copy-start(f32[1,512,32]{1,2,0:T(8,128)} %copy-done.3) | copy-start | bytes 196612
  286.4 4.7 %copy-start.6 = (f32[1,512,32]{1,2,0:T(8,128)S(1)}, f32[1,512,32]{1,2,0:T(8,128)}, u32[]{:S(2)}) copy-start(f32[1,512,32]{1,2,0:T(8,128)} %copy-done.5) | copy-start | bytes 196612
  286.4 4.7 %copy-start.8 = (f32[1,512,32]{1,2,0:T(8,128)S(1)}, f32[1,512,32]{1,2,0:T(8,128)}, u32[]{:S(2)}) copy-start(f32[1,512,32]{1,2,0:T(8,128)} %copy-done.7) | copy-start | bytes 196612
  286.4 4.6 %copy-start.10 = (f32[1,512,32]{1,2,0:T(8,128)S(1)}, f32[1,512,32]{1,2,0:T(8,128)}, u32[]{:S(2)}) copy-start(f32[1,512,32]{1,2,0:T(8,128)} %copy-done.9) | copy-start | bytes 196612
  286.4 4.6 %copy-start.18 = (f32[3,2,4,512]{3,2,1,0:T(4,128)S(1)}, f32[3,2,4,512]{3,2,1,0:T(4,128)}, u32[]{:S(2)}) copy-start(f32[3,2,4,512]{3,2,1,0:T(4,128)} %get-tuple-element.95) | copy-start | bytes 147460
  286.4 4.9 %copy-start.13 = (f32[8,768]{1,0:T(8,128)S(1)}, f32[8,768]{1,0:T(8,128)}, u32[]{:S(2)}) copy-start(f32[8,768]{1,0:T(8,128)} %get-tuple-element.93) | copy-start | bytes 73732
  286.4 4.9 %copy-start.15 = (f32[1,768]{1,0:T(1,128)S(1)}, f32[1,768]{1,0:T(1,128)}, u32[]{:S(2)}) copy-start(f32[1,768]{1,0:T(1,128)} %get-tuple-element.94) | copy-start | bytes 9220
  290.0 59.2 %collective-permute-start.1 = (bf16[2,192,1536]{2,1,0:T(8,128)(2,1)}, bf16[2,192,1536]{2,1,0:T(8,128)(2,1)S(1)}, u32[]{:S(2)}, u32[]{:S(2)}) collective-permute-start(bf16[2,192,1536]{2,1,0:T(8,128)(2,1)} %fusion.1), channel_id=1, source_target_pairs={{0,1},{1,0},{2,3},{3,2},{4,5},{5,4},{6,7},{7,6},{8,9},{9,8},{10,11... | collective-permute-start | bytes 3538952 | tf_op jit(solution)/shard_map/ppermute | solution.py:1636
  290.5 58.6 %collective-permute-start.2 = (bf16[2,192,1536]{2,1,0:T(8,128)(2,1)S(1)}, bf16[2,192,1536]{2,1,0:T(8,128)(2,1)S(1)}, u32[]{:S(2)}, u32[]{:S(2)}) collective-permute-start(bf16[2,192,1536]{2,1,0:T(8,128)(2,1)S(1)} %copy-done.1), channel_id=1, source_target_pairs={{0,4},{2,6},{4,0},{6,2},{1,5},{3,7},{5,1},{7,3},{8,12},{10,14},{12... | collective-permute-start | bytes 3538952 | tf_op jit(solution)/shard_map/ppermute | solution.py:1636
  357.3 1.6 copy-start.2
  358.9 2.1 copy-start
  361.0 1.4 copy-start.17
  361.0 2.0 copy-start.16
  361.0 2.5 copy-start.14
